TPU v7x, 32 devices: a whole 2x2x4 slice. The times are simulated.
32 devices in a mesh: head: 4 (over y, x), seq: 8 (over z, core).
Axes of the slice: x: 2, y: 2, z: 4, core: 2. Of those that a mesh axis runs over, the one named last changes fastest.
Arguments:
- tokens: bfloat16 [4, 2048, 1024], P('head', 'seq'), may hold values from -6 to 6
- doc_ids: int32 [4, 2048], P('head', 'seq'), may hold values from 0 to 7, never falling along the last dimension, each value on 1 to 512 neighbouring positions
- query_weight: bfloat16 [1024, 256], P('seq', 'head'), may hold values from -0.1875 to 0.1875
- key_weight: bfloat16 [1024, 256], P('seq', 'head'), may hold values from -0.1875 to 0.1875
- value_weight: bfloat16 [1024, 1024], P('seq', 'head'), may hold values from -0.1875 to 0.1875
- out_weight: bfloat16 [1024, 1024], P('head', 'seq'), may hold values from -2 to 2
- gate_weight: bfloat16 [1024, 2752], P('seq', 'head'), may hold values from -0.1875 to 0.1875
- up_weight: bfloat16 [1024, 2752], P('seq', 'head'), may hold values from -0.1875 to 0.1875
- down_weight: bfloat16 [2752, 1024], P('head', 'seq'), may hold values from -0.109375 to 0.109375
- mix_gain: bfloat16 [1024], P(('head', 'seq')), may hold values from 0.25 to 1.75
- mlp_gain: bfloat16 [1024], P(('head', 'seq')), may hold values from 0.25 to 1.75
- cotangent: bfloat16 [4, 2048, 1024], P('head', 'seq'), may hold values from -6 to 6
Outputs:
- output: bfloat16 [4, 2048, 1024], P('head', 'seq')
- grad_tokens: float32 [4, 2048, 1024], P('head', 'seq')
- grad_query: float32 [1024, 256], P('seq', 'head')
- grad_key: float32 [1024, 256], P('seq', 'head')
- grad_value: float32 [1024, 1024], P('seq', 'head')
- grad_out: float32 [1024, 1024], P('head', 'seq')
- grad_gate: float32 [1024, 2752], P('seq', 'head')
- grad_up: float32 [1024, 2752], P('seq', 'head')
- grad_down: float32 [2752, 1024], P('head', 'seq')
- grad_mixgain: float32 [1024], P(('head', 'seq'))
- grad_mlpgain: float32 [1024], P(('head', 'seq'))
Inputs may be any that keep to these rules, and one draw needn't show every extreme that they name: `doc_ids`: within each sequence the document numbers never fall; no document is longer than 512 positions, and in each sequence one is exactly that long.
All inputs are finite; a program needn't handle non-finite values.
Results may differ from a plain program's by a relative error of at most 0.019.
Values may be sent and summed in bfloat16 or wider, within the bound.
No kernel may reach another device: no remote copies, remote signals or barrier semaphores. Data moves between devices by JAX's collectives and lax.ppermute only.
A program may use at most 320 MiB of HBM per device.

v0:
```python
import jax
import jax.numpy as jnp
from jax import lax
from jax.sharding import PartitionSpec as P

FDIM = 16
VDIM = 64


EPS = 1e-06
ROOT_HALF = 0.7071067811865476
HIGH = lax.Precision.HIGHEST
LABEL_FAR = 1000000000.0


def carried_in(value, axis, join, neutral):
    count, mine = (lax.axis_size(axis), lax.axis_index(axis))
    pieces = jax.tree.map(lambda part: lax.all_gather(part, axis), value)
    total = jax.tree.map(
        lambda part, zero: jnp.full_like(part, 0) + jnp.asarray(zero, part.dtype), value, neutral
    )

    def lap(position, total):
        longer = join(total, jax.tree.map(lambda part: part[position], pieces))
        return jax.tree.map(lambda new, old: jnp.where(position < mine, new, old), longer, total)

    return lax.fori_loop(0, count - 1, lap, total)


def carried_in_2(value, axis, combine, identity):
    length, place = (lax.axis_size(axis), lax.axis_index(axis))
    everything = jax.tree.map(
        lambda part, kind: lax.all_gather(part.astype(kind), axis),
        value,
        jax.tree.map(lambda a: jnp.bfloat16 if a.dtype == jnp.float32 else a.dtype, value),
    )
    start = jax.tree.map(
        lambda part, zero: jnp.broadcast_to(jnp.asarray(zero, part.dtype), part.shape),
        value,
        identity,
    )

    def lap(k, before):
        at = length - 1 - k
        reached = at > place
        new = combine(
            before, jax.tree.map(lambda part, own: part[at].astype(own.dtype), everything, value)
        )
        return jax.tree.map(lambda a, b: jnp.where(reached, a, b), new, before)

    return lax.fori_loop(0, length, lap, start)


def features(values):
    width = values.shape[-1]
    half = values * 0.5
    lead = values.shape[:-1]
    square = (half[..., :, None] * half[..., None, :]).reshape(lead + (width * width,)) * ROOT_HALF
    return jnp.concatenate([jnp.ones(lead + (1,), jnp.float32), half, square], axis=-1)


def features_back(values, grad):
    width = values.shape[-1]
    half = values * 0.5
    linear = grad[..., 1 : 1 + width]
    square = grad[..., 1 + width :].reshape(grad.shape[:-1] + (width, width))
    paired = (square + jnp.swapaxes(square, -1, -2)) * ROOT_HALF
    return (linear + jnp.einsum("...ij,...j->...i", paired, half, precision=HIGH)) * 0.5


def normalize(values, gain):
    scale = lax.rsqrt(jnp.mean(values * values, axis=-1, keepdims=True) + EPS)
    normed = values * scale
    return (normed, scale, (normed * gain).astype(jnp.bfloat16))


def normalize_back(grad, normed, scale, gain):
    grad_normed = grad * gain
    inner = jnp.mean(grad_normed * normed, axis=-1, keepdims=True)
    return scale * (grad_normed - normed * inner)


def join_forward(earlier, later):
    state_a, norm_a, label_a = earlier
    state_b, norm_b, label_b = later
    equal = (label_a == label_b)[:, None]
    newer = (label_b > label_a)[:, None]
    state = jnp.where(equal, state_a + state_b, jnp.where(newer, state_b, state_a))
    norm = jnp.where(equal, norm_a + norm_b, jnp.where(newer, norm_b, norm_a))
    return (state, norm, jnp.maximum(label_a, label_b))


def join_backward(earlier, later):
    state_e, norm_e, label_e = earlier
    state_l, norm_l, label_l = later
    equal = (label_e == label_l)[:, None]
    lower = (label_l < label_e)[:, None]
    state = jnp.where(equal, state_l + state_e, jnp.where(lower, state_l, state_e))
    norm = jnp.where(equal, norm_l + norm_e, jnp.where(lower, norm_l, norm_e))
    return (state, norm, jnp.minimum(label_e, label_l))


def attend_forward(queries, keys, values, segment):
    batch, rows, heads, vwidth = values.shape
    scores = jnp.einsum("bihf,bjhf->bhij", queries, keys, preferred_element_type=jnp.float32) * 0.25
    place = jnp.arange(rows)
    causal = place[:, None] >= place[None, :]
    same = segment[:, :, None] == segment[:, None, :]
    mask = (causal[None] & same)[:, None].astype(jnp.float32)
    weights = ((1.0 + scores + 0.5 * scores * scores) * mask).astype(jnp.bfloat16)
    final = segment[:, -1]
    tail = (segment == final[:, None]).astype(jnp.float32)
    phik = features(keys.astype(jnp.float32))
    phiq = features(queries.astype(jnp.float32))
    values_wide = values.astype(jnp.float32)
    size = phik.shape[-1]
    tail_state = jnp.einsum(
        "bjhf,bjhe->bhfe", phik * tail[:, :, None, None], values_wide, precision=HIGH
    )
    tail_norm = jnp.einsum("bjhf,bj->bhf", phik, tail, precision=HIGH)
    empty = (
        jnp.zeros((batch, heads * size * vwidth), jnp.float32),
        jnp.zeros((batch, heads * size), jnp.float32),
        jnp.full((batch,), -1.0, jnp.float32),
    )
    carry_state, carry_norm, carry_label = carried_in(
        (tail_state.reshape(batch, -1), tail_norm.reshape(batch, -1), final.astype(jnp.float32)),
        "seq",
        join_forward,
        empty,
    )
    carry_state = carry_state.reshape(batch, heads, size, vwidth)
    carry_norm = carry_norm.reshape(batch, heads, size)
    live = (segment.astype(jnp.float32) == carry_label[:, None]).astype(jnp.float32)
    numer = jnp.einsum("bhij,bjhe->bihe", weights, values, preferred_element_type=jnp.float32)
    numer = numer + live[:, :, None, None] * jnp.einsum(
        "bihf,bhfe->bihe", phiq, carry_state, precision=HIGH
    )
    denom = jnp.swapaxes(jnp.sum(weights.astype(jnp.float32), axis=-1), 1, 2)
    denom = denom + live[:, :, None] * jnp.einsum("bihf,bhf->bih", phiq, carry_norm, precision=HIGH)
    mixed = (numer / denom[..., None]).astype(jnp.bfloat16)
    kept = (
        scores,
        mask,
        weights,
        phiq,
        phik,
        tail,
        live,
        carry_state,
        carry_norm,
        carry_label,
        numer,
        denom,
    )
    return (mixed, kept)


def attend_backward(queries, keys, values, kept, grad_mixed):
    (
        scores,
        mask,
        weights,
        phiq,
        phik,
        tail,
        live,
        carry_state,
        carry_norm,
        carry_label,
        numer,
        denom,
    ) = kept
    batch, rows, heads, vwidth = values.shape
    size = phik.shape[-1]
    grad_wide = grad_mixed.astype(jnp.float32)
    grad_denom = -jnp.sum(grad_wide * numer, axis=-1) / (denom * denom)
    grad_numer = (grad_wide / denom[..., None]).astype(jnp.bfloat16)
    numer_wide = grad_numer.astype(jnp.float32)
    grad_weights = jnp.einsum(
        "bihe,bjhe->bhij", grad_numer, values, preferred_element_type=jnp.float32
    )
    grad_weights = grad_weights + jnp.swapaxes(grad_denom, 1, 2)[..., None]
    grad_scores = (grad_weights * mask * (1.0 + scores)).astype(jnp.bfloat16)
    grad_queries = (
        jnp.einsum("bhij,bjhf->bihf", grad_scores, keys, preferred_element_type=jnp.float32) * 0.25
    )
    grad_keys = (
        jnp.einsum("bhij,bihf->bjhf", grad_scores, queries, preferred_element_type=jnp.float32)
        * 0.25
    )
    grad_values = jnp.einsum(
        "bhij,bihe->bjhe", weights, grad_numer, preferred_element_type=jnp.float32
    )
    live_phiq = phiq * live[:, :, None, None]
    grad_phiq = live[:, :, None, None] * (
        jnp.einsum("bihe,bhfe->bihf", numer_wide, carry_state, precision=HIGH)
        + grad_denom[..., None] * carry_norm[:, None]
    )
    grad_state = jnp.einsum("bihf,bihe->bhfe", live_phiq, numer_wide, precision=HIGH)
    grad_norm = jnp.einsum("bihf,bih->bhf", live_phiq, grad_denom, precision=HIGH)
    empty = (
        jnp.zeros((batch, heads * size * vwidth), jnp.float32),
        jnp.zeros((batch, heads * size), jnp.float32),
        jnp.full((batch,), LABEL_FAR, jnp.float32),
    )
    back_state, back_norm, _ = carried_in_2(
        (grad_state.reshape(batch, -1), grad_norm.reshape(batch, -1), carry_label),
        "seq",
        join_backward,
        empty,
    )
    back_state = back_state.reshape(batch, heads, size, vwidth)
    back_norm = back_norm.reshape(batch, heads, size)
    values_wide = values.astype(jnp.float32)
    grad_phik = tail[:, :, None, None] * (
        jnp.einsum("bjhe,bhfe->bjhf", values_wide, back_state, precision=HIGH) + back_norm[:, None]
    )
    grad_values = grad_values + tail[:, :, None, None] * jnp.einsum(
        "bjhf,bhfe->bjhe", phik, back_state, precision=HIGH
    )
    grad_queries = grad_queries + features_back(queries.astype(jnp.float32), grad_phiq)
    grad_keys = grad_keys + features_back(keys.astype(jnp.float32), grad_phik)
    return (
        grad_queries.astype(jnp.bfloat16),
        grad_keys.astype(jnp.bfloat16),
        grad_values.astype(jnp.bfloat16),
    )


def on_device(
    tokens,
    doc_ids,
    query_weight,
    key_weight,
    value_weight,
    out_weight,
    gate_weight,
    up_weight,
    down_weight,
    mix_gain,
    mlp_gain,
    cotangent,
):
    gain_mix, gain_mlp = (
        lax.all_gather(mix_gain, ("head", "seq"), axis=0, tiled=True),
        lax.all_gather(mlp_gain, ("head", "seq"), axis=0, tiled=True),
    )
    gain_first = gain_mix.astype(jnp.float32)
    gain_second = gain_mlp.astype(jnp.float32)
    pieces = (
        query_weight,
        key_weight,
        value_weight,
        out_weight,
        gate_weight,
        up_weight,
        down_weight,
    )
    pieces = (
        lax.all_gather(query_weight, "head", axis=1, tiled=True),
        lax.all_gather(key_weight, "head", axis=1, tiled=True),
        lax.all_gather(value_weight, "head", axis=1, tiled=True),
        lax.all_gather(out_weight, "head", axis=0, tiled=True),
        lax.all_gather(gate_weight, "head", axis=1, tiled=True),
        lax.all_gather(up_weight, "head", axis=1, tiled=True),
        lax.all_gather(down_weight, "head", axis=0, tiled=True),
    )
    query_full, key_full, value_full, out_full, gate_full, up_full, down_full = (
        lax.all_gather(pieces[0], "seq", axis=0, tiled=True),
        lax.all_gather(pieces[1], "seq", axis=0, tiled=True),
        lax.all_gather(pieces[2], "seq", axis=0, tiled=True),
        lax.all_gather(pieces[3], "seq", axis=1, tiled=True),
        lax.all_gather(pieces[4], "seq", axis=0, tiled=True),
        lax.all_gather(pieces[5], "seq", axis=0, tiled=True),
        lax.all_gather(pieces[6], "seq", axis=1, tiled=True),
    )
    source, source_cot, segment = (tokens, cotangent, doc_ids)
    inputs = source.astype(jnp.float32)
    normed_one, scale_one, inner_one = normalize(inputs, gain_first)
    queries = jnp.einsum(
        "bcd,dh->bch", inner_one, query_full, preferred_element_type=jnp.float32
    ).astype(jnp.bfloat16)
    keys = jnp.einsum(
        "bcd,dh->bch", inner_one, key_full, preferred_element_type=jnp.float32
    ).astype(jnp.bfloat16)
    values = jnp.einsum(
        "bcd,dh->bch", inner_one, value_full, preferred_element_type=jnp.float32
    ).astype(jnp.bfloat16)
    batch, rows = segment.shape
    local_q = queries.reshape(batch, rows, -1, FDIM)
    local_k = keys.reshape(batch, rows, -1, FDIM)
    local_v = values.reshape(batch, rows, -1, VDIM)
    mixed, kept = attend_forward(local_q, local_k, local_v, segment)
    mixed = mixed.reshape(batch, rows, -1)
    branch = jnp.einsum("bce,ed->bcd", mixed, out_full, preferred_element_type=jnp.float32)
    middle = inputs + branch
    normed_two, scale_two, inner_two = normalize(middle, gain_second)
    gate = jnp.einsum("bcd,df->bcf", inner_two, gate_full, preferred_element_type=jnp.float32)
    up = jnp.einsum("bcd,df->bcf", inner_two, up_full, preferred_element_type=jnp.float32)
    active = jax.nn.silu(gate)
    hidden = (active * up).astype(jnp.bfloat16)
    down_part = jnp.einsum("bcf,fd->bcd", hidden, down_full, preferred_element_type=jnp.float32)
    result = middle + down_part
    output = result.astype(jnp.bfloat16)
    grad_down = jnp.einsum("bcf,bcd->fd", hidden, source_cot, preferred_element_type=jnp.float32)
    grad_hidden = jnp.einsum(
        "bcd,fd->bcf", source_cot, down_full, preferred_element_type=jnp.float32
    )
    sigma = jax.nn.sigmoid(gate)
    grad_gatein = (grad_hidden * up * sigma * (1.0 + gate * (1.0 - sigma))).astype(jnp.bfloat16)
    grad_upin = (grad_hidden * active).astype(jnp.bfloat16)
    grad_gate = jnp.einsum(
        "bcd,bcf->df", inner_two, grad_gatein, preferred_element_type=jnp.float32
    )
    grad_up = jnp.einsum("bcd,bcf->df", inner_two, grad_upin, preferred_element_type=jnp.float32)
    grad_inner_two = jnp.einsum(
        "bcf,df->bcd", grad_gatein, gate_full, preferred_element_type=jnp.float32
    )
    grad_inner_two = grad_inner_two + jnp.einsum(
        "bcf,df->bcd", grad_upin, up_full, preferred_element_type=jnp.float32
    )
    grad_mlpgain = jnp.sum(grad_inner_two * normed_two, axis=(0, 1))
    grad_middle = source_cot.astype(jnp.float32) + normalize_back(
        grad_inner_two, normed_two, scale_two, gain_second
    )
    grad_branch = grad_middle.astype(jnp.bfloat16)
    grad_out = jnp.einsum("bce,bcd->ed", mixed, grad_branch, preferred_element_type=jnp.float32)
    grad_mixed = jnp.einsum(
        "bcd,ed->bce", grad_branch, out_full, preferred_element_type=jnp.float32
    ).astype(jnp.bfloat16)
    grad_mixed = grad_mixed.reshape(batch, rows, -1, VDIM)
    grad_q, grad_k, grad_v = attend_backward(local_q, local_k, local_v, kept, grad_mixed)
    grad_q = grad_q.reshape(batch, rows, -1)
    grad_k = grad_k.reshape(batch, rows, -1)
    grad_v = grad_v.reshape(batch, rows, -1)
    grad_query = jnp.einsum("bcd,bch->dh", inner_one, grad_q, preferred_element_type=jnp.float32)
    grad_key = jnp.einsum("bcd,bch->dh", inner_one, grad_k, preferred_element_type=jnp.float32)
    grad_value = jnp.einsum("bcd,bch->dh", inner_one, grad_v, preferred_element_type=jnp.float32)
    grad_inner_one = jnp.einsum(
        "bch,dh->bcd", grad_q, query_full, preferred_element_type=jnp.float32
    )
    grad_inner_one = grad_inner_one + jnp.einsum(
        "bch,dh->bcd", grad_k, key_full, preferred_element_type=jnp.float32
    )
    grad_inner_one = grad_inner_one + jnp.einsum(
        "bch,dh->bcd", grad_v, value_full, preferred_element_type=jnp.float32
    )
    grad_mixgain = jnp.sum(grad_inner_one * normed_one, axis=(0, 1))
    grad_tokens = grad_middle + normalize_back(grad_inner_one, normed_one, scale_one, gain_first)
    summed = (
        lax.psum_scatter(grad_query, "seq", scatter_dimension=0, tiled=True),
        lax.psum_scatter(grad_key, "seq", scatter_dimension=0, tiled=True),
        lax.psum_scatter(grad_value, "seq", scatter_dimension=0, tiled=True),
        lax.psum_scatter(grad_out, "seq", scatter_dimension=1, tiled=True),
        lax.psum_scatter(grad_gate, "seq", scatter_dimension=0, tiled=True),
        lax.psum_scatter(grad_up, "seq", scatter_dimension=0, tiled=True),
        lax.psum_scatter(grad_down, "seq", scatter_dimension=1, tiled=True),
    )
    summed = (
        lax.psum_scatter(
            summed[0].astype(jnp.bfloat16), "head", scatter_dimension=1, tiled=True
        ).astype(jnp.float32),
        lax.psum_scatter(
            summed[1].astype(jnp.bfloat16), "head", scatter_dimension=1, tiled=True
        ).astype(jnp.float32),
        lax.psum_scatter(
            summed[2].astype(jnp.bfloat16), "head", scatter_dimension=1, tiled=True
        ).astype(jnp.float32),
        lax.psum_scatter(
            summed[3].astype(jnp.bfloat16), "head", scatter_dimension=0, tiled=True
        ).astype(jnp.float32),
        lax.psum_scatter(
            summed[4].astype(jnp.bfloat16), "head", scatter_dimension=1, tiled=True
        ).astype(jnp.float32),
        lax.psum_scatter(
            summed[5].astype(jnp.bfloat16), "head", scatter_dimension=1, tiled=True
        ).astype(jnp.float32),
        lax.psum_scatter(
            summed[6].astype(jnp.bfloat16), "head", scatter_dimension=0, tiled=True
        ).astype(jnp.float32),
    )
    gain_sums = (
        lax.psum_scatter(grad_mixgain, ("head", "seq"), scatter_dimension=0, tiled=True),
        lax.psum_scatter(grad_mlpgain, ("head", "seq"), scatter_dimension=0, tiled=True),
    )
    return (
        output,
        grad_tokens,
        summed[0],
        summed[1],
        summed[2],
        summed[3],
        summed[4],
        summed[5],
        summed[6],
        gain_sums[0],
        gain_sums[1],
    )


def solution(mesh):
    placed = (
        P("head", "seq", None),
        P("head", "seq"),
        P("seq", "head"),
        P("seq", "head"),
        P("seq", "head"),
        P("head", "seq"),
        P("seq", "head"),
        P("seq", "head"),
        P("head", "seq"),
        P(("head", "seq")),
        P(("head", "seq")),
        P("head", "seq", None),
    )
    return jax.shard_map(
        on_device,
        mesh=mesh,
        in_specs=placed,
        out_specs=(
            P("head", "seq", None),
            P("head", "seq", None),
            P("seq", "head"),
            P("seq", "head"),
            P("seq", "head"),
            P("head", "seq"),
            P("seq", "head"),
            P("seq", "head"),
            P("head", "seq"),
            P(("head", "seq")),
            P(("head", "seq")),
        ),
        check_vma=False,
    )
```

profile of v0, /device:TPU:0, one launch (start us, length us, event | category | flops | bytes accessed | tf_op | source)
XLA Modules:
  0.0 1304.4 jit_solution(17188036008057129398)
XLA Ops:
  7.2 13.0 all_gather.73
  22.0 40.3 %all-reduce.11 = (bf16[1024]{0:T(1024)(128)(2,1)S(1)}, bf16[1024]{0:T(1024)(128)(2,1)S(1)}) all-reduce(bf16[1024]{0:T(1024)(128)(2,1)S(1)} %dynamic-update-slice, bf16[1024]{0:T(1024)(128)(2,1)S(1)} %dynamic-update-slice.3), channel_id=1, replica_groups=mesh['head'=4,'seq'=8] {'head','seq'}, use_global_device_ids=true, to_apply=%add | all-reduce | flops 2048 | bytes 8192
  63.6 9.0 all_gather.77
  73.8 13.9 %all_gather.78 = bf16[1024,256]{0,1:T(8,128)(2,1)S(1)} all-gather(bf16[128,256]{0,1:T(8,128)(2,1)S(1)} %all_gather.77), channel_id=1, replica_groups=mesh['head'=4,'seq'=8] {'seq'}, dimensions={0}, use_global_device_ids=true | all-gather | bytes 589824 | tf_op jit(solution)/shard_map/all_gather | solution.py:271
  110.2 6.6 fusion
  121.0 8.8 all_gather.82
  130.0 11.9 all_gather.85
  141.9 12.2 all_gather.87
  154.2 10.5 all_gather.89
  166.2 14.1 %all-reduce.1 = f32[8]{0:T(128)S(1)} all-reduce(f32[8]{0:T(128)S(1)} %bitcast_dynamic-update-slice_fusion), channel_id=1, replica_groups=mesh['head'=4,'seq'=8] {'seq'}, use_global_device_ids=true, to_apply=%add.1 | all-reduce | flops 8 | bytes 64
  180.3 8.1 all_gather.75
  188.4 17.2 %all_gather.76 = bf16[1024,256]{0,1:T(8,128)(2,1)S(1)} all-gather(bf16[128,256]{0,1:T(8,128)(2,1)S(1)} %all_gather.75), channel_id=1, replica_groups=mesh['head'=4,'seq'=8] {'seq'}, dimensions={0}, use_global_device_ids=true | all-gather | bytes 589824 | tf_op jit(solution)/shard_map/all_gather | solution.py:270
  215.3 35.7 %all-gather.12.cloned.1.call-done = f32[8,1,279552]{2,1,0:T(1,128)} async-done(((f32[1,1,279552]{2,1,0:T(1,128)}), f32[8,1,279552]{2,1,0:T(1,128)}) %all-gather.12.cloned.1.call-update) | async-done | bytes 8945680 | tf_op jit(solution)/shard_map/all_gather | solution.py:18
  251.1 39.9 %while.38 = (s32[]{:T(128)}, f32[1,279552]{1,0:T(1,128)S(1)}, f32[1,4368]{1,0:T(1,128)S(1)}, f32[1]{0:T(128)}, s32[]{:T(128)}, /*index=5*/f32[8,1]{0,1:T(1,128)S...) while((s32[]{:T(128)}, f32[1,279552]{1,0:T(1,128)S(1)}, ...), condition=%wide.region_2.3_spmd.clone, body=%wide.region_1.2_spmd.clone.sunk | while | flops 1419608 | bytes 3407230 | solution.py:27
  291.5 9.8 reduce.24
  304.8 5.3 fusion.13
  310.1 6.6 fusion.44
  321.0 21.1 %all-gather.16.cloned.1.call-done = bf16[1024,2752]{0,1:T(8,128)(2,1)} async-done(((bf16[128,2752]{0,1:T(8,128)(2,1)}), bf16[1024,2752]{0,1:T(8,128)(2,1)}) %all-gather.16.cloned.1.call-update) | async-done | bytes 5636112 | tf_op jit(solution)/shard_map/all_gather | solution.py:274
  342.1 5.8 fusion.102
  348.0 53.7 %all-gather.18.cloned.1.call-done = bf16[1024,2752]{0,1:T(8,128)(2,1)} async-done(((bf16[128,2752]{0,1:T(8,128)(2,1)}), bf16[1024,2752]{0,1:T(8,128)(2,1)}) %all-gather.18.cloned.1.call-update) | async-done | bytes 5636112 | tf_op jit(solution)/shard_map/all_gather | solution.py:275
  401.7 6.0 fusion.103
  407.7 53.6 %all-gather.20.cloned.1.call-done = bf16[2752,1024]{1,0:T(8,128)(2,1)} async-done(((bf16[2752,128]{1,0:T(8,128)(2,1)}), bf16[2752,1024]{1,0:T(8,128)(2,1)}) %all-gather.20.cloned.1.call-update) | async-done | bytes 5636112 | tf_op jit(solution)/shard_map/all_gather | solution.py:276
  461.3 8.0 multiply_convert_fusion.2
  469.3 5.3 fusion.104
  482.4 6.2 fusion.32
  501.0 5.1 fusion.11
  511.9 15.5 %all-reduce.4 = bf16[8]{0:T(256)(128)(2,1)} all-reduce(bf16[8]{0:T(256)(128)(2,1)S(1)} %dynamic-update-slice.4), channel_id=3, replica_groups=mesh['head'=4,'seq'=8] {'seq'}, use_global_device_ids=true, to_apply=%add.4 | all-reduce | flops 8 | bytes 32
  527.3 6.8 fusion.16
  534.3 15.9 %all_gather.94 = bf16[8,1,4368]{2,1,0:T(2,128)(2,1)} all-gather(bf16[1,1,4368]{2,1,0:T(2,128)(2,1)S(1)} %convert_element_type.348), channel_id=1, replica_groups=mesh['head'=4,'seq'=8] {'seq'}, dimensions={0}, use_global_device_ids=true | all-gather | bytes 78624 | tf_op jit(solution)/shard_map/all_gather | solution.py:33
  554.0 26.1 %all-gather.22.cloned.1.call-done = bf16[8,1,279552]{2,1,0:T(2,128)(2,1)} async-done(((bf16[1,1,279552]{2,1,0:T(2,128)(2,1)}), bf16[8,1,279552]{2,1,0:T(2,128)(2,1)}) %all-gather.22.cloned.1.call-update) | async-done | bytes 4472848 | tf_op jit(solution)/shard_map/all_gather | solution.py:33
  580.1 53.1 %while.39 = (s32[]{:T(128)}, f32[1,279552]{1,0:T(1,128)S(1)}, f32[1,4368]{1,0:T(1,128)S(1)}, f32[1]{0:T(128)}, s32[]{:T(128)}, /*index=5*/bf16[8,1]{0,1:T(2,128)...) while((s32[]{:T(128)}, f32[1,279552]{1,0:T(1,128)S(1)}, ...), condition=%wide.region_8.9_spmd.clone, body=%wide.region_7.8_spmd.clone.sunk | while | flops 1703532 | bytes 2839442 | solution.py:51
  633.2 9.8 reduce.25
  658.6 7.8 fusion.41
  670.2 7.1 fusion.107
  677.5 7.1 fusion.108
  685.6 7.3 fusion.71
  699.3 48.8 %reduce-scatter.29.cloned.1.call-done = f32[128,1024]{1,0:T(8,128)} async-done(((f32[1024,1024]{1,0:T(8,128)}), f32[128,1024]{1,0:T(8,128)}) %reduce-scatter.29.cloned.1.call-update) | async-done | bytes 524304 | tf_op jit(solution)/shard_map/reduce_scatter | solution.py:354
  749.9 115.6 %reduce-scatter.37.cloned.1.call-done = f32[128,2752]{0,1:T(8,128)} async-done(((f32[1024,2752]{0,1:T(8,128)}), f32[128,2752]{0,1:T(8,128)}) %reduce-scatter.37.cloned.1.call-update) | async-done | bytes 1409040 | tf_op jit(solution)/shard_map/reduce_scatter | solution.py:356
  867.9 115.2 %reduce-scatter.39.cloned.1.call-done = f32[128,2752]{0,1:T(8,128)} async-done(((f32[1024,2752]{0,1:T(8,128)}), f32[128,2752]{0,1:T(8,128)}) %reduce-scatter.39.cloned.1.call-update) | async-done | bytes 1409040 | tf_op jit(solution)/shard_map/reduce_scatter | solution.py:357
  985.7 5.6 fusion.46
  991.3 109.3 %reduce-scatter.41.cloned.1.call-done = f32[2752,128]{1,0:T(8,128)} async-done(((f32[2752,1024]{1,0:T(8,128)}), f32[2752,128]{1,0:T(8,128)}) %reduce-scatter.41.cloned.1.call-update) | async-done | bytes 1409040 | tf_op jit(solution)/shard_map/reduce_scatter | solution.py:358
  1104.2 21.8 %reduce-scatter.43.cloned.1.call-done = bf16[64,128]{1,0:T(8,128)(2,1)} async-done(((bf16[256,128]{1,0:T(8,128)(2,1)}), bf16[64,128]{1,0:T(8,128)(2,1)}) %reduce-scatter.43.cloned.1.call-update) | async-done | bytes 16400
  1131.7 39.5 %all-reduce.10 = (f32[1024]{0:T(1024)S(1)}, f32[1024]{0:T(1024)S(1)}) all-reduce(f32[1024]{0:T(1024)S(1)} %get-tuple-element.445, f32[1024]{0:T(1024)S(1)} %get-tuple-element.443), channel_id=18, replica_groups=mesh['head'=4,'seq'=8] {'head','seq'}, use_global_device_ids=true, to_apply=%region_25.26.clone | all-reduce | flops 2048 | bytes 16384
  1175.1 5.3 reduce-scatter.45.cloned.1.call-done
  1181.9 25.9 %reduce-scatter.31.cloned.1.call-done = bf16[128,256]{1,0:T(8,128)(2,1)} async-done(((bf16[128,1024]{1,0:T(8,128)(2,1)}), bf16[128,256]{1,0:T(8,128)(2,1)}) %reduce-scatter.31.cloned.1.call-update) | async-done | bytes 65552 | tf_op jit(solution)/shard_map/reduce_scatter | solution.py:367
  1209.3 27.7 %reduce-scatter.47.cloned.1.call-done = bf16[128,688]{0,1:T(8,128)(2,1)} async-done(((bf16[128,2752]{0,1:T(8,128)(2,1)}), bf16[128,688]{0,1:T(8,128)(2,1)}) %reduce-scatter.47.cloned.1.call-update) | async-done | bytes 176144
  1238.7 27.4 %reduce-scatter.49.cloned.1.call-done = bf16[128,688]{0,1:T(8,128)(2,1)} async-done(((bf16[128,2752]{0,1:T(8,128)(2,1)}), bf16[128,688]{0,1:T(8,128)(2,1)}) %reduce-scatter.49.cloned.1.call-update) | async-done | bytes 176144
  1267.8 27.6 %reduce-scatter.51.cloned.1.call-done = bf16[688,128]{1,0:T(8,128)(2,1)} async-done(((bf16[2752,128]{1,0:T(8,128)(2,1)}), bf16[688,128]{1,0:T(8,128)(2,1)}) %reduce-scatter.51.cloned.1.call-update) | async-done | bytes 176144
  (298 shorter events, 196.1 us)
Async XLA Ops:
  7.2 100.5 %all-gather.10.cloned.1.call-start = ((), (), s32[]{:S(2)}) async-start(), calls=%async_computation.14 | async-start | bytes 2359296 | tf_op jit(solution)/shard_map/all_gather | solution.py:272
  20.3 193.9 %all-reduce.14.cloned.1.call-start = ((), (), s32[]{:S(2)}) async-start(), calls=%async_computation.30 | async-start | bytes 286720
  99.5 8.2 copy-start.3
  106.9 144.2 %all-gather.12.cloned.1.call-start = ((), (), s32[]{:S(2)}) async-start(), calls=%async_computation.15 | async-start | bytes 10063872 | tf_op jit(solution)/shard_map/all_gather | solution.py:18
  110.2 206.6 %copy-start.11 = (bf16[256,1024]{0,1:T(8,128)(2,1)}, bf16[256,1024]{0,1:T(8,128)(2,1)S(1)}, u32[]{:S(2)}) copy-start(bf16[256,1024]{0,1:T(8,128)(2,1)S(1)} %copy.60) | copy-start | bytes 1572868
  110.2 10.8 copy-start.45
  116.8 13.1 %copy-start.42 = (bf16[128,688]{0,1:T(8,128)(2,1)S(1)}, bf16[128,688]{0,1:T(8,128)(2,1)}, u32[]{:S(2)}) copy-start(bf16[128,688]{0,1:T(8,128)(2,1)} %param.22) | copy-start | bytes 528388
  116.8 25.1 %copy-start.43 = (bf16[128,688]{0,1:T(8,128)(2,1)S(1)}, bf16[128,688]{0,1:T(8,128)(2,1)}, u32[]{:S(2)}) copy-start(bf16[128,688]{0,1:T(8,128)(2,1)} %param.23) | copy-start | bytes 528388
  116.8 37.4 %copy-start.44 = (bf16[688,128]{1,0:T(8,128)(2,1)S(1)}, bf16[688,128]{1,0:T(8,128)(2,1)}, u32[]{:S(2)}) copy-start(bf16[688,128]{1,0:T(8,128)(2,1)} %param.24) | copy-start | bytes 528388
  116.8 63.5 %copy-start.47 = (bf16[128,64]{0,1:T(8,128)(2,1)S(1)}, bf16[128,64]{0,1:T(8,128)(2,1)}, u32[]{:S(2)}) copy-start(bf16[128,64]{0,1:T(8,128)(2,1)} %param.18) | copy-start | bytes 49156
  121.0 197.3 %all-gather.14.cloned.1.call-start = ((), (), s32[]{:S(2)}) async-start(), calls=%async_computation.16 | async-start | bytes 2359296 | tf_op jit(solution)/shard_map/all_gather | solution.py:273
  129.9 212.3 %all-gather.16.cloned.1.call-start = ((), (), s32[]{:S(2)}) async-start(), calls=%async_computation.17 | async-start | bytes 6340608 | tf_op jit(solution)/shard_map/all_gather | solution.py:274
  141.8 259.8 %all-gather.18.cloned.1.call-start = ((), (), s32[]{:S(2)}) async-start(), calls=%async_computation.18 | async-start | bytes 6340608 | tf_op jit(solution)/shard_map/all_gather | solution.py:275
  154.2 307.1 %all-gather.20.cloned.1.call-start = ((), (), s32[]{:S(2)}) async-start(), calls=%async_computation.19 | async-start | bytes 6340608 | tf_op jit(solution)/shard_map/all_gather | solution.py:276
  164.8 415.3 %all-gather.22.cloned.1.call-start = ((), (), s32[]{:S(2)}) async-start(), calls=%async_computation.20 | async-start | bytes 10063872 | tf_op jit(solution)/shard_map/all_gather | solution.py:33
  206.5 7.7 copy-start.38
  206.5 7.7 copy-start.18
  209.3 41.8 %copy-start.35 = (f32[256,256]{0,1:T(8,128)}, f32[256,256]{0,1:T(8,128)S(1)}, u32[]{:S(2)}) copy-start(f32[256,256]{0,1:T(8,128)S(1)} %fusion.80) | copy-start | bytes 786436
  310.1 6.7 copy-start.22
  318.2 29.7 %copy-start.29 = (bf16[1,256,16,64]{1,3,2,0:T(8,128)(2,1)}, bf16[1,256,16,64]{1,3,2,0:T(8,128)(2,1)S(1)}, u32[]{:S(2)}) copy-start(bf16[1,256,16,64]{1,3,2,0:T(8,128)(2,1)S(1)} %get-tuple-element.493) | copy-start | bytes 1572868
  320.8 155.8 %copy-start.6 = (f32[1,256,1024]{2,1,0:T(8,128)}, f32[1,256,1024]{2,1,0:T(8,128)S(1)}, u32[]{:S(2)}) copy-start(f32[1,256,1024]{2,1,0:T(8,128)S(1)} %get-tuple-element.496) | copy-start | bytes 3145732
  348.0 113.3 %copy-start.24 = (bf16[1,256,1024]{2,1,0:T(8,128)(2,1)S(1)}, bf16[1,256,1024]{2,1,0:T(8,128)(2,1)}, u32[]{:S(2)}) copy-start(bf16[1,256,1024]{2,1,0:T(8,128)(2,1)} %param.27) | copy-start | bytes 1572868
  493.8 199.1 %reduce-scatter.25.cloned.1.call-start = ((), (), s32[]{:S(2)}) async-start(), calls=%async_computation.21 | async-start | bytes 1179648 | tf_op jit(solution)/shard_map/reduce_scatter | solution.py:352
  500.0 6.1 copy-start.20
  500.4 5.6 copy-start.12
  500.4 5.6 copy-start.14
  500.5 5.6 copy-start.36
  511.0 183.7 %reduce-scatter.33.cloned.1.call-start = ((), (), s32[]{:S(2)}) async-start(), calls=%async_computation.25 | async-start | bytes 4718592 | tf_op jit(solution)/shard_map/reduce_scatter | solution.py:355
  550.2 29.9 %copy-start.48 = (bf16[8]{0:T(256)(128)(2,1)S(1)}, bf16[8]{0:T(256)(128)(2,1)}, u32[]{:S(2)}) copy-start(bf16[8]{0:T(256)(128)(2,1)} %all-reduce.4) | copy-start | bytes 52
  554.0 143.6 %reduce-scatter.27.cloned.1.call-start = ((), (), s32[]{:S(2)}) async-start(), calls=%async_computation.22 | async-start | bytes 1179648 | tf_op jit(solution)/shard_map/reduce_scatter | solution.py:353
  651.1 7.5 copy-start.34
  658.3 8.2 copy-start.15
  658.3 89.8 %reduce-scatter.29.cloned.1.call-start = ((), (), s32[]{:S(2)}) async-start(), calls=%async_computation.23 | async-start | bytes 4718592 | tf_op jit(solution)/shard_map/reduce_scatter | solution.py:354
  658.6 7.9 copy-start.23
  670.2 195.3 %reduce-scatter.37.cloned.1.call-start = ((), (), s32[]{:S(2)}) async-start(), calls=%async_computation.27 | async-start | bytes 12681216 | tf_op jit(solution)/shard_map/reduce_scatter | solution.py:356
  677.4 305.7 %reduce-scatter.39.cloned.1.call-start = ((), (), s32[]{:S(2)}) async-start(), calls=%async_computation.28 | async-start | bytes 12681216 | tf_op jit(solution)/shard_map/reduce_scatter | solution.py:357
  684.6 415.9 %reduce-scatter.41.cloned.1.call-start = ((), (), s32[]{:S(2)}) async-start(), calls=%async_computation.29 | async-start | bytes 12681216 | tf_op jit(solution)/shard_map/reduce_scatter | solution.py:358
  692.9 433.1 %reduce-scatter.43.cloned.1.call-start = ((), (), s32[]{:S(2)}) async-start(), calls=%async_computation.31 | async-start | bytes 81920
  693.9 291.8 %copy-start.7 = (f32[1,256,1024]{2,1,0:T(8,128)S(1)}, f32[1,256,1024]{2,1,0:T(8,128)}, u32[]{:S(2)}) copy-start(f32[1,256,1024]{2,1,0:T(8,128)} %copy-done.6) | copy-start | bytes 3145732
  694.7 478.9 %reduce-scatter.35.cloned.1.call-start = ((), (), s32[]{:S(2)}) async-start(), calls=%async_computation.26 | async-start | bytes 327680 | tf_op jit(solution)/shard_map/reduce_scatter | solution.py:370
  696.5 483.9 %reduce-scatter.45.cloned.1.call-start = ((), (), s32[]{:S(2)}) async-start(), calls=%async_computation.32 | async-start | bytes 81920
  699.2 508.6 %reduce-scatter.31.cloned.1.call-start = ((), (), s32[]{:S(2)}) async-start(), calls=%async_computation.24 | async-start | bytes 327680 | tf_op jit(solution)/shard_map/reduce_scatter | solution.py:367
  749.9 487.1 %reduce-scatter.47.cloned.1.call-start = ((), (), s32[]{:S(2)}) async-start(), calls=%async_computation.33 | async-start | bytes 880640
  867.8 398.2 %reduce-scatter.49.cloned.1.call-start = ((), (), s32[]{:S(2)}) async-start(), calls=%async_computation.34 | async-start | bytes 880640
  985.4 310.0 %reduce-scatter.51.cloned.1.call-start = ((), (), s32[]{:S(2)}) async-start(), calls=%async_computation.35 | async-start | bytes 880640
  985.7 117.2 %copy-start.28 = (bf16[1024,256]{0,1:T(8,128)(2,1)S(1)}, bf16[1024,256]{0,1:T(8,128)(2,1)}, u32[]{:S(2)}) copy-start(bf16[1024,256]{0,1:T(8,128)(2,1)} %copy-done.27) | copy-start | bytes 1572868
  985.7 117.2 %copy-start.32 = (bf16[1,256,16,16]{1,3,2,0:T(8,128)(2,1)S(1)}, bf16[1,256,16,16]{1,3,2,0:T(8,128)(2,1)}, u32[]{:S(2)}) copy-start(bf16[1,256,16,16]{1,3,2,0:T(8,128)(2,1)} %copy-done.31) | copy-start | bytes 393220
  991.3 136.2 %copy-start.17 = (bf16[1,16,64,256]{3,2,1,0:T(8,128)(2,1)S(1)}, bf16[1,16,64,256]{3,2,1,0:T(8,128)(2,1)}, u32[]{:S(2)}) copy-start(bf16[1,16,64,256]{3,2,1,0:T(8,128)(2,1)} %copy-done.16) | copy-start | bytes 1572868
  (24 other events, 64.6 us)
Sparse Core Ops, SparseCore 0:
  20.4 29.1 all-gather.9
  107.0 49.6 all-reduce.13
  158.5 92.5 all-gather.11
  252.6 29.1 all-gather.13
  283.3 58.8 all-gather.15
  343.7 57.9 all-gather.17
  403.3 57.9 all-gather.19
  494.0 86.1 all-gather.21
  583.1 30.8 reduce-scatter.24
  616.2 48.3 reduce-scatter.32
  667.0 30.5 reduce-scatter.26
  699.8 48.2 reduce-scatter.28
  750.5 114.9 reduce-scatter.36
  867.8 115.2 reduce-scatter.38
  985.3 115.1 reduce-scatter.40
  1103.9 22.0 reduce-scatter.42
  1129.2 24.1 reduce-scatter.34
  1156.7 23.6 reduce-scatter.44
  1183.7 24.0 reduce-scatter.30
  1210.9 26.0 reduce-scatter.46
  1240.0 26.0 reduce-scatter.48
  1269.3 26.0 reduce-scatter.50
where the time goes:
time: 1320 us; the launch traced here: 1300 us
  waiting for transfers between devices  716 us (54%)
  blocking collectives  230 us (17%)
  matrix products  140 us (11%)
  other arithmetic  115 us (9%)
  local copies, waits for them, and re-layouts  54.1 us (4%)
  loops' own time  30.2 us (2%)
  between operations  17 us (1%)
    reduce_scatter x1, waiting for transfers between devices, on_device(): lax.psum_scatter(grad_gate, 'seq', scatter_dimension=0, tiled=True)  116 us
    reduce_scatter x1, waiting for transfers between devices, on_device(): lax.psum_scatter(grad_up, 'seq', scatter_dimension=0, tiled=True)  115 us
    unnamed x28, waiting for transfers between devices  110 us
    unnamed x4, blocking collectives  109 us
    reduce_scatter x1, waiting for transfers between devices, on_device(): lax.psum_scatter(grad_down, 'seq', scatter_dimension=1, tiled=True)  109 us
    all_gather x1, waiting for transfers between devices, on_device(): lax.all_gather(pieces[5], 'seq', axis=0, tiled=True)  53.7 us
    all_gather x1, waiting for transfers between devices, on_device(): lax.all_gather(pieces[6], 'seq', axis=1, tiled=True)  53.6 us
    reduce_scatter x1, waiting for transfers between devices, on_device(): lax.psum_scatter(grad_value, 'seq', scatter_dimension=0, tiled=True)  48.8 us
  transfers between devices with their start and end apart: 22, of which 16 were waited for; matrix products, arithmetic and copies ran while one was open for 21% of the time, Pallas kernels for 0%

commit v1 on v0

v1 whole, which is shorter than its diff:
```python
import functools

import jax
import jax.numpy as jnp
from jax import lax
from jax.experimental import pallas as pl
from jax.experimental.pallas import tpu as pltpu
from jax.sharding import PartitionSpec as P

FDIM = 16
VDIM = 64
EPS = 1e-06
ROOT_HALF = 0.7071067811865476
FROWS = 11 * FDIM
F32 = jnp.float32
BF16 = jnp.bfloat16
VMEM_BYTES = 56 * 1024 * 1024

NN = (((1,), (0,)), ((), ()))
NT = (((1,), (1,)), ((), ()))
TN = (((0,), (0,)), ((), ()))


def mm(a, b, dims=NN):
    return lax.dot_general(a, b, dims, preferred_element_type=F32)


def call(body, outs, ins, grid=None, in_specs=None, out_specs=None, scratch=(), flops=0):
    nbytes = sum(x.size * x.dtype.itemsize for x in jax.tree.leaves((ins, outs)))
    kwargs = {}
    if grid is not None:
        kwargs = dict(grid=grid, in_specs=in_specs, out_specs=out_specs)
    return pl.pallas_call(
        body,
        out_shape=outs,
        scratch_shapes=list(scratch),
        compiler_params=pltpu.CompilerParams(vmem_limit_bytes=VMEM_BYTES),
        cost_estimate=pl.CostEstimate(flops=flops, bytes_accessed=nbytes, transcendentals=0),
        **kwargs,
    )(*ins)


def sds(shape, dtype):
    return jax.ShapeDtypeStruct(shape, dtype)


def whole(shape):
    return pl.BlockSpec(shape, lambda r: (0,) * len(shape))


def by_row(shape):
    return pl.BlockSpec((1,) + tuple(shape), lambda r: (r,) + (0,) * len(shape))


def coef(d):
    return ROOT_HALF if d in (0, FDIM // 2) else 1.0


def features(w):
    half = w * 0.5
    rows = [half]
    for d in range(FDIM // 2 + 1):
        other = half if d == 0 else pltpu.roll(half, FDIM - d, 0)
        rows.append(half * other * coef(d))
    first = lax.broadcasted_iota(jnp.int32, half.shape, 0) == 0
    rows.append(jnp.where(first, 1.0, 0.0))
    return jnp.concatenate(rows, axis=0)


def features_back(w, grad):
    half = w * 0.5
    total = grad[:FDIM]
    for d in range(FDIM // 2 + 1):
        part = grad[FDIM * (d + 1) : FDIM * (d + 2)]
        if d == 0:
            total = total + part * half * (2.0 * coef(0))
        else:
            near = part * pltpu.roll(half, FDIM - d, 0)
            far = pltpu.roll(part * half, d, 0)
            total = total + (near + far) * coef(d)
    return total * 0.5


def lanes(shape):
    return lax.broadcasted_iota(jnp.int32, shape, len(shape) - 1)


def one_hot_lanes(rows, index):
    lane = lanes((rows, 128))
    return jnp.where(lane == index, 1.0, 0.0).astype(BF16)


def own_half(x, j, other=None):
    left = lanes(x.shape) < VDIM
    keep = left if j == 0 else jnp.logical_not(left)
    return jnp.where(keep, x, jnp.zeros_like(x) if other is None else other)


def pick_columns(z, column, spots):
    row = lax.broadcasted_iota(jnp.int32, (128, 128), 0)
    hot = jnp.where(column(row), 1.0, 0.0) * jnp.where(spots(lanes((128, 128))), 1.0, 0.0)
    return mm(z, hot.astype(BF16))


def doc_mask(masks, rows):
    seg = masks[0:1, :]
    col = jnp.transpose(masks)[:, 0:1]
    causal = lax.broadcasted_iota(jnp.int32, (rows, rows), 0) >= lax.broadcasted_iota(
        jnp.int32, (rows, rows), 1
    )
    return jnp.logical_and(causal, col == seg)


def with_pair(z, j):
    lane = lanes(z.shape)
    base = VDIM if j == 0 else 0
    high = z.astype(BF16)
    low = (z - high.astype(F32)).astype(BF16)
    zero = jnp.zeros_like(high)
    return jnp.where(lane == base, high, jnp.where(lane == base + 1, low, zero))


def with_ones(x, j):
    lane = lanes(x.shape)
    base = VDIM if j == 0 else 0
    hot = jnp.where(jnp.logical_or(lane == base, lane == base + 1), 1.0, 0.0).astype(x.dtype)
    return own_half(x, j, hot)


def project_body(x_ref, gain_ref, w_ref, masks_ref, h1_ref, qk_ref, v_ref, p_ref, z_ref, wt_ref):
    r = pl.program_id(0)
    heads = qk_ref.shape[1] // (2 * FDIM)
    nb, _, wb = w_ref.shape

    @pl.when(r == 0)
    def _():
        for s in range(nb):
            wt_ref[:, s * wb : (s + 1) * wb] = w_ref[s]
        z_ref[...] = jnp.zeros_like(z_ref)

    x = x_ref[0].astype(F32)
    normed = x * lax.rsqrt(jnp.mean(x * x, axis=-1, keepdims=True) + EPS)
    h1 = (normed * gain_ref[0:1, :]).astype(BF16)
    h1_ref[0] = h1
    nqk = qk_ref.shape[1]
    qk = mm(wt_ref[:nqk, :], h1, NT).astype(BF16)
    qk_ref[0] = qk
    v = mm(h1, wt_ref[nqk:, :], NT).astype(BF16)
    v_ref[0] = v
    tail = masks_ref[0, 1:2, :]
    rows = v.shape[0]
    for pair in range(heads // 2):
        v_pair = v[:, pair * 128 : (pair + 1) * 128]
        both = []
        for j in range(2):
            i = 2 * pair + j
            k = qk[nqk // 2 + i * FDIM : nqk // 2 + (i + 1) * FDIM].astype(F32)
            phi = (features(k) * tail).astype(BF16)
            rhs = jnp.concatenate([v_pair, one_hot_lanes(rows, r * heads + i)], axis=1)
            res = mm(phi, rhs)
            both.append(res[:, :128])
            z_ref[...] += res[:, 128:]
        p_ref[r * (heads // 2) + pair] = own_half(both[0], 0, both[1]).astype(BF16)

    @pl.when(r == pl.num_programs(0) - 1)
    def _():
        p_ref[p_ref.shape[0] - 1] = z_ref[...].astype(BF16)


def project(x, gain, w, masks, heads):
    n, rows, d = x.shape
    nb, total, wb = w.shape
    nqk, nv = 2 * heads * FDIM, heads * VDIM
    pieces = n * heads // 2 + 1
    return call(
        project_body,
        (
            sds((n, rows, d), BF16),
            sds((n, nqk, rows), BF16),
            sds((n, rows, nv), BF16),
            sds((pieces, FROWS, 128), BF16),
        ),
        (x, gain, w, masks),
        grid=(n,),
        in_specs=[by_row((rows, d)), whole(gain.shape), whole(w.shape), by_row(masks.shape[1:])],
        out_specs=[
            by_row((rows, d)),
            by_row((nqk, rows)),
            by_row((rows, nv)),
            whole((pieces, FROWS, 128)),
        ],
        scratch=[pltpu.VMEM((FROWS, 128), F32), pltpu.VMEM((nqk + nv, d), BF16)],
        flops=2 * n * rows * d * (nqk + nv),
    )


def local_body(qk_ref, v_ref, masks_ref, nd_ref):
    nqk = qk_ref.shape[1]
    heads = nqk // (2 * FDIM)
    rows = v_ref.shape[1]
    mask = doc_mask(masks_ref[0], rows)
    for pair in range(heads // 2):
        v_pair = v_ref[0, :, pair * 128 : (pair + 1) * 128]
        acc = None
        for j in range(2):
            i = 2 * pair + j
            q = qk_ref[0, i * FDIM : (i + 1) * FDIM, :]
            k = qk_ref[0, nqk // 2 + i * FDIM : nqk // 2 + (i + 1) * FDIM, :]
            s1 = mm(q, k, TN) * 0.25 + 1.0
            a = jnp.where(mask, 0.5 * s1 * s1 + 0.5, 0.0).astype(BF16)
            ones = own_half(jnp.ones((rows, 128), BF16), j)
            part = mm(a, jnp.concatenate([own_half(v_pair, j), ones], axis=1))
            acc = part if acc is None else acc + part
        nd_ref[0, pair] = acc


def local(qk, v, masks):
    n, nqk, rows = qk.shape
    heads = nqk // (2 * FDIM)
    return call(
        local_body,
        sds((n, heads // 2, rows, 256), F32),
        (qk, v, masks),
        grid=(n,),
        in_specs=[by_row(qk.shape[1:]), by_row(v.shape[1:]), by_row(masks.shape[1:])],
        out_specs=by_row((heads // 2, rows, 256)),
        flops=n * heads * rows * rows * 600,
    )


def joined(first, second, flag):
    return first.astype(F32) + second.astype(F32) * flag


def lane_flags(masks_ref, row, n, heads):
    lane = lanes((1, 128)) % (n * heads) // heads
    flag = jnp.zeros((1, 128), F32)
    for r in range(n):
        flag = jnp.where(lane == r, masks_ref[r, row : row + 1, 0:128], flag)
    return flag


def carry_body(nd_ref, qk_ref, masks_ref, one_ref, two_ref, o_ref, on_ref, inv_ref, c_ref):
    r = pl.program_id(0)
    n = pl.num_programs(0)
    nqk = qk_ref.shape[1]
    heads = nqk // (2 * FDIM)
    last = one_ref.shape[0] - 1

    @pl.when(r == 0)
    def _():
        flag = lane_flags(masks_ref, 3, masks_ref.shape[0], heads)
        c_ref[last] = joined(one_ref[last], two_ref[last], flag).astype(BF16)

    flag = masks_ref[r, 3:4, 0:128]
    live = masks_ref[r, 2:3, :]
    for pair in range(heads // 2):
        at = r * (heads // 2) + pair
        c = joined(one_ref[at], two_ref[at], flag).astype(BF16)
        c_ref[at] = c
        acc = nd_ref[0, pair]
        for j in range(2):
            i = 2 * pair + j
            q = qk_ref[0, i * FDIM : (i + 1) * FDIM, :].astype(F32)
            phi = (features(q) * live).astype(BF16)
            z = pick_columns(
                c_ref[last],
                lambda row: row == r * heads + i,
                lambda lane: (lane < VDIM) if j == 0 else (lane >= VDIM),
            ).astype(BF16)
            acc = acc + mm(phi, jnp.concatenate([own_half(c, j), z], axis=1), TN)
        inv = 1.0 / acc[:, 128:]
        on = acc[:, :128] * inv
        cols = slice(pair * 128, (pair + 1) * 128)
        o_ref[0, :, cols] = on.astype(BF16)
        on_ref[0, :, cols] = on
        inv_ref[0, :, cols] = inv


def carry(nd, qk, masks, one, two):
    n, nqk, rows = qk.shape
    heads = nqk // (2 * FDIM)
    nv = heads * VDIM
    return call(
        carry_body,
        (sds((n, rows, nv), BF16), sds((n, rows, nv), F32), sds((n, rows, nv), F32), sds(one.shape, BF16)),
        (nd, qk, masks, one, two),
        grid=(n,),
        in_specs=[
            by_row(nd.shape[1:]),
            by_row(qk.shape[1:]),
            whole(masks.shape),
            whole(one.shape),
            whole(two.shape),
        ],
        out_specs=[by_row((rows, nv)), by_row((rows, nv)), by_row((rows, nv)), whole(one.shape)],
        flops=n * heads * rows * 1000 * 256,
    )


def middle_body(x_ref, o_ref, wo_ref, gain_ref, y1_ref, h2_ref, wide_ref):
    n, nb, _, wb = wo_ref.shape
    acc = x_ref[...].astype(F32)
    for r in range(n):
        for s in range(nb):
            wide_ref[:, s * wb : (s + 1) * wb] = wo_ref[r, s]
        acc = acc + mm(o_ref[r], wide_ref[...])
    y1_ref[...] = acc
    scale = lax.rsqrt(jnp.mean(acc * acc, axis=-1, keepdims=True) + EPS)
    h2_ref[...] = (acc * scale * gain_ref[0:1, :]).astype(BF16)


def middle(x, o, wo, gain):
    rows, d = x.shape
    return call(
        middle_body,
        (sds((rows, d), F32), sds((rows, d), BF16)),
        (x, o, wo, gain),
        scratch=[pltpu.VMEM((wo.shape[2], d), BF16)],
        flops=2 * rows * d * d,
    )


def widen_body(w_ref, o_ref):
    o_ref[...] = w_ref[0]


def widen(w):
    nb, rows, wb = w.shape
    return pl.pallas_call(
        widen_body,
        out_shape=sds((rows, nb * wb), BF16),
        grid=(nb,),
        in_specs=[pl.BlockSpec((1, rows, wb), lambda s: (s, 0, 0))],
        out_specs=pl.BlockSpec((rows, wb), lambda s: (0, s)),
        compiler_params=pltpu.CompilerParams(vmem_limit_bytes=VMEM_BYTES),
        cost_estimate=pl.CostEstimate(flops=0, bytes_accessed=4 * w.size, transcendentals=0),
    )(w)


def mlp_body(h2_ref, cot_ref, w_ref, dh_ref, out_ref, hid_ref, dg_ref, du_ref):
    ff = hid_ref.shape[1]
    h2 = h2_ref[...]
    gate_w, up_w, down_w = w_ref[0:ff, :], w_ref[ff : 2 * ff, :], w_ref[2 * ff : 3 * ff, :]
    dhid = mm(cot_ref[...], down_w, NT)
    g = mm(h2, gate_w, NT)
    u = mm(h2, up_w, NT)
    sig = jax.nn.sigmoid(g)
    act = g * sig
    hid = (act * u).astype(BF16)
    dg = (dhid * u * sig * (1.0 + g * (1.0 - sig))).astype(BF16)
    du = (dhid * act).astype(BF16)
    hid_ref[...] = hid
    dg_ref[...] = dg
    du_ref[...] = du
    dh_ref[...] = (mm(dg, gate_w) + mm(du, up_w)).astype(BF16)
    out_ref[...] = mm(hid, down_w).astype(BF16)


def mlp(h2, cot, w):
    rows, d = h2.shape
    ff = w.shape[0] // 3
    return call(
        mlp_body,
        (
            sds((rows, d), BF16),
            sds((rows, d), BF16),
            sds((rows, ff), BF16),
            sds((rows, ff), BF16),
            sds((rows, ff), BF16),
        ),
        (h2, cot, w),
        flops=12 * rows * d * ff,
    )


def mlp_grads_body(n, *refs):
    h2, cot, hid, dg, du = (refs[k * n : (k + 1) * n] for k in range(5))
    o_ref = refs[5 * n]
    nb, total, wb = o_ref.shape
    ff = total // 3
    for k, (left, right) in enumerate(((dg, h2), (du, h2), (hid, cot))):
        acc = None
        for r in range(n):
            part = mm(left[r][...], right[r][...], TN)
            acc = part if acc is None else acc + part
        acc = acc.astype(BF16)
        for s in range(nb):
            o_ref[s, k * ff : (k + 1) * ff, :] = acc[:, s * wb : (s + 1) * wb]


def mlp_grads(h2, cot, hid, dg, du, nb):
    n = len(h2)
    d, ff = h2[0].shape[1], hid[0].shape[1]
    return call(
        functools.partial(mlp_grads_body, n),
        sds((nb, 3 * ff, d // nb), BF16),
        (*h2, *cot, *hid, *dg, *du),
        flops=6 * n * h2[0].shape[0] * d * ff,
    )


def turn_body(n, *refs):
    parts, (y1_ref, cot_ref, gain_ref, wo_ref) = refs[:n], refs[n : n + 4]
    dy1_ref, f_ref, do_ref, dgain_ref, wide_ref = refs[n + 4 :]
    dh2 = parts[0][...].astype(F32)
    for r in range(1, n):
        dh2 = dh2 + parts[r][...].astype(F32)
    y1 = y1_ref[...]
    scale = lax.rsqrt(jnp.mean(y1 * y1, axis=-1, keepdims=True) + EPS)
    normed = y1 * scale
    dgain_ref[...] = jnp.sum(dh2 * normed, axis=0, keepdims=True)
    dn = dh2 * gain_ref[0:1, :]
    inner = jnp.mean(dn * normed, axis=-1, keepdims=True)
    dy1 = cot_ref[...].astype(F32) + scale * (dn - normed * inner)
    dy1_ref[...] = dy1
    f = dy1.astype(BF16)
    f_ref[...] = f
    nb, wb = wo_ref.shape[1], wo_ref.shape[3]
    for r in range(n):
        for s in range(nb):
            wide_ref[:, s * wb : (s + 1) * wb] = wo_ref[r, s]
        do_ref[r] = mm(f, wide_ref[...], NT).astype(BF16)


def turn(parts, y1, cot, gain, wo):
    n = len(parts)
    rows, d = y1.shape
    nv = wo.shape[2]
    return call(
        functools.partial(turn_body, n),
        (sds((rows, d), F32), sds((rows, d), BF16), sds((n, rows, nv), BF16), sds((1, d), F32)),
        (*parts, y1, cot, gain, wo),
        scratch=[pltpu.VMEM((nv, d), BF16)],
        flops=2 * rows * d * d,
    )


def back_first_body(do_ref, on_ref, inv_ref, qk_ref, masks_ref, d_ref, p_ref, z_ref):
    r = pl.program_id(0)
    n = pl.num_programs(0)
    nqk = qk_ref.shape[1]
    heads = nqk // (2 * FDIM)
    rows = do_ref.shape[1]

    @pl.when(r == 0)
    def _():
        z_ref[...] = jnp.zeros_like(z_ref)

    live = masks_ref[0, 2:3, :]
    lane = lanes((rows, 128))
    for pair in range(heads // 2):
        cols = slice(pair * 128, (pair + 1) * 128)
        wide = do_ref[0, :, cols].astype(F32) * inv_ref[0, :, cols]
        dnum = wide.astype(BF16)
        prod = -(wide * on_ref[0, :, cols])
        high = prod.astype(BF16)
        low = (prod - high.astype(F32)).astype(BF16)
        both = []
        for j in range(2):
            i = 2 * pair + j
            row = lax.broadcasted_iota(jnp.int32, (128, 128), 0)
            hot = jnp.where((row < VDIM) if j == 0 else (row >= VDIM), 1.0, 0.0).astype(BF16)
            dden = mm(high, hot) + mm(low, hot)
            d_ref[0, i] = own_half(dnum, j, with_pair(dden, j))
            dh = dden.astype(BF16)
            dl = (dden - dh.astype(F32)).astype(BF16)
            zero = jnp.zeros_like(dh)
            spot = r * heads + i
            zext = jnp.where(lane == spot, dh, jnp.where(lane == spot + n * heads, dl, zero))
            q = qk_ref[0, i * FDIM : (i + 1) * FDIM, :].astype(F32)
            phi = (features(q) * live).astype(BF16)
            res = mm(phi, jnp.concatenate([dnum, zext], axis=1))
            both.append(res[:, :128])
            z_ref[...] += res[:, 128:]
        p_ref[r * (heads // 2) + pair] = own_half(both[0], 0, both[1]).astype(BF16)

    @pl.when(r == n - 1)
    def _():
        p_ref[p_ref.shape[0] - 1] = z_ref[...].astype(BF16)


def back_first(do, on, inv, qk, masks):
    n, nqk, rows = qk.shape
    heads = nqk // (2 * FDIM)
    pieces = n * heads // 2 + 1
    return call(
        back_first_body,
        (sds((n, heads, rows, 128), BF16), sds((pieces, FROWS, 128), BF16)),
        (do, on, inv, qk, masks),
        grid=(n,),
        in_specs=[by_row(x.shape[1:]) for x in (do, on, inv, qk, masks)],
        out_specs=[by_row((heads, rows, 128)), whole((pieces, FROWS, 128))],
        scratch=[pltpu.VMEM((FROWS, 128), F32)],
        flops=n * heads * rows * 256 * 600,
    )


def back_local_body(d_ref, qk_ref, v_ref, masks_ref, c_ref, dq_ref, dk_ref, dv_ref):
    r = pl.program_id(0)
    nqk = qk_ref.shape[1]
    heads = nqk // (2 * FDIM)
    rows = v_ref.shape[1]
    masks = masks_ref[0]
    mask = doc_mask(masks, rows)
    live = masks[2:3, :]
    last = c_ref.shape[0] - 1
    for pair in range(heads // 2):
        cols = slice(pair * 128, (pair + 1) * 128)
        v_pair = v_ref[0, :, cols]
        c = c_ref[r * (heads // 2) + pair]
        dv = None
        for j in range(2):
            i = 2 * pair + j
            q = qk_ref[0, i * FDIM : (i + 1) * FDIM, :]
            k = qk_ref[0, nqk // 2 + i * FDIM : nqk // 2 + (i + 1) * FDIM, :]
            s1 = mm(q, k, TN) * 0.25 + 1.0
            a = jnp.where(mask, 0.5 * s1 * s1 + 0.5, 0.0).astype(BF16)
            d = d_ref[0, i]
            da = mm(d, with_ones(v_pair, j), NT)
            ds = jnp.where(mask, da * s1, 0.0).astype(BF16)
            z = pick_columns(
                c_ref[last], lambda row: row == r * heads + i, lambda lane: lane >= 0
            )
            dphi = mm(own_half(c, j, with_pair(z, j)), d, NT) * live
            back = features_back(q.astype(F32), dphi)
            dq_ref[0, i * FDIM : (i + 1) * FDIM, :] = (mm(k, ds, NT) * 0.25 + back).astype(BF16)
            dk_ref[0, i * FDIM : (i + 1) * FDIM, :] = mm(q, ds) * 0.25
            part = mm(own_half(d, j), a, TN)
            dv = part if dv is None else dv + part
        dv_ref[0, cols, :] = dv


def back_local(d, qk, v, masks, c):
    n, nqk, rows = qk.shape
    heads = nqk // (2 * FDIM)
    nv = heads * VDIM
    return call(
        back_local_body,
        (sds((n, nqk // 2, rows), BF16), sds((n, nqk // 2, rows), F32), sds((n, nv, rows), F32)),
        (d, qk, v, masks, c),
        grid=(n,),
        in_specs=[by_row(x.shape[1:]) for x in (d, qk, v, masks)] + [whole(c.shape)],
        out_specs=[by_row((nqk // 2, rows)), by_row((nqk // 2, rows)), by_row((nv, rows))],
        flops=n * heads * rows * rows * 1500,
    )


def back_last_body(
    dq_ref, dk_ref, dv_ref, qk_ref, v_ref, masks_ref, one_ref, two_ref, h1_ref, x_ref, w_ref,
    dh1_ref, dw_ref, dgain_ref, z_ref, wt_ref, acc_ref,
):
    r = pl.program_id(0)
    n = pl.num_programs(0)
    nqk = qk_ref.shape[1]
    heads = nqk // (2 * FDIM)
    nb, _, wb = w_ref.shape
    last = one_ref.shape[0] - 1

    @pl.when(r == 0)
    def _():
        for s in range(nb):
            wt_ref[:, s * wb : (s + 1) * wb] = w_ref[s]
        flag = lane_flags(masks_ref, 4, masks_ref.shape[0], heads)
        z_ref[...] = joined(one_ref[last], two_ref[last], flag).astype(BF16)
        dgain_ref[...] = jnp.zeros_like(dgain_ref)
        acc_ref[...] = jnp.zeros_like(acc_ref)

    flag = masks_ref[r, 4:5, 0:128]
    tail = masks_ref[r, 1:2, :]
    dks, dvs = [], []
    for pair in range(heads // 2):
        cols = slice(pair * 128, (pair + 1) * 128)
        at = r * (heads // 2) + pair
        dp = joined(one_ref[at], two_ref[at], flag).astype(BF16)
        v_pair = v_ref[0, :, cols]
        dv = dv_ref[0, cols, :]
        for j in range(2):
            i = 2 * pair + j
            k = qk_ref[0, nqk // 2 + i * FDIM : nqk // 2 + (i + 1) * FDIM, :].astype(F32)
            spot = r * heads + i
            z = pick_columns(
                z_ref[...],
                lambda row: jnp.logical_or(row == spot, row == spot + n * heads),
                lambda lane: lane >= 0,
            )
            dphi = mm(own_half(dp, j, with_pair(z, j)), with_ones(v_pair, j), NT) * tail
            dk = dk_ref[0, i * FDIM : (i + 1) * FDIM, :] + features_back(k, dphi)
            dks.append(dk.astype(BF16))
            phi = (features(k) * tail).astype(BF16)
            dv = dv + mm(own_half(dp, j), phi, TN)
        dvs.append(dv.astype(BF16))
    d = jnp.concatenate([dq_ref[0]] + dks + dvs, axis=0)
    acc_ref[...] += mm(d, h1_ref[0])
    dh1 = mm(d, wt_ref[...], TN)
    dh1_ref[0] = dh1.astype(BF16)
    x = x_ref[0].astype(F32)
    normed = x * lax.rsqrt(jnp.mean(x * x, axis=-1, keepdims=True) + EPS)
    dgain_ref[...] += jnp.sum(dh1 * normed, axis=0, keepdims=True)

    @pl.when(r == n - 1)
    def _():
        for s in range(nb):
            dw_ref[s] = acc_ref[:, s * wb : (s + 1) * wb].astype(BF16)


def back_last(dq, dk, dv, qk, v, masks, one, two, h1, x, w):
    n, nqk, rows = qk.shape
    nb, total, wb = w.shape
    d = nb * wb
    return call(
        back_last_body,
        (sds((n, rows, d), BF16), sds(w.shape, BF16), sds((1, d), F32)),
        (dq, dk, dv, qk, v, masks, one, two, h1, x, w),
        grid=(n,),
        in_specs=[by_row(y.shape[1:]) for y in (dq, dk, dv, qk, v)]
        + [whole(masks.shape), whole(one.shape), whole(two.shape)]
        + [by_row(h1.shape[1:]), by_row(x.shape[1:]), whole(w.shape)],
        out_specs=[by_row((rows, d)), whole(w.shape), whole((1, d))],
        scratch=[
            pltpu.VMEM((FROWS, 128), BF16),
            pltpu.VMEM((total, d), BF16),
            pltpu.VMEM((total, d), F32),
        ],
        flops=4 * n * rows * d * total,
    )


def out_grads_body(n, o_ref, *refs):
    fs, out_ref = refs[:n], refs[n]
    nb, _, wb = out_ref.shape
    acc = None
    for r in range(n):
        part = mm(o_ref[r], fs[r][...], TN)
        acc = part if acc is None else acc + part
    for s in range(nb):
        out_ref[s] = acc[:, s * wb : (s + 1) * wb].astype(BF16)


def out_grads(o, fs, nb):
    n, rows, nv = o.shape
    d = fs[0].shape[1]
    return call(
        functools.partial(out_grads_body, n),
        sds((nb, nv, d // nb), BF16),
        (o, *fs),
        flops=2 * n * rows * nv * d,
    )


def final_body(n, *refs):
    parts, (x_ref, dy1_ref, gain_ref, o_ref) = refs[:n], refs[n:]
    dh1 = parts[0][...].astype(F32)
    for r in range(1, n):
        dh1 = dh1 + parts[r][...].astype(F32)
    x = x_ref[...].astype(F32)
    scale = lax.rsqrt(jnp.mean(x * x, axis=-1, keepdims=True) + EPS)
    normed = x * scale
    dn = dh1 * gain_ref[0:1, :]
    inner = jnp.mean(dn * normed, axis=-1, keepdims=True)
    o_ref[...] = dy1_ref[...] + scale * (dn - normed * inner)


def final(parts, x, dy1, gain):
    return call(
        functools.partial(final_body, len(parts)), sds(x.shape, F32), (*parts, x, dy1, gain)
    )


def xor_pairs(size, r):
    return [(i, i ^ r) for i in range(size)]


def swap(parts):
    size = lax.axis_size("head")
    return [parts[0]] + [lax.ppermute(parts[r], "head", xor_pairs(size, r)) for r in range(1, size)]


def spread(x):
    return swap([x] * lax.axis_size("head"))


def shifted(x, step):
    size = lax.axis_size("seq")
    return lax.ppermute(x, "seq", [(i, i + step) for i in range(size) if 0 <= i + step < size])


def halved(x):
    size, me = lax.axis_size("seq"), lax.axis_index("seq")
    if size & (size - 1):
        return lax.psum_scatter(x, "seq", tiled=True)
    k = 1
    while k < size:
        x = x.reshape((x.shape[0] // 2, 2) + x.shape[1:])
        bit = (me // k) % 2
        keep = lax.dynamic_index_in_dim(x, bit, 1, keepdims=False)
        send = lax.dynamic_index_in_dim(x, 1 - bit, 1, keepdims=False)
        got = lax.ppermute(send, "seq", xor_pairs(size, k))
        x = (keep.astype(F32) + got.astype(F32)).astype(x.dtype)
        k *= 2
    return x


def carried(x, labels, step, keep):
    size, me = lax.axis_size("seq"), lax.axis_index("seq")
    reach = max(size // 4, 1)
    mine = jnp.take(labels, me, axis=1)
    k = 1
    while 2 * k < reach:
        other = jnp.take(labels, jnp.clip(me - step * k, 0, size - 1), axis=1)
        flag = (other == mine).astype(F32)
        x = keep(x, shifted(x, step * k), flag)
        k *= 2
    near = jnp.take(labels, jnp.clip(me - step, 0, size - 1), axis=1)
    far = jnp.take(labels, jnp.clip(me - step * (1 + k), 0, size - 1), axis=1)
    return shifted(x, step), shifted(x, step * (1 + k)), (near == far).astype(F32)


def on_device(
    tokens, doc_ids, query_weight, key_weight, value_weight, out_weight,
    gate_weight, up_weight, down_weight, mix_gain, mlp_gain, cotangent,
):
    n, blocks = lax.axis_size("head"), lax.axis_size("seq")
    here, me = lax.axis_index("head"), lax.axis_index("seq")
    rows, d = tokens.shape[1:]
    wb = d // blocks
    nb = blocks if wb % 128 == 0 else 1
    heads = query_weight.shape[1] // FDIM
    nqkv = 2 * heads * FDIM + heads * VDIM
    nv = heads * VDIM
    ff = gate_weight.shape[1]
    x, cot = tokens[0], cotangent[0]

    xs = jnp.stack(spread(x))
    small = jnp.concatenate([mix_gain, mlp_gain, doc_ids[0].astype(BF16)])
    small = lax.all_gather(small, "head")
    width = small.shape[1]
    extra = -(-n * width // (16 * wb)) * 16
    small = jnp.pad(small.reshape(-1), (0, extra * wb - n * width)).reshape(extra, wb)
    pack = jnp.concatenate(
        [query_weight.T, key_weight.T, value_weight.T, out_weight, small], axis=0
    )
    pack = lax.all_gather(pack, "seq")
    small = pack[:, nqkv + nv :].reshape(blocks, -1)[:, : n * width].reshape(blocks, n, width)
    piece = mix_gain.shape[0]
    gain_mix = jnp.transpose(small[:, :, :piece], (1, 0, 2)).reshape(1, d).astype(F32)
    gain_mlp = jnp.transpose(small[:, :, piece : 2 * piece], (1, 0, 2)).reshape(1, d).astype(F32)
    docs = jnp.take(small[:, :, 2 * piece :].astype(F32), here ^ jnp.arange(n), axis=1)
    segs = jnp.take(docs, me, axis=0)
    lasts = jnp.transpose(docs[:, :, -1])

    def blocked(w):
        return w if nb == blocks else jnp.transpose(w, (1, 0, 2)).reshape(1, w.shape[1], d)

    def unblocked(w):
        return w if nb == blocks else jnp.transpose(w.reshape(w.shape[1], blocks, wb), (1, 0, 2))

    w_qkv = blocked(pack[:, :nqkv])
    w_out = jnp.stack(spread(blocked(pack[:, nqkv : nqkv + nv])))
    cots = spread(cot)
    mlp_pack = jnp.concatenate([gate_weight.T, up_weight.T, down_weight], axis=0)
    mlp_pack = lax.all_gather(mlp_pack, "seq")
    w_mlp = widen(blocked(mlp_pack))

    before = jnp.where(me > 0, jnp.take(lasts, jnp.maximum(me - 1, 0), axis=1), -1.0)
    final_label = jnp.take(lasts, me, axis=1)
    labels_back = jnp.concatenate([jnp.full((n, 1), -1.0), lasts[:, :-1]], axis=1)

    def join(a, b, flag):
        each = jnp.repeat(flag, heads // 2)[:, None, None]
        lane = jnp.arange(128) % (n * heads) // heads
        both = a[:-1].astype(F32) + b[:-1].astype(F32) * each
        norm = a[-1].astype(F32) + b[-1].astype(F32) * jnp.take(flag, lane)[None]
        return jnp.concatenate([both, norm[None]], axis=0).astype(BF16)

    def flags_of(labels, step):
        reach = max(blocks // 4, 1)
        k = 1
        while 2 * k < reach:
            k *= 2
        near = jnp.take(labels, jnp.clip(me - step, 0, blocks - 1), axis=1)
        far = jnp.take(labels, jnp.clip(me - step * (1 + k), 0, blocks - 1), axis=1)
        return (near == far).astype(F32)

    flat = jnp.ones((1, rows), F32)
    masks = jnp.stack(
        [
            segs,
            (segs == final_label[:, None]).astype(F32),
            (segs == before[:, None]).astype(F32),
            flags_of(lasts, 1)[:, None] * flat,
            flags_of(labels_back, -1)[:, None] * flat,
        ]
        + [jnp.zeros_like(segs)] * 3,
        axis=1,
    )

    h1, qk, v, sums = project(xs, gain_mix, w_qkv, masks, heads)
    one, two, _ = carried(sums, lasts, 1, join)
    nd = local(qk, v, masks)
    o, on, inv, c = carry(nd, qk, masks, one, two)
    o_all = jnp.stack(swap([o[r] for r in range(n)]))
    y1, h2 = middle(x, o_all, w_out, gain_mlp)
    h2s = spread(h2)
    res = [mlp(h2s[r], cots[r], w_mlp) for r in range(n)]
    dparts, oparts, hid, dg, du = ([t[k] for t in res] for k in range(5))
    dparts = swap(dparts)
    dy1, f, do, dgain_mlp = turn(dparts, y1, cot, gain_mlp, w_out)
    do = jnp.stack(swap([do[r] for r in range(n)]))
    dext, dsums = back_first(do, on, inv, qk, masks)
    back_one, back_two, _ = carried(dsums, labels_back, -1, join)
    dq, dk, dv = back_local(dext, qk, v, masks, c)
    dmlp = unblocked(mlp_grads(h2s, cots, hid, dg, du, nb))
    dmlp = lax.psum_scatter(dmlp, "seq", tiled=True)[0].astype(F32)
    oparts = swap(oparts)
    output = y1
    for part in oparts:
        output = output + part.astype(F32)
    fs = spread(f)
    dout = halved(unblocked(out_grads(o, fs, nb)))[0].astype(F32)
    dh1, dqkv, dgain_mix = back_last(dq, dk, dv, qk, v, masks, back_one, back_two, h1, xs, w_qkv)
    dqkv = halved(unblocked(dqkv))[0].astype(F32)
    dh1 = swap([dh1[r] for r in range(n)])
    grad_tokens = final(dh1, x, dy1, gain_mix)

    gains = jnp.stack([dgain_mix[0], dgain_mlp[0]])
    gains = jnp.transpose(gains.reshape(2, n, blocks, piece), (1, 2, 0, 3))
    gains = jnp.take(gains, here ^ jnp.arange(n), axis=0)
    got = swap([gains[r] for r in range(n)])
    total = got[0]
    for part in got[1:]:
        total = total + part
    total = halved(total)[0]

    kq = heads * FDIM
    return (
        output.astype(BF16)[None],
        grad_tokens[None],
        dqkv[:kq].T,
        dqkv[kq : 2 * kq].T,
        dqkv[2 * kq :].T,
        dout,
        dmlp[:ff].T,
        dmlp[ff : 2 * ff].T,
        dmlp[2 * ff :],
        total[0],
        total[1],
    )


def solution(mesh):
    placed = (
        P("head", "seq", None),
        P("head", "seq"),
        P("seq", "head"),
        P("seq", "head"),
        P("seq", "head"),
        P("head", "seq"),
        P("seq", "head"),
        P("seq", "head"),
        P("head", "seq"),
        P(("head", "seq")),
        P(("head", "seq")),
        P("head", "seq", None),
    )
    return jax.shard_map(
        on_device,
        mesh=mesh,
        in_specs=placed,
        out_specs=(
            P("head", "seq", None),
            P("head", "seq", None),
            P("seq", "head"),
            P("seq", "head"),
            P("seq", "head"),
            P("head", "seq"),
            P("seq", "head"),
            P("seq", "head"),
            P("head", "seq"),
            P(("head", "seq")),
            P(("head", "seq")),
        ),
        check_vma=False,
    )
```

time: 1320 us -> 335 us (0.25); the launches traced: 1300 us -> 334 us
  waiting for transfers between devices: 716 us -> 107 us
  blocking collectives: 230 us -> 11.3 us
  matrix products: 140 us -> 0 us
  other arithmetic: 115 us -> 14.2 us
  Pallas kernels: 0 us -> 98.1 us
  starting transfers between devices: 1.38 us -> 60.3 us
  loops' own time: 30.2 us -> 0 us
  local copies, waits for them, and re-layouts: 54.1 us -> 28.2 us
    reduce_scatter x9 -> x1, waiting for transfers between devices: 416 us -> 0.01 us  [on_device(): dmlp = lax.psum_scatter(dmlp, 'seq', tiled=True)[0].astype(F32)]
    all_gather x7 -> x2, waiting for transfers between devices: 190 us -> 0.01 us  [the longest x1 0.01 us: on_device(): pack = lax.all_gather(pack, 'seq')]
    dot_general x36 -> x0, matrix products: 140 us -> none  [the longest x1 8 us: on_device(): jnp.einsum('bcd,fd->bcf', source_cot, down_full, preferred_element_type=j...]
    all_gather x10 -> x0, blocking collectives: 121 us -> none  [the longest x1 17.2 us: on_device(): lax.all_gather(pieces[0], 'seq', axis=0, tiled=True)]
    unnamed x28 -> x3, waiting for transfers between devices: 110 us -> 0.05 us
    ppermute x0 -> x46, waiting for transfers between devices: none -> 107 us  [the longest x33 89.6 us: swap(): lax.ppermute(parts[r], 'head', xor_pairs(size, r))]
    pallas_call x0 -> x16, Pallas kernels: none -> 98.1 us  [the longest x15 91.3 us: call(): pl.pallas_call(body, out_shape=outs, scratch_shapes=list(scratch), compil...]
    unnamed x4 -> x1, blocking collectives: 109 us -> 11.3 us
  transfers between devices with their start and end apart: 22 -> 49, of which waited for: 16 -> 18; matrix products, arithmetic and copies ran while one was open for 21% -> 8% of each run, Pallas kernels for 0% -> 24%
where the time goes in v1:
time: 335 us; the launch traced here: 334 us
  waiting for transfers between devices  107 us (32%)
  Pallas kernels  98.1 us (29%)
  starting transfers between devices  60.3 us (18%)
  local copies, waits for them, and re-layouts  28.2 us (8%)
  between operations  14.9 us (4%)
  other arithmetic  14.2 us (4%)
  blocking collectives  11.3 us (3%)
    pallas_call x15, Pallas kernels, call(): pl.pallas_call(body, out_shape=outs, scratch_shapes=list(scratch), compil...  91.3 us
    ppermute x33, waiting for transfers between devices, swap(): lax.ppermute(parts[r], 'head', xor_pairs(size, r))  89.6 us
    ppermute x33, starting transfers between devices, swap(): lax.ppermute(parts[r], 'head', xor_pairs(size, r))  38.1 us
    unnamed x64, local copies, waits for them, and re-layouts  13.9 us
    ppermute x9, starting transfers between devices, halved(): got = lax.ppermute(send, 'seq', xor_pairs(size, k))  13.2 us
    unnamed x1, blocking collectives  11.3 us
    ppermute x4, waiting for transfers between devices, shifted(): lax.ppermute(x, 'seq', [(i, i + step) for i in range(size) if 0 <= i + st...  10.1 us
    ppermute x4, starting transfers between devices, shifted(): lax.ppermute(x, 'seq', [(i, i + step) for i in range(size) if 0 <= i + st...  8.9 us
  transfers between devices with their start and end apart: 49, of which 18 were waited for; matrix products, arithmetic and copies ran while one was open for 8% of the time, Pallas kernels for 24%

profile of v1, /device:TPU:0, one launch (start us, length us, event | category | flops | bytes accessed | tf_op | source)
XLA Modules:
  0.0 333.9 jit_solution(2790240165138003982)
XLA Ops:
  12.5 11.3 %all-reduce.2 = bf16[1280]{0:T(1024)(128)(2,1)S(1)} all-reduce(bf16[1280]{0:T(1024)(128)(2,1)S(1)} %dynamic-update-slice.2), channel_id=2, replica_groups=mesh['head'=4,'seq'=8] {'head'}, use_global_device_ids=true, to_apply=%add.2 | all-reduce | flops 1280 | bytes 5120
  26.2 1.9 pad_maximum_fusion.2
  29.4 2.4 collective-permute-start
  31.8 12.2 %collective-permute-done.2 = bf16[256,1024]{1,0:T(8,128)(2,1)S(1)} collective-permute-done((bf16[256,1024]{1,0:T(8,128)(2,1)S(1)}, bf16[256,1024]{1,0:T(8,128)(2,1)S(1)}, u32[]{:S(2)}, u32[]{:S(2)}) %collective-permute-start.2) | collective-permute-done | bytes 524320 | tf_op jit(solution)/shard_map/ppermute | solution.py:676
  44.1 7.6 %collective-permute-done.1 = bf16[256,1024]{1,0:T(8,128)(2,1)S(1)} collective-permute-done((bf16[256,1024]{1,0:T(8,128)(2,1)S(1)}, bf16[256,1024]{1,0:T(8,128)(2,1)S(1)}, u32[]{:S(2)}, u32[]{:S(2)}) %collective-permute-start.1) | collective-permute-done | bytes 524320 | tf_op jit(solution)/shard_map/ppermute | solution.py:676
  51.6 1.6 pad_maximum_fusion.x_ref
  53.2 2.1 slice.181.w_ref
  59.4 6.4 %shard_map.203 = (bf16[4,256,1024]{2,1,0:T(8,128)(2,1)}, bf16[4,128,256]{2,1,0:T(8,128)(2,1)}, bf16[4,256,256]{2,1,0:T(8,128)(2,1)}, bf16[9,176,128]{2,1,0:T(8,128)(2,1)}) custom-call(bf16[4,256,1024]{2,1,0:T(8,128)(2,1)} %pad_maximum_fusion.x_ref, f32[1,1024]{1,0:T(1,128)} %reshape.334.gain_ref.refs_6_, bf16[8,384,128]{2,1,0:T(8,128)(2,1)} %slice.181.w_ref, ...), custom_call_target="tpu_custom_call" | custom-call | flops 805306368 | bytes 6209536 | tf_op jit(solution)/shard_map/pallas_call | solution.py:33
  65.8 2.4 collective-permute-start.3
  68.2 3.9 %collective-permute-start.4 = (bf16[9,176,128]{2,1,0:T(8,128)(2,1)}, bf16[9,176,128]{2,1,0:T(8,128)(2,1)}, u32[]{:S(2)}, u32[]{:S(2)}) collective-permute-start(bf16[9,176,128]{2,1,0:T(8,128)(2,1)} %get-tuple-element.56), channel_id=1, source_target_pairs={{0,2},{1,3},{2,4},{3,5},{4,6},{5,7},{8,10},{9,11},{10,12},{11,13},... | collective-permute-start | bytes 1216520 | tf_op jit(solution)/shard_map/ppermute | solution.py:685
  75.3 1.6 collective-permute-start.8
  77.6 5.2 %shard_map.204.nd_ref = f32[4,2,256,256]{3,2,1,0:T(8,128)} custom-call(bf16[4,128,256]{2,1,0:T(8,128)(2,1)} %get-tuple-element.54.qk_ref, bf16[4,256,256]{2,1,0:T(8,128)(2,1)} %get-tuple-element.55.v_ref, f32[4,8,256]{2,1,0:T(8,128)} %stack.76.masks_ref), custom_call_target="tpu_custom_call" | custom-call | flops 629145600 | bytes 2916352 | tf_op jit(solution)/shard_map/pallas_call | solution.py:33
  84.1 6.0 %collective-permute-done.4.two_ref = bf16[9,176,128]{2,1,0:T(8,128)(2,1)} collective-permute-done((bf16[9,176,128]{2,1,0:T(8,128)(2,1)}, bf16[9,176,128]{2,1,0:T(8,128)(2,1)}, u32[]{:S(2)}, u32[]{:S(2)}) %collective-permute-start.4) | collective-permute-done | bytes 405536 | tf_op jit(solution)/shard_map/ppermute | solution.py:685
  90.0 5.6 %shard_map.205 = (bf16[4,256,256]{2,1,0:T(8,128)(2,1)}, f32[4,256,256]{2,1,0:T(8,128)}, f32[4,256,256]{2,1,0:T(8,128)}, bf16[9,176,128]{2,1,0:T(8,128)(2,1)}) custom-call(f32[4,2,256,256]{3,2,1,0:T(8,128)} %shard_map.204.nd_ref, bf16[4,128,256]{2,1,0:T(8,128)(2,1)} %get-tuple-element.54.qk_ref, f32[4,8,256]{2,1,0:T(8,128)} %stack.76.masks_ref, ...), custom_call_target="tpu_custom_call" | custom-call | flops 1048576000 | bytes 6230016 | tf_op jit(solution)/shard_map/pallas_call | solution.py:33
  98.7 1.8 collective-permute-done.9
  102.7 11.5 %collective-permute-done.7 = bf16[256,256]{1,0:T(8,128)(2,1)S(1)} collective-permute-done((bf16[256,256]{1,0:T(8,128)(2,1)S(1)}, bf16[256,256]{1,0:T(8,128)(2,1)S(1)}, u32[]{:S(2)}, u32[]{:S(2)}) %collective-permute-start.7) | collective-permute-done | bytes 131104 | tf_op jit(solution)/shard_map/ppermute | solution.py:676
  114.2 2.9 collective-permute-done.6
  118.0 4.1 %shard_map.206 = (f32[256,1024]{1,0:T(8,128)}, bf16[256,1024]{1,0:T(8,128)(2,1)}) custom-call(bf16[256,1024]{1,0:T(8,128)(2,1)} %bitcast.156, bf16[4,256,256]{2,1,0:T(8,128)(2,1)} %pad_maximum_fusion.3.o_ref, bf16[4,8,256,128]{3,2,1,0:T(8,128)(2,1)} %pad_maximum_fusion.1.wo_ref.refs_7_, f32[1,1024]{1,0:T(1,128)} %reshape.342.gain_ref.refs_6_), custom_call_target="tpu_custom_call" | custom-call | flops 536870912 | bytes 4722688 | tf_op jit(solution)/shard_map/pallas_call | solution.py:33
  126.7 6.8 %shard_map.207.w_ref = bf16[2064,1024]{1,0:T(8,128)(2,1)} custom-call(bf16[8,2064,128]{2,1,0:T(8,128)(2,1)} %bitcast.161), custom_call_target="tpu_custom_call" | custom-call | bytes 8454144 | tf_op jit(solution)/shard_map/pallas_call | solution.py:330
  134.2 6.2 %shard_map.208 = (bf16[256,1024]{1,0:T(8,128)(2,1)}, bf16[256,1024]{1,0:T(8,128)(2,1)}, bf16[256,688]{1,0:T(8,128)(2,1)}, bf16[256,688]{1,0:T(8,128)(2,1)}, bf16[256,688]{1,0:T(8,128)(2,1)}) custom-call(bf16[256,1024]{1,0:T(8,128)(2,1)} %get-tuple-element.59.h2_ref.refs_0_, bf16[256,1024]{1,0:T(8,128)(2,1)} %bitcast.174, bf16[2064,1024]{1,0:T(8,128)(2,1)} %shard_map.207.w_ref), custom_call_target="tpu_custom_call" | custom-call | flops 2164260864 | bytes 7380992 | tf_op jit(solution)/shard_map/pallas_call | solution.py:33
  141.2 6.2 %shard_map.211 = (bf16[256,1024]{1,0:T(8,128)(2,1)}, bf16[256,1024]{1,0:T(8,128)(2,1)}, bf16[256,688]{1,0:T(8,128)(2,1)}, bf16[256,688]{1,0:T(8,128)(2,1)}, bf16[256,688]{1,0:T(8,128)(2,1)}) custom-call(bf16[256,1024]{1,0:T(8,128)(2,1)} %copy-done.20, bf16[256,1024]{1,0:T(8,128)(2,1)} %collective-permute-done.18.cot_ref.refs_7_, ...), custom_call_target="tpu_custom_call" | custom-call | flops 2164260864 | bytes 7380992 | tf_op jit(solution)/shard_map/pallas_call | solution.py:33
  148.5 11.0 %collective-permute-done.14.h2_ref.refs_2_ = bf16[256,1024]{1,0:T(8,128)(2,1)S(1)} collective-permute-done((bf16[256,1024]{1,0:T(8,128)(2,1)}, bf16[256,1024]{1,0:T(8,128)(2,1)S(1)}, u32[]{:S(2)}, u32[]{:S(2)}) %collective-permute-start.14) | collective-permute-done | bytes 524320 | tf_op jit(solution)/shard_map/ppermute | solution.py:676
  160.3 6.2 %shard_map.210 = (bf16[256,1024]{1,0:T(8,128)(2,1)}, bf16[256,1024]{1,0:T(8,128)(2,1)}, bf16[256,688]{1,0:T(8,128)(2,1)}, bf16[256,688]{1,0:T(8,128)(2,1)}, bf16[256,688]{1,0:T(8,128)(2,1)}) custom-call(bf16[256,1024]{1,0:T(8,128)(2,1)} %copy-done.22, bf16[256,1024]{1,0:T(8,128)(2,1)} %copy-done.21, bf16[2064,1024]{1,0:T(8,128)(2,1)} %shard_map.207.w_ref), custom_call_target="tpu_custom_call" | custom-call | flops 2164260864 | bytes 7380992 | tf_op jit(solution)/shard_map/pallas_call | solution.py:33
  168.1 6.2 %shard_map.209 = (bf16[256,1024]{1,0:T(8,128)(2,1)}, bf16[256,1024]{1,0:T(8,128)(2,1)}, bf16[256,688]{1,0:T(8,128)(2,1)}, bf16[256,688]{1,0:T(8,128)(2,1)}, bf16[256,688]{1,0:T(8,128)(2,1)}) custom-call(bf16[256,1024]{1,0:T(8,128)(2,1)} %copy-done.25, bf16[256,1024]{1,0:T(8,128)(2,1)} %copy-done.23, bf16[2064,1024]{1,0:T(8,128)(2,1)} %shard_map.207.w_ref), custom_call_target="tpu_custom_call" | custom-call | flops 2164260864 | bytes 7380992 | tf_op jit(solution)/shard_map/pallas_call | solution.py:33
  174.3 10.3 %shard_map.218 = bf16[8,2064,128]{2,1,0:T(8,128)(2,1)} custom-call(bf16[256,1024]{1,0:T(8,128)(2,1)} %get-tuple-element.59.h2_ref.refs_0_, bf16[256,1024]{1,0:T(8,128)(2,1)} %copy-done.25, bf16[256,1024]{1,0:T(8,128)(2,1)} %copy-done.22, bf16[256,1024]{1,0:T(8,128)(2,1)} %copy-done.20, bf16[256,1024]{1,0:T(8,128)(2,1)} %bitcast.175, ...), custom_call_target="tpu_custom_call" | custom-call | flops 4328521728 | bytes 12648448 | tf_op jit(solution)/shard_map/pallas_call | solution.py:33
  191.2 9.3 %collective-permute-done.20.refs_1_ = bf16[256,1024]{1,0:T(8,128)(2,1)S(1)} collective-permute-done((bf16[256,1024]{1,0:T(8,128)(2,1)S(1)}, bf16[256,1024]{1,0:T(8,128)(2,1)S(1)}, u32[]{:S(2)}, u32[]{:S(2)}) %collective-permute-start.20) | collective-permute-done | bytes 524320 | tf_op jit(solution)/shard_map/ppermute | solution.py:676
  201.0 22.5 %collective-permute-done.21.refs_2_ = bf16[256,1024]{1,0:T(8,128)(2,1)S(1)} collective-permute-done((bf16[256,1024]{1,0:T(8,128)(2,1)S(1)}, bf16[256,1024]{1,0:T(8,128)(2,1)S(1)}, u32[]{:S(2)}, u32[]{:S(2)}) %collective-permute-start.21) | collective-permute-done | bytes 524320 | tf_op jit(solution)/shard_map/ppermute | solution.py:676
  224.5 5.3 %shard_map.212 = (f32[256,1024]{1,0:T(8,128)}, bf16[256,1024]{1,0:T(8,128)(2,1)}, bf16[4,256,256]{2,1,0:T(8,128)(2,1)}, f32[1,1024]{1,0:T(1,128)}) custom-call(bf16[256,1024]{1,0:T(8,128)(2,1)} %get-tuple-element.64.refs_0_, bf16[256,1024]{1,0:T(8,128)(2,1)} %copy-done.7, bf16[256,1024]{1,0:T(8,128)(2,1)} %copy-done.8, bf16[256,1024]{1,0:T(8,128)(2,1)} %copy-done.9, ...), custom_call_target="tpu_custom_call" | custom-call | flops 536870912 | bytes 7872512 | tf_op jit(solution)/shard_map/pallas_call | solution.py:33
  229.8 1.8 fusion.29
  234.5 3.0 collective-permute-done.25
  240.4 3.8 %collective-permute-done.23 = bf16[256,256]{1,0:T(8,128)(2,1)} collective-permute-done((bf16[256,256]{1,0:T(8,128)(2,1)}, bf16[256,256]{1,0:T(8,128)(2,1)}, u32[]{:S(2)}, u32[]{:S(2)}) %collective-permute-start.23) | collective-permute-done | bytes 131104 | tf_op jit(solution)/shard_map/ppermute | solution.py:676
  244.2 1.6 collective-permute-start.35
  245.8 1.8 pad_maximum_fusion.4.do_ref
  247.6 6.0 %shard_map.213 = (bf16[4,4,256,128]{3,2,1,0:T(8,128)(2,1)}, bf16[9,176,128]{2,1,0:T(8,128)(2,1)}) custom-call(bf16[4,256,256]{2,1,0:T(8,128)(2,1)} %pad_maximum_fusion.4.do_ref, f32[4,256,256]{2,1,0:T(8,128)} %get-tuple-element.69.on_ref, f32[4,256,256]{2,1,0:T(8,128)} %get-tuple-element.70.inv_ref, bf16[4,128,256]{2,1,0:T(8,128)(2,1)} %get-tuple-element.54.qk_ref, ...), custom_call_target="tpu_custom_call" | custom-call | flops 629145600 | bytes 4370432 | tf_op jit(solution)/shard_map/pallas_call | solution.py:33
  258.9 7.5 %shard_map.214 = (bf16[4,64,256]{2,1,0:T(8,128)(2,1)}, f32[4,64,256]{2,1,0:T(8,128)}, f32[4,256,256]{2,1,0:T(8,128)}) custom-call(bf16[4,4,256,128]{3,2,1,0:T(8,128)(2,1)} %get-tuple-element.71.d_ref, bf16[4,128,256]{2,1,0:T(8,128)(2,1)} %get-tuple-element.54.qk_ref, bf16[4,256,256]{2,1,0:T(8,128)(2,1)} %get-tuple-element.55.v_ref, ...), custom_call_target="tpu_custom_call" | custom-call | flops 1572864000 | bytes 3715072 | tf_op jit(solution)/shard_map/pallas_call | solution.py:33
  266.4 4.1 %collective-permute-done.27.two_ref = bf16[9,176,128]{2,1,0:T(8,128)(2,1)S(1)} collective-permute-done((bf16[9,176,128]{2,1,0:T(8,128)(2,1)}, bf16[9,176,128]{2,1,0:T(8,128)(2,1)S(1)}, u32[]{:S(2)}, u32[]{:S(2)}) %collective-permute-start.27) | collective-permute-done | bytes 405536 | tf_op jit(solution)/shard_map/ppermute | solution.py:685
  271.3 9.4 %shard_map.215 = (bf16[4,256,1024]{2,1,0:T(8,128)(2,1)}, bf16[8,384,128]{2,1,0:T(8,128)(2,1)}, f32[1,1024]{1,0:T(1,128)}) custom-call(bf16[4,64,256]{2,1,0:T(8,128)(2,1)} %get-tuple-element.73.dq_ref, f32[4,64,256]{2,1,0:T(8,128)} %get-tuple-element.74.dk_ref, f32[4,256,256]{2,1,0:T(8,128)} %get-tuple-element.75.dv_ref, ...), custom_call_target="tpu_custom_call" | custom-call | flops 1610612736 | bytes 10940416 | tf_op jit(solution)/shard_map/pallas_call | solution.py:33
  284.2 1.6 collective-permute-start.40
  285.8 3.2 shard_map.217
  290.7 1.7 collective-permute-start.44
  296.9 3.0 collective-permute-start.45
  302.1 2.0 collective-permute-start.38
  305.4 3.2 collective-permute-done.38
  308.6 3.0 collective-permute-start.39
  311.6 2.3 collective-permute-done.32
  314.0 1.8 collective-permute-start.33
  316.5 2.7 collective-permute-done.29.refs_2_
  320.2 3.6 %shard_map.216 = f32[256,1024]{1,0:T(8,128)} custom-call(bf16[256,1024]{1,0:T(8,128)(2,1)} %get-tuple-element.162.refs_0_, bf16[256,1024]{1,0:T(8,128)(2,1)} %copy-done.10, bf16[256,1024]{1,0:T(8,128)(2,1)} %copy-done.11, bf16[256,1024]{1,0:T(8,128)(2,1)} %copy-done.12, bf16[256,1024]{1,0:T(8,128)(2,1)} %bitcast.157, f32[256,1024]{1,0:T(8,128)} %get-tuple-element.79.refs_5_, ...), custom_call_target="tpu_custom_call" | custom-call | bytes 4722688 | tf_op jit(solution)/shard_map/pallas_call | solution.py:33
  (205 shorter events, 71.3 us)
Async XLA Ops:
  7.2 46.0 %all-gather.6.cloned.1.call-start = ((), (), s32[]{:S(2)}) async-start(), calls=%async_computation.2 | async-start | bytes 1511424 | tf_op jit(solution)/shard_map/all_gather | solution.py:743
  26.2 100.5 %all-gather.8.cloned.1.call-start = ((), (), s32[]{:S(2)}) async-start(), calls=%async_computation.3 | async-start | bytes 4755456 | tf_op jit(solution)/shard_map/all_gather | solution.py:762
  28.2 297.1 %reduce-scatter.2.cloned.1.call-start = ((), (), s32[]{:S(2)}) async-start(), calls=%async_computation.1 | async-start | bytes 4755456 | tf_op jit(solution)/shard_map/reduce_scatter | solution.py:814
  28.2 15.8 %collective-permute-start.2 = (bf16[256,1024]{1,0:T(8,128)(2,1)S(1)}, bf16[256,1024]{1,0:T(8,128)(2,1)S(1)}, u32[]{:S(2)}, u32[]{:S(2)}) collective-permute-start(bf16[256,1024]{1,0:T(8,128)(2,1)S(1)} %bitcast.158), channel_id=1, source_target_pairs={{0,24},{8,16},{16,8},{24,0},{1,25},{9,17},{17,9},{25,1},{2,26},{10... | collective-permute-start | bytes 1572872 | tf_op jit(solution)/shard_map/ppermute | solution.py:676
  28.8 22.8 %collective-permute-start.1 = (bf16[256,1024]{1,0:T(8,128)(2,1)S(1)}, bf16[256,1024]{1,0:T(8,128)(2,1)S(1)}, u32[]{:S(2)}, u32[]{:S(2)}) collective-permute-start(bf16[256,1024]{1,0:T(8,128)(2,1)S(1)} %bitcast.159), channel_id=1, source_target_pairs={{0,16},{8,24},{16,0},{24,8},{1,17},{9,25},{17,1},{25,9},{2,18},{10... | collective-permute-start | bytes 1572872 | tf_op jit(solution)/shard_map/ppermute | solution.py:676
  29.4 22.2 %collective-permute-start = (bf16[256,1024]{1,0:T(8,128)(2,1)S(1)}, bf16[256,1024]{1,0:T(8,128)(2,1)S(1)}, u32[]{:S(2)}, u32[]{:S(2)}) collective-permute-start(bf16[256,1024]{1,0:T(8,128)(2,1)S(1)} %bitcast.160), channel_id=1, source_target_pairs={{0,8},{8,0},{16,24},{24,16},{1,9},{9,1},{17,25},{25,17},{2,10},{10... | collective-permute-start | bytes 1572872 | tf_op jit(solution)/shard_map/ppermute | solution.py:676
  65.8 17.0 %collective-permute-start.3 = (bf16[9,176,128]{2,1,0:T(8,128)(2,1)}, bf16[9,176,128]{2,1,0:T(8,128)(2,1)}, u32[]{:S(2)}, u32[]{:S(2)}) collective-permute-start(bf16[9,176,128]{2,1,0:T(8,128)(2,1)} %get-tuple-element.56), channel_id=1, source_target_pairs={{0,1},{1,2},{2,3},{3,4},{4,5},{5,6},{6,7},{8,9},{9,10},{10,11},{11... | collective-permute-start | bytes 1216520 | tf_op jit(solution)/shard_map/ppermute | solution.py:685
  68.2 21.8 %collective-permute-start.4 = (bf16[9,176,128]{2,1,0:T(8,128)(2,1)}, bf16[9,176,128]{2,1,0:T(8,128)(2,1)}, u32[]{:S(2)}, u32[]{:S(2)}) collective-permute-start(bf16[9,176,128]{2,1,0:T(8,128)(2,1)} %get-tuple-element.56), channel_id=1, source_target_pairs={{0,2},{1,3},{2,4},{3,5},{4,6},{5,7},{8,10},{9,11},{10,12},{11,13},... | collective-permute-start | bytes 1216520 | tf_op jit(solution)/shard_map/ppermute | solution.py:685
  73.4 24.8 %collective-permute-start.10 = (bf16[8,256,128]{2,1,0:T(8,128)(2,1)S(1)}, bf16[8,256,128]{2,1,0:T(8,128)(2,1)S(1)}, u32[]{:S(2)}, u32[]{:S(2)}) collective-permute-start(bf16[8,256,128]{2,1,0:T(8,128)(2,1)S(1)} %get-tuple-element.164), channel_id=1, source_target_pairs={{0,24},{8,16},{16,8},{24,0},{1,25},{9,17},{17,9},{25,1},{2,26},{10... | collective-permute-start | bytes 1572872 | tf_op jit(solution)/shard_map/ppermute | solution.py:676
  74.6 26.0 %collective-permute-start.9 = (bf16[8,256,128]{2,1,0:T(8,128)(2,1)S(1)}, bf16[8,256,128]{2,1,0:T(8,128)(2,1)S(1)}, u32[]{:S(2)}, u32[]{:S(2)}) collective-permute-start(bf16[8,256,128]{2,1,0:T(8,128)(2,1)S(1)} %get-tuple-element.164), channel_id=1, source_target_pairs={{0,16},{8,24},{16,0},{24,8},{1,17},{9,25},{17,1},{25,9},{2,18},{10... | collective-permute-start | bytes 1572872 | tf_op jit(solution)/shard_map/ppermute | solution.py:676
  75.3 25.8 %collective-permute-start.8 = (bf16[8,256,128]{2,1,0:T(8,128)(2,1)S(1)}, bf16[8,256,128]{2,1,0:T(8,128)(2,1)S(1)}, u32[]{:S(2)}, u32[]{:S(2)}) collective-permute-start(bf16[8,256,128]{2,1,0:T(8,128)(2,1)S(1)} %get-tuple-element.164), channel_id=1, source_target_pairs={{0,8},{8,0},{16,24},{24,16},{1,9},{9,1},{17,25},{25,17},{2,10},{10... | collective-permute-start | bytes 1572872 | tf_op jit(solution)/shard_map/ppermute | solution.py:676
  82.8 50.7 %collective-permute-start.18 = (bf16[256,1024]{1,0:T(8,128)(2,1)S(1)}, bf16[256,1024]{1,0:T(8,128)(2,1)}, u32[]{:S(2)}, u32[]{:S(2)}) collective-permute-start(bf16[256,1024]{1,0:T(8,128)(2,1)S(1)} %bitcast.177), channel_id=1, source_target_pairs={{0,24},{8,16},{16,8},{24,0},{1,25},{9,17},{17,9},{25,1},{2,26},{10... | collective-permute-start | bytes 1572872 | tf_op jit(solution)/shard_map/ppermute | solution.py:676
  96.8 17.4 %collective-permute-start.7 = (bf16[256,256]{1,0:T(8,128)(2,1)S(1)}, bf16[256,256]{1,0:T(8,128)(2,1)S(1)}, u32[]{:S(2)}, u32[]{:S(2)}) collective-permute-start(bf16[256,256]{1,0:T(8,128)(2,1)S(1)} %get-tuple-element.173), channel_id=1, source_target_pairs={{0,24},{8,16},{16,8},{24,0},{1,25},{9,17},{17,9},{25,1},{2,26},{10... | collective-permute-start | bytes 393224 | tf_op jit(solution)/shard_map/ppermute | solution.py:676
  98.1 19.0 %collective-permute-start.6 = (bf16[256,256]{1,0:T(8,128)(2,1)S(1)}, bf16[256,256]{1,0:T(8,128)(2,1)S(1)}, u32[]{:S(2)}, u32[]{:S(2)}) collective-permute-start(bf16[256,256]{1,0:T(8,128)(2,1)S(1)} %get-tuple-element.174), channel_id=1, source_target_pairs={{0,16},{8,24},{16,0},{24,8},{1,17},{9,25},{17,1},{25,9},{2,18},{10... | collective-permute-start | bytes 393224 | tf_op jit(solution)/shard_map/ppermute | solution.py:676
  100.6 16.6 %collective-permute-start.5 = (bf16[256,256]{1,0:T(8,128)(2,1)S(1)}, bf16[256,256]{1,0:T(8,128)(2,1)S(1)}, u32[]{:S(2)}, u32[]{:S(2)}) collective-permute-start(bf16[256,256]{1,0:T(8,128)(2,1)S(1)} %get-tuple-element.175), channel_id=1, source_target_pairs={{0,8},{8,0},{16,24},{24,16},{1,9},{9,1},{17,25},{25,17},{2,10},{10... | collective-permute-start | bytes 393224 | tf_op jit(solution)/shard_map/ppermute | solution.py:676
  122.1 18.4 %collective-permute-start.17 = (bf16[256,1024]{1,0:T(8,128)(2,1)}, bf16[256,1024]{1,0:T(8,128)(2,1)S(1)}, u32[]{:S(2)}, u32[]{:S(2)}) collective-permute-start(bf16[256,1024]{1,0:T(8,128)(2,1)} %get-tuple-element.59.h2_ref.refs_0_), channel_id=1, source_target_pairs={{0,24},{8,16},{16,8},{24,0},{1,25},{9,17},{17,9},{25,1},{2,26},{10... | collective-permute-start | bytes 1572872 | tf_op jit(solution)/shard_map/ppermute | solution.py:676
  123.3 25.2 %collective-permute-start.15 = (bf16[256,1024]{1,0:T(8,128)(2,1)S(1)}, bf16[256,1024]{1,0:T(8,128)(2,1)S(1)}, u32[]{:S(2)}, u32[]{:S(2)}) collective-permute-start(bf16[256,1024]{1,0:T(8,128)(2,1)S(1)} %bitcast.178), channel_id=1, source_target_pairs={{0,16},{8,24},{16,0},{24,8},{1,17},{9,25},{17,1},{25,9},{2,18},{10... | collective-permute-start | bytes 1572872 | tf_op jit(solution)/shard_map/ppermute | solution.py:676
  124.0 35.5 %collective-permute-start.14 = (bf16[256,1024]{1,0:T(8,128)(2,1)}, bf16[256,1024]{1,0:T(8,128)(2,1)S(1)}, u32[]{:S(2)}, u32[]{:S(2)}) collective-permute-start(bf16[256,1024]{1,0:T(8,128)(2,1)} %get-tuple-element.59.h2_ref.refs_0_), channel_id=1, source_target_pairs={{0,16},{8,24},{16,0},{24,8},{1,17},{9,25},{17,1},{25,9},{2,18},{10... | collective-permute-start | bytes 1572872 | tf_op jit(solution)/shard_map/ppermute | solution.py:676
  125.3 41.1 %collective-permute-start.12 = (bf16[256,1024]{1,0:T(8,128)(2,1)S(1)}, bf16[256,1024]{1,0:T(8,128)(2,1)S(1)}, u32[]{:S(2)}, u32[]{:S(2)}) collective-permute-start(bf16[256,1024]{1,0:T(8,128)(2,1)S(1)} %bitcast.179), channel_id=1, source_target_pairs={{0,8},{8,0},{16,24},{24,16},{1,9},{9,1},{17,25},{25,17},{2,10},{10... | collective-permute-start | bytes 1572872 | tf_op jit(solution)/shard_map/ppermute | solution.py:676
  133.5 33.0 %collective-permute-start.11 = (bf16[256,1024]{1,0:T(8,128)(2,1)S(1)}, bf16[256,1024]{1,0:T(8,128)(2,1)S(1)}, u32[]{:S(2)}, u32[]{:S(2)}) collective-permute-start(bf16[256,1024]{1,0:T(8,128)(2,1)S(1)} %copy-done.18), channel_id=1, source_target_pairs={{0,8},{8,0},{16,24},{24,16},{1,9},{9,1},{17,25},{25,17},{2,10},{10... | collective-permute-start | bytes 1572872 | tf_op jit(solution)/shard_map/ppermute | solution.py:676
  185.6 14.8 %collective-permute-start.20 = (bf16[256,1024]{1,0:T(8,128)(2,1)S(1)}, bf16[256,1024]{1,0:T(8,128)(2,1)S(1)}, u32[]{:S(2)}, u32[]{:S(2)}) collective-permute-start(bf16[256,1024]{1,0:T(8,128)(2,1)S(1)} %copy-done.24), channel_id=1, source_target_pairs={{0,8},{8,0},{16,24},{24,16},{1,9},{9,1},{17,25},{25,17},{2,10},{10... | collective-permute-start | bytes 1572872 | tf_op jit(solution)/shard_map/ppermute | solution.py:676
  186.2 37.3 %collective-permute-start.21 = (bf16[256,1024]{1,0:T(8,128)(2,1)S(1)}, bf16[256,1024]{1,0:T(8,128)(2,1)S(1)}, u32[]{:S(2)}, u32[]{:S(2)}) collective-permute-start(bf16[256,1024]{1,0:T(8,128)(2,1)S(1)} %copy-done.19), channel_id=1, source_target_pairs={{0,16},{8,24},{16,0},{24,8},{1,17},{9,25},{17,1},{25,9},{2,18},{10... | collective-permute-start | bytes 1572872 | tf_op jit(solution)/shard_map/ppermute | solution.py:676
  187.6 35.9 %collective-permute-start.22 = (bf16[256,1024]{1,0:T(8,128)(2,1)S(1)}, bf16[256,1024]{1,0:T(8,128)(2,1)S(1)}, u32[]{:S(2)}, u32[]{:S(2)}) collective-permute-start(bf16[256,1024]{1,0:T(8,128)(2,1)S(1)} %copy-done.17), channel_id=1, source_target_pairs={{0,24},{8,16},{16,8},{24,0},{1,25},{9,17},{17,9},{25,1},{2,26},{10... | collective-permute-start | bytes 1572872 | tf_op jit(solution)/shard_map/ppermute | solution.py:676
  189.1 64.4 %collective-permute-start.19 = (bf16[256,1024]{1,0:T(8,128)(2,1)}, bf16[256,1024]{1,0:T(8,128)(2,1)S(1)}, u32[]{:S(2)}, u32[]{:S(2)}) collective-permute-start(bf16[256,1024]{1,0:T(8,128)(2,1)} %get-tuple-element.63), channel_id=1, source_target_pairs={{0,24},{8,16},{16,8},{24,0},{1,25},{9,17},{17,9},{25,1},{2,26},{10... | collective-permute-start | bytes 1572872 | tf_op jit(solution)/shard_map/ppermute | solution.py:676
  190.5 64.5 %collective-permute-start.16 = (bf16[256,1024]{1,0:T(8,128)(2,1)}, bf16[256,1024]{1,0:T(8,128)(2,1)S(1)}, u32[]{:S(2)}, u32[]{:S(2)}) collective-permute-start(bf16[256,1024]{1,0:T(8,128)(2,1)} %get-tuple-element.62), channel_id=1, source_target_pairs={{0,16},{8,24},{16,0},{24,8},{1,17},{9,25},{17,1},{25,9},{2,18},{10... | collective-permute-start | bytes 1572872 | tf_op jit(solution)/shard_map/ppermute | solution.py:676
  200.4 55.9 %collective-permute-start.13 = (bf16[256,1024]{1,0:T(8,128)(2,1)}, bf16[256,1024]{1,0:T(8,128)(2,1)S(1)}, u32[]{:S(2)}, u32[]{:S(2)}) collective-permute-start(bf16[256,1024]{1,0:T(8,128)(2,1)} %get-tuple-element.61), channel_id=1, source_target_pairs={{0,8},{8,0},{16,24},{24,16},{1,9},{9,1},{17,25},{25,17},{2,10},{10... | collective-permute-start | bytes 1572872 | tf_op jit(solution)/shard_map/ppermute | solution.py:676
  231.6 6.0 %collective-permute-start.25 = (bf16[256,256]{1,0:T(8,128)(2,1)S(1)}, bf16[256,256]{1,0:T(8,128)(2,1)S(1)}, u32[]{:S(2)}, u32[]{:S(2)}) collective-permute-start(bf16[256,256]{1,0:T(8,128)(2,1)S(1)} %get-tuple-element.169), channel_id=1, source_target_pairs={{0,24},{8,16},{16,8},{24,0},{1,25},{9,17},{17,9},{25,1},{2,26},{10... | collective-permute-start | bytes 393224 | tf_op jit(solution)/shard_map/ppermute | solution.py:676
  233.1 6.0 %collective-permute-start.24 = (bf16[256,256]{1,0:T(8,128)(2,1)}, bf16[256,256]{1,0:T(8,128)(2,1)S(1)}, u32[]{:S(2)}, u32[]{:S(2)}) collective-permute-start(bf16[256,256]{1,0:T(8,128)(2,1)} %get-tuple-element.170), channel_id=1, source_target_pairs={{0,16},{8,24},{16,0},{24,8},{1,17},{9,25},{17,1},{25,9},{2,18},{10... | collective-permute-start | bytes 393224 | tf_op jit(solution)/shard_map/ppermute | solution.py:676
  237.6 6.6 %collective-permute-start.23 = (bf16[256,256]{1,0:T(8,128)(2,1)}, bf16[256,256]{1,0:T(8,128)(2,1)}, u32[]{:S(2)}, u32[]{:S(2)}) collective-permute-start(bf16[256,256]{1,0:T(8,128)(2,1)} %get-tuple-element.171), channel_id=1, source_target_pairs={{0,8},{8,0},{16,24},{24,16},{1,9},{9,1},{17,25},{25,17},{2,10},{10... | collective-permute-start | bytes 393224 | tf_op jit(solution)/shard_map/ppermute | solution.py:676
  239.1 45.1 %collective-permute-start.34 = (bf16[256,1024]{1,0:T(8,128)(2,1)}, bf16[256,1024]{1,0:T(8,128)(2,1)}, u32[]{:S(2)}, u32[]{:S(2)}) collective-permute-start(bf16[256,1024]{1,0:T(8,128)(2,1)} %get-tuple-element.81.refs_0_), channel_id=1, source_target_pairs={{0,8},{8,0},{16,24},{24,16},{1,9},{9,1},{17,25},{25,17},{2,10},{10... | collective-permute-start | bytes 1572872 | tf_op jit(solution)/shard_map/ppermute | solution.py:676
  244.2 41.6 %collective-permute-start.35 = (bf16[256,1024]{1,0:T(8,128)(2,1)}, bf16[256,1024]{1,0:T(8,128)(2,1)}, u32[]{:S(2)}, u32[]{:S(2)}) collective-permute-start(bf16[256,1024]{1,0:T(8,128)(2,1)} %get-tuple-element.81.refs_0_), channel_id=1, source_target_pairs={{0,16},{8,24},{16,0},{24,8},{1,17},{9,25},{17,1},{25,9},{2,18},{10... | collective-permute-start | bytes 1572872 | tf_op jit(solution)/shard_map/ppermute | solution.py:676
  253.6 32.2 %collective-permute-start.36 = (bf16[256,1024]{1,0:T(8,128)(2,1)}, bf16[256,1024]{1,0:T(8,128)(2,1)}, u32[]{:S(2)}, u32[]{:S(2)}) collective-permute-start(bf16[256,1024]{1,0:T(8,128)(2,1)} %get-tuple-element.81.refs_0_), channel_id=1, source_target_pairs={{0,24},{8,16},{16,8},{24,0},{1,25},{9,17},{17,9},{25,1},{2,26},{10... | collective-permute-start | bytes 1572872 | tf_op jit(solution)/shard_map/ppermute | solution.py:676
  255.0 11.4 %collective-permute-start.26 = (bf16[9,176,128]{2,1,0:T(8,128)(2,1)}, bf16[9,176,128]{2,1,0:T(8,128)(2,1)S(1)}, u32[]{:S(2)}, u32[]{:S(2)}) collective-permute-start(bf16[9,176,128]{2,1,0:T(8,128)(2,1)} %get-tuple-element.76), channel_id=1, source_target_pairs={{1,0},{2,1},{3,2},{4,3},{5,4},{6,5},{7,6},{9,8},{10,9},{11,10},{12... | collective-permute-start | bytes 1216520 | tf_op jit(solution)/shard_map/ppermute | solution.py:685
  256.3 14.2 %collective-permute-start.27 = (bf16[9,176,128]{2,1,0:T(8,128)(2,1)}, bf16[9,176,128]{2,1,0:T(8,128)(2,1)S(1)}, u32[]{:S(2)}, u32[]{:S(2)}) collective-permute-start(bf16[9,176,128]{2,1,0:T(8,128)(2,1)} %get-tuple-element.76), channel_id=1, source_target_pairs={{2,0},{3,1},{4,2},{5,3},{6,4},{7,5},{10,8},{11,9},{12,10},{13,11},... | collective-permute-start | bytes 1216520 | tf_op jit(solution)/shard_map/ppermute | solution.py:685
  282.3 6.7 %collective-permute-start.42 = (f32[8,2,32]{2,0,1:T(8,128)S(1)}, f32[8,2,32]{2,0,1:T(8,128)S(1)}, u32[]{:S(2)}, u32[]{:S(2)}) collective-permute-start(f32[8,2,32]{2,0,1:T(8,128)S(1)} %get-tuple-element.179), channel_id=1, source_target_pairs={{0,24},{8,16},{16,8},{24,0},{1,25},{9,17},{17,9},{25,1},{2,26},{10... | collective-permute-start | bytes 6152 | tf_op jit(solution)/shard_map/ppermute | solution.py:676
  283.8 5.2 %collective-permute-start.41 = (f32[8,2,32]{2,0,1:T(8,128)S(1)}, f32[8,2,32]{2,0,1:T(8,128)S(1)}, u32[]{:S(2)}, u32[]{:S(2)}) collective-permute-start(f32[8,2,32]{2,0,1:T(8,128)S(1)} %get-tuple-element.180), channel_id=1, source_target_pairs={{0,16},{8,24},{16,0},{24,8},{1,17},{9,25},{17,1},{25,9},{2,18},{10... | collective-permute-start | bytes 6152 | tf_op jit(solution)/shard_map/ppermute | solution.py:676
  284.2 4.8 %collective-permute-start.40 = (f32[8,2,32]{2,0,1:T(8,128)S(1)}, f32[8,2,32]{2,0,1:T(8,128)S(1)}, u32[]{:S(2)}, u32[]{:S(2)}) collective-permute-start(f32[8,2,32]{2,0,1:T(8,128)S(1)} %get-tuple-element.178), channel_id=1, source_target_pairs={{0,8},{8,0},{16,24},{24,16},{1,9},{9,1},{17,25},{25,17},{2,10},{10... | collective-permute-start | bytes 6152 | tf_op jit(solution)/shard_map/ppermute | solution.py:676
  290.1 11.9 %collective-permute-start.37 = (bf16[4,256,128]{2,1,0:T(8,128)(2,1)S(1)}, bf16[4,256,128]{2,1,0:T(8,128)(2,1)S(1)}, u32[]{:S(2)}, u32[]{:S(2)}) collective-permute-start(bf16[4,256,128]{2,1,0:T(8,128)(2,1)S(1)} %dynamic-slice_bitcast_fusion.1), channel_id=1, source_target_pairs={{0,1},{1,0},{2,3},{3,2},{4,5},{5,4},{6,7},{7,6},{8,9},{9,8},{10,11... | collective-permute-start | bytes 786440 | tf_op jit(solution)/shard_map/ppermute | solution.py:698
  290.7 6.2 %collective-permute-start.44 = (f32[2,2,32]{2,1,0:T(2,128)S(1)}, f32[2,2,32]{2,1,0:T(2,128)S(1)}, u32[]{:S(2)}, u32[]{:S(2)}) collective-permute-start(f32[2,2,32]{2,1,0:T(2,128)S(1)} %fusion.14), channel_id=1, source_target_pairs={{0,2},{1,3},{2,0},{3,1},{4,6},{5,7},{6,4},{7,5},{8,10},{9,11},{10,... | collective-permute-start | bytes 1544 | tf_op jit(solution)/shard_map/ppermute | solution.py:698
  293.4 23.1 %collective-permute-start.28 = (bf16[256,1024]{1,0:T(8,128)(2,1)S(1)}, bf16[256,1024]{1,0:T(8,128)(2,1)S(1)}, u32[]{:S(2)}, u32[]{:S(2)}) collective-permute-start(bf16[256,1024]{1,0:T(8,128)(2,1)S(1)} %get-tuple-element.161), channel_id=1, source_target_pairs={{0,8},{8,0},{16,24},{24,16},{1,9},{9,1},{17,25},{25,17},{2,10},{10... | collective-permute-start | bytes 1572872 | tf_op jit(solution)/shard_map/ppermute | solution.py:676
  294.7 24.5 %collective-permute-start.29 = (bf16[256,1024]{1,0:T(8,128)(2,1)S(1)}, bf16[256,1024]{1,0:T(8,128)(2,1)S(1)}, u32[]{:S(2)}, u32[]{:S(2)}) collective-permute-start(bf16[256,1024]{1,0:T(8,128)(2,1)S(1)} %get-tuple-element.160), channel_id=1, source_target_pairs={{0,16},{8,24},{16,0},{24,8},{1,17},{9,25},{17,1},{25,9},{2,18},{10... | collective-permute-start | bytes 1572872 | tf_op jit(solution)/shard_map/ppermute | solution.py:676
  295.4 23.8 %collective-permute-start.30 = (bf16[256,1024]{1,0:T(8,128)(2,1)S(1)}, bf16[256,1024]{1,0:T(8,128)(2,1)S(1)}, u32[]{:S(2)}, u32[]{:S(2)}) collective-permute-start(bf16[256,1024]{1,0:T(8,128)(2,1)S(1)} %get-tuple-element.159), channel_id=1, source_target_pairs={{0,24},{8,16},{16,8},{24,0},{1,25},{9,17},{17,9},{25,1},{2,26},{10... | collective-permute-start | bytes 1572872 | tf_op jit(solution)/shard_map/ppermute | solution.py:676
  296.9 4.6 %collective-permute-start.45 = (f32[1,2,32]{2,1,0:T(2,128)S(1)}, f32[1,2,32]{2,1,0:T(2,128)S(1)}, u32[]{:S(2)}, u32[]{:S(2)}) collective-permute-start(f32[1,2,32]{2,1,0:T(2,128)S(1)} %constant_dynamic-slice_fusion.7), channel_id=1, source_target_pairs={{0,4},{1,5},{2,6},{3,7},{4,0},{5,1},{6,2},{7,3},{8,12},{9,13},{10,... | collective-permute-start | bytes 776 | tf_op jit(solution)/shard_map/ppermute | solution.py:698
  301.5 2.7 collective-permute-start.31
  302.1 6.4 %collective-permute-start.38 = (bf16[2,256,128]{2,1,0:T(8,128)(2,1)S(1)}, bf16[2,256,128]{2,1,0:T(8,128)(2,1)S(1)}, u32[]{:S(2)}, u32[]{:S(2)}) collective-permute-start(bf16[2,256,128]{2,1,0:T(8,128)(2,1)S(1)} %dynamic-slice_bitcast_fusion.3), channel_id=1, source_target_pairs={{0,2},{1,3},{2,0},{3,1},{4,6},{5,7},{6,4},{7,5},{8,10},{9,11},{10,... | collective-permute-start | bytes 393224 | tf_op jit(solution)/shard_map/ppermute | solution.py:698
  304.3 9.6 %collective-permute-start.32 = (bf16[2,384,128]{2,1,0:T(8,128)(2,1)S(1)}, bf16[2,384,128]{2,1,0:T(8,128)(2,1)S(1)}, u32[]{:S(2)}, u32[]{:S(2)}) collective-permute-start(bf16[2,384,128]{2,1,0:T(8,128)(2,1)S(1)} %dynamic-slice_bitcast_fusion.2), channel_id=1, source_target_pairs={{0,2},{1,3},{2,0},{3,1},{4,6},{5,7},{6,4},{7,5},{8,10},{9,11},{10,... | collective-permute-start | bytes 589832 | tf_op jit(solution)/shard_map/ppermute | solution.py:698
  308.6 7.2 %collective-permute-start.39 = (bf16[1,256,128]{2,1,0:T(8,128)(2,1)S(1)}, bf16[1,256,128]{2,1,0:T(8,128)(2,1)S(1)}, u32[]{:S(2)}, u32[]{:S(2)}) collective-permute-start(bf16[1,256,128]{2,1,0:T(8,128)(2,1)S(1)} %constant_dynamic-slice_fusion.13), channel_id=1, source_target_pairs={{0,4},{1,5},{2,6},{3,7},{4,0},{5,1},{6,2},{7,3},{8,12},{9,13},{10,... | collective-permute-start | bytes 196616 | tf_op jit(solution)/shard_map/ppermute | solution.py:698
  314.0 9.8 %collective-permute-start.33 = (bf16[1,384,128]{2,1,0:T(8,128)(2,1)S(1)}, bf16[1,384,128]{2,1,0:T(8,128)(2,1)S(1)}, u32[]{:S(2)}, u32[]{:S(2)}) collective-permute-start(bf16[1,384,128]{2,1,0:T(8,128)(2,1)S(1)} %constant_dynamic-slice_fusion.14), channel_id=1, source_target_pairs={{0,4},{1,5},{2,6},{3,7},{4,0},{5,1},{6,2},{7,3},{8,12},{9,13},{10,... | collective-permute-start | bytes 294920 | tf_op jit(solution)/shard_map/ppermute | solution.py:698
  (27 other events, 191.7 us)
Sparse Core Ops, SparseCore 0:
  26.3 23.0 all-gather.5
  51.0 54.9 all-gather.7
  184.7 50.3 reduce-scatter.1

commit v2 on v1

v2 whole, which is shorter than its diff:
```python
import functools

import jax
import jax.numpy as jnp
from jax import lax
from jax.experimental import pallas as pl
from jax.experimental.pallas import tpu as pltpu
from jax.sharding import PartitionSpec as P

FDIM = 16
VDIM = 64
EPS = 1e-06
ROOT_HALF = 0.7071067811865476
FROWS = 11 * FDIM
F32 = jnp.float32
BF16 = jnp.bfloat16
VMEM_BYTES = 24 * 1024 * 1024
VMEM_MOST = 56 * 1024 * 1024

NN = (((1,), (0,)), ((), ()))
NT = (((1,), (1,)), ((), ()))
TN = (((0,), (0,)), ((), ()))


def mm(a, b, dims=NN):
    return lax.dot_general(a, b, dims, preferred_element_type=F32)


def call(body, outs, ins, grid=None, in_specs=None, out_specs=None, scratch=(), smem=0, us=5, most=False):
    kwargs = {}
    if smem:
        spaces = [pltpu.SMEM] * smem + [pltpu.VMEM] * (len(ins) - smem)
        kwargs = dict(in_specs=[pl.BlockSpec(memory_space=space) for space in spaces])
    if grid is not None:
        kwargs = dict(grid=grid, in_specs=in_specs, out_specs=out_specs)
    return pl.pallas_call(
        body,
        out_shape=outs,
        scratch_shapes=list(scratch),
        compiler_params=pltpu.CompilerParams(vmem_limit_bytes=VMEM_MOST if most else VMEM_BYTES),
        cost_estimate=pl.CostEstimate(flops=0, bytes_accessed=us * 600000, transcendentals=0),
        **kwargs,
    )(*ins)


def sds(shape, dtype):
    return jax.ShapeDtypeStruct(shape, dtype)


def whole(shape):
    return pl.BlockSpec(shape, lambda r: (0,) * len(shape))


def by_row(shape):
    return pl.BlockSpec((1,) + tuple(shape), lambda r: (r,) + (0,) * len(shape))


def coef(d):
    return ROOT_HALF if d in (0, FDIM // 2) else 1.0


def features(w):
    half = w * 0.5
    rows = [half]
    for d in range(FDIM // 2 + 1):
        other = half if d == 0 else pltpu.roll(half, FDIM - d, 0)
        rows.append(half * other * coef(d))
    first = lax.broadcasted_iota(jnp.int32, half.shape, 0) == 0
    rows.append(jnp.where(first, 1.0, 0.0))
    return jnp.concatenate(rows, axis=0)


def features_back(w, grad):
    half = w * 0.5
    total = grad[:FDIM]
    for d in range(FDIM // 2 + 1):
        part = grad[FDIM * (d + 1) : FDIM * (d + 2)]
        if d == 0:
            total = total + part * half * (2.0 * coef(0))
        else:
            near = part * pltpu.roll(half, FDIM - d, 0)
            far = pltpu.roll(part * half, d, 0)
            total = total + (near + far) * coef(d)
    return total * 0.5


def lanes(shape):
    return lax.broadcasted_iota(jnp.int32, shape, len(shape) - 1)


def one_hot_lanes(rows, index):
    lane = lanes((rows, 128))
    return jnp.where(lane == index, 1.0, 0.0).astype(BF16)


def own_half(x, j, other=None):
    left = lanes(x.shape) < VDIM
    keep = left if j == 0 else jnp.logical_not(left)
    return jnp.where(keep, x, jnp.zeros_like(x) if other is None else other)


def pick_columns(z, column, spots):
    row = lax.broadcasted_iota(jnp.int32, (128, 128), 0)
    hot = jnp.where(column(row), 1.0, 0.0) * jnp.where(spots(lanes((128, 128))), 1.0, 0.0)
    return mm(z, hot.astype(BF16))


def doc_mask(masks, rows):
    seg = masks[0:1, :]
    col = jnp.transpose(masks)[:, 0:1]
    causal = lax.broadcasted_iota(jnp.int32, (rows, rows), 0) >= lax.broadcasted_iota(
        jnp.int32, (rows, rows), 1
    )
    return jnp.logical_and(causal, col == seg)


def with_pair(z, j):
    lane = lanes(z.shape)
    base = VDIM if j == 0 else 0
    high = z.astype(BF16)
    low = (z - high.astype(F32)).astype(BF16)
    zero = jnp.zeros_like(high)
    return jnp.where(lane == base, high, jnp.where(lane == base + 1, low, zero))


def with_ones(x, j):
    lane = lanes(x.shape)
    base = VDIM if j == 0 else 0
    hot = jnp.where(jnp.logical_or(lane == base, lane == base + 1), 1.0, 0.0).astype(x.dtype)
    return own_half(x, j, hot)


def join_rows(refs):
    return refs[0][...] if len(refs) == 1 else jnp.concatenate([one[...] for one in refs], axis=0)


def grouped(refs, n):
    k = len(refs) // n
    return [refs[i * k : (i + 1) * k] for i in range(n)]


def flat(lists):
    return [x for one in lists for x in one]


def take_row(r, groups, ref):
    for index, one in enumerate(groups):
        @pl.when(r == index)
        def _():
            ref[...] = join_rows(one)


def give_row(r, refs, value):
    for index, one in enumerate(refs):
        @pl.when(r == index)
        def _():
            one[...] = value


def pack_body(q_ref, k_ref, v_ref, mix_ref, mlp_ref, docs_ref, pack_ref):
    at = 0
    for one in (q_ref, k_ref):
        pack_ref[at : at + one.shape[0], :] = one[...]
        at += one.shape[0]
    pack_ref[at : at + v_ref.shape[1], :] = v_ref[...].T
    at += v_ref.shape[1]
    wb = pack_ref.shape[1]
    extra = pack_ref.shape[0] - at
    rows = []
    for one in (mix_ref, mlp_ref):
        fill = jnp.zeros((1, wb - one.shape[1]), F32)
        rows.append(jnp.concatenate([one[...].astype(F32), fill], axis=1))
    rows.append(docs_ref[...].astype(F32))
    rows.append(jnp.zeros((extra - 2 - docs_ref.shape[0], wb), F32))
    pack_ref[at:, :] = jnp.concatenate(rows, axis=0).astype(BF16)


def pack_two_body(gate_ref, up_ref, pack_ref):
    ff = gate_ref.shape[0]
    pack_ref[:ff, :] = gate_ref[...]
    pack_ref[ff:, :] = up_ref[...]


def project_body(n, core_ref, x_ref, gain_ref, masks_ref, *refs):
    blocks = grouped(refs[:-6], n)
    h1_ref, qk_ref, v_ref, p_ref, wt_ref, z_ref = refs[-6:]
    r = pl.program_id(0)
    heads = qk_ref.shape[1] // (2 * FDIM)
    total = wt_ref.shape[1]

    @pl.when(r == 0)
    def _():
        x = x_ref[...].astype(F32)
        normed = x * lax.rsqrt(jnp.mean(x * x, axis=-1, keepdims=True) + EPS)
        h1_ref[...] = (normed * gain_ref[0:1, :]).astype(BF16)
        z_ref[...] = jnp.zeros_like(z_ref)

    for index, halves in enumerate(blocks):

        @pl.when(r == index)
        def _():
            for other, half in enumerate(halves):
                count, _, wb = half.shape
                side = core_ref[0] if other == 0 else 1 - core_ref[0]
                for j in range(count):
                    at = j * wb if count * wb == wt_ref.shape[2] else (side * count + j) * wb
                    if not isinstance(at, int):
                        at = pl.multiple_of(at, wb)
                    wt_ref[0, :, pl.ds(at, wb)] = half[j, :total, :]

    h1 = h1_ref[...]
    nqk = qk_ref.shape[1]
    qk = mm(wt_ref[0, :nqk, :], h1, NT).astype(BF16)
    qk_ref[0] = qk
    v = mm(h1, wt_ref[0, nqk:, :], NT).astype(BF16)
    v_ref[0] = v
    tail = masks_ref[1:2, :]
    rows = v.shape[0]
    for pair in range(heads // 2):
        v_pair = v[:, pair * 128 : (pair + 1) * 128]
        both = []
        for j in range(2):
            i = 2 * pair + j
            k = qk[nqk // 2 + i * FDIM : nqk // 2 + (i + 1) * FDIM].astype(F32)
            phi = (features(k) * tail).astype(BF16)
            rhs = jnp.concatenate([v_pair, one_hot_lanes(rows, r * heads + i)], axis=1)
            res = mm(phi, rhs)
            both.append(res[:, :128])
            z_ref[...] += res[:, 128:]
        p_ref[r * (heads // 2) + pair] = own_half(both[0], 0, both[1]).astype(BF16)

    @pl.when(r == pl.num_programs(0) - 1)
    def _():
        p_ref[p_ref.shape[0] - 1] = z_ref[...].astype(BF16)


def project(core, x, gain, masks, blocks, heads):
    n = len(blocks)
    rows, d = x.shape
    nqk, nv = 2 * heads * FDIM, heads * VDIM
    sums = n * heads // 2 + 1
    ins = (core, x, gain, masks, *flat(blocks))
    return call(
        functools.partial(project_body, n),
        (
            sds((rows, d), BF16),
            sds((n, nqk, rows), BF16),
            sds((n, rows, nv), BF16),
            sds((sums, FROWS, 128), BF16),
            sds((n, nqk + nv, d), BF16),
        ),
        ins,
        grid=(n,),
        in_specs=[pl.BlockSpec(memory_space=pltpu.SMEM)] + [whole(x.shape) for x in ins[1:]],
        out_specs=[
            whole((rows, d)),
            by_row((nqk, rows)),
            by_row((rows, nv)),
            whole((sums, FROWS, 128)),
            by_row((nqk + nv, d)),
        ],
        scratch=[pltpu.VMEM((FROWS, 128), F32)],
        us=7,
        most=True,
    )


def local_body(qk_ref, v_ref, masks_ref, nd_ref):
    nqk = qk_ref.shape[1]
    heads = nqk // (2 * FDIM)
    rows = v_ref.shape[1]
    mask = doc_mask(masks_ref[...], rows)
    for pair in range(heads // 2):
        v_pair = v_ref[0, :, pair * 128 : (pair + 1) * 128]
        acc = None
        for j in range(2):
            i = 2 * pair + j
            q = qk_ref[0, i * FDIM : (i + 1) * FDIM, :]
            k = qk_ref[0, nqk // 2 + i * FDIM : nqk // 2 + (i + 1) * FDIM, :]
            s1 = mm(q, k, TN) * 0.25 + 1.0
            a = jnp.where(mask, 0.5 * s1 * s1 + 0.5, 0.0).astype(BF16)
            ones = own_half(jnp.ones((rows, 128), BF16), j)
            part = mm(a, jnp.concatenate([own_half(v_pair, j), ones], axis=1))
            acc = part if acc is None else acc + part
        nd_ref[0, pair] = acc


def local(qk, v, masks):
    n, nqk, rows = qk.shape
    heads = nqk // (2 * FDIM)
    return call(
        local_body,
        sds((n, heads // 2, rows, 256), F32),
        (qk, v, masks),
        grid=(n,),
        in_specs=[by_row(qk.shape[1:]), by_row(v.shape[1:]), whole(masks.shape)],
        out_specs=by_row((heads // 2, rows, 256)),
    )


def joined(first, second, flag):
    return first.astype(F32) + second.astype(F32) * flag


def carry_body(nd_ref, qk_ref, masks_ref, one_ref, two_ref, o_ref, on_ref, inv_ref, c_ref):
    r = pl.program_id(0)
    n = pl.num_programs(0)
    nqk = qk_ref.shape[1]
    heads = nqk // (2 * FDIM)
    last = one_ref.shape[0] - 1

    @pl.when(r == 0)
    def _():
        c_ref[last] = joined(one_ref[last], two_ref[last], masks_ref[3:4, 0:128]).astype(BF16)

    flag = masks_ref[3:4, 0:128]
    live = masks_ref[2:3, :]
    for pair in range(heads // 2):
        at = r * (heads // 2) + pair
        c = joined(one_ref[at], two_ref[at], flag).astype(BF16)
        c_ref[at] = c
        acc = nd_ref[0, pair]
        for j in range(2):
            i = 2 * pair + j
            q = qk_ref[0, i * FDIM : (i + 1) * FDIM, :].astype(F32)
            phi = (features(q) * live).astype(BF16)
            z = pick_columns(
                c_ref[last],
                lambda row: row == r * heads + i,
                lambda lane: (lane < VDIM) if j == 0 else (lane >= VDIM),
            ).astype(BF16)
            acc = acc + mm(phi, jnp.concatenate([own_half(c, j), z], axis=1), TN)
        inv = 1.0 / acc[:, 128:]
        on = acc[:, :128] * inv
        cols = slice(pair * 128, (pair + 1) * 128)
        o_ref[0, :, cols] = on.astype(BF16)
        on_ref[0, :, cols] = on
        inv_ref[0, :, cols] = inv


def carry(nd, qk, masks, one, two):
    n, nqk, rows = qk.shape
    heads = nqk // (2 * FDIM)
    nv = heads * VDIM
    return call(
        carry_body,
        (
            sds((n, rows, nv), BF16),
            sds((n, rows, nv), F32),
            sds((n, rows, nv), F32),
            sds(one.shape, BF16),
        ),
        (nd, qk, masks, one, two),
        grid=(n,),
        in_specs=[
            by_row(nd.shape[1:]),
            by_row(qk.shape[1:]),
            whole(masks.shape),
            whole(one.shape),
            whole(two.shape),
        ],
        out_specs=[by_row((rows, nv))] * 3 + [whole(one.shape)],
        most=True,
    )


def middle_body(x_ref, gain_ref, o_ref, w_ref, y1_ref, *h2_refs):
    n, _, width = o_ref.shape
    acc = x_ref[...].astype(F32)
    for r in range(n):
        acc = acc + mm(o_ref[r], w_ref[r * width : (r + 1) * width, :])
    y1_ref[...] = acc
    scale = lax.rsqrt(jnp.mean(acc * acc, axis=-1, keepdims=True) + EPS)
    give_rows(h2_refs, (acc * scale * gain_ref[0:1, :]).astype(BF16))


def give_rows(refs, value):
    at = 0
    for one in refs:
        one[...] = value[at : at + one.shape[0]]
        at += one.shape[0]


def middle(x, o, wo, gain):
    rows, d = x.shape
    res = call(
        middle_body,
        (sds((rows, d), F32), *[sds((rows // 2, d), BF16)] * 2),
        (x, gain, o, wo),
        us=4,
    )
    return res[0], res[1:]


def spread_out_body(w_ref, out_ref, down_ref):
    nb, _, wb = w_ref.shape
    split = out_ref.shape[0]
    for s in range(nb):
        out_ref[:, s * wb : (s + 1) * wb] = w_ref[s, :split, :]
        down_ref[:, s * wb : (s + 1) * wb] = w_ref[s, split:, :]


def spread_out(w, ff):
    nb, total, wb = w.shape
    d = nb * wb
    return call(spread_out_body, (sds((total - ff, d), BF16), sds((ff, d), BF16)), (w,), us=4)


def prepare_body(n, down_ref, *refs):
    cots, out_ref = refs[:n], refs[n]
    for r in range(n):
        out_ref[r] = mm(cots[r][...], down_ref[...], NT).astype(BF16)


def prepare(down, cots):
    n = len(cots)
    return call(
        functools.partial(prepare_body, n),
        sds((n, cots[0].shape[0], down.shape[0]), BF16),
        (down, *cots),
    )


def widen_body(w_ref, wide_ref):
    nb, _, wb = w_ref.shape
    for s in range(nb):
        wide_ref[:, s * wb : (s + 1) * wb] = w_ref[s]


def widen(w):
    nb, total, wb = w.shape
    return call(widen_body, sds((total, nb * wb), BF16), (w,))


def mlp_body(first_ref, second_ref, dhid_ref, w_ref, dh_ref, hid_ref, dg_ref, du_ref):
    ff = hid_ref.shape[1]
    h2 = join_rows((first_ref, second_ref))
    gate_w, up_w = w_ref[0:ff, :], w_ref[ff : 2 * ff, :]
    dhid = dhid_ref[0].astype(F32)
    g = mm(h2, gate_w, NT)
    u = mm(h2, up_w, NT)
    sig = jax.nn.sigmoid(g)
    act = g * sig
    hid_ref[...] = (act * u).astype(BF16)
    dg = (dhid * u * sig * (1.0 + g * (1.0 - sig))).astype(BF16)
    du = (dhid * act).astype(BF16)
    dg_ref[...] = dg
    du_ref[...] = du
    dh_ref[...] = (mm(dg, gate_w) + mm(du, up_w)).astype(BF16)


def mlp(index, h2, dhid, w):
    half, d = h2[0].shape
    rows = 2 * half
    ff = w.shape[0] // 2
    return call(
        mlp_body,
        (sds((rows, d), BF16), *[sds((rows, ff), BF16)] * 3),
        (*h2, dhid, w),
        grid=(1,),
        in_specs=[whole((half, d))] * 2
        + [pl.BlockSpec((1, rows, ff), lambda r: (index, 0, 0)), whole((2 * ff, d))],
        out_specs=[whole((rows, d))] + [whole((rows, ff))] * 3,
    )


def mlp_out_body(n, w_ref, *refs):
    for r in range(n):
        refs[n + r][...] = mm(refs[r][...], w_ref[...]).astype(BF16)


def mlp_out(hid, w):
    n = len(hid)
    return call(
        functools.partial(mlp_out_body, n),
        [sds((hid[0].shape[0], w.shape[1]), BF16)] * n,
        (w, *hid),
    )


def mlp_grads_body(n, *refs):
    h2, cot = grouped(refs[: 2 * n], n), grouped(refs[2 * n : 3 * n], n)
    hid, dg, du = (refs[(3 + k) * n : (4 + k) * n] for k in range(3))
    o_ref, ff = refs[6 * n], hid[0].shape[1]
    nb, _, wb = o_ref.shape
    for k, (left, right) in enumerate(((dg, h2), (du, h2), (hid, cot))):
        acc = None
        for r in range(n):
            part = mm(left[r][...], join_rows(right[r]), TN)
            acc = part if acc is None else acc + part
        acc = acc.astype(BF16)
        for s in range(nb):
            o_ref[s, k * ff : (k + 1) * ff, :] = acc[:, s * wb : (s + 1) * wb]


def mlp_grads(h2, cot, hid, dg, du, nb):
    n = len(h2)
    d, ff = h2[0][0].shape[1], hid[0].shape[1]
    ins = (*flat(h2), *cot, *hid, *dg, *du)
    return call(
        functools.partial(mlp_grads_body, n),
        sds((nb, 3 * ff, d // nb), BF16),
        ins,
        grid=(1,),
        in_specs=[whole(x.shape) for x in ins],
        out_specs=whole((nb, 3 * ff, d // nb)),
        us=9,
    )


def turn_body(n, y1_ref, cot_ref, gain_ref, *refs):
    parts, w_ref = refs[:n], refs[n]
    dy1_ref, dgain_ref, *f_refs = refs[n + 1 : n + 4]
    do_ref = refs[n + 4]
    rows_of = do_ref.shape[2]
    dh2 = parts[0][...].astype(F32)
    for r in range(1, n):
        dh2 = dh2 + parts[r][...].astype(F32)
    y1 = y1_ref[...]
    scale = lax.rsqrt(jnp.mean(y1 * y1, axis=-1, keepdims=True) + EPS)
    normed = y1 * scale
    dgain_ref[...] = jnp.sum(dh2 * normed, axis=0, keepdims=True)
    dn = dh2 * gain_ref[0:1, :]
    inner = jnp.mean(dn * normed, axis=-1, keepdims=True)
    dy1 = cot_ref[...].astype(F32) + scale * (dn - normed * inner)
    dy1_ref[...] = dy1
    f = dy1.astype(BF16)
    give_rows(f_refs, f)
    for r in range(n):
        do_ref[r] = mm(f, w_ref[r * rows_of : (r + 1) * rows_of, :], NT).astype(BF16)


def turn(parts, y1, cot, gain, wo):
    n = len(parts)
    rows, d = y1.shape
    nv = wo.shape[0] // n
    res = call(
        functools.partial(turn_body, n),
        (
            sds((rows, d), F32),
            sds((1, d), F32),
            sds((rows, d), BF16),
            sds((n, rows, nv), BF16),
        ),
        (y1, cot, gain, *parts, wo),
    )
    return res


def back_first_body(do_ref, on_ref, inv_ref, qk_ref, masks_ref, d_ref, p_ref, z_ref):
    r = pl.program_id(0)
    n = pl.num_programs(0)
    nqk = qk_ref.shape[1]
    heads = nqk // (2 * FDIM)
    rows = do_ref.shape[1]

    @pl.when(r == 0)
    def _():
        z_ref[...] = jnp.zeros_like(z_ref)

    live = masks_ref[2:3, :]
    lane = lanes((rows, 128))
    for pair in range(heads // 2):
        cols = slice(pair * 128, (pair + 1) * 128)
        wide = do_ref[0, :, cols].astype(F32) * inv_ref[0, :, cols]
        dnum = wide.astype(BF16)
        prod = -(wide * on_ref[0, :, cols])
        high = prod.astype(BF16)
        low = (prod - high.astype(F32)).astype(BF16)
        both = []
        for j in range(2):
            i = 2 * pair + j
            row = lax.broadcasted_iota(jnp.int32, (128, 128), 0)
            hot = jnp.where((row < VDIM) if j == 0 else (row >= VDIM), 1.0, 0.0).astype(BF16)
            dden = mm(high, hot) + mm(low, hot)
            d_ref[0, i] = own_half(dnum, j, with_pair(dden, j))
            dh = dden.astype(BF16)
            dl = (dden - dh.astype(F32)).astype(BF16)
            zero = jnp.zeros_like(dh)
            spot = r * heads + i
            zext = jnp.where(lane == spot, dh, jnp.where(lane == spot + n * heads, dl, zero))
            q = qk_ref[0, i * FDIM : (i + 1) * FDIM, :].astype(F32)
            phi = (features(q) * live).astype(BF16)
            res = mm(phi, jnp.concatenate([dnum, zext], axis=1))
            both.append(res[:, :128])
            z_ref[...] += res[:, 128:]
        p_ref[r * (heads // 2) + pair] = own_half(both[0], 0, both[1]).astype(BF16)

    @pl.when(r == n - 1)
    def _():
        p_ref[p_ref.shape[0] - 1] = z_ref[...].astype(BF16)


def back_first(do, on, inv, qk, masks):
    n, nqk, rows = qk.shape
    heads = nqk // (2 * FDIM)
    pieces = n * heads // 2 + 1
    return call(
        back_first_body,
        (sds((n, heads, rows, 128), BF16), sds((pieces, FROWS, 128), BF16)),
        (do, on, inv, qk, masks),
        grid=(n,),
        in_specs=[by_row(x.shape[1:]) for x in (do, on, inv, qk)] + [whole(masks.shape)],
        out_specs=[by_row((heads, rows, 128)), whole((pieces, FROWS, 128))],
        scratch=[pltpu.VMEM((FROWS, 128), F32)],
    )


def back_local_body(d_ref, qk_ref, v_ref, masks_ref, c_ref, dq_ref, dk_ref, dv_ref):
    r = pl.program_id(0)
    nqk = qk_ref.shape[1]
    heads = nqk // (2 * FDIM)
    rows = v_ref.shape[1]
    masks = masks_ref[...]
    mask = doc_mask(masks, rows)
    live = masks[2:3, :]
    last = c_ref.shape[0] - 1
    for pair in range(heads // 2):
        cols = slice(pair * 128, (pair + 1) * 128)
        v_pair = v_ref[0, :, cols]
        c = c_ref[r * (heads // 2) + pair]
        dv = None
        for j in range(2):
            i = 2 * pair + j
            q = qk_ref[0, i * FDIM : (i + 1) * FDIM, :]
            k = qk_ref[0, nqk // 2 + i * FDIM : nqk // 2 + (i + 1) * FDIM, :]
            s1 = mm(q, k, TN) * 0.25 + 1.0
            a = jnp.where(mask, 0.5 * s1 * s1 + 0.5, 0.0).astype(BF16)
            d = d_ref[0, i]
            da = mm(d, with_ones(v_pair, j), NT)
            ds = jnp.where(mask, da * s1, 0.0).astype(BF16)
            z = pick_columns(
                c_ref[last], lambda row: row == r * heads + i, lambda lane: lane >= 0
            )
            dphi = mm(own_half(c, j, with_pair(z, j)), d, NT) * live
            back = features_back(q.astype(F32), dphi)
            dq_ref[0, i * FDIM : (i + 1) * FDIM, :] = (mm(k, ds, NT) * 0.25 + back).astype(BF16)
            dk_ref[0, i * FDIM : (i + 1) * FDIM, :] = mm(q, ds) * 0.25
            part = mm(own_half(d, j), a, TN)
            dv = part if dv is None else dv + part
        dv_ref[0, cols, :] = dv


def back_local(d, qk, v, masks, c):
    n, nqk, rows = qk.shape
    heads = nqk // (2 * FDIM)
    nv = heads * VDIM
    return call(
        back_local_body,
        (sds((n, nqk // 2, rows), BF16), sds((n, nqk // 2, rows), F32), sds((n, nv, rows), F32)),
        (d, qk, v, masks, c),
        grid=(n,),
        in_specs=[by_row(x.shape[1:]) for x in (d, qk, v)] + [whole(masks.shape), whole(c.shape)],
        out_specs=[by_row((nqk // 2, rows)), by_row((nqk // 2, rows)), by_row((nv, rows))],
    )


def back_last_body(
    where_ref, dq_ref, dk_ref, dv_ref, qk_ref, v_ref, masks_ref, one_ref, two_ref, h1_ref, wt_ref,
    gain_ref, x_ref, dy1_ref, dgain_mlp_ref, grad_ref, *refs,
):
    *dw_refs, dgain_ref, z_ref, acc_ref, wide_ref = refs
    r = pl.program_id(0)
    n = pl.num_programs(0)
    nqk = qk_ref.shape[1]
    heads = nqk // (2 * FDIM)
    nb, wb = dw_refs[0].shape[1] * len(dw_refs), dw_refs[0].shape[3]
    last = one_ref.shape[0] - 1
    flag = masks_ref[4:5, 0:128]
    tail = masks_ref[1:2, :]

    @pl.when(r == 0)
    def _():
        z_ref[...] = joined(one_ref[last], two_ref[last], flag).astype(BF16)
        acc_ref[...] = jnp.zeros_like(acc_ref)

    dks, dvs = [], []
    for pair in range(heads // 2):
        cols = slice(pair * 128, (pair + 1) * 128)
        at = r * (heads // 2) + pair
        dp = joined(one_ref[at], two_ref[at], flag).astype(BF16)
        v_pair = v_ref[0, :, cols]
        dv = dv_ref[0, cols, :]
        for j in range(2):
            i = 2 * pair + j
            k = qk_ref[0, nqk // 2 + i * FDIM : nqk // 2 + (i + 1) * FDIM, :].astype(F32)
            spot = r * heads + i
            z = pick_columns(
                z_ref[...],
                lambda row: jnp.logical_or(row == spot, row == spot + n * heads),
                lambda lane: lane >= 0,
            )
            dphi = mm(own_half(dp, j, with_pair(z, j)), with_ones(v_pair, j), NT) * tail
            dk = dk_ref[0, i * FDIM : (i + 1) * FDIM, :] + features_back(k, dphi)
            dks.append(dk.astype(BF16))
            phi = (features(k) * tail).astype(BF16)
            dv = dv + mm(own_half(dp, j), phi, TN)
        dvs.append(dv.astype(BF16))
    d = jnp.concatenate([dq_ref[0]] + dks + dvs, axis=0)
    total = d.shape[0]
    wide_ref[...] = mm(d, h1_ref[...]).astype(BF16)
    give_blocks(where_ref[where_ref.shape[0] - 1], wide_ref, [one.at[r, :, 0:total, :] for one in dw_refs])
    acc_ref[...] += mm(d, wt_ref[0], TN)

    @pl.when(r == n - 1)
    def _():
        dh1 = acc_ref[...]
        x = x_ref[...].astype(F32)
        scale = lax.rsqrt(jnp.mean(x * x, axis=-1, keepdims=True) + EPS)
        normed = x * scale
        dgain_ref[0:1, :] = jnp.sum(dh1 * normed, axis=0, keepdims=True)
        dgain_ref[1:2, :] = dgain_mlp_ref[...]
        dn = dh1 * gain_ref[0:1, :]
        inner = jnp.mean(dn * normed, axis=-1, keepdims=True)
        grad_ref[...] = dy1_ref[...] + scale * (dn - normed * inner)
        if nb > 1:
            groups = dw_refs[0].shape[0]
            across = groups * nb * wb // dgain_ref.shape[1]
            for q in range(groups):
                for tile in range(nb // across):
                    at = where_ref[q] * (nb // across) + tile
                    both = dgain_ref[:, pl.ds(pl.multiple_of(at * wb, wb), wb)]
                    high = both.astype(BF16).astype(F32)
                    fill = jnp.zeros((dw_refs[0].shape[2] - total - 4, wb), F32)
                    block = jnp.concatenate([high, both - high, fill], axis=0).astype(BF16)
                    for one in dw_refs:
                        for s in range(tile * across // 2, (tile + 1) * across // 2):
                            one[q, s, total:, :] = block


def give_blocks(core, wide_ref, refs):
    count, _, wb = refs[0].shape
    for index, one in enumerate(refs):
        for z in range(count):
            at = (2 * z + jnp.where(index == 0, core, 1 - core)) * wb if len(refs) == 2 else 0
            if len(refs) == 2:
                at = pl.multiple_of(at, wb)
            one[z] = wide_ref[:, pl.ds(at, wb)]


def back_last(where, dq, dk, dv, qk, v, masks, one, two, h1, w, gain, x, dy1, dgain_mlp, nb):
    n, nqk, rows = qk.shape
    _, total, d = w.shape
    shapes = [(n, 1, total + 16, d)] if nb == 1 else [(n, nb // 2, total + 16, d // nb)] * 2
    ins = (where, dq, dk, dv, qk, v, masks, one, two, h1, w, gain, x, dy1, dgain_mlp)
    return call(
        back_last_body,
        (sds((rows, d), F32), *[sds(shape, BF16) for shape in shapes], sds((2, d), F32)),
        ins,
        grid=(n,),
        in_specs=[pl.BlockSpec(memory_space=pltpu.SMEM)]
        + [by_row(y.shape[1:]) for y in (dq, dk, dv, qk, v)]
        + [whole(y.shape) for y in (masks, one, two, h1)]
        + [by_row(w.shape[1:])]
        + [whole(y.shape) for y in (gain, x, dy1, dgain_mlp)],
        out_specs=[whole((rows, d)), *[whole(shape) for shape in shapes], whole((2, d))],
        scratch=[
            pltpu.VMEM((FROWS, 128), BF16),
            pltpu.VMEM((rows, d), F32),
            pltpu.VMEM((total, d), BF16),
        ],
        us=10,
        most=True,
    )


def out_grads_body(n, core_ref, f_ref, *refs):
    o_ref, outs, wide_ref = refs[0], refs[1:-1], refs[-1]
    for r in range(n):
        wide_ref[...] = mm(o_ref[r], f_ref[...], TN).astype(BF16)
        give_blocks(core_ref[0], wide_ref, [one.at[r] for one in outs])


def out_grads(core, o, f, nb):
    n, _, nv = o.shape
    d = f.shape[1]
    shapes = [(n, 1, nv, d)] if nb == 1 else [(n, nb // 2, nv, d // nb)] * 2
    return call(
        functools.partial(out_grads_body, n),
        [sds(shape, BF16) for shape in shapes],
        (core, f, o),
        scratch=[pltpu.VMEM((nv, d), BF16)],
        smem=1,
        us=3,
    )


def xor_pairs(size, r):
    return [(i, i ^ r) for i in range(size)]


def swap(parts):
    size = lax.axis_size("head")
    return [parts[0]] + [lax.ppermute(parts[r], "head", xor_pairs(size, r)) for r in range(1, size)]


def halves(x):
    return [x[: x.shape[0] // 2], x[x.shape[0] // 2 :]]


def sum_parts(parts):
    total = parts[0].astype(F32)
    for part in parts[1:]:
        total = total + part.astype(F32)
    return total.astype(parts[0].dtype)


def spread(x):
    return [[one] for one in swap([x] * lax.axis_size("head"))]


def spread_halves(pair):
    size = lax.axis_size("head")
    a, b = pair

    def send(x, r):
        return lax.ppermute(x, "head", xor_pairs(size, r))

    if size != 4:
        return [[a, b]] + [[send(a, r), send(b, r)] for r in range(1, size)]
    ax, by = send(a, 1), send(b, 2)
    ay, bx = send(a, 2), send(b, 1)
    return [[a, b], [ax, bx], [ay, by], [send(ax, 2), send(by, 1)]]


def shifted(x, step):
    size = lax.axis_size("seq")
    return lax.ppermute(x, "seq", [(i, i + step) for i in range(size) if 0 <= i + step < size])


def halved(x, first=1, stop=None):
    size, me = lax.axis_size("seq"), lax.axis_index("seq")
    k = first
    while k < (stop or size):
        x = x.reshape((x.shape[0] // 2, 2) + x.shape[1:])
        bit = (me // k) % 2
        keep = lax.dynamic_index_in_dim(x, bit, 1, keepdims=False)
        send = lax.dynamic_index_in_dim(x, 1 - bit, 1, keepdims=False)
        got = lax.ppermute(send, "seq", xor_pairs(size, k))
        x = (keep.astype(F32) + got.astype(F32)).astype(x.dtype)
        k *= 2
    return x


def carried(x, labels, step, join, before):
    size, me = lax.axis_size("seq"), lax.axis_index("seq")
    reach = max(size // 4, 1)
    k = 1
    while 2 * k < reach:
        other = jnp.take(labels, jnp.clip(me - step * k, 0, size - 1))
        flag = (other == jnp.take(labels, me)).astype(F32)
        x = join(x, shifted(x, step * k), flag)
        k *= 2
    one = shifted(x, step)
    one, before = lax.optimization_barrier((one, before))
    return one, shifted(one, step * k)


def on_device(
    tokens, doc_ids, query_weight, key_weight, value_weight, out_weight,
    gate_weight, up_weight, down_weight, mix_gain, mlp_gain, cotangent,
):
    n, blocks = lax.axis_size("head"), lax.axis_size("seq")
    here, me = lax.axis_index("head"), lax.axis_index("seq")
    rows, d = tokens.shape[1:]
    wb = d // blocks
    nb = blocks if wb % 128 == 0 else 1
    heads = query_weight.shape[1] // FDIM
    nqkv = 2 * heads * FDIM + heads * VDIM
    nv = heads * VDIM
    ff = gate_weight.shape[1]
    x, cot = tokens[0], cotangent[0]

    piece = mix_gain.shape[0]
    doc_rows = rows // wb
    extra = -(-(2 + doc_rows) // 16) * 16
    pack = call(
        pack_body,
        sds((nqkv + extra, wb), BF16),
        (
            query_weight.T, key_weight.T, value_weight, mix_gain.reshape(1, -1), mlp_gain.reshape(1, -1),
            doc_ids.reshape(doc_rows, wb),
        ),
        us=2,
        most=True,
    )
    out_slices = swap([out_weight] * n)
    pack = lax.all_gather(pack, "seq")
    down_late, pack = lax.optimization_barrier((down_weight, pack))
    second = lax.all_gather(jnp.concatenate([*out_slices, down_late], axis=0), "seq")

    def gathered(w):
        return w if nb == blocks else jnp.transpose(w, (1, 0, 2)).reshape(1, w.shape[1], d)

    def unblocked(w):
        if nb == blocks:
            return w
        w = w.reshape(w.shape[1:-1] + (blocks, wb))
        return jnp.moveaxis(w, -2, 0)

    core = (me % 2).reshape(1)
    half = blocks // 2
    mine = lax.dynamic_slice_in_dim(pack, core[0] * half, half)
    other = lax.dynamic_slice_in_dim(pack, (1 - core[0]) * half, half)
    mine = swap([mine] * n)
    pairs = [[mine[0], other]]
    pairs += [[one, lax.ppermute(one, "seq", xor_pairs(blocks, 1))] for one in mine[1:]]
    small = jnp.stack([jnp.stack([one[:, nqkv : nqkv + 2, :piece] for one in pair]) for pair in pairs])
    small = jnp.take(jnp.take(small, here ^ jnp.arange(n), axis=0), core[0] ^ jnp.arange(2), axis=1)
    gains = jnp.transpose(small.reshape(n, blocks, 2, piece), (2, 0, 1, 3)).reshape(2, 1, d)
    gain_mix, gain_mlp = gains[0].astype(F32), gains[1].astype(F32)
    docs = pack[:, nqkv + 2 : nqkv + 2 + doc_rows].reshape(blocks, rows).astype(F32)
    segs = jnp.take(docs, me, axis=0)
    lasts = docs[:, -1]
    if nb != blocks:
        pairs = [
            [gathered(jnp.where(core[0] == 0, jnp.concatenate(p), jnp.concatenate(p[::-1])))] for p in pairs
        ]
    cot_late, pairs[1:] = lax.optimization_barrier((cot, pairs[1:]))
    wide = call(pack_two_body, sds((2 * ff, wb), BF16), (gate_weight.T, up_weight.T), us=2)

    before = jnp.where(me > 0, jnp.take(lasts, jnp.maximum(me - 1, 0)), -1.0)
    final_label = jnp.take(lasts, me)
    labels_back = jnp.concatenate([jnp.full((1,), -1.0), lasts[:-1]])

    def join(a, b, flag):
        return (a.astype(F32) + b.astype(F32) * flag).astype(BF16)

    def flag_of(labels, step):
        reach = max(blocks // 4, 1)
        k = 1
        while 2 * k < reach:
            k *= 2
        near = jnp.take(labels, jnp.clip(me - step, 0, blocks - 1))
        far = jnp.take(labels, jnp.clip(me - step * (1 + k), 0, blocks - 1))
        return (near == far).astype(F32)

    masks = jnp.stack(
        [
            segs,
            (segs == final_label).astype(F32),
            (segs == before).astype(F32),
            jnp.full((rows,), 1.0) * flag_of(lasts, 1),
            jnp.full((rows,), 1.0) * flag_of(labels_back, -1),
        ]
        + [jnp.zeros_like(segs)] * 3
    )

    h1, qk, v, sums, w_qkv = project(core, x, gain_mix, masks, pairs, heads)
    cots = swap([cot_late] * n)
    nd = local(qk, v, masks)
    one, two = carried(sums, lasts, 1, join, nd)
    wide, two = lax.optimization_barrier((wide, two))
    w_mlp = widen(gathered(lax.all_gather(wide, "seq")))
    w_out, w_down = spread_out(gathered(second), ff)
    dhid = prepare(w_down, cots)
    two, w_out = lax.optimization_barrier((two, w_out))
    o, on, inv, c = carry(nd, qk, masks, one, two)
    y1, h2 = middle(x, o, w_out, gain_mlp)
    h2s = spread_halves(h2)
    res = [mlp(r, h2s[r], dhid, w_mlp) for r in range(n)]
    dparts, hid, dg, du = ([t[k] for t in res] for k in range(4))
    dparts = swap(dparts)
    oparts = mlp_out(hid, w_down)
    dmlp = mlp_grads(h2s, cots, hid, dg, du, nb)
    dparts, oparts, dmlp = lax.optimization_barrier((dparts, oparts, dmlp))
    dy1, dgain_mlp, f, do = turn(dparts, y1, cot, gain_mlp, w_out)
    oparts, f = lax.optimization_barrier((oparts, f))
    oparts = swap(oparts)
    dext, dsums = back_first(do, on, inv, qk, masks)
    dq, dk, dv = back_local(dext, qk, v, masks, c)
    back_one, back_two = carried(dsums, labels_back, -1, join, (dq, dk, dv))

    def split(w):
        if nb == blocks:
            return w
        w = unblocked(w[0][:, 0][None])
        w = jnp.moveaxis(w.reshape((half, 2) + w.shape[1:]), 2, 0)
        return [lax.dynamic_index_in_dim(w, bit, 2, keepdims=False) for bit in (core[0], 1 - core[0])]

    def reduced(keep, give):
        got = lax.ppermute(give, "seq", xor_pairs(blocks, 1))
        w = (keep.astype(F32) + got.astype(F32)).astype(BF16)
        w = sum_parts(swap([w[r] for r in range(n)]))
        return halved(w, 2)

    dout = reduced(*split(out_grads(core, o, f, nb)))
    dmlp, back_two, oparts = lax.optimization_barrier((dmlp, back_two, oparts))
    dmlp = lax.psum_scatter(unblocked(dmlp), "seq", tiled=True)[0].astype(F32)
    where = jnp.concatenate([here ^ jnp.arange(n, dtype=jnp.int32), core])
    grad_tokens, *dqkv, dgains = back_last(
        where, dq, dk, dv, qk, v, masks, back_one, back_two, h1, w_qkv, gain_mix, x, dy1, dgain_mlp, nb
    )
    dqkv = reduced(*split(dqkv))[0].astype(F32)
    dout = dout[0].astype(F32)
    if nb == blocks:
        parts = dqkv[nqkv : nqkv + 2] + dqkv[nqkv + 2 : nqkv + 4]
        total = lax.dynamic_slice_in_dim(parts, me % (wb // piece) * piece, piece, axis=1)
    else:
        total = lax.psum_scatter(dgains, ("head", "seq"), scatter_dimension=1, tiled=True)
    output = y1
    for part in oparts:
        output = output + part.astype(F32)

    kq = heads * FDIM
    return (
        output.astype(BF16)[None],
        grad_tokens[None],
        dqkv[:kq].T,
        dqkv[kq : 2 * kq].T,
        dqkv[2 * kq : nqkv].T,
        dout,
        dmlp[:ff].T,
        dmlp[ff : 2 * ff].T,
        dmlp[2 * ff :],
        total[0],
        total[1],
    )


def solution(mesh):
    placed = (
        P("head", "seq", None),
        P("head", "seq"),
        P("seq", "head"),
        P("seq", "head"),
        P("seq", "head"),
        P("head", "seq"),
        P("seq", "head"),
        P("seq", "head"),
        P("head", "seq"),
        P(("head", "seq")),
        P(("head", "seq")),
        P("head", "seq", None),
    )
    return jax.shard_map(
        on_device,
        mesh=mesh,
        in_specs=placed,
        out_specs=(
            P("head", "seq", None),
            P("head", "seq", None),
            P("seq", "head"),
            P("seq", "head"),
            P("seq", "head"),
            P("head", "seq"),
            P("seq", "head"),
            P("seq", "head"),
            P("head", "seq"),
            P(("head", "seq")),
            P(("head", "seq")),
        ),
        check_vma=False,
    )
```

time: 335 us -> 280 us (0.84)
  waiting for transfers between devices: 107 us -> 80.3 us
  Pallas kernels: 98.1 us -> 74.5 us
  starting transfers between devices: 60.3 us -> 46.9 us
  other arithmetic: 14.2 us -> 6.79 us
  local copies, waits for them, and re-layouts: 28.2 us -> 35.4 us
  blocking collectives: 11.3 us -> 16.5 us
  between operations: 14.9 us -> 18.6 us
    ppermute x33 -> x21, waiting for transfers between devices: 89.6 us -> 49.8 us  [swap(): lax.ppermute(parts[r], 'head', xor_pairs(size, r))]
    pallas_call x15 -> x20, Pallas kernels: 91.3 us -> 74.5 us  [call(): pl.pallas_call(body, out_shape=outs, scratch_shapes=list(scratch), compil...]
    all_gather x0 -> x1, blocking collectives: none -> 16.5 us  [on_device(): pack = lax.all_gather(pack, 'seq')]
    ppermute x0 -> x11, waiting for transfers between devices: none -> 14.6 us  [the longest x6 9.47 us: send(): return lax.ppermute(x, 'head', xor_pairs(size, r))]
    unnamed x64 -> x134, local copies, waits for them, and re-layouts: 13.9 us -> 26.6 us
    ppermute x33 -> x21, starting transfers between devices: 38.1 us -> 25.7 us  [swap(): lax.ppermute(parts[r], 'head', xor_pairs(size, r))]
    unnamed x1 -> x0, blocking collectives: 11.3 us -> none
    ppermute x4, waiting for transfers between devices: 10.1 us -> 0.55 us  [shifted(): lax.ppermute(x, 'seq', [(i, i + step) for i in range(size) if 0 <= i + st...]
  transfers between devices with their start and end apart: 49 -> 43, of which waited for: 18 -> 19; matrix products, arithmetic and copies ran while one was open for 8% -> 5% of each run, Pallas kernels for 24% -> 24%
where the time goes in v2:
time: 280 us; the launch traced here: 279 us
  waiting for transfers between devices  80.3 us (29%)
  Pallas kernels  74.5 us (27%)
  starting transfers between devices  46.9 us (17%)
  local copies, waits for them, and re-layouts  35.4 us (13%)
  between operations  18.6 us (7%)
  blocking collectives  16.5 us (6%)
  other arithmetic  6.79 us (2%)
    pallas_call x20, Pallas kernels, call(): pl.pallas_call(body, out_shape=outs, scratch_shapes=list(scratch), compil...  74.5 us
    ppermute x21, waiting for transfers between devices, swap(): lax.ppermute(parts[r], 'head', xor_pairs(size, r))  49.8 us
    unnamed x134, local copies, waits for them, and re-layouts  26.6 us
    ppermute x21, starting transfers between devices, swap(): lax.ppermute(parts[r], 'head', xor_pairs(size, r))  25.7 us
    all_gather x1, blocking collectives, on_device(): pack = lax.all_gather(pack, 'seq')  16.5 us
    ppermute x4, waiting for transfers between devices, halved(): got = lax.ppermute(send, 'seq', xor_pairs(size, k))  11.6 us
    ppermute x6, waiting for transfers between devices, send(): return lax.ppermute(x, 'head', xor_pairs(size, r))  9.47 us
    ppermute x4, starting transfers between devices, shifted(): lax.ppermute(x, 'seq', [(i, i + step) for i in range(size) if 0 <= i + st...  8.34 us
  transfers between devices with their start and end apart: 43, of which 19 were waited for; matrix products, arithmetic and copies ran while one was open for 5% of the time, Pallas kernels for 24%

profile of v2, /device:TPU:0, one launch (start us, length us, event | category | flops | bytes accessed | tf_op | source)
XLA Modules:
  0.0 279.0 jit_solution(1290110298841332080)
XLA Ops:
  7.2 3.0 %collective-permute-start.8 = (bf16[256,128]{1,0:T(8,128)(2,1)}, bf16[256,128]{1,0:T(8,128)(2,1)S(1)}, u32[]{:S(2)}, u32[]{:S(2)}) collective-permute-start(bf16[256,128]{1,0:T(8,128)(2,1)} %param.17), channel_id=1, source_target_pairs={{0,8},{8,0},{16,24},{24,16},{1,9},{9,1},{17,25},{25,17},{2,10},{10... | collective-permute-start | bytes 196616 | tf_op jit(solution)/shard_map/ppermute | solution.py:794
  10.2 1.5 collective-permute-start.9
  11.8 1.6 shard_map.203
  13.4 16.5 %all-gather = bf16[3200,128]{1,0:T(8,128)(2,1)S(1)} all-gather(bf16[400,128]{1,0:T(8,128)(2,1)} %shard_map.203), channel_id=2, replica_groups=mesh['head'=4,'seq'=8] {'seq'}, dimensions={0}, use_global_device_ids=true | all-gather | bytes 921600 | tf_op jit(solution)/shard_map/all_gather | solution.py:888
  35.0 1.5 collective-permute-start.2
  43.3 2.4 collective-permute-done.refs_2_
  45.8 9.4 %collective-permute-done.2.refs_4_ = bf16[4,400,128]{2,1,0:T(8,128)(2,1)S(1)} collective-permute-done((bf16[4,400,128]{2,1,0:T(8,128)(2,1)S(1)}, bf16[4,400,128]{2,1,0:T(8,128)(2,1)S(1)}, u32[]{:S(2)}, u32[]{:S(2)}) %collective-permute-start.2) | collective-permute-done | bytes 409632 | tf_op jit(solution)/shard_map/ppermute | solution.py:794
  60.5 7.8 %shard_map.204 = (bf16[256,1024]{1,0:T(8,128)(2,1)}, bf16[4,128,256]{2,1,0:T(8,128)(2,1)}, bf16[4,256,256]{2,1,0:T(8,128)(2,1)}, bf16[9,176,128]{2,1,0:T(8,128)(2,1)}, bf16[4,384,1024]{2,1,0:T(8,128)(2,1)}) custom-call(s32[1]{0:T(128)} %bitcast.24.core_ref, bf16[256,1024]{1,0:T(8,128)(2,1)} %bitcast.141, f32[1,1024]{1,0:T(1,128)} %reshape.351.gain_ref, ...), custom_call_target="tpu_custom_call" | custom-call | bytes 4200000 | tf_op jit(solution)/shard_map/pallas_call | solution.py:36
  68.2 2.0 collective-permute-start.6
  72.3 3.2 %shard_map.205.nd_ref = f32[4,2,256,256]{3,2,1,0:T(8,128)S(1)} custom-call(bf16[4,128,256]{2,1,0:T(8,128)(2,1)S(1)} %copy-done.4, bf16[4,256,256]{2,1,0:T(8,128)(2,1)S(1)} %copy-done.8, f32[8,256]{1,0:T(8,128)S(1)} %copy-done.31), custom_call_target="tpu_custom_call" | custom-call | bytes 3000000 | tf_op jit(solution)/shard_map/pallas_call | solution.py:36
  76.7 3.8 %collective-permute-start.7 = (bf16[9,176,128]{2,1,0:T(8,128)(2,1)S(1)}, bf16[9,176,128]{2,1,0:T(8,128)(2,1)S(1)}, u32[]{:S(2)}, u32[]{:S(2)}) collective-permute-start(bf16[9,176,128]{2,1,0:T(8,128)(2,1)S(1)} %collective-permute-done.6.one_ref), channel_id=1, source_target_pairs={{0,1},{1,2},{2,3},{3,4},{4,5},{5,6},{6,7},{8,9},{9,10},{10,11},{11... | collective-permute-start | bytes 1216520 | tf_op jit(solution)/shard_map/ppermute | solution.py:828
  83.8 1.7 collective-permute-start.13
  85.5 2.0 copy-done.13
  88.6 6.4 %shard_map.208 = (bf16[4,256,256]{2,1,0:T(8,128)(2,1)}, f32[4,256,256]{2,1,0:T(8,128)}, f32[4,256,256]{2,1,0:T(8,128)}, bf16[9,176,128]{2,1,0:T(8,128)(2,1)}) custom-call(f32[4,2,256,256]{3,2,1,0:T(8,128)} %copy-done.3, bf16[4,128,256]{2,1,0:T(8,128)(2,1)} %get-tuple-element.101.qk_ref, f32[8,256]{1,0:T(8,128)} %stack.86.masks_ref, ...), custom_call_target="tpu_custom_call" | custom-call | bytes 3000000 | tf_op jit(solution)/shard_map/pallas_call | solution.py:36
  96.2 1.6 shard_map.209
  101.9 1.7 collective-permute-start.15
  103.6 6.5 %collective-permute-done.14.first_ref.refs_2_ = bf16[128,1024]{1,0:T(8,128)(2,1)} collective-permute-done((bf16[128,1024]{1,0:T(8,128)(2,1)}, bf16[128,1024]{1,0:T(8,128)(2,1)}, u32[]{:S(2)}, u32[]{:S(2)}) %collective-permute-start.14) | collective-permute-done | bytes 262176 | tf_op jit(solution)/shard_map/ppermute | solution.py:817
  111.7 2.9 %collective-permute-done.18.second_ref.refs_5_ = bf16[128,1024]{1,0:T(8,128)(2,1)} collective-permute-done((bf16[128,1024]{1,0:T(8,128)(2,1)}, bf16[128,1024]{1,0:T(8,128)(2,1)}, u32[]{:S(2)}, u32[]{:S(2)}) %collective-permute-start.18) | collective-permute-done | bytes 262176 | tf_op jit(solution)/shard_map/ppermute | solution.py:817
  116.2 3.1 %shard_map.210.dhid_ref = bf16[4,256,688]{2,1,0:T(8,128)(2,1)S(1)} custom-call(bf16[688,1024]{1,0:T(8,128)(2,1)S(1)} %get-tuple-element.114.down_ref.w_ref, bf16[256,1024]{1,0:T(8,128)(2,1)S(1)} %bitcast.138, bf16[256,1024]{1,0:T(8,128)(2,1)S(1)} %copy-done.16, bf16[256,1024]{1,0:T(8,128)(2,1)} %collective-permute-done.12.refs_2_.refs_10_, ...), custom_call_target="tpu_custom_call" | custom-call | bytes 3000000 | tf_op jit(solution)/shard_map/pallas_call | solution.py:36
  119.3 3.7 %all-gather.8.cloned.1.call-done = bf16[11008,128]{1,0:T(8,128)(2,1)} async-done(((bf16[1376,128]{1,0:T(8,128)(2,1)}), bf16[11008,128]{1,0:T(8,128)(2,1)}) %all-gather.8.cloned.1.call-update) | async-done | bytes 2818064 | tf_op jit(solution)/shard_map/all_gather | solution.py:954
  122.9 1.8 copy-done.14
  125.5 3.9 %shard_map.214 = (bf16[256,1024]{1,0:T(8,128)(2,1)}, bf16[256,688]{1,0:T(8,128)(2,1)S(1)}, bf16[256,688]{1,0:T(8,128)(2,1)S(1)}, bf16[256,688]{1,0:T(8,128)(2,1)S(1)}) custom-call(bf16[128,1024]{1,0:T(8,128)(2,1)} %collective-permute-done.17.first_ref.refs_4_, bf16[128,1024]{1,0:T(8,128)(2,1)} %collective-permute-done.18.second_ref.refs_5_, ...), custom_call_target="tpu_custom_call" | custom-call | bytes 3000000 | tf_op jit(solution)/shard_map/pallas_call | solution.py:36
  130.9 3.9 %shard_map.213 = (bf16[256,1024]{1,0:T(8,128)(2,1)}, bf16[256,688]{1,0:T(8,128)(2,1)S(1)}, bf16[256,688]{1,0:T(8,128)(2,1)S(1)}, bf16[256,688]{1,0:T(8,128)(2,1)S(1)}) custom-call(bf16[128,1024]{1,0:T(8,128)(2,1)} %collective-permute-done.14.first_ref.refs_2_, bf16[128,1024]{1,0:T(8,128)(2,1)} %collective-permute-done.15.second_ref.refs_3_, ...), custom_call_target="tpu_custom_call" | custom-call | bytes 3000000 | tf_op jit(solution)/shard_map/pallas_call | solution.py:36
  136.3 3.9 %shard_map.215 = (bf16[256,1024]{1,0:T(8,128)(2,1)}, bf16[256,688]{1,0:T(8,128)(2,1)S(1)}, bf16[256,688]{1,0:T(8,128)(2,1)S(1)}, bf16[256,688]{1,0:T(8,128)(2,1)S(1)}) custom-call(bf16[128,1024]{1,0:T(8,128)(2,1)} %collective-permute-done.20.first_ref.refs_6_, bf16[128,1024]{1,0:T(8,128)(2,1)} %collective-permute-done.21.second_ref.refs_7_, ...), custom_call_target="tpu_custom_call" | custom-call | bytes 3000000 | tf_op jit(solution)/shard_map/pallas_call | solution.py:36
  140.8 3.1 %shard_map.212 = (bf16[256,1024]{1,0:T(8,128)(2,1)S(1)}, bf16[256,688]{1,0:T(8,128)(2,1)S(1)}, bf16[256,688]{1,0:T(8,128)(2,1)S(1)}, bf16[256,688]{1,0:T(8,128)(2,1)S(1)}) custom-call(bf16[128,1024]{1,0:T(8,128)(2,1)} %get-tuple-element.112.first_ref.refs_0_, bf16[128,1024]{1,0:T(8,128)(2,1)} %get-tuple-element.113.second_ref.refs_1_, ...), custom_call_target="tpu_custom_call" | custom-call | bytes 3000000 | tf_op jit(solution)/shard_map/pallas_call | solution.py:36
  144.7 1.8 shard_map.216
  149.7 6.8 %shard_map.217 = bf16[8,2064,128]{2,1,0:T(8,128)(2,1)S(1)} custom-call(bf16[128,1024]{1,0:T(8,128)(2,1)} %get-tuple-element.112.first_ref.refs_0_, bf16[128,1024]{1,0:T(8,128)(2,1)} %get-tuple-element.113.second_ref.refs_1_, bf16[128,1024]{1,0:T(8,128)(2,1)} %collective-permute-done.14.first_ref.refs_2_, ...), custom_call_target="tpu_custom_call" | custom-call | bytes 5400000 | tf_op jit(solution)/shard_map/pallas_call | solution.py:36
  156.5 2.1 copy-done
  158.5 1.6 collective-permute-done.22.refs_3_
  161.4 2.9 %shard_map.218 = (f32[256,1024]{1,0:T(8,128)S(1)}, f32[1,1024]{1,0:T(1,128)S(1)}, bf16[256,1024]{1,0:T(8,128)(2,1)S(1)}, bf16[4,256,256]{2,1,0:T(8,128)(2,1)S(1)}) custom-call(f32[256,1024]{1,0:T(8,128)S(1)} %copy-done.11, bf16[256,1024]{1,0:T(8,128)(2,1)S(1)} %bitcast.140, f32[1,1024]{1,0:T(1,128)S(1)} %reshape.350.gain_ref, ...), custom_call_target="tpu_custom_call" | custom-call | bytes 3000000 | tf_op jit(solution)/shard_map/pallas_call | solution.py:36
  165.4 3.6 %shard_map.219 = (bf16[4,4,256,128]{3,2,1,0:T(8,128)(2,1)S(1)}, bf16[9,176,128]{2,1,0:T(8,128)(2,1)S(1)}) custom-call(bf16[4,256,256]{2,1,0:T(8,128)(2,1)S(1)} %get-tuple-element.142.do_ref, f32[4,256,256]{2,1,0:T(8,128)S(1)} %copy-done.22, f32[4,256,256]{2,1,0:T(8,128)S(1)} %copy-done.23, bf16[4,128,256]{2,1,0:T(8,128)(2,1)S(1)} %copy-done.5, ...), custom_call_target="tpu_custom_call" | custom-call | bytes 3000000 | tf_op jit(solution)/shard_map/pallas_call | solution.py:36
  170.4 1.5 collective-permute-start.25
  173.9 5.4 %shard_map.220 = (bf16[4,64,256]{2,1,0:T(8,128)(2,1)S(1)}, f32[4,64,256]{2,1,0:T(8,128)S(1)}, f32[4,256,256]{2,1,0:T(8,128)S(1)}) custom-call(bf16[4,4,256,128]{3,2,1,0:T(8,128)(2,1)S(1)} %get-tuple-element.146.d_ref, bf16[4,128,256]{2,1,0:T(8,128)(2,1)S(1)} %copy-done.5, bf16[4,256,256]{2,1,0:T(8,128)(2,1)S(1)} %copy-done.9, f32[8,256]{1,0:T(8,128)S(1)} %copy-done.32, ...), custom_call_target="tpu_custom_call" | custom-call | bytes 3000000 | tf_op jit(solution)/shard_map/pallas_call | solution.py:36
  181.6 3.4 %collective-permute-done.25 = bf16[256,1024]{1,0:T(8,128)(2,1)S(1)} collective-permute-done((bf16[256,1024]{1,0:T(8,128)(2,1)S(1)}, bf16[256,1024]{1,0:T(8,128)(2,1)S(1)}, u32[]{:S(2)}, u32[]{:S(2)}) %collective-permute-start.25) | collective-permute-done | bytes 524320 | tf_op jit(solution)/shard_map/ppermute | solution.py:794
  185.1 12.7 %collective-permute-done.26 = bf16[256,1024]{1,0:T(8,128)(2,1)S(1)} collective-permute-done((bf16[256,1024]{1,0:T(8,128)(2,1)S(1)}, bf16[256,1024]{1,0:T(8,128)(2,1)S(1)}, u32[]{:S(2)}, u32[]{:S(2)}) %collective-permute-start.26) | collective-permute-done | bytes 524320 | tf_op jit(solution)/shard_map/ppermute | solution.py:794
  200.8 11.7 %shard_map.221 = (f32[256,1024]{1,0:T(8,128)}, bf16[4,4,400,128]{3,2,1,0:T(8,128)(2,1)}, bf16[4,4,400,128]{3,2,1,0:T(8,128)(2,1)}, f32[2,1024]{1,0:T(2,128)}) custom-call(s32[5]{0:T(128)} %pad_add_fusion.where_ref, bf16[4,64,256]{2,1,0:T(8,128)(2,1)} %copy-done.36, f32[4,64,256]{2,1,0:T(8,128)} %copy-done.33, f32[4,256,256]{2,1,0:T(8,128)} %copy-done.21, ...), custom_call_target="tpu_custom_call" | custom-call | bytes 6000000 | tf_op jit(solution)/shard_map/pallas_call | solution.py:36
  214.4 3.4 %collective-permute-done.34 = bf16[4,4,256,128]{3,2,1,0:T(8,128)(2,1)S(1)} collective-permute-done((bf16[4,4,256,128]{3,2,1,0:T(8,128)(2,1)S(1)}, bf16[4,4,256,128]{3,2,1,0:T(8,128)(2,1)S(1)}, u32[]{:S(2)}, u32[]{:S(2)}) %collective-permute-start.34) | collective-permute-done | bytes 1048608 | tf_op jit(solution)/shard_map/ppermute | solution.py:982
  218.3 1.9 collective-permute-start.36
  221.7 2.0 add_convert_fusion
  224.0 1.9 collective-permute-start.30
  230.0 2.1 collective-permute-done.36
  232.1 1.8 collective-permute-done.37
  234.0 1.7 collective-permute-start.38
  235.8 6.0 %collective-permute-done.29 = bf16[4,400,128]{2,1,0:T(8,128)(2,1)S(1)} collective-permute-done((bf16[4,400,128]{2,1,0:T(8,128)(2,1)S(1)}, bf16[4,400,128]{2,1,0:T(8,128)(2,1)S(1)}, u32[]{:S(2)}, u32[]{:S(2)}) %collective-permute-start.29) | collective-permute-done | bytes 409632 | tf_op jit(solution)/shard_map/ppermute | solution.py:794
  241.8 8.9 %collective-permute-done.31 = bf16[4,400,128]{2,1,0:T(8,128)(2,1)S(1)} collective-permute-done((bf16[4,400,128]{2,1,0:T(8,128)(2,1)S(1)}, bf16[4,400,128]{2,1,0:T(8,128)(2,1)S(1)}, u32[]{:S(2)}, u32[]{:S(2)}) %collective-permute-start.31) | collective-permute-done | bytes 409632 | tf_op jit(solution)/shard_map/ppermute | solution.py:794
  252.5 1.7 collective-permute-start.39
  254.4 5.8 %collective-permute-done.32 = bf16[2,400,128]{1,2,0:T(8,128)(2,1)S(1)} collective-permute-done((bf16[2,400,128]{1,2,0:T(8,128)(2,1)S(1)}, bf16[2,400,128]{1,2,0:T(8,128)(2,1)S(1)}, u32[]{:S(2)}, u32[]{:S(2)}) %collective-permute-start.32) | collective-permute-done | bytes 204832 | tf_op jit(solution)/shard_map/ppermute | solution.py:839
  261.6 5.8 %collective-permute-done.33 = bf16[1,400,128]{1,2,0:T(8,128)(2,1)S(1)} collective-permute-done((bf16[1,400,128]{1,2,0:T(8,128)(2,1)S(1)}, bf16[1,400,128]{1,2,0:T(8,128)(2,1)S(1)}, u32[]{:S(2)}, u32[]{:S(2)}) %collective-permute-start.33) | collective-permute-done | bytes 102432 | tf_op jit(solution)/shard_map/ppermute | solution.py:839
  (263 shorter events, 65.1 us)
Async XLA Ops:
  7.2 78.4 %all-gather.6.cloned.1.call-start = ((), (), s32[]{:S(2)}) async-start(), calls=%async_computation.2 | async-start | bytes 3944448 | tf_op jit(solution)/shard_map/all_gather | solution.py:890
  7.2 23.5 %collective-permute-start.8 = (bf16[256,128]{1,0:T(8,128)(2,1)}, bf16[256,128]{1,0:T(8,128)(2,1)S(1)}, u32[]{:S(2)}, u32[]{:S(2)}) collective-permute-start(bf16[256,128]{1,0:T(8,128)(2,1)} %param.17), channel_id=1, source_target_pairs={{0,8},{8,0},{16,24},{24,16},{1,9},{9,1},{17,25},{25,17},{2,10},{10... | collective-permute-start | bytes 196616 | tf_op jit(solution)/shard_map/ppermute | solution.py:794
  10.2 20.5 %collective-permute-start.9 = (bf16[256,128]{1,0:T(8,128)(2,1)}, bf16[256,128]{1,0:T(8,128)(2,1)S(1)}, u32[]{:S(2)}, u32[]{:S(2)}) collective-permute-start(bf16[256,128]{1,0:T(8,128)(2,1)} %param.17), channel_id=1, source_target_pairs={{0,16},{8,24},{16,0},{24,8},{1,17},{9,25},{17,1},{25,9},{2,18},{10... | collective-permute-start | bytes 196616 | tf_op jit(solution)/shard_map/ppermute | solution.py:794
  11.7 19.1 %collective-permute-start.10 = (bf16[256,128]{1,0:T(8,128)(2,1)}, bf16[256,128]{1,0:T(8,128)(2,1)S(1)}, u32[]{:S(2)}, u32[]{:S(2)}) collective-permute-start(bf16[256,128]{1,0:T(8,128)(2,1)} %param.17), channel_id=1, source_target_pairs={{0,24},{8,16},{16,8},{24,0},{1,25},{9,17},{17,9},{25,1},{2,26},{10... | collective-permute-start | bytes 196616 | tf_op jit(solution)/shard_map/ppermute | solution.py:794
  32.6 90.4 %all-gather.8.cloned.1.call-start = ((), (), s32[]{:S(2)}) async-start(), calls=%async_computation.3 | async-start | bytes 3170304 | tf_op jit(solution)/shard_map/all_gather | solution.py:954
  33.5 26.9 %copy-start.44 = (bf16[4,400,128]{2,1,0:T(8,128)(2,1)}, bf16[4,400,128]{2,1,0:T(8,128)(2,1)S(1)}, u32[]{:S(2)}) copy-start(bf16[4,400,128]{2,1,0:T(8,128)(2,1)S(1)} %get-tuple-element.290.refs_0_) | copy-start | bytes 1228804
  33.5 12.3 %collective-permute-start = (bf16[4,400,128]{2,1,0:T(8,128)(2,1)S(1)}, bf16[4,400,128]{2,1,0:T(8,128)(2,1)S(1)}, u32[]{:S(2)}, u32[]{:S(2)}) collective-permute-start(bf16[4,400,128]{2,1,0:T(8,128)(2,1)S(1)} %get-tuple-element.290.refs_0_), channel_id=1, source_target_pairs={{0,8},{8,0},{16,24},{24,16},{1,9},{9,1},{17,25},{25,17},{2,10},{10... | collective-permute-start | bytes 1228808 | tf_op jit(solution)/shard_map/ppermute | solution.py:794
  35.0 20.2 %collective-permute-start.2 = (bf16[4,400,128]{2,1,0:T(8,128)(2,1)S(1)}, bf16[4,400,128]{2,1,0:T(8,128)(2,1)S(1)}, u32[]{:S(2)}, u32[]{:S(2)}) collective-permute-start(bf16[4,400,128]{2,1,0:T(8,128)(2,1)S(1)} %get-tuple-element.290.refs_0_), channel_id=1, source_target_pairs={{0,16},{8,24},{16,0},{24,8},{1,17},{9,25},{17,1},{25,9},{2,18},{10... | collective-permute-start | bytes 1228808 | tf_op jit(solution)/shard_map/ppermute | solution.py:794
  36.5 18.7 %collective-permute-start.4 = (bf16[4,400,128]{2,1,0:T(8,128)(2,1)S(1)}, bf16[4,400,128]{2,1,0:T(8,128)(2,1)S(1)}, u32[]{:S(2)}, u32[]{:S(2)}) collective-permute-start(bf16[4,400,128]{2,1,0:T(8,128)(2,1)S(1)} %get-tuple-element.290.refs_0_), channel_id=1, source_target_pairs={{0,24},{8,16},{16,8},{24,0},{1,25},{9,17},{17,9},{25,1},{2,26},{10... | collective-permute-start | bytes 1228808 | tf_op jit(solution)/shard_map/ppermute | solution.py:794
  43.2 27.0 %copy-start.31 = (f32[8,256]{1,0:T(8,128)S(1)}, f32[8,256]{1,0:T(8,128)}, u32[]{:S(2)}) copy-start(f32[8,256]{1,0:T(8,128)} %stack.86.masks_ref) | copy-start | bytes 24580
  45.8 10.0 %collective-permute-start.1 = (bf16[4,400,128]{2,1,0:T(8,128)(2,1)S(1)}, bf16[4,400,128]{2,1,0:T(8,128)(2,1)S(1)}, u32[]{:S(2)}, u32[]{:S(2)}) collective-permute-start(bf16[4,400,128]{2,1,0:T(8,128)(2,1)S(1)} %collective-permute-done.refs_2_), channel_id=1, source_target_pairs={{0,1},{1,0},{2,3},{3,2},{4,5},{5,4},{6,7},{7,6},{8,9},{9,8},{10,11... | collective-permute-start | bytes 1228808 | tf_op jit(solution)/shard_map/ppermute | solution.py:907
  55.2 1.7 collective-permute-start.3
  55.2 2.3 collective-permute-start.5
  60.4 20.1 %copy-start.34 = (bf16[128,688]{0,1:T(8,128)(2,1)S(1)}, bf16[128,688]{0,1:T(8,128)(2,1)}, u32[]{:S(2)}) copy-start(bf16[128,688]{0,1:T(8,128)(2,1)} %param.18) | copy-start | bytes 528388
  60.5 21.4 %copy-start.6 = (bf16[1,256,1024]{2,1,0:T(8,128)(2,1)S(1)}, bf16[1,256,1024]{2,1,0:T(8,128)(2,1)}, u32[]{:S(2)}) copy-start(bf16[1,256,1024]{2,1,0:T(8,128)(2,1)} %param.23) | copy-start | bytes 1572868
  68.2 8.5 %collective-permute-start.6 = (bf16[9,176,128]{2,1,0:T(8,128)(2,1)}, bf16[9,176,128]{2,1,0:T(8,128)(2,1)S(1)}, u32[]{:S(2)}, u32[]{:S(2)}) collective-permute-start(bf16[9,176,128]{2,1,0:T(8,128)(2,1)} %get-tuple-element.103), channel_id=1, source_target_pairs={{0,1},{1,2},{2,3},{3,4},{4,5},{5,6},{6,7},{8,9},{9,10},{10,11},{11... | collective-permute-start | bytes 1216520 | tf_op jit(solution)/shard_map/ppermute | solution.py:828
  76.7 5.1 %collective-permute-start.7 = (bf16[9,176,128]{2,1,0:T(8,128)(2,1)S(1)}, bf16[9,176,128]{2,1,0:T(8,128)(2,1)S(1)}, u32[]{:S(2)}, u32[]{:S(2)}) collective-permute-start(bf16[9,176,128]{2,1,0:T(8,128)(2,1)S(1)} %collective-permute-done.6.one_ref), channel_id=1, source_target_pairs={{0,1},{1,2},{2,3},{3,4},{4,5},{5,6},{6,7},{8,9},{9,10},{10,11},{11... | collective-permute-start | bytes 1216520 | tf_op jit(solution)/shard_map/ppermute | solution.py:828
  81.8 188.5 %reduce-scatter.2.cloned.1.call-start = ((), (), s32[]{:S(2)}) async-start(), calls=%async_computation.1 | async-start | bytes 4755456 | tf_op jit(solution)/shard_map/reduce_scatter | solution.py:989
  81.9 18.6 %collective-permute-start.11 = (bf16[256,1024]{1,0:T(8,128)(2,1)S(1)}, bf16[256,1024]{1,0:T(8,128)(2,1)S(1)}, u32[]{:S(2)}, u32[]{:S(2)}) collective-permute-start(bf16[256,1024]{1,0:T(8,128)(2,1)S(1)} %bitcast.135), channel_id=1, source_target_pairs={{0,8},{8,0},{16,24},{24,16},{1,9},{9,1},{17,25},{25,17},{2,10},{10... | collective-permute-start | bytes 1572872 | tf_op jit(solution)/shard_map/ppermute | solution.py:794
  82.4 19.5 %collective-permute-start.12 = (bf16[256,1024]{1,0:T(8,128)(2,1)S(1)}, bf16[256,1024]{1,0:T(8,128)(2,1)}, u32[]{:S(2)}, u32[]{:S(2)}) collective-permute-start(bf16[256,1024]{1,0:T(8,128)(2,1)S(1)} %bitcast.136), channel_id=1, source_target_pairs={{0,16},{8,24},{16,0},{24,8},{1,17},{9,25},{17,1},{25,9},{2,18},{10... | collective-permute-start | bytes 1572872 | tf_op jit(solution)/shard_map/ppermute | solution.py:794
  83.8 31.4 %collective-permute-start.13 = (bf16[256,1024]{1,0:T(8,128)(2,1)S(1)}, bf16[256,1024]{1,0:T(8,128)(2,1)}, u32[]{:S(2)}, u32[]{:S(2)}) collective-permute-start(bf16[256,1024]{1,0:T(8,128)(2,1)S(1)} %bitcast.137), channel_id=1, source_target_pairs={{0,24},{8,16},{16,8},{24,0},{1,25},{9,17},{17,9},{25,1},{2,26},{10... | collective-permute-start | bytes 1572872 | tf_op jit(solution)/shard_map/ppermute | solution.py:794
  98.8 11.4 %collective-permute-start.14 = (bf16[128,1024]{1,0:T(8,128)(2,1)}, bf16[128,1024]{1,0:T(8,128)(2,1)}, u32[]{:S(2)}, u32[]{:S(2)}) collective-permute-start(bf16[128,1024]{1,0:T(8,128)(2,1)} %get-tuple-element.112.first_ref.refs_0_), channel_id=1, source_target_pairs={{0,8},{8,0},{16,24},{24,16},{1,9},{9,1},{17,25},{25,17},{2,10},{10... | collective-permute-start | bytes 786440 | tf_op jit(solution)/shard_map/ppermute | solution.py:817
  99.1 15.5 %collective-permute-start.18 = (bf16[128,1024]{1,0:T(8,128)(2,1)}, bf16[128,1024]{1,0:T(8,128)(2,1)}, u32[]{:S(2)}, u32[]{:S(2)}) collective-permute-start(bf16[128,1024]{1,0:T(8,128)(2,1)} %get-tuple-element.113.second_ref.refs_1_), channel_id=1, source_target_pairs={{0,16},{8,24},{16,0},{24,8},{1,17},{9,25},{17,1},{25,9},{2,18},{10... | collective-permute-start | bytes 786440 | tf_op jit(solution)/shard_map/ppermute | solution.py:817
  101.3 24.2 %collective-permute-start.17 = (bf16[128,1024]{1,0:T(8,128)(2,1)}, bf16[128,1024]{1,0:T(8,128)(2,1)}, u32[]{:S(2)}, u32[]{:S(2)}) collective-permute-start(bf16[128,1024]{1,0:T(8,128)(2,1)} %get-tuple-element.112.first_ref.refs_0_), channel_id=1, source_target_pairs={{0,16},{8,24},{16,0},{24,8},{1,17},{9,25},{17,1},{25,9},{2,18},{10... | collective-permute-start | bytes 786440 | tf_op jit(solution)/shard_map/ppermute | solution.py:817
  101.9 29.0 %collective-permute-start.15 = (bf16[128,1024]{1,0:T(8,128)(2,1)}, bf16[128,1024]{1,0:T(8,128)(2,1)}, u32[]{:S(2)}, u32[]{:S(2)}) collective-permute-start(bf16[128,1024]{1,0:T(8,128)(2,1)} %get-tuple-element.113.second_ref.refs_1_), channel_id=1, source_target_pairs={{0,8},{8,0},{16,24},{24,16},{1,9},{9,1},{17,25},{25,17},{2,10},{10... | collective-permute-start | bytes 786440 | tf_op jit(solution)/shard_map/ppermute | solution.py:817
  110.2 26.2 %collective-permute-start.20 = (bf16[128,1024]{1,0:T(8,128)(2,1)}, bf16[128,1024]{1,0:T(8,128)(2,1)}, u32[]{:S(2)}, u32[]{:S(2)}) collective-permute-start(bf16[128,1024]{1,0:T(8,128)(2,1)} %collective-permute-done.14.first_ref.refs_2_), channel_id=1, source_target_pairs={{0,16},{8,24},{16,0},{24,8},{1,17},{9,25},{17,1},{25,9},{2,18},{10... | collective-permute-start | bytes 786440 | tf_op jit(solution)/shard_map/ppermute | solution.py:817
  114.6 21.7 %collective-permute-start.21 = (bf16[128,1024]{1,0:T(8,128)(2,1)}, bf16[128,1024]{1,0:T(8,128)(2,1)}, u32[]{:S(2)}, u32[]{:S(2)}) collective-permute-start(bf16[128,1024]{1,0:T(8,128)(2,1)} %collective-permute-done.18.second_ref.refs_5_), channel_id=1, source_target_pairs={{0,8},{8,0},{16,24},{24,16},{1,9},{9,1},{17,25},{25,17},{2,10},{10... | collective-permute-start | bytes 786440 | tf_op jit(solution)/shard_map/ppermute | solution.py:817
  129.4 29.1 %collective-permute-start.19 = (bf16[256,1024]{1,0:T(8,128)(2,1)}, bf16[256,1024]{1,0:T(8,128)(2,1)}, u32[]{:S(2)}, u32[]{:S(2)}) collective-permute-start(bf16[256,1024]{1,0:T(8,128)(2,1)} %get-tuple-element.119), channel_id=1, source_target_pairs={{0,16},{8,24},{16,0},{24,8},{1,17},{9,25},{17,1},{25,9},{2,18},{10... | collective-permute-start | bytes 1572872 | tf_op jit(solution)/shard_map/ppermute | solution.py:794
  134.8 23.7 %collective-permute-start.16 = (bf16[256,1024]{1,0:T(8,128)(2,1)}, bf16[256,1024]{1,0:T(8,128)(2,1)}, u32[]{:S(2)}, u32[]{:S(2)}) collective-permute-start(bf16[256,1024]{1,0:T(8,128)(2,1)} %get-tuple-element.118), channel_id=1, source_target_pairs={{0,8},{8,0},{16,24},{24,16},{1,9},{9,1},{17,25},{25,17},{2,10},{10... | collective-permute-start | bytes 1572872 | tf_op jit(solution)/shard_map/ppermute | solution.py:794
  140.2 19.9 %collective-permute-start.22 = (bf16[256,1024]{1,0:T(8,128)(2,1)}, bf16[256,1024]{1,0:T(8,128)(2,1)}, u32[]{:S(2)}, u32[]{:S(2)}) collective-permute-start(bf16[256,1024]{1,0:T(8,128)(2,1)} %get-tuple-element.120), channel_id=1, source_target_pairs={{0,24},{8,16},{16,8},{24,0},{1,25},{9,17},{17,9},{25,1},{2,26},{10... | collective-permute-start | bytes 1572872 | tf_op jit(solution)/shard_map/ppermute | solution.py:794
  169.1 11.3 %collective-permute-start.23 = (bf16[9,176,128]{2,1,0:T(8,128)(2,1)S(1)}, bf16[9,176,128]{2,1,0:T(8,128)(2,1)S(1)}, u32[]{:S(2)}, u32[]{:S(2)}) collective-permute-start(bf16[9,176,128]{2,1,0:T(8,128)(2,1)S(1)} %get-tuple-element.145), channel_id=1, source_target_pairs={{1,0},{2,1},{3,2},{4,3},{5,4},{6,5},{7,6},{9,8},{10,9},{11,10},{12... | collective-permute-start | bytes 1216520 | tf_op jit(solution)/shard_map/ppermute | solution.py:828
  170.4 14.7 %collective-permute-start.25 = (bf16[256,1024]{1,0:T(8,128)(2,1)S(1)}, bf16[256,1024]{1,0:T(8,128)(2,1)S(1)}, u32[]{:S(2)}, u32[]{:S(2)}) collective-permute-start(bf16[256,1024]{1,0:T(8,128)(2,1)S(1)} %copy-done.43), channel_id=1, source_target_pairs={{0,8},{8,0},{16,24},{24,16},{1,9},{9,1},{17,25},{25,17},{2,10},{10... | collective-permute-start | bytes 1572872 | tf_op jit(solution)/shard_map/ppermute | solution.py:794
  171.9 25.9 %collective-permute-start.26 = (bf16[256,1024]{1,0:T(8,128)(2,1)S(1)}, bf16[256,1024]{1,0:T(8,128)(2,1)S(1)}, u32[]{:S(2)}, u32[]{:S(2)}) collective-permute-start(bf16[256,1024]{1,0:T(8,128)(2,1)S(1)} %copy-done.41), channel_id=1, source_target_pairs={{0,16},{8,24},{16,0},{24,8},{1,17},{9,25},{17,1},{25,9},{2,18},{10... | collective-permute-start | bytes 1572872 | tf_op jit(solution)/shard_map/ppermute | solution.py:794
  173.4 24.5 %collective-permute-start.27 = (bf16[256,1024]{1,0:T(8,128)(2,1)S(1)}, bf16[256,1024]{1,0:T(8,128)(2,1)S(1)}, u32[]{:S(2)}, u32[]{:S(2)}) collective-permute-start(bf16[256,1024]{1,0:T(8,128)(2,1)S(1)} %copy-done.39), channel_id=1, source_target_pairs={{0,24},{8,16},{16,8},{24,0},{1,25},{9,17},{17,9},{25,1},{2,26},{10... | collective-permute-start | bytes 1572872 | tf_op jit(solution)/shard_map/ppermute | solution.py:794
  180.3 20.4 %copy-start.59 = (bf16[9,176,128]{2,1,0:T(8,128)(2,1)}, bf16[9,176,128]{2,1,0:T(8,128)(2,1)S(1)}, u32[]{:S(2)}) copy-start(bf16[9,176,128]{2,1,0:T(8,128)(2,1)S(1)} %collective-permute-done.23.one_ref) | copy-start | bytes 1216516
  180.3 19.1 %collective-permute-start.24 = (bf16[9,176,128]{2,1,0:T(8,128)(2,1)S(1)}, bf16[9,176,128]{2,1,0:T(8,128)(2,1)S(1)}, u32[]{:S(2)}, u32[]{:S(2)}) collective-permute-start(bf16[9,176,128]{2,1,0:T(8,128)(2,1)S(1)} %collective-permute-done.23.one_ref), channel_id=1, source_target_pairs={{1,0},{2,1},{3,2},{4,3},{5,4},{6,5},{7,6},{9,8},{10,9},{11,10},{12... | collective-permute-start | bytes 1216520 | tf_op jit(solution)/shard_map/ppermute | solution.py:828
  212.5 9.2 %collective-permute-start.28 = (bf16[4,4,400,128]{3,2,1,0:T(8,128)(2,1)}, bf16[4,4,400,128]{3,2,1,0:T(8,128)(2,1)}, u32[]{:S(2)}, u32[]{:S(2)}) collective-permute-start(bf16[4,4,400,128]{3,2,1,0:T(8,128)(2,1)} %get-tuple-element.172), channel_id=1, source_target_pairs={{0,1},{1,0},{2,3},{3,2},{4,5},{5,4},{6,7},{7,6},{8,9},{9,8},{10,11... | collective-permute-start | bytes 4915208 | tf_op jit(solution)/shard_map/ppermute | solution.py:982
  213.8 3.9 %collective-permute-start.34 = (bf16[4,4,256,128]{3,2,1,0:T(8,128)(2,1)S(1)}, bf16[4,4,256,128]{3,2,1,0:T(8,128)(2,1)S(1)}, u32[]{:S(2)}, u32[]{:S(2)}) collective-permute-start(bf16[4,4,256,128]{3,2,1,0:T(8,128)(2,1)S(1)} %get-tuple-element.175), channel_id=1, source_target_pairs={{0,1},{1,0},{2,3},{3,2},{4,5},{5,4},{6,7},{7,6},{8,9},{9,8},{10,11... | collective-permute-start | bytes 3145736 | tf_op jit(solution)/shard_map/ppermute | solution.py:982
  218.1 9.2 %collective-permute-start.35 = (bf16[4,256,128]{2,1,0:T(8,128)(2,1)S(1)}, bf16[4,256,128]{2,1,0:T(8,128)(2,1)S(1)}, u32[]{:S(2)}, u32[]{:S(2)}) collective-permute-start(bf16[4,256,128]{2,1,0:T(8,128)(2,1)S(1)} %get-tuple-element.286), channel_id=1, source_target_pairs={{0,8},{8,0},{16,24},{24,16},{1,9},{9,1},{17,25},{25,17},{2,10},{10... | collective-permute-start | bytes 786440 | tf_op jit(solution)/shard_map/ppermute | solution.py:794
  218.3 13.8 %collective-permute-start.36 = (bf16[4,256,128]{2,1,0:T(8,128)(2,1)S(1)}, bf16[4,256,128]{2,1,0:T(8,128)(2,1)S(1)}, u32[]{:S(2)}, u32[]{:S(2)}) collective-permute-start(bf16[4,256,128]{2,1,0:T(8,128)(2,1)S(1)} %get-tuple-element.288), channel_id=1, source_target_pairs={{0,16},{8,24},{16,0},{24,8},{1,17},{9,25},{17,1},{25,9},{2,18},{10... | collective-permute-start | bytes 786440 | tf_op jit(solution)/shard_map/ppermute | solution.py:794
  220.2 13.7 %collective-permute-start.37 = (bf16[4,256,128]{2,1,0:T(8,128)(2,1)S(1)}, bf16[4,256,128]{2,1,0:T(8,128)(2,1)S(1)}, u32[]{:S(2)}, u32[]{:S(2)}) collective-permute-start(bf16[4,256,128]{2,1,0:T(8,128)(2,1)S(1)} %get-tuple-element.287), channel_id=1, source_target_pairs={{0,24},{8,16},{16,8},{24,0},{1,25},{9,17},{17,9},{25,1},{2,26},{10... | collective-permute-start | bytes 786440 | tf_op jit(solution)/shard_map/ppermute | solution.py:794
  223.8 18.0 %collective-permute-start.29 = (bf16[4,400,128]{2,1,0:T(8,128)(2,1)S(1)}, bf16[4,400,128]{2,1,0:T(8,128)(2,1)S(1)}, u32[]{:S(2)}, u32[]{:S(2)}) collective-permute-start(bf16[4,400,128]{2,1,0:T(8,128)(2,1)S(1)} %get-tuple-element.280), channel_id=1, source_target_pairs={{0,8},{8,0},{16,24},{24,16},{1,9},{9,1},{17,25},{25,17},{2,10},{10... | collective-permute-start | bytes 1228808 | tf_op jit(solution)/shard_map/ppermute | solution.py:794
  224.0 17.8 %collective-permute-start.30 = (bf16[4,400,128]{2,1,0:T(8,128)(2,1)S(1)}, bf16[4,400,128]{2,1,0:T(8,128)(2,1)S(1)}, u32[]{:S(2)}, u32[]{:S(2)}) collective-permute-start(bf16[4,400,128]{2,1,0:T(8,128)(2,1)S(1)} %get-tuple-element.282), channel_id=1, source_target_pairs={{0,16},{8,24},{16,0},{24,8},{1,17},{9,25},{17,1},{25,9},{2,18},{10... | collective-permute-start | bytes 1228808 | tf_op jit(solution)/shard_map/ppermute | solution.py:794
  227.3 23.3 %collective-permute-start.31 = (bf16[4,400,128]{2,1,0:T(8,128)(2,1)S(1)}, bf16[4,400,128]{2,1,0:T(8,128)(2,1)S(1)}, u32[]{:S(2)}, u32[]{:S(2)}) collective-permute-start(bf16[4,400,128]{2,1,0:T(8,128)(2,1)S(1)} %get-tuple-element.281), channel_id=1, source_target_pairs={{0,24},{8,16},{16,8},{24,0},{1,25},{9,17},{17,9},{25,1},{2,26},{10... | collective-permute-start | bytes 1228808 | tf_op jit(solution)/shard_map/ppermute | solution.py:794
  234.0 18.4 %collective-permute-start.38 = (bf16[2,256,128]{2,1,0:T(8,128)(2,1)S(1)}, bf16[2,256,128]{2,1,0:T(8,128)(2,1)S(1)}, u32[]{:S(2)}, u32[]{:S(2)}) collective-permute-start(bf16[2,256,128]{2,1,0:T(8,128)(2,1)S(1)} %dynamic-slice_bitcast_fusion), channel_id=1, source_target_pairs={{0,2},{1,3},{2,0},{3,1},{4,6},{5,7},{6,4},{7,5},{8,10},{9,11},{10,... | collective-permute-start | bytes 393224 | tf_op jit(solution)/shard_map/ppermute | solution.py:839
  251.1 9.1 %collective-permute-start.32 = (bf16[2,400,128]{1,2,0:T(8,128)(2,1)S(1)}, bf16[2,400,128]{1,2,0:T(8,128)(2,1)S(1)}, u32[]{:S(2)}, u32[]{:S(2)}) collective-permute-start(bf16[2,400,128]{1,2,0:T(8,128)(2,1)S(1)} %bitcast.154), channel_id=1, source_target_pairs={{0,2},{1,3},{2,0},{3,1},{4,6},{5,7},{6,4},{7,5},{8,10},{9,11},{10,... | collective-permute-start | bytes 614408 | tf_op jit(solution)/shard_map/ppermute | solution.py:839
  252.5 8.4 %collective-permute-start.39 = (bf16[1,256,128]{2,1,0:T(8,128)(2,1)S(1)}, bf16[1,256,128]{2,1,0:T(8,128)(2,1)S(1)}, u32[]{:S(2)}, u32[]{:S(2)}) collective-permute-start(bf16[1,256,128]{2,1,0:T(8,128)(2,1)S(1)} %constant_dynamic-slice_fusion.7), channel_id=1, source_target_pairs={{0,4},{1,5},{2,6},{3,7},{4,0},{5,1},{6,2},{7,3},{8,12},{9,13},{10,... | collective-permute-start | bytes 196616 | tf_op jit(solution)/shard_map/ppermute | solution.py:839
  260.3 7.2 %collective-permute-start.33 = (bf16[1,400,128]{1,2,0:T(8,128)(2,1)S(1)}, bf16[1,400,128]{1,2,0:T(8,128)(2,1)S(1)}, u32[]{:S(2)}, u32[]{:S(2)}) collective-permute-start(bf16[1,400,128]{1,2,0:T(8,128)(2,1)S(1)} %constant_dynamic-slice_fusion.8), channel_id=1, source_target_pairs={{0,4},{1,5},{2,6},{3,7},{4,0},{5,1},{6,2},{7,3},{8,12},{9,13},{10,... | collective-permute-start | bytes 307208 | tf_op jit(solution)/shard_map/ppermute | solution.py:839
  (58 other events, 326.6 us)
Sparse Core Ops, SparseCore 0:
  32.7 42.4 all-gather.5
  82.0 40.9 all-gather.7
  199.5 52.3 reduce-scatter.1

commit v3 on v2

--- a/solution.py
+++ b/solution.py
@@ -16,6 +16,8 @@
 BF16 = jnp.bfloat16
 VMEM_BYTES = 24 * 1024 * 1024
 VMEM_MOST = 56 * 1024 * 1024
+K1MOST = True
+FAR = False
 
 NN = (((1,), (0,)), ((), ()))
 NT = (((1,), (1,)), ((), ()))
@@ -90,7 +92,8 @@
 
 def one_hot_lanes(rows, index):
     lane = lanes((rows, 128))
-    return jnp.where(lane == index, 1.0, 0.0).astype(BF16)
+    hot = jnp.logical_or(lane == index, lane == index + FDIM)
+    return jnp.where(hot, 1.0, 0.0).astype(BF16)
 
 
 def own_half(x, j, other=None):
@@ -120,13 +123,21 @@
     high = z.astype(BF16)
     low = (z - high.astype(F32)).astype(BF16)
     zero = jnp.zeros_like(high)
-    return jnp.where(lane == base, high, jnp.where(lane == base + 1, low, zero))
+    return jnp.where(lane == base, high, jnp.where(lane == base + FDIM, low, zero))
+
+
+def moved_pair(z, spot, j):
+    base = VDIM if j == 0 else 0
+    z = pltpu.roll(z, lax.rem(base - spot + 128, 128), 1)
+    lane = lanes(z.shape)
+    keep = jnp.logical_or(lane == base, lane == base + FDIM)
+    return jnp.where(keep, z, 0.0).astype(BF16)
 
 
 def with_ones(x, j):
     lane = lanes(x.shape)
     base = VDIM if j == 0 else 0
-    hot = jnp.where(jnp.logical_or(lane == base, lane == base + 1), 1.0, 0.0).astype(x.dtype)
+    hot = jnp.where(jnp.logical_or(lane == base, lane == base + FDIM), 1.0, 0.0).astype(x.dtype)
     return own_half(x, j, hot)
 
 
@@ -181,18 +192,33 @@
     pack_ref[ff:, :] = up_ref[...]
 
 
-def project_body(n, core_ref, x_ref, gain_ref, masks_ref, *refs):
-    blocks = grouped(refs[:-6], n)
-    h1_ref, qk_ref, v_ref, p_ref, wt_ref, z_ref = refs[-6:]
+def project_body(n, piece, where_ref, x_ref, gain_ref, masks_ref, *refs):
+    blocks = grouped(refs[:-7], n)
+    h1_ref, qk_ref, v_ref, p_ref, wt_ref, gains_ref, z_ref = refs[-7:]
     r = pl.program_id(0)
     heads = qk_ref.shape[1] // (2 * FDIM)
     total = wt_ref.shape[1]
+    core = where_ref[n]
 
     @pl.when(r == 0)
     def _():
+        if piece:
+            for q, halves in enumerate(blocks):
+                for other, half in enumerate(halves):
+                    count, _, wb = half.shape
+                    tile = jnp.zeros((16, wb), F32)
+                    for j in range(count):
+                        one = half[j, total : total + 16, :].astype(F32)
+                        one = jnp.where(lanes(one.shape) < piece, one, 0.0)
+                        tile = tile + (one if j == 0 else pltpu.roll(one, j * piece, 1))
+                    side = core if other == 0 else 1 - core
+                    at = pl.multiple_of((where_ref[q] * 2 + side) * wb, wb)
+                    gains_ref[:, pl.ds(at, wb)] = tile[:8]
+        else:
+            gains_ref[...] = gain_ref[...]
         x = x_ref[...].astype(F32)
         normed = x * lax.rsqrt(jnp.mean(x * x, axis=-1, keepdims=True) + EPS)
-        h1_ref[...] = (normed * gain_ref[0:1, :]).astype(BF16)
+        h1_ref[...] = (normed * gains_ref[0:1, :]).astype(BF16)
         z_ref[...] = jnp.zeros_like(z_ref)
 
     for index, halves in enumerate(blocks):
@@ -201,7 +227,7 @@
         def _():
             for other, half in enumerate(halves):
                 count, _, wb = half.shape
-                side = core_ref[0] if other == 0 else 1 - core_ref[0]
+                side = core if other == 0 else 1 - core
                 for j in range(count):
                     at = j * wb if count * wb == wt_ref.shape[2] else (side * count + j) * wb
                     if not isinstance(at, int):
@@ -234,20 +260,21 @@
         p_ref[p_ref.shape[0] - 1] = z_ref[...].astype(BF16)
 
 
-def project(core, x, gain, masks, blocks, heads):
+def project(where, x, gain, masks, blocks, heads, piece):
     n = len(blocks)
     rows, d = x.shape
     nqk, nv = 2 * heads * FDIM, heads * VDIM
     sums = n * heads // 2 + 1
-    ins = (core, x, gain, masks, *flat(blocks))
+    ins = (where, x, gain, masks, *flat(blocks))
     return call(
-        functools.partial(project_body, n),
+        functools.partial(project_body, n, piece),
         (
             sds((rows, d), BF16),
             sds((n, nqk, rows), BF16),
             sds((n, rows, nv), BF16),
             sds((sums, FROWS, 128), BF16),
             sds((n, nqk + nv, d), BF16),
+            sds((8, d), F32),
         ),
         ins,
         grid=(n,),
@@ -258,10 +285,11 @@
             by_row((rows, nv)),
             whole((sums, FROWS, 128)),
             by_row((nqk + nv, d)),
+            whole((8, d)),
         ],
         scratch=[pltpu.VMEM((FROWS, 128), F32)],
         us=7,
-        most=True,
+        most=K1MOST,
     )
 
 
@@ -371,7 +399,7 @@
         acc = acc + mm(o_ref[r], w_ref[r * width : (r + 1) * width, :])
     y1_ref[...] = acc
     scale = lax.rsqrt(jnp.mean(acc * acc, axis=-1, keepdims=True) + EPS)
-    give_rows(h2_refs, (acc * scale * gain_ref[0:1, :]).astype(BF16))
+    give_rows(h2_refs, (acc * scale * gain_ref[1:2, :]).astype(BF16))
 
 
 def give_rows(refs, value):
@@ -520,7 +548,7 @@
     scale = lax.rsqrt(jnp.mean(y1 * y1, axis=-1, keepdims=True) + EPS)
     normed = y1 * scale
     dgain_ref[...] = jnp.sum(dh2 * normed, axis=0, keepdims=True)
-    dn = dh2 * gain_ref[0:1, :]
+    dn = dh2 * gain_ref[1:2, :]
     inner = jnp.mean(dn * normed, axis=-1, keepdims=True)
     dy1 = cot_ref[...].astype(F32) + scale * (dn - normed * inner)
     dy1_ref[...] = dy1
@@ -629,10 +657,8 @@
             d = d_ref[0, i]
             da = mm(d, with_ones(v_pair, j), NT)
             ds = jnp.where(mask, da * s1, 0.0).astype(BF16)
-            z = pick_columns(
-                c_ref[last], lambda row: row == r * heads + i, lambda lane: lane >= 0
-            )
-            dphi = mm(own_half(c, j, with_pair(z, j)), d, NT) * live
+            z = moved_pair(c_ref[last].astype(F32), r * heads + i, j)
+            dphi = mm(own_half(c, j, z), d, NT) * live
             back = features_back(q.astype(F32), dphi)
             dq_ref[0, i * FDIM : (i + 1) * FDIM, :] = (mm(k, ds, NT) * 0.25 + back).astype(BF16)
             dk_ref[0, i * FDIM : (i + 1) * FDIM, :] = mm(q, ds) * 0.25
@@ -671,7 +697,7 @@
 
     @pl.when(r == 0)
     def _():
-        z_ref[...] = joined(one_ref[last], two_ref[last], flag).astype(BF16)
+        z_ref[...] = joined(one_ref[last], two_ref[last], flag)
         acc_ref[...] = jnp.zeros_like(acc_ref)
 
     dks, dvs = [], []
@@ -684,13 +710,8 @@
         for j in range(2):
             i = 2 * pair + j
             k = qk_ref[0, nqk // 2 + i * FDIM : nqk // 2 + (i + 1) * FDIM, :].astype(F32)
-            spot = r * heads + i
-            z = pick_columns(
-                z_ref[...],
-                lambda row: jnp.logical_or(row == spot, row == spot + n * heads),
-                lambda lane: lane >= 0,
-            )
-            dphi = mm(own_half(dp, j, with_pair(z, j)), with_ones(v_pair, j), NT) * tail
+            z = moved_pair(z_ref[...], r * heads + i, j)
+            dphi = mm(own_half(dp, j, z), with_ones(v_pair, j), NT) * tail
             dk = dk_ref[0, i * FDIM : (i + 1) * FDIM, :] + features_back(k, dphi)
             dks.append(dk.astype(BF16))
             phi = (features(k) * tail).astype(BF16)
@@ -699,7 +720,7 @@
     d = jnp.concatenate([dq_ref[0]] + dks + dvs, axis=0)
     total = d.shape[0]
     wide_ref[...] = mm(d, h1_ref[...]).astype(BF16)
-    give_blocks(where_ref[where_ref.shape[0] - 1], wide_ref, [one.at[r, :, 0:total, :] for one in dw_refs])
+    give_blocks(where_ref, wide_ref, [one.at[r, :, 0:total, :] for one in dw_refs])
     acc_ref[...] += mm(d, wt_ref[0], TN)
 
     @pl.when(r == n - 1)
@@ -714,27 +735,30 @@
         inner = jnp.mean(dn * normed, axis=-1, keepdims=True)
         grad_ref[...] = dy1_ref[...] + scale * (dn - normed * inner)
         if nb > 1:
-            groups = dw_refs[0].shape[0]
+            groups, count = dw_refs[0].shape[:2]
             across = groups * nb * wb // dgain_ref.shape[1]
+            tiles = nb // across
             for q in range(groups):
-                for tile in range(nb // across):
-                    at = where_ref[q] * (nb // across) + tile
+                for z in range(count):
+                    at = where_ref[q] * tiles + (where_ref[groups + 1] ^ z) * 2 // across
                     both = dgain_ref[:, pl.ds(pl.multiple_of(at * wb, wb), wb)]
                     high = both.astype(BF16).astype(F32)
                     fill = jnp.zeros((dw_refs[0].shape[2] - total - 4, wb), F32)
                     block = jnp.concatenate([high, both - high, fill], axis=0).astype(BF16)
                     for one in dw_refs:
-                        for s in range(tile * across // 2, (tile + 1) * across // 2):
-                            one[q, s, total:, :] = block
-
-
-def give_blocks(core, wide_ref, refs):
+                        one[q, z, total:, :] = block
+
+
+def give_blocks(where_ref, wide_ref, refs):
     count, _, wb = refs[0].shape
+    last = where_ref.shape[0] - 1
     for index, one in enumerate(refs):
         for z in range(count):
-            at = (2 * z + jnp.where(index == 0, core, 1 - core)) * wb if len(refs) == 2 else 0
+            at = 0
             if len(refs) == 2:
-                at = pl.multiple_of(at, wb)
+                core = where_ref[last - 1]
+                side = core if index == 0 else 1 - core
+                at = pl.multiple_of(((where_ref[last] ^ z) * 2 + side) * wb, wb)
             one[z] = wide_ref[:, pl.ds(at, wb)]
 
 
@@ -755,7 +779,7 @@
         + [whole(y.shape) for y in (gain, x, dy1, dgain_mlp)],
         out_specs=[whole((rows, d)), *[whole(shape) for shape in shapes], whole((2, d))],
         scratch=[
-            pltpu.VMEM((FROWS, 128), BF16),
+            pltpu.VMEM((FROWS, 128), F32),
             pltpu.VMEM((rows, d), F32),
             pltpu.VMEM((total, d), BF16),
         ],
@@ -764,21 +788,21 @@
     )
 
 
-def out_grads_body(n, core_ref, f_ref, *refs):
+def out_grads_body(n, where_ref, f_ref, *refs):
     o_ref, outs, wide_ref = refs[0], refs[1:-1], refs[-1]
     for r in range(n):
         wide_ref[...] = mm(o_ref[r], f_ref[...], TN).astype(BF16)
-        give_blocks(core_ref[0], wide_ref, [one.at[r] for one in outs])
-
-
-def out_grads(core, o, f, nb):
+        give_blocks(where_ref, wide_ref, [one.at[r] for one in outs])
+
+
+def out_grads(where, o, f, nb):
     n, _, nv = o.shape
     d = f.shape[1]
     shapes = [(n, 1, nv, d)] if nb == 1 else [(n, nb // 2, nv, d // nb)] * 2
     return call(
         functools.partial(out_grads_body, n),
         [sds(shape, BF16) for shape in shapes],
-        (core, f, o),
+        (where, f, o),
         scratch=[pltpu.VMEM((nv, d), BF16)],
         smem=1,
         us=3,
@@ -828,18 +852,19 @@
     return lax.ppermute(x, "seq", [(i, i + step) for i in range(size) if 0 <= i + step < size])
 
 
-def halved(x, first=1, stop=None):
-    size, me = lax.axis_size("seq"), lax.axis_index("seq")
-    k = first
-    while k < (stop or size):
-        x = x.reshape((x.shape[0] // 2, 2) + x.shape[1:])
-        bit = (me // k) % 2
-        keep = lax.dynamic_index_in_dim(x, bit, 1, keepdims=False)
-        send = lax.dynamic_index_in_dim(x, 1 - bit, 1, keepdims=False)
-        got = lax.ppermute(send, "seq", xor_pairs(size, k))
-        x = (keep.astype(F32) + got.astype(F32)).astype(x.dtype)
-        k *= 2
-    return x
+def over_z(x):
+    count, size = x.shape[0], lax.axis_size("seq")
+    if count <= 4:
+        parts = [lax.ppermute(x[k], "seq", xor_pairs(size, 2 * k)) for k in range(1, count)]
+        total = x[0].astype(F32)
+        for part in parts:
+            total = total + part.astype(F32)
+        return total
+    while count > 1:
+        count //= 2
+        got = lax.ppermute(x[count:], "seq", xor_pairs(size, 2 * count))
+        x = (x[:count].astype(F32) + got.astype(F32)).astype(x.dtype)
+    return x[0].astype(F32)
 
 
 def carried(x, labels, step, join, before):
@@ -899,16 +924,20 @@
         return jnp.moveaxis(w, -2, 0)
 
     core = (me % 2).reshape(1)
+    where = jnp.concatenate([here ^ jnp.arange(n, dtype=jnp.int32), core, (me // 2).reshape(1)])
     half = blocks // 2
     mine = lax.dynamic_slice_in_dim(pack, core[0] * half, half)
     other = lax.dynamic_slice_in_dim(pack, (1 - core[0]) * half, half)
     mine = swap([mine] * n)
     pairs = [[mine[0], other]]
     pairs += [[one, lax.ppermute(one, "seq", xor_pairs(blocks, 1))] for one in mine[1:]]
-    small = jnp.stack([jnp.stack([one[:, nqkv : nqkv + 2, :piece] for one in pair]) for pair in pairs])
-    small = jnp.take(jnp.take(small, here ^ jnp.arange(n), axis=0), core[0] ^ jnp.arange(2), axis=1)
-    gains = jnp.transpose(small.reshape(n, blocks, 2, piece), (2, 0, 1, 3)).reshape(2, 1, d)
-    gain_mix, gain_mlp = gains[0].astype(F32), gains[1].astype(F32)
+    if nb == blocks:
+        gain_in = jnp.zeros((8, 128), F32)
+    else:
+        small = jnp.stack([jnp.stack([one[:, nqkv : nqkv + 2, :piece] for one in pair]) for pair in pairs])
+        small = jnp.take(jnp.take(small, here ^ jnp.arange(n), axis=0), core[0] ^ jnp.arange(2), axis=1)
+        gain_in = jnp.transpose(small.reshape(n, blocks, 2, piece), (2, 0, 1, 3)).reshape(2, d)
+        gain_in = jnp.pad(gain_in.astype(F32), ((0, 6), (0, 0)))
     docs = pack[:, nqkv + 2 : nqkv + 2 + doc_rows].reshape(blocks, rows).astype(F32)
     segs = jnp.take(docs, me, axis=0)
     lasts = docs[:, -1]
@@ -946,27 +975,31 @@
         + [jnp.zeros_like(segs)] * 3
     )
 
-    h1, qk, v, sums, w_qkv = project(core, x, gain_mix, masks, pairs, heads)
+    h1, qk, v, sums, w_qkv, gains = project(
+        where, x, gain_in, masks, pairs, heads, piece if nb == blocks else 0
+    )
     cots = swap([cot_late] * n)
     nd = local(qk, v, masks)
     one, two = carried(sums, lasts, 1, join, nd)
-    wide, two = lax.optimization_barrier((wide, two))
+    w_out, w_down = spread_out(gathered(second), ff)
+    wide, one, w_out = lax.optimization_barrier((wide, one, w_out))
     w_mlp = widen(gathered(lax.all_gather(wide, "seq")))
-    w_out, w_down = spread_out(gathered(second), ff)
     dhid = prepare(w_down, cots)
-    two, w_out = lax.optimization_barrier((two, w_out))
     o, on, inv, c = carry(nd, qk, masks, one, two)
-    y1, h2 = middle(x, o, w_out, gain_mlp)
+    y1, h2 = middle(x, o, w_out, gains)
     h2s = spread_halves(h2)
-    res = [mlp(r, h2s[r], dhid, w_mlp) for r in range(n)]
+    res = [None] * n
+    held = h2s[n - 1]
+    for r in range(n - 1, -1, -1):
+        res[r] = mlp(r, held, dhid, w_mlp)
+        if r:
+            held, res[r] = lax.optimization_barrier((list(h2s[r - 1]), list(res[r])))
     dparts, hid, dg, du = ([t[k] for t in res] for k in range(4))
     dparts = swap(dparts)
     oparts = mlp_out(hid, w_down)
     dmlp = mlp_grads(h2s, cots, hid, dg, du, nb)
     dparts, oparts, dmlp = lax.optimization_barrier((dparts, oparts, dmlp))
-    dy1, dgain_mlp, f, do = turn(dparts, y1, cot, gain_mlp, w_out)
-    oparts, f = lax.optimization_barrier((oparts, f))
-    oparts = swap(oparts)
+    dy1, dgain_mlp, f, do = turn(dparts, y1, cot, gains, w_out)
     dext, dsums = back_first(do, on, inv, qk, masks)
     dq, dk, dv = back_local(dext, qk, v, masks, c)
     back_one, back_two = carried(dsums, labels_back, -1, join, (dq, dk, dv))
@@ -976,23 +1009,28 @@
             return w
         w = unblocked(w[0][:, 0][None])
         w = jnp.moveaxis(w.reshape((half, 2) + w.shape[1:]), 2, 0)
+        w = jnp.take(w, (me // 2) ^ jnp.arange(half), axis=1)
         return [lax.dynamic_index_in_dim(w, bit, 2, keepdims=False) for bit in (core[0], 1 - core[0])]
 
-    def reduced(keep, give):
+    def pooled(keep, give):
         got = lax.ppermute(give, "seq", xor_pairs(blocks, 1))
-        w = (keep.astype(F32) + got.astype(F32)).astype(BF16)
-        w = sum_parts(swap([w[r] for r in range(n)]))
-        return halved(w, 2)
-
-    dout = reduced(*split(out_grads(core, o, f, nb)))
-    dmlp, back_two, oparts = lax.optimization_barrier((dmlp, back_two, oparts))
+        return [(keep[r].astype(F32) + got[r].astype(F32)).astype(BF16) for r in range(n)]
+
+    dout = sum_parts(swap(pooled(*split(out_grads(where, o, f, nb)))))
+    dmlp, back_two, dout = lax.optimization_barrier((dmlp, back_two, dout))
     dmlp = lax.psum_scatter(unblocked(dmlp), "seq", tiled=True)[0].astype(F32)
-    where = jnp.concatenate([here ^ jnp.arange(n, dtype=jnp.int32), core])
     grad_tokens, *dqkv, dgains = back_last(
-        where, dq, dk, dv, qk, v, masks, back_one, back_two, h1, w_qkv, gain_mix, x, dy1, dgain_mlp, nb
-    )
-    dqkv = reduced(*split(dqkv))[0].astype(F32)
-    dout = dout[0].astype(F32)
+        where, dq, dk, dv, qk, v, masks, back_one, back_two, h1, w_qkv, gains, x, dy1, dgain_mlp, nb
+    )
+    near = [lax.ppermute(oparts[r], "head", xor_pairs(n, r)) for r in range(1, n - 1)]
+    near, dqkv = lax.optimization_barrier((near, dqkv))
+    dqkv = pooled(*split(dqkv))
+    far = lax.ppermute(oparts[n - 1], "head", xor_pairs(n, n - 1))
+    if FAR:
+        far, dqkv = lax.optimization_barrier((far, dqkv))
+    dqkv = over_z(sum_parts(swap(dqkv)))
+    oparts = [oparts[0], *near, far]
+    dout = over_z(dout)
     if nb == blocks:
         parts = dqkv[nqkv : nqkv + 2] + dqkv[nqkv + 2 : nqkv + 4]
         total = lax.dynamic_slice_in_dim(parts, me % (wb // piece) * piece, piece, axis=1)

time: 280 us -> 265 us (0.946)
  waiting for transfers between devices: 80.3 us -> 68.2 us
  Pallas kernels: 74.5 us -> 70.2 us
    ppermute x21 -> x18, waiting for transfers between devices: 49.8 us -> 30.8 us  [swap(): lax.ppermute(parts[r], 'head', xor_pairs(size, r))]
    ppermute x6, waiting for transfers between devices: 9.47 us -> 16.5 us  [send(): return lax.ppermute(x, 'head', xor_pairs(size, r))]
    ppermute x6 -> x11, starting transfers between devices: 6.1 us -> 12 us  [the longest x6 8.04 us: over_z(): lax.ppermute(x[k], 'seq', xor_pairs(size, 2 * k))]
    ppermute x6 -> x11, waiting for transfers between devices: 15 us -> 20.2 us  [the longest x6 8.91 us: over_z(): lax.ppermute(x[k], 'seq', xor_pairs(size, 2 * k))]
    pallas_call x20, Pallas kernels: 74.5 us -> 70.2 us  [call(): pl.pallas_call(body, out_shape=outs, scratch_shapes=list(scratch), compil...]
    all_gather x1, waiting for transfers between devices: 3.67 us -> 0.01 us  [on_device(): w_mlp = widen(gathered(lax.all_gather(wide, 'seq')))]
    ppermute x21 -> x18, starting transfers between devices: 25.7 us -> 22.2 us  [swap(): lax.ppermute(parts[r], 'head', xor_pairs(size, r))]
    unnamed x134 -> x130, local copies, waits for them, and re-layouts: 26.6 us -> 26.9 us
  transfers between devices with their start and end apart: 43 -> 45, of which waited for: 19 -> 16; matrix products, arithmetic and copies ran while one was open for 5% -> 5% of each run, Pallas kernels for 24% -> 25%
where the time goes in v3:
time: 265 us; the launch traced here: 264 us
  Pallas kernels  70.2 us (26%)
  waiting for transfers between devices  68.2 us (26%)
  starting transfers between devices  49.6 us (19%)
  local copies, waits for them, and re-layouts  32.6 us (12%)
  between operations  18.5 us (7%)
  blocking collectives  16.5 us (6%)
  other arithmetic  8.08 us (3%)
    pallas_call x20, Pallas kernels, call(): pl.pallas_call(body, out_shape=outs, scratch_shapes=list(scratch), compil...  70.2 us
    ppermute x18, waiting for transfers between devices, swap(): lax.ppermute(parts[r], 'head', xor_pairs(size, r))  30.8 us
    unnamed x130, local copies, waits for them, and re-layouts  26.9 us
    ppermute x18, starting transfers between devices, swap(): lax.ppermute(parts[r], 'head', xor_pairs(size, r))  22.2 us
    ppermute x6, waiting for transfers between devices, send(): return lax.ppermute(x, 'head', xor_pairs(size, r))  16.5 us
    all_gather x1, blocking collectives, on_device(): pack = lax.all_gather(pack, 'seq')  16.5 us
    ppermute x6, waiting for transfers between devices, over_z(): lax.ppermute(x[k], 'seq', xor_pairs(size, 2 * k))  8.91 us
    ppermute x4, starting transfers between devices, shifted(): lax.ppermute(x, 'seq', [(i, i + step) for i in range(size) if 0 <= i + st...  8.58 us
  transfers between devices with their start and end apart: 45, of which 16 were waited for; matrix products, arithmetic and copies ran while one was open for 5% of the time, Pallas kernels for 25%

profile of v3, /device:TPU:0, one launch (start us, length us, event | category | flops | bytes accessed | tf_op | source)
XLA Modules:
  0.0 263.6 jit_solution(13537651050406759970)
XLA Ops:
  7.2 3.0 %collective-permute-start.8 = (bf16[256,128]{1,0:T(8,128)(2,1)}, bf16[256,128]{1,0:T(8,128)(2,1)S(1)}, u32[]{:S(2)}, u32[]{:S(2)}) collective-permute-start(bf16[256,128]{1,0:T(8,128)(2,1)} %param.17), channel_id=1, source_target_pairs={{0,16},{8,24},{16,0},{24,8},{1,17},{9,25},{17,1},{25,9},{2,18},{10... | collective-permute-start | bytes 196616 | tf_op jit(solution)/shard_map/ppermute | solution.py:818
  10.3 1.5 collective-permute-start.7
  11.8 1.6 shard_map.203
  13.4 16.5 %all-gather = bf16[3200,128]{1,0:T(8,128)(2,1)S(1)} all-gather(bf16[400,128]{1,0:T(8,128)(2,1)} %shard_map.203), channel_id=2, replica_groups=mesh['head'=4,'seq'=8] {'seq'}, dimensions={0}, use_global_device_ids=true | all-gather | bytes 921600 | tf_op jit(solution)/shard_map/all_gather | solution.py:913
  32.6 2.4 collective-permute-start.4
  41.5 4.3 %collective-permute-done.4.refs_6_ = bf16[4,400,128]{2,1,0:T(8,128)(2,1)S(1)} collective-permute-done((bf16[4,400,128]{2,1,0:T(8,128)(2,1)S(1)}, bf16[4,400,128]{2,1,0:T(8,128)(2,1)S(1)}, u32[]{:S(2)}, u32[]{:S(2)}) %collective-permute-start.4) | collective-permute-done | bytes 409632 | tf_op jit(solution)/shard_map/ppermute | solution.py:818
  45.8 8.2 %collective-permute-done.2.refs_4_ = bf16[4,400,128]{2,1,0:T(8,128)(2,1)S(1)} collective-permute-done((bf16[4,400,128]{2,1,0:T(8,128)(2,1)S(1)}, bf16[4,400,128]{2,1,0:T(8,128)(2,1)S(1)}, u32[]{:S(2)}, u32[]{:S(2)}) %collective-permute-start.2) | collective-permute-done | bytes 409632 | tf_op jit(solution)/shard_map/ppermute | solution.py:818
  57.1 7.9 %shard_map.204 = (bf16[256,1024]{1,0:T(8,128)(2,1)}, bf16[4,128,256]{2,1,0:T(8,128)(2,1)}, bf16[4,256,256]{2,1,0:T(8,128)(2,1)}, bf16[9,176,128]{2,1,0:T(8,128)(...) custom-call(s32[6]{0:T(128)} %pad_add_fusion.where_ref, bf16[256,1024]{1,0:T(8,128)(2,1)} %bitcast.102, ...), custom_call_target="tpu_custom_call" | custom-call | bytes 4200000 | tf_op jit(solution)/shard_map/pallas_call | solution.py:38
  64.9 2.0 collective-permute-start.6
  69.7 3.2 %shard_map.205.nd_ref = f32[4,2,256,256]{3,2,1,0:T(8,128)S(1)} custom-call(bf16[4,128,256]{2,1,0:T(8,128)(2,1)S(1)} %copy-done.4, bf16[4,256,256]{2,1,0:T(8,128)(2,1)S(1)} %copy-done.9, f32[8,256]{1,0:T(8,128)S(1)} %copy-done.34), custom_call_target="tpu_custom_call" | custom-call | bytes 3000000 | tf_op jit(solution)/shard_map/pallas_call | solution.py:38
  75.0 2.0 copy-done.14
  78.1 3.9 %collective-permute-start.10 = (bf16[9,176,128]{2,1,0:T(8,128)(2,1)}, bf16[9,176,128]{2,1,0:T(8,128)(2,1)S(1)}, u32[]{:S(2)}, u32[]{:S(2)}) collective-permute-start(bf16[9,176,128]{2,1,0:T(8,128)(2,1)} %copy-done.57), channel_id=1, source_target_pairs={{0,1},{1,2},{2,3},{3,4},{4,5},{5,6},{6,7},{8,9},{9,10},{10,11},{11... | collective-permute-start | bytes 1216520 | tf_op jit(solution)/shard_map/ppermute | solution.py:852
  82.0 1.6 collective-permute-start.19
  83.6 1.4 collective-permute-start.18
  86.4 5.7 %shard_map.208 = (bf16[4,256,256]{2,1,0:T(8,128)(2,1)}, f32[4,256,256]{2,1,0:T(8,128)}, f32[4,256,256]{2,1,0:T(8,128)}, bf16[9,176,128]{2,1,0:T(8,128)(2,1)}) custom-call(f32[4,2,256,256]{3,2,1,0:T(8,128)} %copy-done.1, bf16[4,128,256]{2,1,0:T(8,128)(2,1)} %get-tuple-element.116.qk_ref, f32[8,256]{1,0:T(8,128)} %stack.18.masks_ref, ...), custom_call_target="tpu_custom_call" | custom-call | bytes 3000000 | tf_op jit(solution)/shard_map/pallas_call | solution.py:38
  93.2 1.6 shard_map.209
  95.8 1.5 collective-permute-start.11
  97.9 16.5 %collective-permute-done.11.first_ref.refs_2_ = bf16[128,1024]{1,0:T(8,128)(2,1)S(1)} collective-permute-done((bf16[128,1024]{1,0:T(8,128)(2,1)}, bf16[128,1024]{1,0:T(8,128)(2,1)S(1)}, u32[]{:S(2)}, u32[]{:S(2)}) %collective-permute-start.11) | collective-permute-done | bytes 262176 | tf_op jit(solution)/shard_map/ppermute | solution.py:841
  118.5 1.8 shard_map.210.dhid_ref
  122.8 1.8 copy-done.15
  125.4 3.9 %shard_map.212 = (bf16[256,1024]{1,0:T(8,128)(2,1)}, bf16[256,688]{1,0:T(8,128)(2,1)S(1)}, bf16[256,688]{1,0:T(8,128)(2,1)S(1)}, bf16[256,688]{1,0:T(8,128)(2,1)S(1)}) custom-call(bf16[128,1024]{1,0:T(8,128)(2,1)} %collective-permute-done.15.first_ref.refs_6_, bf16[128,1024]{1,0:T(8,128)(2,1)} %collective-permute-done.16.second_ref.refs_7_, ...), custom_call_target="tpu_custom_call" | custom-call | bytes 3000000 | tf_op jit(solution)/shard_map/pallas_call | solution.py:38
  129.3 1.5 collective-permute-start.22
  130.8 3.8 %shard_map.213 = (bf16[256,1024]{1,0:T(8,128)(2,1)}, bf16[256,688]{1,0:T(8,128)(2,1)S(1)}, bf16[256,688]{1,0:T(8,128)(2,1)S(1)}, bf16[256,688]{1,0:T(8,128)(2,1)S(1)}) custom-call(bf16[128,1024]{1,0:T(8,128)(2,1)} %collective-permute-done.13.first_ref.refs_4_, bf16[128,1024]{1,0:T(8,128)(2,1)S(1)} %collective-permute-done.14.second_ref.refs_5_, ...), custom_call_target="tpu_custom_call" | custom-call | bytes 3000000 | tf_op jit(solution)/shard_map/pallas_call | solution.py:38
  135.4 3.8 %shard_map.214 = (bf16[256,1024]{1,0:T(8,128)(2,1)}, bf16[256,688]{1,0:T(8,128)(2,1)S(1)}, bf16[256,688]{1,0:T(8,128)(2,1)S(1)}, bf16[256,688]{1,0:T(8,128)(2,1)S(1)}) custom-call(bf16[128,1024]{1,0:T(8,128)(2,1)S(1)} %collective-permute-done.11.first_ref.refs_2_, bf16[128,1024]{1,0:T(8,128)(2,1)} %collective-permute-done.12.second_ref.refs_3_, ...), custom_call_target="tpu_custom_call" | custom-call | bytes 3000000 | tf_op jit(solution)/shard_map/pallas_call | solution.py:38
  140.5 3.1 %shard_map.215 = (bf16[256,1024]{1,0:T(8,128)(2,1)S(1)}, bf16[256,688]{1,0:T(8,128)(2,1)S(1)}, bf16[256,688]{1,0:T(8,128)(2,1)S(1)}, bf16[256,688]{1,0:T(8,128)(2,1)S(1)}) custom-call(bf16[128,1024]{1,0:T(8,128)(2,1)} %get-tuple-element.147.first_ref.refs_0_, bf16[128,1024]{1,0:T(8,128)(2,1)} %get-tuple-element.148.second_ref.refs_1_, ...), custom_call_target="tpu_custom_call" | custom-call | bytes 3000000 | tf_op jit(solution)/shard_map/pallas_call | solution.py:38
  144.4 1.8 shard_map.216
  149.5 6.1 %shard_map.217 = bf16[8,2064,128]{2,1,0:T(8,128)(2,1)S(1)} custom-call(bf16[128,1024]{1,0:T(8,128)(2,1)} %get-tuple-element.147.first_ref.refs_0_, bf16[128,1024]{1,0:T(8,128)(2,1)} %get-tuple-element.148.second_ref.refs_1_, bf16[128,1024]{1,0:T(8,128)(2,1)S(1)} %collective-permute-done.11.first_ref.refs_2_, ...), custom_call_target="tpu_custom_call" | custom-call | bytes 5400000 | tf_op jit(solution)/shard_map/pallas_call | solution.py:38
  155.6 2.0 copy-done
  159.9 2.8 %shard_map.218 = (f32[256,1024]{1,0:T(8,128)S(1)}, f32[1,1024]{1,0:T(1,128)S(1)}, bf16[256,1024]{1,0:T(8,128)(2,1)S(1)}, bf16[4,256,256]{2,1,0:T(8,128)(2,1)S(1)}) custom-call(f32[256,1024]{1,0:T(8,128)S(1)} %copy-done.12, bf16[256,1024]{1,0:T(8,128)(2,1)S(1)} %bitcast.101, f32[8,1024]{1,0:T(8,128)S(1)} %copy-done.36, bf16[256,1024]{1,0:T(8,128)(2,1)S(1)} %copy-done.32, ...), custom_call_target="tpu_custom_call" | custom-call | bytes 3000000 | tf_op jit(solution)/shard_map/pallas_call | solution.py:38
  163.7 1.7 shard_map.221
  165.6 3.6 %shard_map.219 = (bf16[4,4,256,128]{3,2,1,0:T(8,128)(2,1)S(1)}, bf16[9,176,128]{2,1,0:T(8,128)(2,1)S(1)}) custom-call(bf16[4,256,256]{2,1,0:T(8,128)(2,1)S(1)} %get-tuple-element.176.do_ref, f32[4,256,256]{2,1,0:T(8,128)S(1)} %copy-done.25, f32[4,256,256]{2,1,0:T(8,128)S(1)} %copy-done.26, bf16[4,128,256]{2,1,0:T(8,128)(2,1)S(1)} %copy-done.5, ...), custom_call_target="tpu_custom_call" | custom-call | bytes 3000000 | tf_op jit(solution)/shard_map/pallas_call | solution.py:38
  171.7 1.5 collective-permute-start.30
  174.5 5.3 %shard_map.220 = (bf16[4,64,256]{2,1,0:T(8,128)(2,1)S(1)}, f32[4,64,256]{2,1,0:T(8,128)S(1)}, f32[4,256,256]{2,1,0:T(8,128)S(1)}) custom-call(bf16[4,4,256,128]{3,2,1,0:T(8,128)(2,1)S(1)} %get-tuple-element.179.d_ref, bf16[4,128,256]{2,1,0:T(8,128)(2,1)S(1)} %copy-done.5, bf16[4,256,256]{2,1,0:T(8,128)(2,1)S(1)} %copy-done.10, f32[8,256]{1,0:T(8,128)S(1)} %copy-done.35, ...), custom_call_target="tpu_custom_call" | custom-call | bytes 3000000 | tf_op jit(solution)/shard_map/pallas_call | solution.py:38
  181.2 4.8 %collective-permute-done.30 = bf16[4,256,128]{2,1,0:T(8,128)(2,1)S(1)} collective-permute-done((bf16[4,256,128]{2,1,0:T(8,128)(2,1)S(1)}, bf16[4,256,128]{2,1,0:T(8,128)(2,1)S(1)}, u32[]{:S(2)}, u32[]{:S(2)}) %collective-permute-start.30) | collective-permute-done | bytes 262176 | tf_op jit(solution)/shard_map/ppermute | solution.py:818
  185.9 1.7 collective-permute-done.29
  191.0 10.5 %shard_map.222 = (f32[256,1024]{1,0:T(8,128)}, bf16[4,4,400,128]{3,2,1,0:T(8,128)(2,1)}, bf16[4,4,400,128]{3,2,1,0:T(8,128)(2,1)}, f32[2,1024]{1,0:T(2,128)}) custom-call(s32[6]{0:T(128)} %pad_add_fusion.where_ref, bf16[4,64,256]{2,1,0:T(8,128)(2,1)} %copy-done.40, f32[4,64,256]{2,1,0:T(8,128)} %copy-done.37, f32[4,256,256]{2,1,0:T(8,128)} %copy-done.28, ...), custom_call_target="tpu_custom_call" | custom-call | bytes 6000000 | tf_op jit(solution)/shard_map/pallas_call | solution.py:38
  202.9 2.0 collective-permute-done.24
  205.3 1.4 collective-permute-start.31
  206.7 1.9 collective-permute-done.32
  208.6 1.6 fusion.8
  215.1 6.0 %collective-permute-done.31 = bf16[256,1024]{1,0:T(8,128)(2,1)} collective-permute-done((bf16[256,1024]{1,0:T(8,128)(2,1)S(1)}, bf16[256,1024]{1,0:T(8,128)(2,1)}, u32[]{:S(2)}, u32[]{:S(2)}) %collective-permute-start.31) | collective-permute-done | bytes 524320 | tf_op jit(solution)/shard_map/ppermute | solution.py:1028
  221.2 2.3 fusion.3
  223.5 5.6 %collective-permute-done.33 = bf16[4,400,128]{2,1,0:T(8,128)(2,1)S(1)} collective-permute-done((bf16[4,400,128]{2,1,0:T(8,128)(2,1)S(1)}, bf16[4,400,128]{2,1,0:T(8,128)(2,1)S(1)}, u32[]{:S(2)}, u32[]{:S(2)}) %collective-permute-start.33) | collective-permute-done | bytes 409632 | tf_op jit(solution)/shard_map/ppermute | solution.py:818
  229.1 2.4 collective-permute-start.40
  231.5 6.3 %collective-permute-done.35 = bf16[4,400,128]{2,1,0:T(8,128)(2,1)S(1)} collective-permute-done((bf16[4,400,128]{2,1,0:T(8,128)(2,1)S(1)}, bf16[4,400,128]{2,1,0:T(8,128)(2,1)S(1)}, u32[]{:S(2)}, u32[]{:S(2)}) %collective-permute-start.35) | collective-permute-done | bytes 409632 | tf_op jit(solution)/shard_map/ppermute | solution.py:818
  240.4 2.9 %collective-permute-start.38 = (bf16[400,128]{1,0:T(8,128)(2,1)S(1)}, bf16[400,128]{1,0:T(8,128)(2,1)S(1)}, u32[]{:S(2)}, u32[]{:S(2)}) collective-permute-start(bf16[400,128]{1,0:T(8,128)(2,1)S(1)} %get-tuple-element.318), channel_id=1, source_target_pairs={{0,6},{1,7},{2,4},{3,5},{4,2},{5,3},{6,0},{7,1},{8,14},{9,15},{10,... | collective-permute-start | bytes 307208 | tf_op jit(solution)/shard_map/ppermute | solution.py:858
  244.3 4.5 %collective-permute-done.38 = bf16[400,128]{1,0:T(8,128)(2,1)S(1)} collective-permute-done((bf16[400,128]{1,0:T(8,128)(2,1)S(1)}, bf16[400,128]{1,0:T(8,128)(2,1)S(1)}, u32[]{:S(2)}, u32[]{:S(2)}) %collective-permute-start.38) | collective-permute-done | bytes 102432 | tf_op jit(solution)/shard_map/ppermute | solution.py:858
  248.8 4.1 %collective-permute-done.37 = bf16[400,128]{1,0:T(8,128)(2,1)S(1)} collective-permute-done((bf16[400,128]{1,0:T(8,128)(2,1)S(1)}, bf16[400,128]{1,0:T(8,128)(2,1)S(1)}, u32[]{:S(2)}, u32[]{:S(2)}) %collective-permute-start.37) | collective-permute-done | bytes 102432 | tf_op jit(solution)/shard_map/ppermute | solution.py:858
  (230 shorter events, 57.7 us)
Async XLA Ops:
  7.2 23.7 %copy-start.61 = (bf16[688,128]{1,0:T(8,128)(2,1)S(1)}, bf16[688,128]{1,0:T(8,128)(2,1)}, u32[]{:S(2)}) copy-start(bf16[688,128]{1,0:T(8,128)(2,1)} %param.20) | copy-start | bytes 528388
  7.2 67.2 %all-gather.6.cloned.1.call-start = ((), (), s32[]{:S(2)}) async-start(), calls=%async_computation.2 | async-start | bytes 3944448 | tf_op jit(solution)/shard_map/all_gather | solution.py:915
  7.2 23.6 %collective-permute-start.8 = (bf16[256,128]{1,0:T(8,128)(2,1)}, bf16[256,128]{1,0:T(8,128)(2,1)S(1)}, u32[]{:S(2)}, u32[]{:S(2)}) collective-permute-start(bf16[256,128]{1,0:T(8,128)(2,1)} %param.17), channel_id=1, source_target_pairs={{0,16},{8,24},{16,0},{24,8},{1,17},{9,25},{17,1},{25,9},{2,18},{10... | collective-permute-start | bytes 196616 | tf_op jit(solution)/shard_map/ppermute | solution.py:818
  10.3 20.5 %collective-permute-start.7 = (bf16[256,128]{1,0:T(8,128)(2,1)}, bf16[256,128]{1,0:T(8,128)(2,1)S(1)}, u32[]{:S(2)}, u32[]{:S(2)}) collective-permute-start(bf16[256,128]{1,0:T(8,128)(2,1)} %param.17), channel_id=1, source_target_pairs={{0,8},{8,0},{16,24},{24,16},{1,9},{9,1},{17,25},{25,17},{2,10},{10... | collective-permute-start | bytes 196616 | tf_op jit(solution)/shard_map/ppermute | solution.py:818
  11.8 19.1 %collective-permute-start.9 = (bf16[256,128]{1,0:T(8,128)(2,1)}, bf16[256,128]{1,0:T(8,128)(2,1)S(1)}, u32[]{:S(2)}, u32[]{:S(2)}) collective-permute-start(bf16[256,128]{1,0:T(8,128)(2,1)} %param.17), channel_id=1, source_target_pairs={{0,24},{8,16},{16,8},{24,0},{1,25},{9,17},{17,9},{25,1},{2,26},{10... | collective-permute-start | bytes 196616 | tf_op jit(solution)/shard_map/ppermute | solution.py:818
  31.7 91.1 %all-gather.8.cloned.1.call-start = ((), (), s32[]{:S(2)}) async-start(), calls=%async_computation.3 | async-start | bytes 3170304 | tf_op jit(solution)/shard_map/all_gather | solution.py:986
  32.6 24.4 %copy-start.49 = (bf16[4,400,128]{2,1,0:T(8,128)(2,1)}, bf16[4,400,128]{2,1,0:T(8,128)(2,1)S(1)}, u32[]{:S(2)}) copy-start(bf16[4,400,128]{2,1,0:T(8,128)(2,1)S(1)} %get-tuple-element.316.refs_0_) | copy-start | bytes 1228804
  32.6 13.2 %collective-permute-start.4 = (bf16[4,400,128]{2,1,0:T(8,128)(2,1)S(1)}, bf16[4,400,128]{2,1,0:T(8,128)(2,1)S(1)}, u32[]{:S(2)}, u32[]{:S(2)}) collective-permute-start(bf16[4,400,128]{2,1,0:T(8,128)(2,1)S(1)} %get-tuple-element.316.refs_0_), channel_id=1, source_target_pairs={{0,24},{8,16},{16,8},{24,0},{1,25},{9,17},{17,9},{25,1},{2,26},{10... | collective-permute-start | bytes 1228808 | tf_op jit(solution)/shard_map/ppermute | solution.py:818
  35.0 18.9 %collective-permute-start.2 = (bf16[4,400,128]{2,1,0:T(8,128)(2,1)S(1)}, bf16[4,400,128]{2,1,0:T(8,128)(2,1)S(1)}, u32[]{:S(2)}, u32[]{:S(2)}) collective-permute-start(bf16[4,400,128]{2,1,0:T(8,128)(2,1)S(1)} %get-tuple-element.316.refs_0_), channel_id=1, source_target_pairs={{0,16},{8,24},{16,0},{24,8},{1,17},{9,25},{17,1},{25,9},{2,18},{10... | collective-permute-start | bytes 1228808 | tf_op jit(solution)/shard_map/ppermute | solution.py:818
  35.5 18.6 %collective-permute-start = (bf16[4,400,128]{2,1,0:T(8,128)(2,1)S(1)}, bf16[4,400,128]{2,1,0:T(8,128)(2,1)S(1)}, u32[]{:S(2)}, u32[]{:S(2)}) collective-permute-start(bf16[4,400,128]{2,1,0:T(8,128)(2,1)S(1)} %get-tuple-element.316.refs_0_), channel_id=1, source_target_pairs={{0,8},{8,0},{16,24},{24,16},{1,9},{9,1},{17,25},{25,17},{2,10},{10... | collective-permute-start | bytes 1228808 | tf_op jit(solution)/shard_map/ppermute | solution.py:818
  45.8 9.9 %collective-permute-start.5 = (bf16[4,400,128]{2,1,0:T(8,128)(2,1)S(1)}, bf16[4,400,128]{2,1,0:T(8,128)(2,1)S(1)}, u32[]{:S(2)}, u32[]{:S(2)}) collective-permute-start(bf16[4,400,128]{2,1,0:T(8,128)(2,1)S(1)} %collective-permute-done.4.refs_6_), channel_id=1, source_target_pairs={{0,1},{1,0},{2,3},{3,2},{4,5},{5,4},{6,7},{7,6},{8,9},{9,8},{10,11... | collective-permute-start | bytes 1228808 | tf_op jit(solution)/shard_map/ppermute | solution.py:933
  54.0 1.8 collective-permute-start.3
  54.1 2.2 collective-permute-start.1
  64.9 9.3 %collective-permute-start.6 = (bf16[9,176,128]{2,1,0:T(8,128)(2,1)}, bf16[9,176,128]{2,1,0:T(8,128)(2,1)S(1)}, u32[]{:S(2)}, u32[]{:S(2)}) collective-permute-start(bf16[9,176,128]{2,1,0:T(8,128)(2,1)} %get-tuple-element.118), channel_id=1, source_target_pairs={{0,1},{1,2},{2,3},{3,4},{4,5},{5,6},{6,7},{8,9},{9,10},{10,11},{11... | collective-permute-start | bytes 1216520 | tf_op jit(solution)/shard_map/ppermute | solution.py:852
  78.1 176.9 %reduce-scatter.2.cloned.1.call-start = ((), (), s32[]{:S(2)}) async-start(), calls=%async_computation.1 | async-start | bytes 4755456 | tf_op jit(solution)/shard_map/reduce_scatter | solution.py:1021
  78.1 7.4 %collective-permute-start.10 = (bf16[9,176,128]{2,1,0:T(8,128)(2,1)}, bf16[9,176,128]{2,1,0:T(8,128)(2,1)S(1)}, u32[]{:S(2)}, u32[]{:S(2)}) collective-permute-start(bf16[9,176,128]{2,1,0:T(8,128)(2,1)} %copy-done.57), channel_id=1, source_target_pairs={{0,1},{1,2},{2,3},{3,4},{4,5},{5,6},{6,7},{8,9},{9,10},{10,11},{11... | collective-permute-start | bytes 1216520 | tf_op jit(solution)/shard_map/ppermute | solution.py:852
  82.0 34.5 %collective-permute-start.19 = (bf16[256,1024]{1,0:T(8,128)(2,1)}, bf16[256,1024]{1,0:T(8,128)(2,1)S(1)}, u32[]{:S(2)}, u32[]{:S(2)}) collective-permute-start(bf16[256,1024]{1,0:T(8,128)(2,1)} %bitcast.96), channel_id=1, source_target_pairs={{0,24},{8,16},{16,8},{24,0},{1,25},{9,17},{17,9},{25,1},{2,26},{10... | collective-permute-start | bytes 1572872 | tf_op jit(solution)/shard_map/ppermute | solution.py:818
  83.6 33.6 %collective-permute-start.18 = (bf16[256,1024]{1,0:T(8,128)(2,1)}, bf16[256,1024]{1,0:T(8,128)(2,1)S(1)}, u32[]{:S(2)}, u32[]{:S(2)}) collective-permute-start(bf16[256,1024]{1,0:T(8,128)(2,1)} %bitcast.97), channel_id=1, source_target_pairs={{0,16},{8,24},{16,0},{24,8},{1,17},{9,25},{17,1},{25,9},{2,18},{10... | collective-permute-start | bytes 1572872 | tf_op jit(solution)/shard_map/ppermute | solution.py:818
  85.0 33.5 %collective-permute-start.17 = (bf16[256,1024]{1,0:T(8,128)(2,1)}, bf16[256,1024]{1,0:T(8,128)(2,1)S(1)}, u32[]{:S(2)}, u32[]{:S(2)}) collective-permute-start(bf16[256,1024]{1,0:T(8,128)(2,1)} %bitcast.98), channel_id=1, source_target_pairs={{0,8},{8,0},{16,24},{24,16},{1,9},{9,1},{17,25},{25,17},{2,10},{10... | collective-permute-start | bytes 1572872 | tf_op jit(solution)/shard_map/ppermute | solution.py:818
  92.1 26.4 %copy-start.6 = (bf16[1,256,1024]{2,1,0:T(8,128)(2,1)S(1)}, bf16[1,256,1024]{2,1,0:T(8,128)(2,1)}, u32[]{:S(2)}) copy-start(bf16[1,256,1024]{2,1,0:T(8,128)(2,1)} %param.23) | copy-start | bytes 1572868
  95.8 18.6 %collective-permute-start.11 = (bf16[128,1024]{1,0:T(8,128)(2,1)}, bf16[128,1024]{1,0:T(8,128)(2,1)S(1)}, u32[]{:S(2)}, u32[]{:S(2)}) collective-permute-start(bf16[128,1024]{1,0:T(8,128)(2,1)} %get-tuple-element.147.first_ref.refs_0_), channel_id=1, source_target_pairs={{0,8},{8,0},{16,24},{24,16},{1,9},{9,1},{17,25},{25,17},{2,10},{10... | collective-permute-start | bytes 786440 | tf_op jit(solution)/shard_map/ppermute | solution.py:841
  97.3 17.9 %collective-permute-start.14 = (bf16[128,1024]{1,0:T(8,128)(2,1)}, bf16[128,1024]{1,0:T(8,128)(2,1)S(1)}, u32[]{:S(2)}, u32[]{:S(2)}) collective-permute-start(bf16[128,1024]{1,0:T(8,128)(2,1)} %get-tuple-element.148.second_ref.refs_1_), channel_id=1, source_target_pairs={{0,16},{8,24},{16,0},{24,8},{1,17},{9,25},{17,1},{25,9},{2,18},{10... | collective-permute-start | bytes 786440 | tf_op jit(solution)/shard_map/ppermute | solution.py:841
  114.4 10.9 %collective-permute-start.15 = (bf16[128,1024]{1,0:T(8,128)(2,1)S(1)}, bf16[128,1024]{1,0:T(8,128)(2,1)}, u32[]{:S(2)}, u32[]{:S(2)}) collective-permute-start(bf16[128,1024]{1,0:T(8,128)(2,1)S(1)} %collective-permute-done.11.first_ref.refs_2_), channel_id=1, source_target_pairs={{0,16},{8,24},{16,0},{24,8},{1,17},{9,25},{17,1},{25,9},{2,18},{10... | collective-permute-start | bytes 786440 | tf_op jit(solution)/shard_map/ppermute | solution.py:841
  115.2 10.1 %collective-permute-start.16 = (bf16[128,1024]{1,0:T(8,128)(2,1)S(1)}, bf16[128,1024]{1,0:T(8,128)(2,1)}, u32[]{:S(2)}, u32[]{:S(2)}) collective-permute-start(bf16[128,1024]{1,0:T(8,128)(2,1)S(1)} %collective-permute-done.14.second_ref.refs_5_), channel_id=1, source_target_pairs={{0,8},{8,0},{16,24},{24,16},{1,9},{9,1},{17,25},{25,17},{2,10},{10... | collective-permute-start | bytes 786440 | tf_op jit(solution)/shard_map/ppermute | solution.py:841
  116.5 12.8 %collective-permute-start.13 = (bf16[128,1024]{1,0:T(8,128)(2,1)}, bf16[128,1024]{1,0:T(8,128)(2,1)}, u32[]{:S(2)}, u32[]{:S(2)}) collective-permute-start(bf16[128,1024]{1,0:T(8,128)(2,1)} %get-tuple-element.147.first_ref.refs_0_), channel_id=1, source_target_pairs={{0,16},{8,24},{16,0},{24,8},{1,17},{9,25},{17,1},{25,9},{2,18},{10... | collective-permute-start | bytes 786440 | tf_op jit(solution)/shard_map/ppermute | solution.py:841
  117.2 17.4 %collective-permute-start.12 = (bf16[128,1024]{1,0:T(8,128)(2,1)}, bf16[128,1024]{1,0:T(8,128)(2,1)}, u32[]{:S(2)}, u32[]{:S(2)}) collective-permute-start(bf16[128,1024]{1,0:T(8,128)(2,1)} %get-tuple-element.148.second_ref.refs_1_), channel_id=1, source_target_pairs={{0,8},{8,0},{16,24},{24,16},{1,9},{9,1},{17,25},{25,17},{2,10},{10... | collective-permute-start | bytes 786440 | tf_op jit(solution)/shard_map/ppermute | solution.py:841
  129.3 28.3 %collective-permute-start.22 = (bf16[256,1024]{1,0:T(8,128)(2,1)}, bf16[256,1024]{1,0:T(8,128)(2,1)}, u32[]{:S(2)}, u32[]{:S(2)}) collective-permute-start(bf16[256,1024]{1,0:T(8,128)(2,1)} %get-tuple-element.152), channel_id=1, source_target_pairs={{0,24},{8,16},{16,8},{24,0},{1,25},{9,17},{17,9},{25,1},{2,26},{10... | collective-permute-start | bytes 1572872 | tf_op jit(solution)/shard_map/ppermute | solution.py:818
  134.6 22.9 %collective-permute-start.21 = (bf16[256,1024]{1,0:T(8,128)(2,1)}, bf16[256,1024]{1,0:T(8,128)(2,1)}, u32[]{:S(2)}, u32[]{:S(2)}) collective-permute-start(bf16[256,1024]{1,0:T(8,128)(2,1)} %get-tuple-element.151), channel_id=1, source_target_pairs={{0,16},{8,24},{16,0},{24,8},{1,17},{9,25},{17,1},{25,9},{2,18},{10... | collective-permute-start | bytes 1572872 | tf_op jit(solution)/shard_map/ppermute | solution.py:818
  139.2 18.4 %collective-permute-start.20 = (bf16[256,1024]{1,0:T(8,128)(2,1)}, bf16[256,1024]{1,0:T(8,128)(2,1)}, u32[]{:S(2)}, u32[]{:S(2)}) collective-permute-start(bf16[256,1024]{1,0:T(8,128)(2,1)} %get-tuple-element.150), channel_id=1, source_target_pairs={{0,8},{8,0},{16,24},{24,16},{1,9},{9,1},{17,25},{25,17},{2,10},{10... | collective-permute-start | bytes 1572872 | tf_op jit(solution)/shard_map/ppermute | solution.py:818
  165.5 5.2 %collective-permute-start.27 = (bf16[4,4,256,128]{3,2,1,0:T(8,128)(2,1)S(1)}, bf16[4,4,256,128]{3,2,1,0:T(8,128)(2,1)S(1)}, u32[]{:S(2)}, u32[]{:S(2)}) collective-permute-start(bf16[4,4,256,128]{3,2,1,0:T(8,128)(2,1)S(1)} %get-tuple-element.189), channel_id=1, source_target_pairs={{0,1},{1,0},{2,3},{3,2},{4,5},{5,4},{6,7},{7,6},{8,9},{9,8},{10,11... | collective-permute-start | bytes 3145736 | tf_op jit(solution)/shard_map/ppermute | solution.py:1016
  169.2 10.6 %collective-permute-start.25 = (bf16[9,176,128]{2,1,0:T(8,128)(2,1)S(1)}, bf16[9,176,128]{2,1,0:T(8,128)(2,1)S(1)}, u32[]{:S(2)}, u32[]{:S(2)}) collective-permute-start(bf16[9,176,128]{2,1,0:T(8,128)(2,1)S(1)} %get-tuple-element.184), channel_id=1, source_target_pairs={{1,0},{2,1},{3,2},{4,3},{5,4},{6,5},{7,6},{9,8},{10,9},{11,10},{12... | collective-permute-start | bytes 1216520 | tf_op jit(solution)/shard_map/ppermute | solution.py:852
  170.9 10.3 %collective-permute-start.28 = (bf16[4,256,128]{2,1,0:T(8,128)(2,1)S(1)}, bf16[4,256,128]{2,1,0:T(8,128)(2,1)S(1)}, u32[]{:S(2)}, u32[]{:S(2)}) collective-permute-start(bf16[4,256,128]{2,1,0:T(8,128)(2,1)S(1)} %get-tuple-element.309), channel_id=1, source_target_pairs={{0,8},{8,0},{16,24},{24,16},{1,9},{9,1},{17,25},{25,17},{2,10},{10... | collective-permute-start | bytes 786440 | tf_op jit(solution)/shard_map/ppermute | solution.py:818
  171.7 14.2 %collective-permute-start.30 = (bf16[4,256,128]{2,1,0:T(8,128)(2,1)S(1)}, bf16[4,256,128]{2,1,0:T(8,128)(2,1)S(1)}, u32[]{:S(2)}, u32[]{:S(2)}) collective-permute-start(bf16[4,256,128]{2,1,0:T(8,128)(2,1)S(1)} %get-tuple-element.310), channel_id=1, source_target_pairs={{0,24},{8,16},{16,8},{24,0},{1,25},{9,17},{17,9},{25,1},{2,26},{10... | collective-permute-start | bytes 786440 | tf_op jit(solution)/shard_map/ppermute | solution.py:818
  173.2 14.4 %collective-permute-start.29 = (bf16[4,256,128]{2,1,0:T(8,128)(2,1)S(1)}, bf16[4,256,128]{2,1,0:T(8,128)(2,1)S(1)}, u32[]{:S(2)}, u32[]{:S(2)}) collective-permute-start(bf16[4,256,128]{2,1,0:T(8,128)(2,1)S(1)} %get-tuple-element.311), channel_id=1, source_target_pairs={{0,16},{8,24},{16,0},{24,8},{1,17},{9,25},{17,1},{25,9},{2,18},{10... | collective-permute-start | bytes 786440 | tf_op jit(solution)/shard_map/ppermute | solution.py:818
  179.9 8.0 %collective-permute-start.26 = (bf16[9,176,128]{2,1,0:T(8,128)(2,1)S(1)}, bf16[9,176,128]{2,1,0:T(8,128)(2,1)S(1)}, u32[]{:S(2)}, u32[]{:S(2)}) collective-permute-start(bf16[9,176,128]{2,1,0:T(8,128)(2,1)S(1)} %collective-permute-done.25.one_ref), channel_id=1, source_target_pairs={{1,0},{2,1},{3,2},{4,3},{5,4},{6,5},{7,6},{9,8},{10,9},{11,10},{12... | collective-permute-start | bytes 1216520 | tf_op jit(solution)/shard_map/ppermute | solution.py:852
  189.0 13.9 %collective-permute-start.23 = (bf16[256,1024]{1,0:T(8,128)(2,1)S(1)}, bf16[256,1024]{1,0:T(8,128)(2,1)S(1)}, u32[]{:S(2)}, u32[]{:S(2)}) collective-permute-start(bf16[256,1024]{1,0:T(8,128)(2,1)S(1)} %copy-done.48), channel_id=1, source_target_pairs={{0,8},{8,0},{16,24},{24,16},{1,9},{9,1},{17,25},{25,17},{2,10},{10... | collective-permute-start | bytes 1572872 | tf_op jit(solution)/shard_map/ppermute | solution.py:1025
  190.3 14.6 %collective-permute-start.24 = (bf16[256,1024]{1,0:T(8,128)(2,1)S(1)}, bf16[256,1024]{1,0:T(8,128)(2,1)S(1)}, u32[]{:S(2)}, u32[]{:S(2)}) collective-permute-start(bf16[256,1024]{1,0:T(8,128)(2,1)S(1)} %copy-done.46), channel_id=1, source_target_pairs={{0,16},{8,24},{16,0},{24,8},{1,17},{9,25},{17,1},{25,9},{2,18},{10... | collective-permute-start | bytes 1572872 | tf_op jit(solution)/shard_map/ppermute | solution.py:1025
  204.9 3.7 %collective-permute-start.32 = (bf16[4,4,400,128]{3,2,1,0:T(8,128)(2,1)}, bf16[4,4,400,128]{3,2,1,0:T(8,128)(2,1)S(1)}, u32[]{:S(2)}, u32[]{:S(2)}) collective-permute-start(bf16[4,4,400,128]{3,2,1,0:T(8,128)(2,1)} %get-tuple-element.202), channel_id=1, source_target_pairs={{0,1},{1,0},{2,3},{3,2},{4,5},{5,4},{6,7},{7,6},{8,9},{9,8},{10,11... | collective-permute-start | bytes 4915208 | tf_op jit(solution)/shard_map/ppermute | solution.py:1016
  205.3 15.8 %collective-permute-start.31 = (bf16[256,1024]{1,0:T(8,128)(2,1)S(1)}, bf16[256,1024]{1,0:T(8,128)(2,1)}, u32[]{:S(2)}, u32[]{:S(2)}) collective-permute-start(bf16[256,1024]{1,0:T(8,128)(2,1)S(1)} %copy-done.44), channel_id=1, source_target_pairs={{0,24},{8,16},{16,8},{24,0},{1,25},{9,17},{17,9},{25,1},{2,26},{10... | collective-permute-start | bytes 1572872 | tf_op jit(solution)/shard_map/ppermute | solution.py:1028
  210.2 18.9 %collective-permute-start.33 = (bf16[4,400,128]{2,1,0:T(8,128)(2,1)S(1)}, bf16[4,400,128]{2,1,0:T(8,128)(2,1)S(1)}, u32[]{:S(2)}, u32[]{:S(2)}) collective-permute-start(bf16[4,400,128]{2,1,0:T(8,128)(2,1)S(1)} %get-tuple-element.306), channel_id=1, source_target_pairs={{0,8},{8,0},{16,24},{24,16},{1,9},{9,1},{17,25},{25,17},{2,10},{10... | collective-permute-start | bytes 1228808 | tf_op jit(solution)/shard_map/ppermute | solution.py:818
  211.1 26.6 %collective-permute-start.35 = (bf16[4,400,128]{2,1,0:T(8,128)(2,1)S(1)}, bf16[4,400,128]{2,1,0:T(8,128)(2,1)S(1)}, u32[]{:S(2)}, u32[]{:S(2)}) collective-permute-start(bf16[4,400,128]{2,1,0:T(8,128)(2,1)S(1)} %get-tuple-element.307), channel_id=1, source_target_pairs={{0,24},{8,16},{16,8},{24,0},{1,25},{9,17},{17,9},{25,1},{2,26},{10... | collective-permute-start | bytes 1228808 | tf_op jit(solution)/shard_map/ppermute | solution.py:818
  212.5 25.2 %collective-permute-start.34 = (bf16[4,400,128]{2,1,0:T(8,128)(2,1)S(1)}, bf16[4,400,128]{2,1,0:T(8,128)(2,1)S(1)}, u32[]{:S(2)}, u32[]{:S(2)}) collective-permute-start(bf16[4,400,128]{2,1,0:T(8,128)(2,1)S(1)} %get-tuple-element.308), channel_id=1, source_target_pairs={{0,16},{8,24},{16,0},{24,8},{1,17},{9,25},{17,1},{25,9},{2,18},{10... | collective-permute-start | bytes 1228808 | tf_op jit(solution)/shard_map/ppermute | solution.py:818
  213.8 29.5 %collective-permute-start.39 = (bf16[256,128]{1,0:T(8,128)(2,1)S(1)}, bf16[256,128]{1,0:T(8,128)(2,1)S(1)}, u32[]{:S(2)}, u32[]{:S(2)}) collective-permute-start(bf16[256,128]{1,0:T(8,128)(2,1)S(1)} %get-tuple-element.320), channel_id=1, source_target_pairs={{0,2},{1,3},{2,0},{3,1},{4,6},{5,7},{6,4},{7,5},{8,10},{9,11},{10,... | collective-permute-start | bytes 196616 | tf_op jit(solution)/shard_map/ppermute | solution.py:858
  221.1 22.2 %collective-permute-start.41 = (bf16[256,128]{1,0:T(8,128)(2,1)S(1)}, bf16[256,128]{1,0:T(8,128)(2,1)S(1)}, u32[]{:S(2)}, u32[]{:S(2)}) collective-permute-start(bf16[256,128]{1,0:T(8,128)(2,1)S(1)} %get-tuple-element.321), channel_id=1, source_target_pairs={{0,6},{1,7},{2,4},{3,5},{4,2},{5,3},{6,0},{7,1},{8,14},{9,15},{10,... | collective-permute-start | bytes 196616 | tf_op jit(solution)/shard_map/ppermute | solution.py:858
  229.1 14.2 %collective-permute-start.40 = (bf16[256,128]{1,0:T(8,128)(2,1)S(1)}, bf16[256,128]{1,0:T(8,128)(2,1)S(1)}, u32[]{:S(2)}, u32[]{:S(2)}) collective-permute-start(bf16[256,128]{1,0:T(8,128)(2,1)S(1)} %get-tuple-element.322), channel_id=1, source_target_pairs={{0,4},{1,5},{2,6},{3,7},{4,0},{5,1},{6,2},{7,3},{8,12},{9,13},{10,... | collective-permute-start | bytes 196616 | tf_op jit(solution)/shard_map/ppermute | solution.py:858
  239.0 5.2 %collective-permute-start.36 = (bf16[400,128]{1,0:T(8,128)(2,1)S(1)}, bf16[400,128]{1,0:T(8,128)(2,1)S(1)}, u32[]{:S(2)}, u32[]{:S(2)}) collective-permute-start(bf16[400,128]{1,0:T(8,128)(2,1)S(1)} %get-tuple-element.317), channel_id=1, source_target_pairs={{0,2},{1,3},{2,0},{3,1},{4,6},{5,7},{6,4},{7,5},{8,10},{9,11},{10,... | collective-permute-start | bytes 307208 | tf_op jit(solution)/shard_map/ppermute | solution.py:858
  240.4 8.4 %collective-permute-start.38 = (bf16[400,128]{1,0:T(8,128)(2,1)S(1)}, bf16[400,128]{1,0:T(8,128)(2,1)S(1)}, u32[]{:S(2)}, u32[]{:S(2)}) collective-permute-start(bf16[400,128]{1,0:T(8,128)(2,1)S(1)} %get-tuple-element.318), channel_id=1, source_target_pairs={{0,6},{1,7},{2,4},{3,5},{4,2},{5,3},{6,0},{7,1},{8,14},{9,15},{10,... | collective-permute-start | bytes 307208 | tf_op jit(solution)/shard_map/ppermute | solution.py:858
  243.3 9.6 %collective-permute-start.37 = (bf16[400,128]{1,0:T(8,128)(2,1)S(1)}, bf16[400,128]{1,0:T(8,128)(2,1)S(1)}, u32[]{:S(2)}, u32[]{:S(2)}) collective-permute-start(bf16[400,128]{1,0:T(8,128)(2,1)S(1)} %get-tuple-element.319), channel_id=1, source_target_pairs={{0,4},{1,5},{2,6},{3,7},{4,0},{5,1},{6,2},{7,3},{8,12},{9,13},{10,... | collective-permute-start | bytes 307208 | tf_op jit(solution)/shard_map/ppermute | solution.py:858
  (59 other events, 263.8 us)
Sparse Core Ops, SparseCore 0:
  31.8 42.4 all-gather.5
  78.2 37.2 all-gather.7
  188.0 56.1 reduce-scatter.1

commit v4 on v3

--- a/solution.py
+++ b/solution.py
@@ -911,9 +911,8 @@
     )
     out_slices = swap([out_weight] * n)
     pack = lax.all_gather(pack, "seq")
-    down_late, pack = lax.optimization_barrier((down_weight, pack))
-    second = lax.all_gather(jnp.concatenate([*out_slices, down_late], axis=0), "seq")
-
+    near_cots = [lax.ppermute(cot, "head", xor_pairs(n, r)) for r in range(1, n - 1)]
+    near_cots, pack = lax.optimization_barrier((near_cots, pack))
     def gathered(w):
         return w if nb == blocks else jnp.transpose(w, (1, 0, 2)).reshape(1, w.shape[1], d)
 
@@ -928,7 +927,38 @@
     half = blocks // 2
     mine = lax.dynamic_slice_in_dim(pack, core[0] * half, half)
     other = lax.dynamic_slice_in_dim(pack, (1 - core[0]) * half, half)
+    down_late, mine = lax.optimization_barrier((down_weight, mine))
+    second = lax.all_gather(jnp.concatenate([*out_slices, down_late], axis=0), "seq")
+
+    docs = pack[:, nqkv + 2 : nqkv + 2 + doc_rows].reshape(blocks, rows).astype(F32)
+    segs = jnp.take(docs, me, axis=0)
+    lasts = docs[:, -1]
+    before = jnp.where(me > 0, jnp.take(lasts, jnp.maximum(me - 1, 0)), -1.0)
+    final_label = jnp.take(lasts, me)
+    labels_back = jnp.concatenate([jnp.full((1,), -1.0), lasts[:-1]])
+
+    def flag_of(labels, step):
+        reach = max(blocks // 4, 1)
+        k = 1
+        while 2 * k < reach:
+            k *= 2
+        near = jnp.take(labels, jnp.clip(me - step, 0, blocks - 1))
+        far = jnp.take(labels, jnp.clip(me - step * (1 + k), 0, blocks - 1))
+        return (near == far).astype(F32)
+
+    masks = jnp.stack(
+        [
+            segs,
+            (segs == final_label).astype(F32),
+            (segs == before).astype(F32),
+            jnp.full((rows,), 1.0) * flag_of(lasts, 1),
+            jnp.full((rows,), 1.0) * flag_of(labels_back, -1),
+        ]
+        + [jnp.zeros_like(segs)] * 3
+    )
+
     mine = swap([mine] * n)
+    mine[1], masks = lax.optimization_barrier((mine[1], masks))
     pairs = [[mine[0], other]]
     pairs += [[one, lax.ppermute(one, "seq", xor_pairs(blocks, 1))] for one in mine[1:]]
     if nb == blocks:
@@ -938,9 +968,6 @@
         small = jnp.take(jnp.take(small, here ^ jnp.arange(n), axis=0), core[0] ^ jnp.arange(2), axis=1)
         gain_in = jnp.transpose(small.reshape(n, blocks, 2, piece), (2, 0, 1, 3)).reshape(2, d)
         gain_in = jnp.pad(gain_in.astype(F32), ((0, 6), (0, 0)))
-    docs = pack[:, nqkv + 2 : nqkv + 2 + doc_rows].reshape(blocks, rows).astype(F32)
-    segs = jnp.take(docs, me, axis=0)
-    lasts = docs[:, -1]
     if nb != blocks:
         pairs = [
             [gathered(jnp.where(core[0] == 0, jnp.concatenate(p), jnp.concatenate(p[::-1])))] for p in pairs
@@ -948,37 +975,13 @@
     cot_late, pairs[1:] = lax.optimization_barrier((cot, pairs[1:]))
     wide = call(pack_two_body, sds((2 * ff, wb), BF16), (gate_weight.T, up_weight.T), us=2)
 
-    before = jnp.where(me > 0, jnp.take(lasts, jnp.maximum(me - 1, 0)), -1.0)
-    final_label = jnp.take(lasts, me)
-    labels_back = jnp.concatenate([jnp.full((1,), -1.0), lasts[:-1]])
-
     def join(a, b, flag):
         return (a.astype(F32) + b.astype(F32) * flag).astype(BF16)
 
-    def flag_of(labels, step):
-        reach = max(blocks // 4, 1)
-        k = 1
-        while 2 * k < reach:
-            k *= 2
-        near = jnp.take(labels, jnp.clip(me - step, 0, blocks - 1))
-        far = jnp.take(labels, jnp.clip(me - step * (1 + k), 0, blocks - 1))
-        return (near == far).astype(F32)
-
-    masks = jnp.stack(
-        [
-            segs,
-            (segs == final_label).astype(F32),
-            (segs == before).astype(F32),
-            jnp.full((rows,), 1.0) * flag_of(lasts, 1),
-            jnp.full((rows,), 1.0) * flag_of(labels_back, -1),
-        ]
-        + [jnp.zeros_like(segs)] * 3
-    )
-
     h1, qk, v, sums, w_qkv, gains = project(
         where, x, gain_in, masks, pairs, heads, piece if nb == blocks else 0
     )
-    cots = swap([cot_late] * n)
+    cots = [cot, *near_cots, lax.ppermute(cot_late, "head", xor_pairs(n, n - 1))]
     nd = local(qk, v, masks)
     one, two = carried(sums, lasts, 1, join, nd)
     w_out, w_down = spread_out(gathered(second), ff)

time: 265 us -> 260 us (0.981)
    ppermute x6, waiting for transfers between devices: 16.5 us -> 5.44 us  [send(): return lax.ppermute(x, 'head', xor_pairs(size, r))]
    all_gather x1, waiting for transfers between devices: 0.01 us -> 7.4 us  [on_device(): w_mlp = widen(gathered(lax.all_gather(wide, 'seq')))]
    ppermute x0 -> x3, starting transfers between devices: none -> 5.06 us  [the longest x2 3.44 us: on_device(): lax.ppermute(cot, 'head', xor_pairs(n, r))]
    ppermute x18 -> x15, starting transfers between devices: 22.2 us -> 18.7 us  [swap(): lax.ppermute(parts[r], 'head', xor_pairs(size, r))]
    ppermute x18 -> x15, waiting for transfers between devices: 30.8 us -> 30.7 us  [swap(): lax.ppermute(parts[r], 'head', xor_pairs(size, r))]
  transfers between devices with their start and end apart: 45 -> 45, of which waited for: 16 -> 19; matrix products, arithmetic and copies ran while one was open for 5% -> 5% of each run, Pallas kernels for 25% -> 25%
where the time goes in v4:
time: 260 us; the launch traced here: 259 us
  Pallas kernels  70.3 us (27%)
  waiting for transfers between devices  66.9 us (26%)
  starting transfers between devices  47 us (18%)
  local copies, waits for them, and re-layouts  31.1 us (12%)
  between operations  18.5 us (7%)
  blocking collectives  16.6 us (6%)
  other arithmetic  8.1 us (3%)
    pallas_call x20, Pallas kernels, call(): pl.pallas_call(body, out_shape=outs, scratch_shapes=list(scratch), compil...  70.3 us
    ppermute x15, waiting for transfers between devices, swap(): lax.ppermute(parts[r], 'head', xor_pairs(size, r))  30.7 us
    unnamed x130, local copies, waits for them, and re-layouts  25.3 us
    ppermute x15, starting transfers between devices, swap(): lax.ppermute(parts[r], 'head', xor_pairs(size, r))  18.7 us
    all_gather x1, blocking collectives, on_device(): pack = lax.all_gather(pack, 'seq')  16.6 us
    ppermute x6, waiting for transfers between devices, over_z(): lax.ppermute(x[k], 'seq', xor_pairs(size, 2 * k))  8.17 us
    ppermute x4, starting transfers between devices, shifted(): lax.ppermute(x, 'seq', [(i, i + step) for i in range(size) if 0 <= i + st...  8.07 us
    all_gather x1, waiting for transfers between devices, on_device(): w_mlp = widen(gathered(lax.all_gather(wide, 'seq')))  7.4 us
  transfers between devices with their start and end apart: 45, of which 19 were waited for; matrix products, arithmetic and copies ran while one was open for 5% of the time, Pallas kernels for 25%

profile of v4, /device:TPU:0, one launch (start us, length us, event | category | flops | bytes accessed | tf_op | source)
XLA Modules:
  0.0 258.5 jit_solution(15368841664479936482)
XLA Ops:
  7.2 3.0 %collective-permute-start.10 = (bf16[256,128]{1,0:T(8,128)(2,1)}, bf16[256,128]{1,0:T(8,128)(2,1)S(1)}, u32[]{:S(2)}, u32[]{:S(2)}) collective-permute-start(bf16[256,128]{1,0:T(8,128)(2,1)} %param.17), channel_id=1, source_target_pairs={{0,16},{8,24},{16,0},{24,8},{1,17},{9,25},{17,1},{25,9},{2,18},{10... | collective-permute-start | bytes 196616 | tf_op jit(solution)/shard_map/ppermute | solution.py:818
  11.8 1.9 collective-permute-start.1
  15.2 1.6 shard_map.203
  16.9 16.6 %all-gather = bf16[3200,128]{1,0:T(8,128)(2,1)S(1)} all-gather(bf16[400,128]{1,0:T(8,128)(2,1)} %shard_map.203), channel_id=2, replica_groups=mesh['head'=4,'seq'=8] {'seq'}, dimensions={0}, use_global_device_ids=true | all-gather | bytes 921600 | tf_op jit(solution)/shard_map/all_gather | solution.py:913
  36.8 1.5 collective-permute-start.4
  45.9 10.9 %collective-permute-done.2.refs_2_ = bf16[4,400,128]{2,1,0:T(8,128)(2,1)S(1)} collective-permute-done((bf16[4,400,128]{2,1,0:T(8,128)(2,1)S(1)}, bf16[4,400,128]{2,1,0:T(8,128)(2,1)S(1)}, u32[]{:S(2)}, u32[]{:S(2)}) %collective-permute-start.2) | collective-permute-done | bytes 409632 | tf_op jit(solution)/shard_map/ppermute | solution.py:818
  60.6 7.9 %shard_map.204 = (bf16[256,1024]{1,0:T(8,128)(2,1)}, bf16[4,128,256]{2,1,0:T(8,128)(2,1)}, bf16[4,256,256]{2,1,0:T(8,128)(2,1)}, bf16[9,176,128]{2,1,0:T(8,128)(...) custom-call(s32[6]{0:T(128)} %pad_add_fusion.where_ref, bf16[256,1024]{1,0:T(8,128)(2,1)} %bitcast.102, ...), custom_call_target="tpu_custom_call" | custom-call | bytes 4200000 | tf_op jit(solution)/shard_map/pallas_call | solution.py:38
  68.5 2.1 collective-permute-start.8
  73.4 3.2 %shard_map.205.nd_ref = f32[4,2,256,256]{3,2,1,0:T(8,128)S(1)} custom-call(bf16[4,128,256]{2,1,0:T(8,128)(2,1)S(1)} %copy-done.4, bf16[4,256,256]{2,1,0:T(8,128)(2,1)S(1)} %copy-done.9, f32[8,256]{1,0:T(8,128)S(1)} %copy-done.36), custom_call_target="tpu_custom_call" | custom-call | bytes 3000000 | tf_op jit(solution)/shard_map/pallas_call | solution.py:38
  78.7 2.0 copy-done.14
  81.8 3.2 %collective-permute-start.12 = (bf16[9,176,128]{2,1,0:T(8,128)(2,1)}, bf16[9,176,128]{2,1,0:T(8,128)(2,1)S(1)}, u32[]{:S(2)}, u32[]{:S(2)}) collective-permute-start(bf16[9,176,128]{2,1,0:T(8,128)(2,1)} %copy-done.57), channel_id=1, source_target_pairs={{0,1},{1,2},{2,3},{3,4},{4,5},{5,6},{6,7},{8,9},{9,10},{10,11},{11... | collective-permute-start | bytes 1216520 | tf_op jit(solution)/shard_map/ppermute | solution.py:852
  85.0 1.6 collective-permute-start.19
  87.4 5.7 %shard_map.208 = (bf16[4,256,256]{2,1,0:T(8,128)(2,1)}, f32[4,256,256]{2,1,0:T(8,128)}, f32[4,256,256]{2,1,0:T(8,128)}, bf16[9,176,128]{2,1,0:T(8,128)(2,1)}) custom-call(f32[4,2,256,256]{3,2,1,0:T(8,128)} %copy-done.1, bf16[4,128,256]{2,1,0:T(8,128)(2,1)} %get-tuple-element.124.qk_ref, f32[8,256]{1,0:T(8,128)} %stack.18.masks_ref, ...), custom_call_target="tpu_custom_call" | custom-call | bytes 3000000 | tf_op jit(solution)/shard_map/pallas_call | solution.py:38
  94.3 1.6 shard_map.209
  98.9 4.6 %collective-permute-done.13.first_ref.refs_2_ = bf16[128,1024]{1,0:T(8,128)(2,1)S(1)} collective-permute-done((bf16[128,1024]{1,0:T(8,128)(2,1)}, bf16[128,1024]{1,0:T(8,128)(2,1)S(1)}, u32[]{:S(2)}, u32[]{:S(2)}) %collective-permute-start.13) | collective-permute-done | bytes 262176 | tf_op jit(solution)/shard_map/ppermute | solution.py:841
  105.9 1.6 collective-permute-start.15
  107.8 1.8 shard_map.210.dhid_ref
  110.4 7.4 %all-gather.8.cloned.1.call-done = bf16[11008,128]{1,0:T(8,128)(2,1)} async-done(((bf16[1376,128]{1,0:T(8,128)(2,1)}), bf16[11008,128]{1,0:T(8,128)(2,1)}) %all-gather.8.cloned.1.call-update) | async-done | bytes 2818064 | tf_op jit(solution)/shard_map/all_gather | solution.py:989
  117.8 1.8 copy-done.15
  120.4 3.9 %shard_map.212 = (bf16[256,1024]{1,0:T(8,128)(2,1)}, bf16[256,688]{1,0:T(8,128)(2,1)S(1)}, bf16[256,688]{1,0:T(8,128)(2,1)S(1)}, bf16[256,688]{1,0:T(8,128)(2,1)S(1)}) custom-call(bf16[128,1024]{1,0:T(8,128)(2,1)} %collective-permute-done.17.first_ref.refs_6_, bf16[128,1024]{1,0:T(8,128)(2,1)} %collective-permute-done.18.second_ref.refs_7_, ...), custom_call_target="tpu_custom_call" | custom-call | bytes 3000000 | tf_op jit(solution)/shard_map/pallas_call | solution.py:38
  124.4 2.4 collective-permute-start.22
  126.7 3.8 %shard_map.213 = (bf16[256,1024]{1,0:T(8,128)(2,1)}, bf16[256,688]{1,0:T(8,128)(2,1)S(1)}, bf16[256,688]{1,0:T(8,128)(2,1)S(1)}, bf16[256,688]{1,0:T(8,128)(2,1)S(1)}) custom-call(bf16[128,1024]{1,0:T(8,128)(2,1)} %collective-permute-done.15.first_ref.refs_4_, bf16[128,1024]{1,0:T(8,128)(2,1)S(1)} %collective-permute-done.16.second_ref.refs_5_, ...), custom_call_target="tpu_custom_call" | custom-call | bytes 3000000 | tf_op jit(solution)/shard_map/pallas_call | solution.py:38
  131.1 3.8 %shard_map.214 = (bf16[256,1024]{1,0:T(8,128)(2,1)}, bf16[256,688]{1,0:T(8,128)(2,1)S(1)}, bf16[256,688]{1,0:T(8,128)(2,1)S(1)}, bf16[256,688]{1,0:T(8,128)(2,1)S(1)}) custom-call(bf16[128,1024]{1,0:T(8,128)(2,1)S(1)} %collective-permute-done.13.first_ref.refs_2_, bf16[128,1024]{1,0:T(8,128)(2,1)} %collective-permute-done.14.second_ref.refs_3_, ...), custom_call_target="tpu_custom_call" | custom-call | bytes 3000000 | tf_op jit(solution)/shard_map/pallas_call | solution.py:38
  135.5 3.1 %shard_map.215 = (bf16[256,1024]{1,0:T(8,128)(2,1)S(1)}, bf16[256,688]{1,0:T(8,128)(2,1)S(1)}, bf16[256,688]{1,0:T(8,128)(2,1)S(1)}, bf16[256,688]{1,0:T(8,128)(2,1)S(1)}) custom-call(bf16[128,1024]{1,0:T(8,128)(2,1)} %get-tuple-element.157.first_ref.refs_0_, bf16[128,1024]{1,0:T(8,128)(2,1)} %get-tuple-element.158.second_ref.refs_1_, ...), custom_call_target="tpu_custom_call" | custom-call | bytes 3000000 | tf_op jit(solution)/shard_map/pallas_call | solution.py:38
  139.5 1.8 shard_map.216
  144.6 6.3 %shard_map.217 = bf16[8,2064,128]{2,1,0:T(8,128)(2,1)S(1)} custom-call(bf16[128,1024]{1,0:T(8,128)(2,1)} %get-tuple-element.157.first_ref.refs_0_, bf16[128,1024]{1,0:T(8,128)(2,1)} %get-tuple-element.158.second_ref.refs_1_, bf16[128,1024]{1,0:T(8,128)(2,1)S(1)} %collective-permute-done.13.first_ref.refs_2_, ...), custom_call_target="tpu_custom_call" | custom-call | bytes 5400000 | tf_op jit(solution)/shard_map/pallas_call | solution.py:38
  150.9 1.9 copy-done
  155.2 2.8 %shard_map.218 = (f32[256,1024]{1,0:T(8,128)S(1)}, f32[1,1024]{1,0:T(1,128)S(1)}, bf16[256,1024]{1,0:T(8,128)(2,1)S(1)}, bf16[4,256,256]{2,1,0:T(8,128)(2,1)S(1)}) custom-call(f32[256,1024]{1,0:T(8,128)S(1)} %copy-done.12, bf16[256,1024]{1,0:T(8,128)(2,1)S(1)} %bitcast.101, f32[8,1024]{1,0:T(8,128)S(1)} %copy-done.38, bf16[256,1024]{1,0:T(8,128)(2,1)S(1)} %copy-done.34, ...), custom_call_target="tpu_custom_call" | custom-call | bytes 3000000 | tf_op jit(solution)/shard_map/pallas_call | solution.py:38
  159.0 1.7 shard_map.221
  160.9 3.6 %shard_map.219 = (bf16[4,4,256,128]{3,2,1,0:T(8,128)(2,1)S(1)}, bf16[9,176,128]{2,1,0:T(8,128)(2,1)S(1)}) custom-call(bf16[4,256,256]{2,1,0:T(8,128)(2,1)S(1)} %get-tuple-element.186.do_ref, f32[4,256,256]{2,1,0:T(8,128)S(1)} %copy-done.27, f32[4,256,256]{2,1,0:T(8,128)S(1)} %copy-done.28, bf16[4,128,256]{2,1,0:T(8,128)(2,1)S(1)} %copy-done.5, ...), custom_call_target="tpu_custom_call" | custom-call | bytes 3000000 | tf_op jit(solution)/shard_map/pallas_call | solution.py:38
  166.2 1.5 collective-permute-start.28
  169.7 5.3 %shard_map.220 = (bf16[4,64,256]{2,1,0:T(8,128)(2,1)S(1)}, f32[4,64,256]{2,1,0:T(8,128)S(1)}, f32[4,256,256]{2,1,0:T(8,128)S(1)}) custom-call(bf16[4,4,256,128]{3,2,1,0:T(8,128)(2,1)S(1)} %get-tuple-element.189.d_ref, bf16[4,128,256]{2,1,0:T(8,128)(2,1)S(1)} %copy-done.5, bf16[4,256,256]{2,1,0:T(8,128)(2,1)S(1)} %copy-done.10, f32[8,256]{1,0:T(8,128)S(1)} %copy-done.37, ...), custom_call_target="tpu_custom_call" | custom-call | bytes 3000000 | tf_op jit(solution)/shard_map/pallas_call | solution.py:38
  176.4 5.5 %collective-permute-done.30 = bf16[4,256,128]{2,1,0:T(8,128)(2,1)S(1)} collective-permute-done((bf16[4,256,128]{2,1,0:T(8,128)(2,1)S(1)}, bf16[4,256,128]{2,1,0:T(8,128)(2,1)S(1)}, u32[]{:S(2)}, u32[]{:S(2)}) %collective-permute-start.30) | collective-permute-done | bytes 262176 | tf_op jit(solution)/shard_map/ppermute | solution.py:818
  181.9 1.7 collective-permute-done.29
  187.0 10.4 %shard_map.222 = (f32[256,1024]{1,0:T(8,128)}, bf16[4,4,400,128]{3,2,1,0:T(8,128)(2,1)}, bf16[4,4,400,128]{3,2,1,0:T(8,128)(2,1)}, f32[2,1024]{1,0:T(2,128)}) custom-call(s32[6]{0:T(128)} %pad_add_fusion.where_ref, bf16[4,64,256]{2,1,0:T(8,128)(2,1)} %copy-done.42, f32[4,64,256]{2,1,0:T(8,128)} %copy-done.39, f32[4,256,256]{2,1,0:T(8,128)} %copy-done.30, ...), custom_call_target="tpu_custom_call" | custom-call | bytes 6000000 | tf_op jit(solution)/shard_map/pallas_call | solution.py:38
  197.4 2.1 collective-permute-done.23
  199.5 1.7 collective-permute-done.24
  202.0 3.0 %collective-permute-done.32 = bf16[4,4,400,128]{3,2,1,0:T(8,128)(2,1)S(1)} collective-permute-done((bf16[4,4,400,128]{3,2,1,0:T(8,128)(2,1)}, bf16[4,4,400,128]{3,2,1,0:T(8,128)(2,1)S(1)}, u32[]{:S(2)}, u32[]{:S(2)}) %collective-permute-start.32) | collective-permute-done | bytes 1638432 | tf_op jit(solution)/shard_map/ppermute | solution.py:1019
  205.0 1.6 fusion.8
  208.5 1.6 collective-permute-start.34
  210.8 6.4 %collective-permute-done.31 = bf16[256,1024]{1,0:T(8,128)(2,1)} collective-permute-done((bf16[256,1024]{1,0:T(8,128)(2,1)S(1)}, bf16[256,1024]{1,0:T(8,128)(2,1)}, u32[]{:S(2)}, u32[]{:S(2)}) %collective-permute-start.31) | collective-permute-done | bytes 524320 | tf_op jit(solution)/shard_map/ppermute | solution.py:1031
  217.3 2.3 fusion.3
  219.6 5.5 %collective-permute-done.33 = bf16[4,400,128]{2,1,0:T(8,128)(2,1)S(1)} collective-permute-done((bf16[4,400,128]{2,1,0:T(8,128)(2,1)S(1)}, bf16[4,400,128]{2,1,0:T(8,128)(2,1)S(1)}, u32[]{:S(2)}, u32[]{:S(2)}) %collective-permute-start.33) | collective-permute-done | bytes 409632 | tf_op jit(solution)/shard_map/ppermute | solution.py:818
  225.1 2.0 collective-permute-start.40
  227.0 7.0 %collective-permute-done.35 = bf16[4,400,128]{2,1,0:T(8,128)(2,1)S(1)} collective-permute-done((bf16[4,400,128]{2,1,0:T(8,128)(2,1)S(1)}, bf16[4,400,128]{2,1,0:T(8,128)(2,1)S(1)}, u32[]{:S(2)}, u32[]{:S(2)}) %collective-permute-start.35) | collective-permute-done | bytes 409632 | tf_op jit(solution)/shard_map/ppermute | solution.py:818
  236.1 1.8 collective-permute-start.38
  240.4 3.4 %collective-permute-done.38 = bf16[400,128]{1,0:T(8,128)(2,1)S(1)} collective-permute-done((bf16[400,128]{1,0:T(8,128)(2,1)S(1)}, bf16[400,128]{1,0:T(8,128)(2,1)S(1)}, u32[]{:S(2)}, u32[]{:S(2)}) %collective-permute-start.38) | collective-permute-done | bytes 102432 | tf_op jit(solution)/shard_map/ppermute | solution.py:858
  243.7 4.1 %collective-permute-done.37 = bf16[400,128]{1,0:T(8,128)(2,1)S(1)} collective-permute-done((bf16[400,128]{1,0:T(8,128)(2,1)S(1)}, bf16[400,128]{1,0:T(8,128)(2,1)S(1)}, u32[]{:S(2)}, u32[]{:S(2)}) %collective-permute-start.37) | collective-permute-done | bytes 102432 | tf_op jit(solution)/shard_map/ppermute | solution.py:858
  (230 shorter events, 57.6 us)
Async XLA Ops:
  7.2 70.7 %all-gather.6.cloned.1.call-start = ((), (), s32[]{:S(2)}) async-start(), calls=%async_computation.2 | async-start | bytes 3944448 | tf_op jit(solution)/shard_map/all_gather | solution.py:931
  7.2 27.1 %collective-permute-start.10 = (bf16[256,128]{1,0:T(8,128)(2,1)}, bf16[256,128]{1,0:T(8,128)(2,1)S(1)}, u32[]{:S(2)}, u32[]{:S(2)}) collective-permute-start(bf16[256,128]{1,0:T(8,128)(2,1)} %param.17), channel_id=1, source_target_pairs={{0,16},{8,24},{16,0},{24,8},{1,17},{9,25},{17,1},{25,9},{2,18},{10... | collective-permute-start | bytes 196616 | tf_op jit(solution)/shard_map/ppermute | solution.py:818
  10.3 24.1 %collective-permute-start.9 = (bf16[256,128]{1,0:T(8,128)(2,1)}, bf16[256,128]{1,0:T(8,128)(2,1)S(1)}, u32[]{:S(2)}, u32[]{:S(2)}) collective-permute-start(bf16[256,128]{1,0:T(8,128)(2,1)} %param.17), channel_id=1, source_target_pairs={{0,8},{8,0},{16,24},{24,16},{1,9},{9,1},{17,25},{25,17},{2,10},{10... | collective-permute-start | bytes 196616 | tf_op jit(solution)/shard_map/ppermute | solution.py:818
  11.8 22.6 %collective-permute-start.11 = (bf16[256,128]{1,0:T(8,128)(2,1)}, bf16[256,128]{1,0:T(8,128)(2,1)S(1)}, u32[]{:S(2)}, u32[]{:S(2)}) collective-permute-start(bf16[256,128]{1,0:T(8,128)(2,1)} %param.17), channel_id=1, source_target_pairs={{0,24},{8,16},{16,8},{24,0},{1,25},{9,17},{17,9},{25,1},{2,26},{10... | collective-permute-start | bytes 196616 | tf_op jit(solution)/shard_map/ppermute | solution.py:818
  11.8 22.6 %collective-permute-start.1 = (bf16[256,1024]{1,0:T(8,128)(2,1)}, bf16[256,1024]{1,0:T(8,128)(2,1)S(1)}, u32[]{:S(2)}, u32[]{:S(2)}) collective-permute-start(bf16[256,1024]{1,0:T(8,128)(2,1)} %bitcast.96), channel_id=1, source_target_pairs={{0,16},{8,24},{16,0},{24,8},{1,17},{9,25},{17,1},{25,9},{2,18},{10... | collective-permute-start | bytes 1572872 | tf_op jit(solution)/shard_map/ppermute | solution.py:914
  13.7 20.7 %collective-permute-start = (bf16[256,1024]{1,0:T(8,128)(2,1)}, bf16[256,1024]{1,0:T(8,128)(2,1)S(1)}, u32[]{:S(2)}, u32[]{:S(2)}) collective-permute-start(bf16[256,1024]{1,0:T(8,128)(2,1)} %bitcast.97), channel_id=1, source_target_pairs={{0,8},{8,0},{16,24},{24,16},{1,9},{9,1},{17,25},{25,17},{2,10},{10... | collective-permute-start | bytes 1572872 | tf_op jit(solution)/shard_map/ppermute | solution.py:914
  34.4 34.0 %copy-start.16 = (bf16[256,1024]{1,0:T(8,128)(2,1)}, bf16[256,1024]{1,0:T(8,128)(2,1)S(1)}, u32[]{:S(2)}) copy-start(bf16[256,1024]{1,0:T(8,128)(2,1)S(1)} %collective-permute-done.1.refs_2_.refs_10_) | copy-start | bytes 1572868
  34.5 34.0 %copy-start.19 = (bf16[256,1024]{1,0:T(8,128)(2,1)}, bf16[256,1024]{1,0:T(8,128)(2,1)S(1)}, u32[]{:S(2)}) copy-start(bf16[256,1024]{1,0:T(8,128)(2,1)S(1)} %collective-permute-done.refs_1_.refs_9_) | copy-start | bytes 1572868
  35.4 25.2 %copy-start.51 = (bf16[4,400,128]{2,1,0:T(8,128)(2,1)}, bf16[4,400,128]{2,1,0:T(8,128)(2,1)S(1)}, u32[]{:S(2)}) copy-start(bf16[4,400,128]{2,1,0:T(8,128)(2,1)S(1)} %get-tuple-element.114.refs_0_) | copy-start | bytes 1228804
  36.2 81.6 %all-gather.8.cloned.1.call-start = ((), (), s32[]{:S(2)}) async-start(), calls=%async_computation.3 | async-start | bytes 3170304 | tf_op jit(solution)/shard_map/all_gather | solution.py:989
  36.3 20.6 %collective-permute-start.6 = (bf16[4,400,128]{2,1,0:T(8,128)(2,1)S(1)}, bf16[4,400,128]{2,1,0:T(8,128)(2,1)S(1)}, u32[]{:S(2)}, u32[]{:S(2)}) collective-permute-start(bf16[4,400,128]{2,1,0:T(8,128)(2,1)S(1)} %get-tuple-element.114.refs_0_), channel_id=1, source_target_pairs={{0,24},{8,16},{16,8},{24,0},{1,25},{9,17},{17,9},{25,1},{2,26},{10... | collective-permute-start | bytes 1228808 | tf_op jit(solution)/shard_map/ppermute | solution.py:818
  36.8 20.2 %collective-permute-start.4 = (bf16[4,400,128]{2,1,0:T(8,128)(2,1)S(1)}, bf16[4,400,128]{2,1,0:T(8,128)(2,1)S(1)}, u32[]{:S(2)}, u32[]{:S(2)}) collective-permute-start(bf16[4,400,128]{2,1,0:T(8,128)(2,1)S(1)} %get-tuple-element.114.refs_0_), channel_id=1, source_target_pairs={{0,16},{8,24},{16,0},{24,8},{1,17},{9,25},{17,1},{25,9},{2,18},{10... | collective-permute-start | bytes 1228808 | tf_op jit(solution)/shard_map/ppermute | solution.py:818
  38.4 18.5 %collective-permute-start.2 = (bf16[4,400,128]{2,1,0:T(8,128)(2,1)S(1)}, bf16[4,400,128]{2,1,0:T(8,128)(2,1)S(1)}, u32[]{:S(2)}, u32[]{:S(2)}) collective-permute-start(bf16[4,400,128]{2,1,0:T(8,128)(2,1)S(1)} %get-tuple-element.114.refs_0_), channel_id=1, source_target_pairs={{0,8},{8,0},{16,24},{24,16},{1,9},{9,1},{17,25},{25,17},{2,10},{10... | collective-permute-start | bytes 1228808 | tf_op jit(solution)/shard_map/ppermute | solution.py:818
  56.8 1.8 collective-permute-start.7
  57.1 2.3 collective-permute-start.5
  57.4 2.5 collective-permute-start.3
  68.5 9.4 %collective-permute-start.8 = (bf16[9,176,128]{2,1,0:T(8,128)(2,1)}, bf16[9,176,128]{2,1,0:T(8,128)(2,1)S(1)}, u32[]{:S(2)}, u32[]{:S(2)}) collective-permute-start(bf16[9,176,128]{2,1,0:T(8,128)(2,1)} %get-tuple-element.126), channel_id=1, source_target_pairs={{0,1},{1,2},{2,3},{3,4},{4,5},{5,6},{6,7},{8,9},{9,10},{10,11},{11... | collective-permute-start | bytes 1216520 | tf_op jit(solution)/shard_map/ppermute | solution.py:852
  81.7 168.2 %reduce-scatter.2.cloned.1.call-start = ((), (), s32[]{:S(2)}) async-start(), calls=%async_computation.1 | async-start | bytes 4755456 | tf_op jit(solution)/shard_map/reduce_scatter | solution.py:1024
  81.8 4.9 %collective-permute-start.12 = (bf16[9,176,128]{2,1,0:T(8,128)(2,1)}, bf16[9,176,128]{2,1,0:T(8,128)(2,1)S(1)}, u32[]{:S(2)}, u32[]{:S(2)}) collective-permute-start(bf16[9,176,128]{2,1,0:T(8,128)(2,1)} %copy-done.57), channel_id=1, source_target_pairs={{0,1},{1,2},{2,3},{3,4},{4,5},{5,6},{6,7},{8,9},{9,10},{10,11},{11... | collective-permute-start | bytes 1216520 | tf_op jit(solution)/shard_map/ppermute | solution.py:852
  85.0 22.7 %collective-permute-start.19 = (bf16[256,1024]{1,0:T(8,128)(2,1)}, bf16[256,1024]{1,0:T(8,128)(2,1)S(1)}, u32[]{:S(2)}, u32[]{:S(2)}) collective-permute-start(bf16[256,1024]{1,0:T(8,128)(2,1)} %bitcast.98), channel_id=1, source_target_pairs={{0,24},{8,16},{16,8},{24,0},{1,25},{9,17},{17,9},{25,1},{2,26},{10... | collective-permute-start | bytes 1572872 | tf_op jit(solution)/shard_map/ppermute | solution.py:984
  96.9 6.6 %collective-permute-start.13 = (bf16[128,1024]{1,0:T(8,128)(2,1)}, bf16[128,1024]{1,0:T(8,128)(2,1)S(1)}, u32[]{:S(2)}, u32[]{:S(2)}) collective-permute-start(bf16[128,1024]{1,0:T(8,128)(2,1)} %get-tuple-element.157.first_ref.refs_0_), channel_id=1, source_target_pairs={{0,8},{8,0},{16,24},{24,16},{1,9},{9,1},{17,25},{25,17},{2,10},{10... | collective-permute-start | bytes 786440 | tf_op jit(solution)/shard_map/ppermute | solution.py:841
  98.4 7.4 %collective-permute-start.16 = (bf16[128,1024]{1,0:T(8,128)(2,1)}, bf16[128,1024]{1,0:T(8,128)(2,1)S(1)}, u32[]{:S(2)}, u32[]{:S(2)}) collective-permute-start(bf16[128,1024]{1,0:T(8,128)(2,1)} %get-tuple-element.158.second_ref.refs_1_), channel_id=1, source_target_pairs={{0,16},{8,24},{16,0},{24,8},{1,17},{9,25},{17,1},{25,9},{2,18},{10... | collective-permute-start | bytes 786440 | tf_op jit(solution)/shard_map/ppermute | solution.py:841
  103.6 16.9 %collective-permute-start.17 = (bf16[128,1024]{1,0:T(8,128)(2,1)S(1)}, bf16[128,1024]{1,0:T(8,128)(2,1)}, u32[]{:S(2)}, u32[]{:S(2)}) collective-permute-start(bf16[128,1024]{1,0:T(8,128)(2,1)S(1)} %collective-permute-done.13.first_ref.refs_2_), channel_id=1, source_target_pairs={{0,16},{8,24},{16,0},{24,8},{1,17},{9,25},{17,1},{25,9},{2,18},{10... | collective-permute-start | bytes 786440 | tf_op jit(solution)/shard_map/ppermute | solution.py:841
  105.7 14.7 %collective-permute-start.18 = (bf16[128,1024]{1,0:T(8,128)(2,1)S(1)}, bf16[128,1024]{1,0:T(8,128)(2,1)}, u32[]{:S(2)}, u32[]{:S(2)}) collective-permute-start(bf16[128,1024]{1,0:T(8,128)(2,1)S(1)} %collective-permute-done.16.second_ref.refs_5_), channel_id=1, source_target_pairs={{0,8},{8,0},{16,24},{24,16},{1,9},{9,1},{17,25},{25,17},{2,10},{10... | collective-permute-start | bytes 786440 | tf_op jit(solution)/shard_map/ppermute | solution.py:841
  105.9 18.5 %collective-permute-start.15 = (bf16[128,1024]{1,0:T(8,128)(2,1)}, bf16[128,1024]{1,0:T(8,128)(2,1)}, u32[]{:S(2)}, u32[]{:S(2)}) collective-permute-start(bf16[128,1024]{1,0:T(8,128)(2,1)} %get-tuple-element.157.first_ref.refs_0_), channel_id=1, source_target_pairs={{0,16},{8,24},{16,0},{24,8},{1,17},{9,25},{17,1},{25,9},{2,18},{10... | collective-permute-start | bytes 786440 | tf_op jit(solution)/shard_map/ppermute | solution.py:841
  107.5 23.1 %collective-permute-start.14 = (bf16[128,1024]{1,0:T(8,128)(2,1)}, bf16[128,1024]{1,0:T(8,128)(2,1)}, u32[]{:S(2)}, u32[]{:S(2)}) collective-permute-start(bf16[128,1024]{1,0:T(8,128)(2,1)} %get-tuple-element.158.second_ref.refs_1_), channel_id=1, source_target_pairs={{0,8},{8,0},{16,24},{24,16},{1,9},{9,1},{17,25},{25,17},{2,10},{10... | collective-permute-start | bytes 786440 | tf_op jit(solution)/shard_map/ppermute | solution.py:841
  124.4 28.5 %collective-permute-start.22 = (bf16[256,1024]{1,0:T(8,128)(2,1)}, bf16[256,1024]{1,0:T(8,128)(2,1)}, u32[]{:S(2)}, u32[]{:S(2)}) collective-permute-start(bf16[256,1024]{1,0:T(8,128)(2,1)} %get-tuple-element.162), channel_id=1, source_target_pairs={{0,24},{8,16},{16,8},{24,0},{1,25},{9,17},{17,9},{25,1},{2,26},{10... | collective-permute-start | bytes 1572872 | tf_op jit(solution)/shard_map/ppermute | solution.py:818
  130.6 22.3 %collective-permute-start.21 = (bf16[256,1024]{1,0:T(8,128)(2,1)}, bf16[256,1024]{1,0:T(8,128)(2,1)}, u32[]{:S(2)}, u32[]{:S(2)}) collective-permute-start(bf16[256,1024]{1,0:T(8,128)(2,1)} %get-tuple-element.161), channel_id=1, source_target_pairs={{0,16},{8,24},{16,0},{24,8},{1,17},{9,25},{17,1},{25,9},{2,18},{10... | collective-permute-start | bytes 1572872 | tf_op jit(solution)/shard_map/ppermute | solution.py:818
  135.0 17.9 %collective-permute-start.20 = (bf16[256,1024]{1,0:T(8,128)(2,1)}, bf16[256,1024]{1,0:T(8,128)(2,1)}, u32[]{:S(2)}, u32[]{:S(2)}) collective-permute-start(bf16[256,1024]{1,0:T(8,128)(2,1)} %get-tuple-element.160), channel_id=1, source_target_pairs={{0,8},{8,0},{16,24},{24,16},{1,9},{9,1},{17,25},{25,17},{2,10},{10... | collective-permute-start | bytes 1572872 | tf_op jit(solution)/shard_map/ppermute | solution.py:818
  160.8 5.2 %collective-permute-start.27 = (bf16[4,4,256,128]{3,2,1,0:T(8,128)(2,1)S(1)}, bf16[4,4,256,128]{3,2,1,0:T(8,128)(2,1)S(1)}, u32[]{:S(2)}, u32[]{:S(2)}) collective-permute-start(bf16[4,4,256,128]{3,2,1,0:T(8,128)(2,1)S(1)} %get-tuple-element.199), channel_id=1, source_target_pairs={{0,1},{1,0},{2,3},{3,2},{4,5},{5,4},{6,7},{7,6},{8,9},{9,8},{10,11... | collective-permute-start | bytes 3145736 | tf_op jit(solution)/shard_map/ppermute | solution.py:1019
  164.5 10.6 %collective-permute-start.25 = (bf16[9,176,128]{2,1,0:T(8,128)(2,1)S(1)}, bf16[9,176,128]{2,1,0:T(8,128)(2,1)S(1)}, u32[]{:S(2)}, u32[]{:S(2)}) collective-permute-start(bf16[9,176,128]{2,1,0:T(8,128)(2,1)S(1)} %get-tuple-element.194), channel_id=1, source_target_pairs={{1,0},{2,1},{3,2},{4,3},{5,4},{6,5},{7,6},{9,8},{10,9},{11,10},{12... | collective-permute-start | bytes 1216520 | tf_op jit(solution)/shard_map/ppermute | solution.py:852
  166.2 10.3 %collective-permute-start.28 = (bf16[4,256,128]{2,1,0:T(8,128)(2,1)S(1)}, bf16[4,256,128]{2,1,0:T(8,128)(2,1)S(1)}, u32[]{:S(2)}, u32[]{:S(2)}) collective-permute-start(bf16[4,256,128]{2,1,0:T(8,128)(2,1)S(1)} %get-tuple-element.319), channel_id=1, source_target_pairs={{0,8},{8,0},{16,24},{24,16},{1,9},{9,1},{17,25},{25,17},{2,10},{10... | collective-permute-start | bytes 786440 | tf_op jit(solution)/shard_map/ppermute | solution.py:818
  167.7 14.2 %collective-permute-start.30 = (bf16[4,256,128]{2,1,0:T(8,128)(2,1)S(1)}, bf16[4,256,128]{2,1,0:T(8,128)(2,1)S(1)}, u32[]{:S(2)}, u32[]{:S(2)}) collective-permute-start(bf16[4,256,128]{2,1,0:T(8,128)(2,1)S(1)} %get-tuple-element.320), channel_id=1, source_target_pairs={{0,24},{8,16},{16,8},{24,0},{1,25},{9,17},{17,9},{25,1},{2,26},{10... | collective-permute-start | bytes 786440 | tf_op jit(solution)/shard_map/ppermute | solution.py:818
  169.2 14.4 %collective-permute-start.29 = (bf16[4,256,128]{2,1,0:T(8,128)(2,1)S(1)}, bf16[4,256,128]{2,1,0:T(8,128)(2,1)S(1)}, u32[]{:S(2)}, u32[]{:S(2)}) collective-permute-start(bf16[4,256,128]{2,1,0:T(8,128)(2,1)S(1)} %get-tuple-element.321), channel_id=1, source_target_pairs={{0,16},{8,24},{16,0},{24,8},{1,17},{9,25},{17,1},{25,9},{2,18},{10... | collective-permute-start | bytes 786440 | tf_op jit(solution)/shard_map/ppermute | solution.py:818
  175.1 8.7 %collective-permute-start.26 = (bf16[9,176,128]{2,1,0:T(8,128)(2,1)S(1)}, bf16[9,176,128]{2,1,0:T(8,128)(2,1)S(1)}, u32[]{:S(2)}, u32[]{:S(2)}) collective-permute-start(bf16[9,176,128]{2,1,0:T(8,128)(2,1)S(1)} %collective-permute-done.25.one_ref), channel_id=1, source_target_pairs={{1,0},{2,1},{3,2},{4,3},{5,4},{6,5},{7,6},{9,8},{10,9},{11,10},{12... | collective-permute-start | bytes 1216520 | tf_op jit(solution)/shard_map/ppermute | solution.py:852
  185.0 14.5 %collective-permute-start.23 = (bf16[256,1024]{1,0:T(8,128)(2,1)S(1)}, bf16[256,1024]{1,0:T(8,128)(2,1)S(1)}, u32[]{:S(2)}, u32[]{:S(2)}) collective-permute-start(bf16[256,1024]{1,0:T(8,128)(2,1)S(1)} %copy-done.50), channel_id=1, source_target_pairs={{0,8},{8,0},{16,24},{24,16},{1,9},{9,1},{17,25},{25,17},{2,10},{10... | collective-permute-start | bytes 1572872 | tf_op jit(solution)/shard_map/ppermute | solution.py:1028
  186.5 14.8 %collective-permute-start.24 = (bf16[256,1024]{1,0:T(8,128)(2,1)S(1)}, bf16[256,1024]{1,0:T(8,128)(2,1)S(1)}, u32[]{:S(2)}, u32[]{:S(2)}) collective-permute-start(bf16[256,1024]{1,0:T(8,128)(2,1)S(1)} %copy-done.48), channel_id=1, source_target_pairs={{0,16},{8,24},{16,0},{24,8},{1,17},{9,25},{17,1},{25,9},{2,18},{10... | collective-permute-start | bytes 1572872 | tf_op jit(solution)/shard_map/ppermute | solution.py:1028
  201.2 3.8 %collective-permute-start.32 = (bf16[4,4,400,128]{3,2,1,0:T(8,128)(2,1)}, bf16[4,4,400,128]{3,2,1,0:T(8,128)(2,1)S(1)}, u32[]{:S(2)}, u32[]{:S(2)}) collective-permute-start(bf16[4,4,400,128]{3,2,1,0:T(8,128)(2,1)} %get-tuple-element.212), channel_id=1, source_target_pairs={{0,1},{1,0},{2,3},{3,2},{4,5},{5,4},{6,7},{7,6},{8,9},{9,8},{10,11... | collective-permute-start | bytes 4915208 | tf_op jit(solution)/shard_map/ppermute | solution.py:1019
  201.5 15.8 %collective-permute-start.31 = (bf16[256,1024]{1,0:T(8,128)(2,1)S(1)}, bf16[256,1024]{1,0:T(8,128)(2,1)}, u32[]{:S(2)}, u32[]{:S(2)}) collective-permute-start(bf16[256,1024]{1,0:T(8,128)(2,1)S(1)} %copy-done.46), channel_id=1, source_target_pairs={{0,24},{8,16},{16,8},{24,0},{1,25},{9,17},{17,9},{25,1},{2,26},{10... | collective-permute-start | bytes 1572872 | tf_op jit(solution)/shard_map/ppermute | solution.py:1031
  206.6 18.5 %collective-permute-start.33 = (bf16[4,400,128]{2,1,0:T(8,128)(2,1)S(1)}, bf16[4,400,128]{2,1,0:T(8,128)(2,1)S(1)}, u32[]{:S(2)}, u32[]{:S(2)}) collective-permute-start(bf16[4,400,128]{2,1,0:T(8,128)(2,1)S(1)} %get-tuple-element.316), channel_id=1, source_target_pairs={{0,8},{8,0},{16,24},{24,16},{1,9},{9,1},{17,25},{25,17},{2,10},{10... | collective-permute-start | bytes 1228808 | tf_op jit(solution)/shard_map/ppermute | solution.py:818
  207.2 26.9 %collective-permute-start.35 = (bf16[4,400,128]{2,1,0:T(8,128)(2,1)S(1)}, bf16[4,400,128]{2,1,0:T(8,128)(2,1)S(1)}, u32[]{:S(2)}, u32[]{:S(2)}) collective-permute-start(bf16[4,400,128]{2,1,0:T(8,128)(2,1)S(1)} %get-tuple-element.317), channel_id=1, source_target_pairs={{0,24},{8,16},{16,8},{24,0},{1,25},{9,17},{17,9},{25,1},{2,26},{10... | collective-permute-start | bytes 1228808 | tf_op jit(solution)/shard_map/ppermute | solution.py:818
  208.5 25.6 %collective-permute-start.34 = (bf16[4,400,128]{2,1,0:T(8,128)(2,1)S(1)}, bf16[4,400,128]{2,1,0:T(8,128)(2,1)S(1)}, u32[]{:S(2)}, u32[]{:S(2)}) collective-permute-start(bf16[4,400,128]{2,1,0:T(8,128)(2,1)S(1)} %get-tuple-element.318), channel_id=1, source_target_pairs={{0,16},{8,24},{16,0},{24,8},{1,17},{9,25},{17,1},{25,9},{2,18},{10... | collective-permute-start | bytes 1228808 | tf_op jit(solution)/shard_map/ppermute | solution.py:818
  210.2 27.7 %collective-permute-start.39 = (bf16[256,128]{1,0:T(8,128)(2,1)S(1)}, bf16[256,128]{1,0:T(8,128)(2,1)S(1)}, u32[]{:S(2)}, u32[]{:S(2)}) collective-permute-start(bf16[256,128]{1,0:T(8,128)(2,1)S(1)} %get-tuple-element.330), channel_id=1, source_target_pairs={{0,2},{1,3},{2,0},{3,1},{4,6},{5,7},{6,4},{7,5},{8,10},{9,11},{10,... | collective-permute-start | bytes 196616 | tf_op jit(solution)/shard_map/ppermute | solution.py:858
  217.3 21.7 %collective-permute-start.41 = (bf16[256,128]{1,0:T(8,128)(2,1)S(1)}, bf16[256,128]{1,0:T(8,128)(2,1)S(1)}, u32[]{:S(2)}, u32[]{:S(2)}) collective-permute-start(bf16[256,128]{1,0:T(8,128)(2,1)S(1)} %get-tuple-element.331), channel_id=1, source_target_pairs={{0,6},{1,7},{2,4},{3,5},{4,2},{5,3},{6,0},{7,1},{8,14},{9,15},{10,... | collective-permute-start | bytes 196616 | tf_op jit(solution)/shard_map/ppermute | solution.py:858
  225.1 13.9 %collective-permute-start.40 = (bf16[256,128]{1,0:T(8,128)(2,1)S(1)}, bf16[256,128]{1,0:T(8,128)(2,1)S(1)}, u32[]{:S(2)}, u32[]{:S(2)}) collective-permute-start(bf16[256,128]{1,0:T(8,128)(2,1)S(1)} %get-tuple-element.332), channel_id=1, source_target_pairs={{0,4},{1,5},{2,6},{3,7},{4,0},{5,1},{6,2},{7,3},{8,12},{9,13},{10,... | collective-permute-start | bytes 196616 | tf_op jit(solution)/shard_map/ppermute | solution.py:858
  235.4 5.0 %collective-permute-start.36 = (bf16[400,128]{1,0:T(8,128)(2,1)S(1)}, bf16[400,128]{1,0:T(8,128)(2,1)S(1)}, u32[]{:S(2)}, u32[]{:S(2)}) collective-permute-start(bf16[400,128]{1,0:T(8,128)(2,1)S(1)} %get-tuple-element.327), channel_id=1, source_target_pairs={{0,2},{1,3},{2,0},{3,1},{4,6},{5,7},{6,4},{7,5},{8,10},{9,11},{10,... | collective-permute-start | bytes 307208 | tf_op jit(solution)/shard_map/ppermute | solution.py:858
  236.1 7.6 %collective-permute-start.38 = (bf16[400,128]{1,0:T(8,128)(2,1)S(1)}, bf16[400,128]{1,0:T(8,128)(2,1)S(1)}, u32[]{:S(2)}, u32[]{:S(2)}) collective-permute-start(bf16[400,128]{1,0:T(8,128)(2,1)S(1)} %get-tuple-element.328), channel_id=1, source_target_pairs={{0,6},{1,7},{2,4},{3,5},{4,2},{5,3},{6,0},{7,1},{8,14},{9,15},{10,... | collective-permute-start | bytes 307208 | tf_op jit(solution)/shard_map/ppermute | solution.py:858
  237.9 9.9 %collective-permute-start.37 = (bf16[400,128]{1,0:T(8,128)(2,1)S(1)}, bf16[400,128]{1,0:T(8,128)(2,1)S(1)}, u32[]{:S(2)}, u32[]{:S(2)}) collective-permute-start(bf16[400,128]{1,0:T(8,128)(2,1)S(1)} %get-tuple-element.329), channel_id=1, source_target_pairs={{0,4},{1,5},{2,6},{3,7},{4,0},{5,1},{6,2},{7,3},{8,12},{9,13},{10,... | collective-permute-start | bytes 307208 | tf_op jit(solution)/shard_map/ppermute | solution.py:858
  (59 other events, 316.6 us)
Sparse Core Ops, SparseCore 0:
  36.3 40.0 all-gather.5
  81.8 35.9 all-gather.7
  184.0 55.0 reduce-scatter.1

commit v5 on v4

--- a/solution.py
+++ b/solution.py
@@ -985,7 +985,7 @@
     nd = local(qk, v, masks)
     one, two = carried(sums, lasts, 1, join, nd)
     w_out, w_down = spread_out(gathered(second), ff)
-    wide, one, w_out = lax.optimization_barrier((wide, one, w_out))
+    wide, one = lax.optimization_barrier((wide, one))
     w_mlp = widen(gathered(lax.all_gather(wide, "seq")))
     dhid = prepare(w_down, cots)
     o, on, inv, c = carry(nd, qk, masks, one, two)
@@ -1000,10 +1000,11 @@
     dparts, hid, dg, du = ([t[k] for t in res] for k in range(4))
     dparts = swap(dparts)
     oparts = mlp_out(hid, w_down)
-    dmlp = mlp_grads(h2s, cots, hid, dg, du, nb)
-    dparts, oparts, dmlp = lax.optimization_barrier((dparts, oparts, dmlp))
+    dparts, oparts = lax.optimization_barrier((dparts, oparts))
     dy1, dgain_mlp, f, do = turn(dparts, y1, cot, gains, w_out)
     dext, dsums = back_first(do, on, inv, qk, masks)
+    hid_late, dg, du, dsums = lax.optimization_barrier((hid, dg, du, dsums))
+    dmlp = mlp_grads(h2s, cots, hid_late, dg, du, nb)
     dq, dk, dv = back_local(dext, qk, v, masks, c)
     back_one, back_two = carried(dsums, labels_back, -1, join, (dq, dk, dv))
 

time: 260 us -> 255 us (0.981)
  starting transfers between devices: 47 us -> 55.2 us
  waiting for transfers between devices: 66.9 us -> 58.9 us
  local copies, waits for them, and re-layouts: 31.1 us -> 28.2 us
  Pallas kernels: 70.3 us -> 67.6 us
    ppermute x6, starting transfers between devices: 6.21 us -> 13.2 us  [over_z(): lax.ppermute(x[k], 'seq', xor_pairs(size, 2 * k))]
    all_gather x1, waiting for transfers between devices: 7.4 us -> 3.85 us  [on_device(): w_mlp = widen(gathered(lax.all_gather(wide, 'seq')))]
    unnamed x130 -> x126, local copies, waits for them, and re-layouts: 25.3 us -> 22.4 us
    pallas_call x20, Pallas kernels: 70.3 us -> 67.6 us  [call(): pl.pallas_call(body, out_shape=outs, scratch_shapes=list(scratch), compil...]
where the time goes in v5:
time: 255 us; the launch traced here: 254 us
  Pallas kernels  67.6 us (27%)
  waiting for transfers between devices  58.9 us (23%)
  starting transfers between devices  55.2 us (22%)
  local copies, waits for them, and re-layouts  28.2 us (11%)
  between operations  18.5 us (7%)
  blocking collectives  16.6 us (7%)
  other arithmetic  9.22 us (4%)
    pallas_call x20, Pallas kernels, call(): pl.pallas_call(body, out_shape=outs, scratch_shapes=list(scratch), compil...  67.6 us
    ppermute x15, waiting for transfers between devices, swap(): lax.ppermute(parts[r], 'head', xor_pairs(size, r))  28.4 us
    unnamed x126, local copies, waits for them, and re-layouts  22.4 us
    ppermute x15, starting transfers between devices, swap(): lax.ppermute(parts[r], 'head', xor_pairs(size, r))  18.9 us
    all_gather x1, blocking collectives, on_device(): pack = lax.all_gather(pack, 'seq')  16.6 us
    ppermute x6, starting transfers between devices, over_z(): lax.ppermute(x[k], 'seq', xor_pairs(size, 2 * k))  13.2 us
    ppermute x6, waiting for transfers between devices, over_z(): lax.ppermute(x[k], 'seq', xor_pairs(size, 2 * k))  9.09 us
    ppermute x4, starting transfers between devices, shifted(): lax.ppermute(x, 'seq', [(i, i + step) for i in range(size) if 0 <= i + st...  7.91 us
  transfers between devices with their start and end apart: 45, of which 19 were waited for; matrix products, arithmetic and copies ran while one was open for 5% of the time, Pallas kernels for 25%

profile of v5, /device:TPU:0, one launch (start us, length us, event | category | flops | bytes accessed | tf_op | source)
XLA Modules:
  0.0 254.3 jit_solution(3827544571611252718)
XLA Ops:
  7.2 3.0 %collective-permute-start.11 = (bf16[256,128]{1,0:T(8,128)(2,1)}, bf16[256,128]{1,0:T(8,128)(2,1)S(1)}, u32[]{:S(2)}, u32[]{:S(2)}) collective-permute-start(bf16[256,128]{1,0:T(8,128)(2,1)} %param.17), channel_id=1, source_target_pairs={{0,16},{8,24},{16,0},{24,8},{1,17},{9,25},{17,1},{25,9},{2,18},{10... | collective-permute-start | bytes 196616 | tf_op jit(solution)/shard_map/ppermute | solution.py:818
  11.8 1.9 collective-permute-start.1
  15.2 1.6 shard_map.203
  16.9 16.6 %all-gather = bf16[3200,128]{1,0:T(8,128)(2,1)S(1)} all-gather(bf16[400,128]{1,0:T(8,128)(2,1)} %shard_map.203), channel_id=2, replica_groups=mesh['head'=4,'seq'=8] {'seq'}, dimensions={0}, use_global_device_ids=true | all-gather | bytes 921600 | tf_op jit(solution)/shard_map/all_gather | solution.py:913
  36.9 1.5 collective-permute-start.4
  46.0 10.9 %collective-permute-done.2.refs_2_ = bf16[4,400,128]{2,1,0:T(8,128)(2,1)S(1)} collective-permute-done((bf16[4,400,128]{2,1,0:T(8,128)(2,1)S(1)}, bf16[4,400,128]{2,1,0:T(8,128)(2,1)S(1)}, u32[]{:S(2)}, u32[]{:S(2)}) %collective-permute-start.2) | collective-permute-done | bytes 409632 | tf_op jit(solution)/shard_map/ppermute | solution.py:818
  60.6 7.9 %shard_map.204 = (bf16[256,1024]{1,0:T(8,128)(2,1)}, bf16[4,128,256]{2,1,0:T(8,128)(2,1)}, bf16[4,256,256]{2,1,0:T(8,128)(2,1)}, bf16[9,176,128]{2,1,0:T(8,128)(...) custom-call(s32[6]{0:T(128)} %pad_add_fusion.where_ref, bf16[256,1024]{1,0:T(8,128)(2,1)} %bitcast.102, ...), custom_call_target="tpu_custom_call" | custom-call | bytes 4200000 | tf_op jit(solution)/shard_map/pallas_call | solution.py:38
  68.6 2.1 collective-permute-start.8
  73.5 3.2 %shard_map.205.nd_ref = f32[4,2,256,256]{3,2,1,0:T(8,128)S(1)} custom-call(bf16[4,128,256]{2,1,0:T(8,128)(2,1)S(1)} %copy-done.4, bf16[4,256,256]{2,1,0:T(8,128)(2,1)S(1)} %copy-done.8, f32[8,256]{1,0:T(8,128)S(1)} %copy-done.33), custom_call_target="tpu_custom_call" | custom-call | bytes 3000000 | tf_op jit(solution)/shard_map/pallas_call | solution.py:38
  78.1 3.1 %collective-permute-start.9 = (bf16[9,176,128]{2,1,0:T(8,128)(2,1)S(1)}, bf16[9,176,128]{2,1,0:T(8,128)(2,1)S(1)}, u32[]{:S(2)}, u32[]{:S(2)}) collective-permute-start(bf16[9,176,128]{2,1,0:T(8,128)(2,1)S(1)} %collective-permute-done.8.one_ref), channel_id=1, source_target_pairs={{0,1},{1,2},{2,3},{3,4},{4,5},{5,6},{6,7},{8,9},{9,10},{10,11},{11... | collective-permute-start | bytes 1216520 | tf_op jit(solution)/shard_map/ppermute | solution.py:852
  81.2 1.6 collective-permute-start.19
  83.7 5.7 %shard_map.207 = (bf16[4,256,256]{2,1,0:T(8,128)(2,1)}, f32[4,256,256]{2,1,0:T(8,128)}, f32[4,256,256]{2,1,0:T(8,128)}, bf16[9,176,128]{2,1,0:T(8,128)(2,1)}) custom-call(f32[4,2,256,256]{3,2,1,0:T(8,128)} %copy-done.1, bf16[4,128,256]{2,1,0:T(8,128)(2,1)} %get-tuple-element.135.qk_ref, f32[8,256]{1,0:T(8,128)} %stack.18.masks_ref, ...), custom_call_target="tpu_custom_call" | custom-call | bytes 3000000 | tf_op jit(solution)/shard_map/pallas_call | solution.py:38
  89.4 2.0 copy-done.13
  92.6 1.6 shard_map.209
  97.1 5.2 %collective-permute-done.13.first_ref.refs_2_ = bf16[128,1024]{1,0:T(8,128)(2,1)} collective-permute-done((bf16[128,1024]{1,0:T(8,128)(2,1)}, bf16[128,1024]{1,0:T(8,128)(2,1)}, u32[]{:S(2)}, u32[]{:S(2)}) %collective-permute-start.13) | collective-permute-done | bytes 262176 | tf_op jit(solution)/shard_map/ppermute | solution.py:841
  104.6 1.7 collective-permute-start.15
  108.4 1.8 shard_map.210.dhid_ref
  110.2 3.9 %all-gather.8.cloned.1.call-done = bf16[11008,128]{1,0:T(8,128)(2,1)} async-done(((bf16[1376,128]{1,0:T(8,128)(2,1)}), bf16[11008,128]{1,0:T(8,128)(2,1)}) %all-gather.8.cloned.1.call-update) | async-done | bytes 2818064 | tf_op jit(solution)/shard_map/all_gather | solution.py:989
  114.1 1.8 copy-done.14
  116.7 3.1 %shard_map.212 = (bf16[256,1024]{1,0:T(8,128)(2,1)S(1)}, bf16[256,688]{1,0:T(8,128)(2,1)S(1)}, bf16[256,688]{1,0:T(8,128)(2,1)S(1)}, bf16[256,688]{1,0:T(8,128)(2,1)S(1)}) custom-call(bf16[128,1024]{1,0:T(8,128)(2,1)} %collective-permute-done.17.first_ref.refs_6_, bf16[128,1024]{1,0:T(8,128)(2,1)} %collective-permute-done.18.second_ref.refs_7_, ...), custom_call_target="tpu_custom_call" | custom-call | bytes 3000000 | tf_op jit(solution)/shard_map/pallas_call | solution.py:38
  119.8 2.4 collective-permute-start.22
  122.3 3.1 %shard_map.213 = (bf16[256,1024]{1,0:T(8,128)(2,1)S(1)}, bf16[256,688]{1,0:T(8,128)(2,1)S(1)}, bf16[256,688]{1,0:T(8,128)(2,1)S(1)}, bf16[256,688]{1,0:T(8,128)(2,1)S(1)}) custom-call(bf16[128,1024]{1,0:T(8,128)(2,1)} %collective-permute-done.15.first_ref.refs_4_, bf16[128,1024]{1,0:T(8,128)(2,1)} %collective-permute-done.16.second_ref.refs_5_, ...), custom_call_target="tpu_custom_call" | custom-call | bytes 3000000 | tf_op jit(solution)/shard_map/pallas_call | solution.py:38
  126.0 3.1 %shard_map.214 = (bf16[256,1024]{1,0:T(8,128)(2,1)S(1)}, bf16[256,688]{1,0:T(8,128)(2,1)S(1)}, bf16[256,688]{1,0:T(8,128)(2,1)S(1)}, bf16[256,688]{1,0:T(8,128)(2,1)S(1)}) custom-call(bf16[128,1024]{1,0:T(8,128)(2,1)} %collective-permute-done.13.first_ref.refs_2_, bf16[128,1024]{1,0:T(8,128)(2,1)} %collective-permute-done.14.second_ref.refs_3_, ...), custom_call_target="tpu_custom_call" | custom-call | bytes 3000000 | tf_op jit(solution)/shard_map/pallas_call | solution.py:38
  129.8 3.2 %shard_map.215 = (bf16[256,1024]{1,0:T(8,128)(2,1)S(1)}, bf16[256,688]{1,0:T(8,128)(2,1)S(1)}, bf16[256,688]{1,0:T(8,128)(2,1)S(1)}, bf16[256,688]{1,0:T(8,128)(2,1)S(1)}) custom-call(bf16[128,1024]{1,0:T(8,128)(2,1)} %get-tuple-element.167.first_ref.refs_0_, bf16[128,1024]{1,0:T(8,128)(2,1)} %get-tuple-element.168.second_ref.refs_1_, ...), custom_call_target="tpu_custom_call" | custom-call | bytes 3000000 | tf_op jit(solution)/shard_map/pallas_call | solution.py:38
  133.0 2.0 shard_map.216
  137.4 8.7 %collective-permute-done.21.refs_2_ = bf16[256,1024]{1,0:T(8,128)(2,1)S(1)} collective-permute-done((bf16[256,1024]{1,0:T(8,128)(2,1)S(1)}, bf16[256,1024]{1,0:T(8,128)(2,1)S(1)}, u32[]{:S(2)}, u32[]{:S(2)}) %collective-permute-start.21) | collective-permute-done | bytes 524320 | tf_op jit(solution)/shard_map/ppermute | solution.py:818
  148.6 1.7 shard_map.221
  150.5 3.7 %shard_map.218 = (bf16[4,4,256,128]{3,2,1,0:T(8,128)(2,1)S(1)}, bf16[9,176,128]{2,1,0:T(8,128)(2,1)S(1)}) custom-call(bf16[4,256,256]{2,1,0:T(8,128)(2,1)S(1)} %get-tuple-element.188.do_ref, f32[4,256,256]{2,1,0:T(8,128)S(1)} %copy-done.26, f32[4,256,256]{2,1,0:T(8,128)S(1)} %copy-done.27, bf16[4,128,256]{2,1,0:T(8,128)(2,1)S(1)} %copy-done.5, ...), custom_call_target="tpu_custom_call" | custom-call | bytes 3000000 | tf_op jit(solution)/shard_map/pallas_call | solution.py:38
  155.9 1.5 collective-permute-start.28
  159.4 5.4 %shard_map.219 = (bf16[4,64,256]{2,1,0:T(8,128)(2,1)S(1)}, f32[4,64,256]{2,1,0:T(8,128)S(1)}, f32[4,256,256]{2,1,0:T(8,128)S(1)}) custom-call(bf16[4,4,256,128]{3,2,1,0:T(8,128)(2,1)S(1)} %get-tuple-element.191.d_ref, bf16[4,128,256]{2,1,0:T(8,128)(2,1)S(1)} %copy-done.5, bf16[4,256,256]{2,1,0:T(8,128)(2,1)S(1)} %copy-done.9, f32[8,256]{1,0:T(8,128)S(1)} %copy-done.34, ...), custom_call_target="tpu_custom_call" | custom-call | bytes 3000000 | tf_op jit(solution)/shard_map/pallas_call | solution.py:38
  168.5 6.1 %shard_map.220 = bf16[8,2064,128]{2,1,0:T(8,128)(2,1)S(1)} custom-call(bf16[128,1024]{1,0:T(8,128)(2,1)} %get-tuple-element.167.first_ref.refs_0_, bf16[128,1024]{1,0:T(8,128)(2,1)} %get-tuple-element.168.second_ref.refs_1_, bf16[128,1024]{1,0:T(8,128)(2,1)} %collective-permute-done.13.first_ref.refs_2_, ...), custom_call_target="tpu_custom_call" | custom-call | bytes 5400000 | tf_op jit(solution)/shard_map/pallas_call | solution.py:38
  174.6 2.0 copy-done
  182.1 10.4 %shard_map.222 = (f32[256,1024]{1,0:T(8,128)}, bf16[4,4,400,128]{3,2,1,0:T(8,128)(2,1)}, bf16[4,4,400,128]{3,2,1,0:T(8,128)(2,1)}, f32[2,1024]{1,0:T(2,128)}) custom-call(s32[6]{0:T(128)} %pad_add_fusion.where_ref, bf16[4,64,256]{2,1,0:T(8,128)(2,1)} %copy-done.39, f32[4,64,256]{2,1,0:T(8,128)} %copy-done.36, f32[4,256,256]{2,1,0:T(8,128)} %copy-done.29, ...), custom_call_target="tpu_custom_call" | custom-call | bytes 6000000 | tf_op jit(solution)/shard_map/pallas_call | solution.py:38
  193.8 1.5 collective-permute-done.24
  196.8 2.2 collective-permute-done.32
  199.0 1.6 fusion.8
  201.2 2.5 %collective-permute-start.35 = (bf16[4,400,128]{2,1,0:T(8,128)(2,1)S(1)}, bf16[4,400,128]{2,1,0:T(8,128)(2,1)S(1)}, u32[]{:S(2)}, u32[]{:S(2)}) collective-permute-start(bf16[4,400,128]{2,1,0:T(8,128)(2,1)S(1)} %get-tuple-element.339), channel_id=1, source_target_pairs={{0,24},{8,16},{16,8},{24,0},{1,25},{9,17},{17,9},{25,1},{2,26},{10... | collective-permute-start | bytes 1228808 | tf_op jit(solution)/shard_map/ppermute | solution.py:818
  204.2 2.8 %collective-permute-start.39 = (bf16[256,128]{1,0:T(8,128)(2,1)S(1)}, bf16[256,128]{1,0:T(8,128)(2,1)S(1)}, u32[]{:S(2)}, u32[]{:S(2)}) collective-permute-start(bf16[256,128]{1,0:T(8,128)(2,1)S(1)} %get-tuple-element.352), channel_id=1, source_target_pairs={{0,2},{1,3},{2,0},{3,1},{4,6},{5,7},{6,4},{7,5},{8,10},{9,11},{10,... | collective-permute-start | bytes 196616 | tf_op jit(solution)/shard_map/ppermute | solution.py:858
  207.0 4.2 %collective-permute-done.31 = bf16[256,1024]{1,0:T(8,128)(2,1)} collective-permute-done((bf16[256,1024]{1,0:T(8,128)(2,1)S(1)}, bf16[256,1024]{1,0:T(8,128)(2,1)}, u32[]{:S(2)}, u32[]{:S(2)}) %collective-permute-start.31) | collective-permute-done | bytes 524320 | tf_op jit(solution)/shard_map/ppermute | solution.py:1032
  211.2 3.4 %collective-permute-start.41 = (bf16[256,128]{1,0:T(8,128)(2,1)S(1)}, bf16[256,128]{1,0:T(8,128)(2,1)S(1)}, u32[]{:S(2)}, u32[]{:S(2)}) collective-permute-start(bf16[256,128]{1,0:T(8,128)(2,1)S(1)} %get-tuple-element.353), channel_id=1, source_target_pairs={{0,6},{1,7},{2,4},{3,5},{4,2},{5,3},{6,0},{7,1},{8,14},{9,15},{10,... | collective-permute-start | bytes 196616 | tf_op jit(solution)/shard_map/ppermute | solution.py:858
  214.6 2.3 fusion.3
  216.9 2.9 %collective-permute-done.33 = bf16[4,400,128]{2,1,0:T(8,128)(2,1)S(1)} collective-permute-done((bf16[4,400,128]{2,1,0:T(8,128)(2,1)S(1)}, bf16[4,400,128]{2,1,0:T(8,128)(2,1)S(1)}, u32[]{:S(2)}, u32[]{:S(2)}) %collective-permute-start.33) | collective-permute-done | bytes 409632 | tf_op jit(solution)/shard_map/ppermute | solution.py:818
  219.8 2.7 %collective-permute-start.40 = (bf16[256,128]{1,0:T(8,128)(2,1)S(1)}, bf16[256,128]{1,0:T(8,128)(2,1)S(1)}, u32[]{:S(2)}, u32[]{:S(2)}) collective-permute-start(bf16[256,128]{1,0:T(8,128)(2,1)S(1)} %get-tuple-element.354), channel_id=1, source_target_pairs={{0,4},{1,5},{2,6},{3,7},{4,0},{5,1},{6,2},{7,3},{8,12},{9,13},{10,... | collective-permute-start | bytes 196616 | tf_op jit(solution)/shard_map/ppermute | solution.py:858
  222.6 5.6 %collective-permute-done.35 = bf16[4,400,128]{2,1,0:T(8,128)(2,1)S(1)} collective-permute-done((bf16[4,400,128]{2,1,0:T(8,128)(2,1)S(1)}, bf16[4,400,128]{2,1,0:T(8,128)(2,1)S(1)}, u32[]{:S(2)}, u32[]{:S(2)}) %collective-permute-start.35) | collective-permute-done | bytes 409632 | tf_op jit(solution)/shard_map/ppermute | solution.py:818
  229.5 2.8 %collective-permute-start.36 = (bf16[400,128]{1,0:T(8,128)(2,1)S(1)}, bf16[400,128]{1,0:T(8,128)(2,1)S(1)}, u32[]{:S(2)}, u32[]{:S(2)}) collective-permute-start(bf16[400,128]{1,0:T(8,128)(2,1)S(1)} %get-tuple-element.349), channel_id=1, source_target_pairs={{0,2},{1,3},{2,0},{3,1},{4,6},{5,7},{6,4},{7,5},{8,10},{9,11},{10,... | collective-permute-start | bytes 307208 | tf_op jit(solution)/shard_map/ppermute | solution.py:858
  232.2 1.6 collective-permute-start.38
  235.5 4.3 %collective-permute-done.38 = bf16[400,128]{1,0:T(8,128)(2,1)S(1)} collective-permute-done((bf16[400,128]{1,0:T(8,128)(2,1)S(1)}, bf16[400,128]{1,0:T(8,128)(2,1)S(1)}, u32[]{:S(2)}, u32[]{:S(2)}) %collective-permute-start.38) | collective-permute-done | bytes 102432 | tf_op jit(solution)/shard_map/ppermute | solution.py:858
  239.7 3.9 %collective-permute-done.37 = bf16[400,128]{1,0:T(8,128)(2,1)S(1)} collective-permute-done((bf16[400,128]{1,0:T(8,128)(2,1)S(1)}, bf16[400,128]{1,0:T(8,128)(2,1)S(1)}, u32[]{:S(2)}, u32[]{:S(2)}) %collective-permute-start.37) | collective-permute-done | bytes 102432 | tf_op jit(solution)/shard_map/ppermute | solution.py:858
  (226 shorter events, 57.8 us)
Async XLA Ops:
  7.2 82.2 %all-gather.6.cloned.1.call-start = ((), (), s32[]{:S(2)}) async-start(), calls=%async_computation.2 | async-start | bytes 3944448 | tf_op jit(solution)/shard_map/all_gather | solution.py:931
  7.2 27.1 %collective-permute-start.11 = (bf16[256,128]{1,0:T(8,128)(2,1)}, bf16[256,128]{1,0:T(8,128)(2,1)S(1)}, u32[]{:S(2)}, u32[]{:S(2)}) collective-permute-start(bf16[256,128]{1,0:T(8,128)(2,1)} %param.17), channel_id=1, source_target_pairs={{0,16},{8,24},{16,0},{24,8},{1,17},{9,25},{17,1},{25,9},{2,18},{10... | collective-permute-start | bytes 196616 | tf_op jit(solution)/shard_map/ppermute | solution.py:818
  10.3 24.1 %collective-permute-start.10 = (bf16[256,128]{1,0:T(8,128)(2,1)}, bf16[256,128]{1,0:T(8,128)(2,1)S(1)}, u32[]{:S(2)}, u32[]{:S(2)}) collective-permute-start(bf16[256,128]{1,0:T(8,128)(2,1)} %param.17), channel_id=1, source_target_pairs={{0,8},{8,0},{16,24},{24,16},{1,9},{9,1},{17,25},{25,17},{2,10},{10... | collective-permute-start | bytes 196616 | tf_op jit(solution)/shard_map/ppermute | solution.py:818
  11.8 22.6 %collective-permute-start.12 = (bf16[256,128]{1,0:T(8,128)(2,1)}, bf16[256,128]{1,0:T(8,128)(2,1)S(1)}, u32[]{:S(2)}, u32[]{:S(2)}) collective-permute-start(bf16[256,128]{1,0:T(8,128)(2,1)} %param.17), channel_id=1, source_target_pairs={{0,24},{8,16},{16,8},{24,0},{1,25},{9,17},{17,9},{25,1},{2,26},{10... | collective-permute-start | bytes 196616 | tf_op jit(solution)/shard_map/ppermute | solution.py:818
  11.8 22.6 %collective-permute-start.1 = (bf16[256,1024]{1,0:T(8,128)(2,1)}, bf16[256,1024]{1,0:T(8,128)(2,1)S(1)}, u32[]{:S(2)}, u32[]{:S(2)}) collective-permute-start(bf16[256,1024]{1,0:T(8,128)(2,1)} %bitcast.96), channel_id=1, source_target_pairs={{0,16},{8,24},{16,0},{24,8},{1,17},{9,25},{17,1},{25,9},{2,18},{10... | collective-permute-start | bytes 1572872 | tf_op jit(solution)/shard_map/ppermute | solution.py:914
  13.7 20.7 %collective-permute-start = (bf16[256,1024]{1,0:T(8,128)(2,1)}, bf16[256,1024]{1,0:T(8,128)(2,1)S(1)}, u32[]{:S(2)}, u32[]{:S(2)}) collective-permute-start(bf16[256,1024]{1,0:T(8,128)(2,1)} %bitcast.97), channel_id=1, source_target_pairs={{0,8},{8,0},{16,24},{24,16},{1,9},{9,1},{17,25},{25,17},{2,10},{10... | collective-permute-start | bytes 1572872 | tf_op jit(solution)/shard_map/ppermute | solution.py:914
  34.4 34.1 %copy-start.15 = (bf16[256,1024]{1,0:T(8,128)(2,1)}, bf16[256,1024]{1,0:T(8,128)(2,1)S(1)}, u32[]{:S(2)}) copy-start(bf16[256,1024]{1,0:T(8,128)(2,1)S(1)} %collective-permute-done.1.refs_2_.refs_10_) | copy-start | bytes 1572868
  34.5 34.1 %copy-start.18 = (bf16[256,1024]{1,0:T(8,128)(2,1)}, bf16[256,1024]{1,0:T(8,128)(2,1)S(1)}, u32[]{:S(2)}) copy-start(bf16[256,1024]{1,0:T(8,128)(2,1)S(1)} %collective-permute-done.refs_1_.refs_9_) | copy-start | bytes 1572868
  35.4 25.2 %copy-start.48 = (bf16[4,400,128]{2,1,0:T(8,128)(2,1)}, bf16[4,400,128]{2,1,0:T(8,128)(2,1)S(1)}, u32[]{:S(2)}) copy-start(bf16[4,400,128]{2,1,0:T(8,128)(2,1)S(1)} %get-tuple-element.125.refs_0_) | copy-start | bytes 1228804
  36.2 77.9 %all-gather.8.cloned.1.call-start = ((), (), s32[]{:S(2)}) async-start(), calls=%async_computation.3 | async-start | bytes 3170304 | tf_op jit(solution)/shard_map/all_gather | solution.py:989
  36.3 20.6 %collective-permute-start.6 = (bf16[4,400,128]{2,1,0:T(8,128)(2,1)S(1)}, bf16[4,400,128]{2,1,0:T(8,128)(2,1)S(1)}, u32[]{:S(2)}, u32[]{:S(2)}) collective-permute-start(bf16[4,400,128]{2,1,0:T(8,128)(2,1)S(1)} %get-tuple-element.125.refs_0_), channel_id=1, source_target_pairs={{0,24},{8,16},{16,8},{24,0},{1,25},{9,17},{17,9},{25,1},{2,26},{10... | collective-permute-start | bytes 1228808 | tf_op jit(solution)/shard_map/ppermute | solution.py:818
  36.9 20.2 %collective-permute-start.4 = (bf16[4,400,128]{2,1,0:T(8,128)(2,1)S(1)}, bf16[4,400,128]{2,1,0:T(8,128)(2,1)S(1)}, u32[]{:S(2)}, u32[]{:S(2)}) collective-permute-start(bf16[4,400,128]{2,1,0:T(8,128)(2,1)S(1)} %get-tuple-element.125.refs_0_), channel_id=1, source_target_pairs={{0,16},{8,24},{16,0},{24,8},{1,17},{9,25},{17,1},{25,9},{2,18},{10... | collective-permute-start | bytes 1228808 | tf_op jit(solution)/shard_map/ppermute | solution.py:818
  38.4 18.5 %collective-permute-start.2 = (bf16[4,400,128]{2,1,0:T(8,128)(2,1)S(1)}, bf16[4,400,128]{2,1,0:T(8,128)(2,1)S(1)}, u32[]{:S(2)}, u32[]{:S(2)}) collective-permute-start(bf16[4,400,128]{2,1,0:T(8,128)(2,1)S(1)} %get-tuple-element.125.refs_0_), channel_id=1, source_target_pairs={{0,8},{8,0},{16,24},{24,16},{1,9},{9,1},{17,25},{25,17},{2,10},{10... | collective-permute-start | bytes 1228808 | tf_op jit(solution)/shard_map/ppermute | solution.py:818
  56.9 1.8 collective-permute-start.7
  57.1 2.3 collective-permute-start.5
  57.4 2.5 collective-permute-start.3
  68.6 9.5 %collective-permute-start.8 = (bf16[9,176,128]{2,1,0:T(8,128)(2,1)}, bf16[9,176,128]{2,1,0:T(8,128)(2,1)S(1)}, u32[]{:S(2)}, u32[]{:S(2)}) collective-permute-start(bf16[9,176,128]{2,1,0:T(8,128)(2,1)} %get-tuple-element.137), channel_id=1, source_target_pairs={{0,1},{1,2},{2,3},{3,4},{4,5},{5,6},{6,7},{8,9},{9,10},{10,11},{11... | collective-permute-start | bytes 1216520 | tf_op jit(solution)/shard_map/ppermute | solution.py:852
  78.1 167.6 %reduce-scatter.2.cloned.1.call-start = ((), (), s32[]{:S(2)}) async-start(), calls=%async_computation.1 | async-start | bytes 4755456 | tf_op jit(solution)/shard_map/reduce_scatter | solution.py:1025
  78.1 4.8 %collective-permute-start.9 = (bf16[9,176,128]{2,1,0:T(8,128)(2,1)S(1)}, bf16[9,176,128]{2,1,0:T(8,128)(2,1)S(1)}, u32[]{:S(2)}, u32[]{:S(2)}) collective-permute-start(bf16[9,176,128]{2,1,0:T(8,128)(2,1)S(1)} %collective-permute-done.8.one_ref), channel_id=1, source_target_pairs={{0,1},{1,2},{2,3},{3,4},{4,5},{5,6},{6,7},{8,9},{9,10},{10,11},{11... | collective-permute-start | bytes 1216520 | tf_op jit(solution)/shard_map/ppermute | solution.py:852
  81.2 25.3 %collective-permute-start.19 = (bf16[256,1024]{1,0:T(8,128)(2,1)S(1)}, bf16[256,1024]{1,0:T(8,128)(2,1)S(1)}, u32[]{:S(2)}, u32[]{:S(2)}) collective-permute-start(bf16[256,1024]{1,0:T(8,128)(2,1)S(1)} %bitcast.98), channel_id=1, source_target_pairs={{0,24},{8,16},{16,8},{24,0},{1,25},{9,17},{17,9},{25,1},{2,26},{10... | collective-permute-start | bytes 1572872 | tf_op jit(solution)/shard_map/ppermute | solution.py:984
  95.2 7.1 %collective-permute-start.13 = (bf16[128,1024]{1,0:T(8,128)(2,1)}, bf16[128,1024]{1,0:T(8,128)(2,1)}, u32[]{:S(2)}, u32[]{:S(2)}) collective-permute-start(bf16[128,1024]{1,0:T(8,128)(2,1)} %get-tuple-element.167.first_ref.refs_0_), channel_id=1, source_target_pairs={{0,8},{8,0},{16,24},{24,16},{1,9},{9,1},{17,25},{25,17},{2,10},{10... | collective-permute-start | bytes 786440 | tf_op jit(solution)/shard_map/ppermute | solution.py:841
  96.7 7.9 %collective-permute-start.16 = (bf16[128,1024]{1,0:T(8,128)(2,1)}, bf16[128,1024]{1,0:T(8,128)(2,1)}, u32[]{:S(2)}, u32[]{:S(2)}) collective-permute-start(bf16[128,1024]{1,0:T(8,128)(2,1)} %get-tuple-element.168.second_ref.refs_1_), channel_id=1, source_target_pairs={{0,16},{8,24},{16,0},{24,8},{1,17},{9,25},{17,1},{25,9},{2,18},{10... | collective-permute-start | bytes 786440 | tf_op jit(solution)/shard_map/ppermute | solution.py:841
  102.3 14.4 %collective-permute-start.17 = (bf16[128,1024]{1,0:T(8,128)(2,1)}, bf16[128,1024]{1,0:T(8,128)(2,1)}, u32[]{:S(2)}, u32[]{:S(2)}) collective-permute-start(bf16[128,1024]{1,0:T(8,128)(2,1)} %collective-permute-done.13.first_ref.refs_2_), channel_id=1, source_target_pairs={{0,16},{8,24},{16,0},{24,8},{1,17},{9,25},{17,1},{25,9},{2,18},{10... | collective-permute-start | bytes 786440 | tf_op jit(solution)/shard_map/ppermute | solution.py:841
  104.5 12.2 %collective-permute-start.18 = (bf16[128,1024]{1,0:T(8,128)(2,1)}, bf16[128,1024]{1,0:T(8,128)(2,1)}, u32[]{:S(2)}, u32[]{:S(2)}) collective-permute-start(bf16[128,1024]{1,0:T(8,128)(2,1)} %collective-permute-done.16.second_ref.refs_5_), channel_id=1, source_target_pairs={{0,8},{8,0},{16,24},{24,16},{1,9},{9,1},{17,25},{25,17},{2,10},{10... | collective-permute-start | bytes 786440 | tf_op jit(solution)/shard_map/ppermute | solution.py:841
  104.6 15.2 %collective-permute-start.15 = (bf16[128,1024]{1,0:T(8,128)(2,1)}, bf16[128,1024]{1,0:T(8,128)(2,1)}, u32[]{:S(2)}, u32[]{:S(2)}) collective-permute-start(bf16[128,1024]{1,0:T(8,128)(2,1)} %get-tuple-element.167.first_ref.refs_0_), channel_id=1, source_target_pairs={{0,16},{8,24},{16,0},{24,8},{1,17},{9,25},{17,1},{25,9},{2,18},{10... | collective-permute-start | bytes 786440 | tf_op jit(solution)/shard_map/ppermute | solution.py:841
  106.3 19.1 %collective-permute-start.14 = (bf16[128,1024]{1,0:T(8,128)(2,1)}, bf16[128,1024]{1,0:T(8,128)(2,1)}, u32[]{:S(2)}, u32[]{:S(2)}) collective-permute-start(bf16[128,1024]{1,0:T(8,128)(2,1)} %get-tuple-element.168.second_ref.refs_1_), channel_id=1, source_target_pairs={{0,8},{8,0},{16,24},{24,16},{1,9},{9,1},{17,25},{25,17},{2,10},{10... | collective-permute-start | bytes 786440 | tf_op jit(solution)/shard_map/ppermute | solution.py:841
  119.8 17.6 %collective-permute-start.22 = (bf16[256,1024]{1,0:T(8,128)(2,1)S(1)}, bf16[256,1024]{1,0:T(8,128)(2,1)S(1)}, u32[]{:S(2)}, u32[]{:S(2)}) collective-permute-start(bf16[256,1024]{1,0:T(8,128)(2,1)S(1)} %get-tuple-element.172), channel_id=1, source_target_pairs={{0,24},{8,16},{16,8},{24,0},{1,25},{9,17},{17,9},{25,1},{2,26},{10... | collective-permute-start | bytes 1572872 | tf_op jit(solution)/shard_map/ppermute | solution.py:818
  125.4 20.7 %collective-permute-start.21 = (bf16[256,1024]{1,0:T(8,128)(2,1)S(1)}, bf16[256,1024]{1,0:T(8,128)(2,1)S(1)}, u32[]{:S(2)}, u32[]{:S(2)}) collective-permute-start(bf16[256,1024]{1,0:T(8,128)(2,1)S(1)} %get-tuple-element.171), channel_id=1, source_target_pairs={{0,16},{8,24},{16,0},{24,8},{1,17},{9,25},{17,1},{25,9},{2,18},{10... | collective-permute-start | bytes 1572872 | tf_op jit(solution)/shard_map/ppermute | solution.py:818
  129.1 17.0 %collective-permute-start.20 = (bf16[256,1024]{1,0:T(8,128)(2,1)S(1)}, bf16[256,1024]{1,0:T(8,128)(2,1)S(1)}, u32[]{:S(2)}, u32[]{:S(2)}) collective-permute-start(bf16[256,1024]{1,0:T(8,128)(2,1)S(1)} %get-tuple-element.170), channel_id=1, source_target_pairs={{0,8},{8,0},{16,24},{24,16},{1,9},{9,1},{17,25},{25,17},{2,10},{10... | collective-permute-start | bytes 1572872 | tf_op jit(solution)/shard_map/ppermute | solution.py:818
  150.4 5.2 %collective-permute-start.27 = (bf16[4,4,256,128]{3,2,1,0:T(8,128)(2,1)S(1)}, bf16[4,4,256,128]{3,2,1,0:T(8,128)(2,1)S(1)}, u32[]{:S(2)}, u32[]{:S(2)}) collective-permute-start(bf16[4,4,256,128]{3,2,1,0:T(8,128)(2,1)S(1)} %get-tuple-element.221), channel_id=1, source_target_pairs={{0,1},{1,0},{2,3},{3,2},{4,5},{5,4},{6,7},{7,6},{8,9},{9,8},{10,11... | collective-permute-start | bytes 3145736 | tf_op jit(solution)/shard_map/ppermute | solution.py:1020
  154.2 13.0 %collective-permute-start.25 = (bf16[9,176,128]{2,1,0:T(8,128)(2,1)S(1)}, bf16[9,176,128]{2,1,0:T(8,128)(2,1)S(1)}, u32[]{:S(2)}, u32[]{:S(2)}) collective-permute-start(bf16[9,176,128]{2,1,0:T(8,128)(2,1)S(1)} %get-tuple-element.205), channel_id=1, source_target_pairs={{1,0},{2,1},{3,2},{4,3},{5,4},{6,5},{7,6},{9,8},{10,9},{11,10},{12... | collective-permute-start | bytes 1216520 | tf_op jit(solution)/shard_map/ppermute | solution.py:852
  155.9 20.8 %collective-permute-start.28 = (bf16[4,256,128]{2,1,0:T(8,128)(2,1)S(1)}, bf16[4,256,128]{2,1,0:T(8,128)(2,1)S(1)}, u32[]{:S(2)}, u32[]{:S(2)}) collective-permute-start(bf16[4,256,128]{2,1,0:T(8,128)(2,1)S(1)} %get-tuple-element.341), channel_id=1, source_target_pairs={{0,8},{8,0},{16,24},{24,16},{1,9},{9,1},{17,25},{25,17},{2,10},{10... | collective-permute-start | bytes 786440 | tf_op jit(solution)/shard_map/ppermute | solution.py:818
  157.4 19.2 %collective-permute-start.30 = (bf16[4,256,128]{2,1,0:T(8,128)(2,1)S(1)}, bf16[4,256,128]{2,1,0:T(8,128)(2,1)}, u32[]{:S(2)}, u32[]{:S(2)}) collective-permute-start(bf16[4,256,128]{2,1,0:T(8,128)(2,1)S(1)} %get-tuple-element.342), channel_id=1, source_target_pairs={{0,24},{8,16},{16,8},{24,0},{1,25},{9,17},{17,9},{25,1},{2,26},{10... | collective-permute-start | bytes 786440 | tf_op jit(solution)/shard_map/ppermute | solution.py:818
  158.9 17.8 %collective-permute-start.29 = (bf16[4,256,128]{2,1,0:T(8,128)(2,1)S(1)}, bf16[4,256,128]{2,1,0:T(8,128)(2,1)}, u32[]{:S(2)}, u32[]{:S(2)}) collective-permute-start(bf16[4,256,128]{2,1,0:T(8,128)(2,1)S(1)} %get-tuple-element.343), channel_id=1, source_target_pairs={{0,16},{8,24},{16,0},{24,8},{1,17},{9,25},{17,1},{25,9},{2,18},{10... | collective-permute-start | bytes 786440 | tf_op jit(solution)/shard_map/ppermute | solution.py:818
  167.2 10.8 %collective-permute-start.26 = (bf16[9,176,128]{2,1,0:T(8,128)(2,1)S(1)}, bf16[9,176,128]{2,1,0:T(8,128)(2,1)S(1)}, u32[]{:S(2)}, u32[]{:S(2)}) collective-permute-start(bf16[9,176,128]{2,1,0:T(8,128)(2,1)S(1)} %collective-permute-done.25.one_ref), channel_id=1, source_target_pairs={{1,0},{2,1},{3,2},{4,3},{5,4},{6,5},{7,6},{9,8},{10,9},{11,10},{12... | collective-permute-start | bytes 1216520 | tf_op jit(solution)/shard_map/ppermute | solution.py:852
  179.1 14.6 %collective-permute-start.23 = (bf16[256,1024]{1,0:T(8,128)(2,1)S(1)}, bf16[256,1024]{1,0:T(8,128)(2,1)S(1)}, u32[]{:S(2)}, u32[]{:S(2)}) collective-permute-start(bf16[256,1024]{1,0:T(8,128)(2,1)S(1)} %copy-done.47), channel_id=1, source_target_pairs={{0,8},{8,0},{16,24},{24,16},{1,9},{9,1},{17,25},{25,17},{2,10},{10... | collective-permute-start | bytes 1572872 | tf_op jit(solution)/shard_map/ppermute | solution.py:1029
  180.6 14.7 %collective-permute-start.24 = (bf16[256,1024]{1,0:T(8,128)(2,1)S(1)}, bf16[256,1024]{1,0:T(8,128)(2,1)S(1)}, u32[]{:S(2)}, u32[]{:S(2)}) collective-permute-start(bf16[256,1024]{1,0:T(8,128)(2,1)S(1)} %copy-done.45), channel_id=1, source_target_pairs={{0,16},{8,24},{16,0},{24,8},{1,17},{9,25},{17,1},{25,9},{2,18},{10... | collective-permute-start | bytes 1572872 | tf_op jit(solution)/shard_map/ppermute | solution.py:1029
  195.3 3.7 %collective-permute-start.32 = (bf16[4,4,400,128]{3,2,1,0:T(8,128)(2,1)}, bf16[4,4,400,128]{3,2,1,0:T(8,128)(2,1)S(1)}, u32[]{:S(2)}, u32[]{:S(2)}) collective-permute-start(bf16[4,4,400,128]{3,2,1,0:T(8,128)(2,1)} %get-tuple-element.234), channel_id=1, source_target_pairs={{0,1},{1,0},{2,3},{3,2},{4,5},{5,4},{6,7},{7,6},{8,9},{9,8},{10,11... | collective-permute-start | bytes 4915208 | tf_op jit(solution)/shard_map/ppermute | solution.py:1020
  195.4 15.8 %collective-permute-start.31 = (bf16[256,1024]{1,0:T(8,128)(2,1)S(1)}, bf16[256,1024]{1,0:T(8,128)(2,1)}, u32[]{:S(2)}, u32[]{:S(2)}) collective-permute-start(bf16[256,1024]{1,0:T(8,128)(2,1)S(1)} %copy-done.43), channel_id=1, source_target_pairs={{0,24},{8,16},{16,8},{24,0},{1,25},{9,17},{17,9},{25,1},{2,26},{10... | collective-permute-start | bytes 1572872 | tf_op jit(solution)/shard_map/ppermute | solution.py:1032
  200.6 19.2 %collective-permute-start.33 = (bf16[4,400,128]{2,1,0:T(8,128)(2,1)S(1)}, bf16[4,400,128]{2,1,0:T(8,128)(2,1)S(1)}, u32[]{:S(2)}, u32[]{:S(2)}) collective-permute-start(bf16[4,400,128]{2,1,0:T(8,128)(2,1)S(1)} %get-tuple-element.338), channel_id=1, source_target_pairs={{0,8},{8,0},{16,24},{24,16},{1,9},{9,1},{17,25},{25,17},{2,10},{10... | collective-permute-start | bytes 1228808 | tf_op jit(solution)/shard_map/ppermute | solution.py:818
  201.2 26.9 %collective-permute-start.35 = (bf16[4,400,128]{2,1,0:T(8,128)(2,1)S(1)}, bf16[4,400,128]{2,1,0:T(8,128)(2,1)S(1)}, u32[]{:S(2)}, u32[]{:S(2)}) collective-permute-start(bf16[4,400,128]{2,1,0:T(8,128)(2,1)S(1)} %get-tuple-element.339), channel_id=1, source_target_pairs={{0,24},{8,16},{16,8},{24,0},{1,25},{9,17},{17,9},{25,1},{2,26},{10... | collective-permute-start | bytes 1228808 | tf_op jit(solution)/shard_map/ppermute | solution.py:818
  203.8 24.4 %collective-permute-start.34 = (bf16[4,400,128]{2,1,0:T(8,128)(2,1)S(1)}, bf16[4,400,128]{2,1,0:T(8,128)(2,1)S(1)}, u32[]{:S(2)}, u32[]{:S(2)}) collective-permute-start(bf16[4,400,128]{2,1,0:T(8,128)(2,1)S(1)} %get-tuple-element.340), channel_id=1, source_target_pairs={{0,16},{8,24},{16,0},{24,8},{1,17},{9,25},{17,1},{25,9},{2,18},{10... | collective-permute-start | bytes 1228808 | tf_op jit(solution)/shard_map/ppermute | solution.py:818
  204.2 29.6 %collective-permute-start.39 = (bf16[256,128]{1,0:T(8,128)(2,1)S(1)}, bf16[256,128]{1,0:T(8,128)(2,1)S(1)}, u32[]{:S(2)}, u32[]{:S(2)}) collective-permute-start(bf16[256,128]{1,0:T(8,128)(2,1)S(1)} %get-tuple-element.352), channel_id=1, source_target_pairs={{0,2},{1,3},{2,0},{3,1},{4,6},{5,7},{6,4},{7,5},{8,10},{9,11},{10,... | collective-permute-start | bytes 196616 | tf_op jit(solution)/shard_map/ppermute | solution.py:858
  211.2 22.6 %collective-permute-start.41 = (bf16[256,128]{1,0:T(8,128)(2,1)S(1)}, bf16[256,128]{1,0:T(8,128)(2,1)S(1)}, u32[]{:S(2)}, u32[]{:S(2)}) collective-permute-start(bf16[256,128]{1,0:T(8,128)(2,1)S(1)} %get-tuple-element.353), channel_id=1, source_target_pairs={{0,6},{1,7},{2,4},{3,5},{4,2},{5,3},{6,0},{7,1},{8,14},{9,15},{10,... | collective-permute-start | bytes 196616 | tf_op jit(solution)/shard_map/ppermute | solution.py:858
  219.8 14.0 %collective-permute-start.40 = (bf16[256,128]{1,0:T(8,128)(2,1)S(1)}, bf16[256,128]{1,0:T(8,128)(2,1)S(1)}, u32[]{:S(2)}, u32[]{:S(2)}) collective-permute-start(bf16[256,128]{1,0:T(8,128)(2,1)S(1)} %get-tuple-element.354), channel_id=1, source_target_pairs={{0,4},{1,5},{2,6},{3,7},{4,0},{5,1},{6,2},{7,3},{8,12},{9,13},{10,... | collective-permute-start | bytes 196616 | tf_op jit(solution)/shard_map/ppermute | solution.py:858
  229.5 6.0 %collective-permute-start.36 = (bf16[400,128]{1,0:T(8,128)(2,1)S(1)}, bf16[400,128]{1,0:T(8,128)(2,1)S(1)}, u32[]{:S(2)}, u32[]{:S(2)}) collective-permute-start(bf16[400,128]{1,0:T(8,128)(2,1)S(1)} %get-tuple-element.349), channel_id=1, source_target_pairs={{0,2},{1,3},{2,0},{3,1},{4,6},{5,7},{6,4},{7,5},{8,10},{9,11},{10,... | collective-permute-start | bytes 307208 | tf_op jit(solution)/shard_map/ppermute | solution.py:858
  232.2 7.5 %collective-permute-start.38 = (bf16[400,128]{1,0:T(8,128)(2,1)S(1)}, bf16[400,128]{1,0:T(8,128)(2,1)S(1)}, u32[]{:S(2)}, u32[]{:S(2)}) collective-permute-start(bf16[400,128]{1,0:T(8,128)(2,1)S(1)} %get-tuple-element.350), channel_id=1, source_target_pairs={{0,6},{1,7},{2,4},{3,5},{4,2},{5,3},{6,0},{7,1},{8,14},{9,15},{10,... | collective-permute-start | bytes 307208 | tf_op jit(solution)/shard_map/ppermute | solution.py:858
  233.8 9.8 %collective-permute-start.37 = (bf16[400,128]{1,0:T(8,128)(2,1)S(1)}, bf16[400,128]{1,0:T(8,128)(2,1)S(1)}, u32[]{:S(2)}, u32[]{:S(2)}) collective-permute-start(bf16[400,128]{1,0:T(8,128)(2,1)S(1)} %get-tuple-element.351), channel_id=1, source_target_pairs={{0,4},{1,5},{2,6},{3,7},{4,0},{5,1},{6,2},{7,3},{8,12},{9,13},{10,... | collective-permute-start | bytes 307208 | tf_op jit(solution)/shard_map/ppermute | solution.py:858
  (57 other events, 329.8 us)
Sparse Core Ops, SparseCore 0:
  36.4 40.0 all-gather.5
  78.7 35.3 all-gather.7
  178.1 56.6 reduce-scatter.1

commit v6 on v5

--- a/solution.py
+++ b/solution.py
@@ -506,33 +506,49 @@
     )
 
 
+def down_grads_body(n, *refs):
+    hid, cot, o_ref = refs[:n], refs[n : 2 * n], refs[2 * n]
+    nb, _, wb = o_ref.shape
+    acc = None
+    for r in range(n):
+        part = mm(hid[r][...], cot[r][...], TN)
+        acc = part if acc is None else acc + part
+    for s in range(nb):
+        o_ref[s] = acc[:, s * wb : (s + 1) * wb].astype(BF16)
+
+
+def down_grads(hid, cot, nb):
+    n = len(hid)
+    ff, d = hid[0].shape[1], cot[0].shape[1]
+    return call(
+        functools.partial(down_grads_body, n), sds((nb, ff, d // nb), BF16), (*hid, *cot), us=3
+    )
+
+
 def mlp_grads_body(n, *refs):
-    h2, cot = grouped(refs[: 2 * n], n), grouped(refs[2 * n : 3 * n], n)
-    hid, dg, du = (refs[(3 + k) * n : (4 + k) * n] for k in range(3))
-    o_ref, ff = refs[6 * n], hid[0].shape[1]
-    nb, _, wb = o_ref.shape
-    for k, (left, right) in enumerate(((dg, h2), (du, h2), (hid, cot))):
+    h2 = grouped(refs[: 2 * n], n)
+    dg, du, down_ref, o_ref = refs[2 * n : 3 * n], refs[3 * n : 4 * n], refs[4 * n], refs[4 * n + 1]
+    nb, ff, wb = down_ref.shape
+    for k, left in enumerate((dg, du)):
         acc = None
         for r in range(n):
-            part = mm(left[r][...], join_rows(right[r]), TN)
+            part = mm(left[r][...], join_rows(h2[r]), TN)
             acc = part if acc is None else acc + part
         acc = acc.astype(BF16)
         for s in range(nb):
             o_ref[s, k * ff : (k + 1) * ff, :] = acc[:, s * wb : (s + 1) * wb]
-
-
-def mlp_grads(h2, cot, hid, dg, du, nb):
+    for s in range(nb):
+        o_ref[s, 2 * ff :, :] = down_ref[s]
+
+
+def mlp_grads(h2, dg, du, down):
     n = len(h2)
-    d, ff = h2[0][0].shape[1], hid[0].shape[1]
-    ins = (*flat(h2), *cot, *hid, *dg, *du)
+    nb, ff, wb = down.shape
     return call(
         functools.partial(mlp_grads_body, n),
-        sds((nb, 3 * ff, d // nb), BF16),
-        ins,
-        grid=(1,),
-        in_specs=[whole(x.shape) for x in ins],
-        out_specs=whole((nb, 3 * ff, d // nb)),
-        us=9,
+        sds((nb, 3 * ff, wb), BF16),
+        (*flat(h2), *dg, *du, down),
+        us=6,
     )
 
 
@@ -1000,11 +1016,12 @@
     dparts, hid, dg, du = ([t[k] for t in res] for k in range(4))
     dparts = swap(dparts)
     oparts = mlp_out(hid, w_down)
-    dparts, oparts = lax.optimization_barrier((dparts, oparts))
+    ddown = down_grads(hid, cots, nb)
+    dparts, oparts, ddown = lax.optimization_barrier((dparts, oparts, ddown))
     dy1, dgain_mlp, f, do = turn(dparts, y1, cot, gains, w_out)
     dext, dsums = back_first(do, on, inv, qk, masks)
-    hid_late, dg, du, dsums = lax.optimization_barrier((hid, dg, du, dsums))
-    dmlp = mlp_grads(h2s, cots, hid_late, dg, du, nb)
+    dg, du, dsums = lax.optimization_barrier((dg, du, dsums))
+    dmlp = mlp_grads(h2s, dg, du, ddown)
     dq, dk, dv = back_local(dext, qk, v, masks, c)
     back_one, back_two = carried(dsums, labels_back, -1, join, (dq, dk, dv))
 

time: 255 us -> 255 us (level)
    unnamed x126 -> x132, local copies, waits for them, and re-layouts: 22.4 us -> 20.8 us
    pallas_call x20 -> x21, Pallas kernels: 67.6 us -> 67.7 us  [call(): pl.pallas_call(body, out_shape=outs, scratch_shapes=list(scratch), compil...]
  transfers between devices with their start and end apart: 45 -> 45, of which waited for: 19 -> 19; matrix products, arithmetic and copies ran while one was open for 5% -> 6% of each run, Pallas kernels for 25% -> 25%
where the time goes in v6:
time: 255 us; the launch traced here: 254 us
  Pallas kernels  67.7 us (27%)
  waiting for transfers between devices  59 us (23%)
  starting transfers between devices  55 us (22%)
  local copies, waits for them, and re-layouts  26.6 us (10%)
  between operations  18.6 us (7%)
  blocking collectives  16.6 us (7%)
  other arithmetic  10.3 us (4%)
    pallas_call x21, Pallas kernels, call(): pl.pallas_call(body, out_shape=outs, scratch_shapes=list(scratch), compil...  67.7 us
    ppermute x15, waiting for transfers between devices, swap(): lax.ppermute(parts[r], 'head', xor_pairs(size, r))  28.3 us
    unnamed x132, local copies, waits for them, and re-layouts  20.8 us
    ppermute x15, starting transfers between devices, swap(): lax.ppermute(parts[r], 'head', xor_pairs(size, r))  18.9 us
    all_gather x1, blocking collectives, on_device(): pack = lax.all_gather(pack, 'seq')  16.6 us
    ppermute x6, starting transfers between devices, over_z(): lax.ppermute(x[k], 'seq', xor_pairs(size, 2 * k))  13.1 us
    ppermute x6, waiting for transfers between devices, over_z(): lax.ppermute(x[k], 'seq', xor_pairs(size, 2 * k))  9.08 us
    ppermute x4, starting transfers between devices, shifted(): lax.ppermute(x, 'seq', [(i, i + step) for i in range(size) if 0 <= i + st...  7.94 us
  transfers between devices with their start and end apart: 45, of which 19 were waited for; matrix products, arithmetic and copies ran while one was open for 6% of the time, Pallas kernels for 25%

profile of v6, /device:TPU:0, one launch (start us, length us, event | category | flops | bytes accessed | tf_op | source)
XLA Modules:
  0.0 253.8 jit_solution(487281573902416330)
XLA Ops:
  7.2 3.0 %collective-permute-start.11 = (bf16[256,128]{1,0:T(8,128)(2,1)}, bf16[256,128]{1,0:T(8,128)(2,1)S(1)}, u32[]{:S(2)}, u32[]{:S(2)}) collective-permute-start(bf16[256,128]{1,0:T(8,128)(2,1)} %param.17), channel_id=1, source_target_pairs={{0,16},{8,24},{16,0},{24,8},{1,17},{9,25},{17,1},{25,9},{2,18},{10... | collective-permute-start | bytes 196616 | tf_op jit(solution)/shard_map/ppermute | solution.py:834
  11.8 1.9 collective-permute-start.1
  15.2 1.6 shard_map.203
  16.9 16.6 %all-gather = bf16[3200,128]{1,0:T(8,128)(2,1)S(1)} all-gather(bf16[400,128]{1,0:T(8,128)(2,1)} %shard_map.203), channel_id=2, replica_groups=mesh['head'=4,'seq'=8] {'seq'}, dimensions={0}, use_global_device_ids=true | all-gather | bytes 921600 | tf_op jit(solution)/shard_map/all_gather | solution.py:929
  36.9 1.5 collective-permute-start.4
  46.0 10.9 %collective-permute-done.2.refs_2_ = bf16[4,400,128]{2,1,0:T(8,128)(2,1)S(1)} collective-permute-done((bf16[4,400,128]{2,1,0:T(8,128)(2,1)S(1)}, bf16[4,400,128]{2,1,0:T(8,128)(2,1)S(1)}, u32[]{:S(2)}, u32[]{:S(2)}) %collective-permute-start.2) | collective-permute-done | bytes 409632 | tf_op jit(solution)/shard_map/ppermute | solution.py:834
  60.6 7.9 %shard_map.204 = (bf16[256,1024]{1,0:T(8,128)(2,1)}, bf16[4,128,256]{2,1,0:T(8,128)(2,1)}, bf16[4,256,256]{2,1,0:T(8,128)(2,1)}, bf16[9,176,128]{2,1,0:T(8,128)(...) custom-call(s32[6]{0:T(128)} %pad_add_fusion.where_ref, bf16[256,1024]{1,0:T(8,128)(2,1)} %bitcast.102, ...), custom_call_target="tpu_custom_call" | custom-call | bytes 4200000 | tf_op jit(solution)/shard_map/pallas_call | solution.py:38
  68.6 2.1 collective-permute-start.8
  73.5 3.2 %shard_map.205.nd_ref = f32[4,2,256,256]{3,2,1,0:T(8,128)S(1)} custom-call(bf16[4,128,256]{2,1,0:T(8,128)(2,1)S(1)} %copy-done.4, bf16[4,256,256]{2,1,0:T(8,128)(2,1)S(1)} %copy-done.8, f32[8,256]{1,0:T(8,128)S(1)} %copy-done.32), custom_call_target="tpu_custom_call" | custom-call | bytes 3000000 | tf_op jit(solution)/shard_map/pallas_call | solution.py:38
  78.1 3.1 %collective-permute-start.9 = (bf16[9,176,128]{2,1,0:T(8,128)(2,1)S(1)}, bf16[9,176,128]{2,1,0:T(8,128)(2,1)S(1)}, u32[]{:S(2)}, u32[]{:S(2)}) collective-permute-start(bf16[9,176,128]{2,1,0:T(8,128)(2,1)S(1)} %collective-permute-done.8.one_ref), channel_id=1, source_target_pairs={{0,1},{1,2},{2,3},{3,4},{4,5},{5,6},{6,7},{8,9},{9,10},{10,11},{11... | collective-permute-start | bytes 1216520 | tf_op jit(solution)/shard_map/ppermute | solution.py:868
  81.3 1.6 collective-permute-start.19
  83.7 5.7 %shard_map.207 = (bf16[4,256,256]{2,1,0:T(8,128)(2,1)}, f32[4,256,256]{2,1,0:T(8,128)}, f32[4,256,256]{2,1,0:T(8,128)}, bf16[9,176,128]{2,1,0:T(8,128)(2,1)}) custom-call(f32[4,2,256,256]{3,2,1,0:T(8,128)} %copy-done.1, bf16[4,128,256]{2,1,0:T(8,128)(2,1)} %get-tuple-element.132.qk_ref, f32[8,256]{1,0:T(8,128)} %stack.18.masks_ref, ...), custom_call_target="tpu_custom_call" | custom-call | bytes 3000000 | tf_op jit(solution)/shard_map/pallas_call | solution.py:38
  89.4 2.0 copy-done.12
  92.6 1.6 shard_map.209
  97.1 5.2 %collective-permute-done.13.first_ref.refs_2_ = bf16[128,1024]{1,0:T(8,128)(2,1)} collective-permute-done((bf16[128,1024]{1,0:T(8,128)(2,1)}, bf16[128,1024]{1,0:T(8,128)(2,1)}, u32[]{:S(2)}, u32[]{:S(2)}) %collective-permute-start.13) | collective-permute-done | bytes 262176 | tf_op jit(solution)/shard_map/ppermute | solution.py:857
  104.7 1.6 collective-permute-start.15
  108.4 1.8 shard_map.210.dhid_ref
  110.2 3.9 %all-gather.8.cloned.1.call-done = bf16[11008,128]{1,0:T(8,128)(2,1)} async-done(((bf16[1376,128]{1,0:T(8,128)(2,1)}), bf16[11008,128]{1,0:T(8,128)(2,1)}) %all-gather.8.cloned.1.call-update) | async-done | bytes 2818064 | tf_op jit(solution)/shard_map/all_gather | solution.py:1005
  114.1 1.8 copy-done.13
  116.7 3.1 %shard_map.212 = (bf16[256,1024]{1,0:T(8,128)(2,1)S(1)}, bf16[256,688]{1,0:T(8,128)(2,1)S(1)}, bf16[256,688]{1,0:T(8,128)(2,1)S(1)}, bf16[256,688]{1,0:T(8,128)(2,1)S(1)}) custom-call(bf16[128,1024]{1,0:T(8,128)(2,1)} %collective-permute-done.17.first_ref.refs_6_, bf16[128,1024]{1,0:T(8,128)(2,1)} %collective-permute-done.18.second_ref.refs_7_, ...), custom_call_target="tpu_custom_call" | custom-call | bytes 3000000 | tf_op jit(solution)/shard_map/pallas_call | solution.py:38
  119.9 2.4 collective-permute-start.22
  122.3 3.1 %shard_map.213 = (bf16[256,1024]{1,0:T(8,128)(2,1)S(1)}, bf16[256,688]{1,0:T(8,128)(2,1)S(1)}, bf16[256,688]{1,0:T(8,128)(2,1)S(1)}, bf16[256,688]{1,0:T(8,128)(2,1)S(1)}) custom-call(bf16[128,1024]{1,0:T(8,128)(2,1)} %collective-permute-done.15.first_ref.refs_4_, bf16[128,1024]{1,0:T(8,128)(2,1)} %collective-permute-done.16.second_ref.refs_5_, ...), custom_call_target="tpu_custom_call" | custom-call | bytes 3000000 | tf_op jit(solution)/shard_map/pallas_call | solution.py:38
  126.0 3.1 %shard_map.214 = (bf16[256,1024]{1,0:T(8,128)(2,1)S(1)}, bf16[256,688]{1,0:T(8,128)(2,1)S(1)}, bf16[256,688]{1,0:T(8,128)(2,1)S(1)}, bf16[256,688]{1,0:T(8,128)(2,1)S(1)}) custom-call(bf16[128,1024]{1,0:T(8,128)(2,1)} %collective-permute-done.13.first_ref.refs_2_, bf16[128,1024]{1,0:T(8,128)(2,1)} %collective-permute-done.14.second_ref.refs_3_, ...), custom_call_target="tpu_custom_call" | custom-call | bytes 3000000 | tf_op jit(solution)/shard_map/pallas_call | solution.py:38
  129.8 3.1 %shard_map.215 = (bf16[256,1024]{1,0:T(8,128)(2,1)S(1)}, bf16[256,688]{1,0:T(8,128)(2,1)S(1)}, bf16[256,688]{1,0:T(8,128)(2,1)S(1)}, bf16[256,688]{1,0:T(8,128)(2,1)S(1)}) custom-call(bf16[128,1024]{1,0:T(8,128)(2,1)} %get-tuple-element.164.first_ref.refs_0_, bf16[128,1024]{1,0:T(8,128)(2,1)} %get-tuple-element.165.second_ref.refs_1_, ...), custom_call_target="tpu_custom_call" | custom-call | bytes 3000000 | tf_op jit(solution)/shard_map/pallas_call | solution.py:38
  132.9 2.0 shard_map.216
  135.0 1.7 shard_map.217.refs_16_
  136.8 9.4 %collective-permute-done.21.refs_2_ = bf16[256,1024]{1,0:T(8,128)(2,1)S(1)} collective-permute-done((bf16[256,1024]{1,0:T(8,128)(2,1)S(1)}, bf16[256,1024]{1,0:T(8,128)(2,1)S(1)}, u32[]{:S(2)}, u32[]{:S(2)}) %collective-permute-start.21) | collective-permute-done | bytes 524320 | tf_op jit(solution)/shard_map/ppermute | solution.py:834
  148.7 1.7 shard_map.222
  150.6 3.6 %shard_map.219 = (bf16[4,4,256,128]{3,2,1,0:T(8,128)(2,1)S(1)}, bf16[9,176,128]{2,1,0:T(8,128)(2,1)S(1)}) custom-call(bf16[4,256,256]{2,1,0:T(8,128)(2,1)S(1)} %get-tuple-element.185.do_ref, f32[4,256,256]{2,1,0:T(8,128)S(1)} %copy-done.25, f32[4,256,256]{2,1,0:T(8,128)S(1)} %copy-done.26, bf16[4,128,256]{2,1,0:T(8,128)(2,1)S(1)} %copy-done.5, ...), custom_call_target="tpu_custom_call" | custom-call | bytes 3000000 | tf_op jit(solution)/shard_map/pallas_call | solution.py:38
  160.4 5.3 %shard_map.220 = (bf16[4,64,256]{2,1,0:T(8,128)(2,1)S(1)}, f32[4,64,256]{2,1,0:T(8,128)S(1)}, f32[4,256,256]{2,1,0:T(8,128)S(1)}) custom-call(bf16[4,4,256,128]{3,2,1,0:T(8,128)(2,1)S(1)} %get-tuple-element.188.d_ref, bf16[4,128,256]{2,1,0:T(8,128)(2,1)S(1)} %copy-done.5, bf16[4,256,256]{2,1,0:T(8,128)(2,1)S(1)} %copy-done.9, f32[8,256]{1,0:T(8,128)S(1)} %copy-done.33, ...), custom_call_target="tpu_custom_call" | custom-call | bytes 3000000 | tf_op jit(solution)/shard_map/pallas_call | solution.py:38
  169.3 4.7 %shard_map.221 = bf16[8,2064,128]{2,1,0:T(8,128)(2,1)S(1)} custom-call(bf16[128,1024]{1,0:T(8,128)(2,1)} %get-tuple-element.164.first_ref.refs_0_, bf16[128,1024]{1,0:T(8,128)(2,1)} %get-tuple-element.165.second_ref.refs_1_, bf16[128,1024]{1,0:T(8,128)(2,1)} %collective-permute-done.13.first_ref.refs_2_, ...), custom_call_target="tpu_custom_call" | custom-call | bytes 3600000 | tf_op jit(solution)/shard_map/pallas_call | solution.py:38
  174.1 2.0 copy-done
  181.6 10.4 %shard_map.223 = (f32[256,1024]{1,0:T(8,128)}, bf16[4,4,400,128]{3,2,1,0:T(8,128)(2,1)}, bf16[4,4,400,128]{3,2,1,0:T(8,128)(2,1)}, f32[2,1024]{1,0:T(2,128)}) custom-call(s32[6]{0:T(128)} %pad_add_fusion.where_ref, bf16[4,64,256]{2,1,0:T(8,128)(2,1)} %copy-done.38, f32[4,64,256]{2,1,0:T(8,128)} %copy-done.35, f32[4,256,256]{2,1,0:T(8,128)} %copy-done.28, ...), custom_call_target="tpu_custom_call" | custom-call | bytes 6000000 | tf_op jit(solution)/shard_map/pallas_call | solution.py:38
  193.3 1.5 collective-permute-done.24
  197.1 1.6 collective-permute-done.32
  198.6 1.6 fusion.8
  201.0 2.1 collective-permute-start.35
  203.8 2.7 %collective-permute-start.39 = (bf16[256,128]{1,0:T(8,128)(2,1)S(1)}, bf16[256,128]{1,0:T(8,128)(2,1)S(1)}, u32[]{:S(2)}, u32[]{:S(2)}) collective-permute-start(bf16[256,128]{1,0:T(8,128)(2,1)S(1)} %get-tuple-element.346), channel_id=1, source_target_pairs={{0,2},{1,3},{2,0},{3,1},{4,6},{5,7},{6,4},{7,5},{8,10},{9,11},{10,... | collective-permute-start | bytes 196616 | tf_op jit(solution)/shard_map/ppermute | solution.py:874
  206.5 5.0 %collective-permute-done.31 = bf16[256,1024]{1,0:T(8,128)(2,1)} collective-permute-done((bf16[256,1024]{1,0:T(8,128)(2,1)S(1)}, bf16[256,1024]{1,0:T(8,128)(2,1)}, u32[]{:S(2)}, u32[]{:S(2)}) %collective-permute-start.31) | collective-permute-done | bytes 524320 | tf_op jit(solution)/shard_map/ppermute | solution.py:1049
  211.4 3.6 %collective-permute-start.41 = (bf16[256,128]{1,0:T(8,128)(2,1)S(1)}, bf16[256,128]{1,0:T(8,128)(2,1)S(1)}, u32[]{:S(2)}, u32[]{:S(2)}) collective-permute-start(bf16[256,128]{1,0:T(8,128)(2,1)S(1)} %get-tuple-element.347), channel_id=1, source_target_pairs={{0,6},{1,7},{2,4},{3,5},{4,2},{5,3},{6,0},{7,1},{8,14},{9,15},{10,... | collective-permute-start | bytes 196616 | tf_op jit(solution)/shard_map/ppermute | solution.py:874
  215.0 2.3 fusion.3
  217.3 2.8 %collective-permute-done.33 = bf16[4,400,128]{2,1,0:T(8,128)(2,1)S(1)} collective-permute-done((bf16[4,400,128]{2,1,0:T(8,128)(2,1)S(1)}, bf16[4,400,128]{2,1,0:T(8,128)(2,1)S(1)}, u32[]{:S(2)}, u32[]{:S(2)}) %collective-permute-start.33) | collective-permute-done | bytes 409632 | tf_op jit(solution)/shard_map/ppermute | solution.py:834
  220.1 2.9 %collective-permute-start.40 = (bf16[256,128]{1,0:T(8,128)(2,1)S(1)}, bf16[256,128]{1,0:T(8,128)(2,1)S(1)}, u32[]{:S(2)}, u32[]{:S(2)}) collective-permute-start(bf16[256,128]{1,0:T(8,128)(2,1)S(1)} %get-tuple-element.348), channel_id=1, source_target_pairs={{0,4},{1,5},{2,6},{3,7},{4,0},{5,1},{6,2},{7,3},{8,12},{9,13},{10,... | collective-permute-start | bytes 196616 | tf_op jit(solution)/shard_map/ppermute | solution.py:874
  223.0 5.1 %collective-permute-done.35 = bf16[4,400,128]{2,1,0:T(8,128)(2,1)S(1)} collective-permute-done((bf16[4,400,128]{2,1,0:T(8,128)(2,1)S(1)}, bf16[4,400,128]{2,1,0:T(8,128)(2,1)S(1)}, u32[]{:S(2)}, u32[]{:S(2)}) %collective-permute-start.35) | collective-permute-done | bytes 409632 | tf_op jit(solution)/shard_map/ppermute | solution.py:834
  229.3 2.4 collective-permute-start.36
  231.8 1.6 collective-permute-start.38
  235.0 4.1 %collective-permute-done.38 = bf16[400,128]{1,0:T(8,128)(2,1)S(1)} collective-permute-done((bf16[400,128]{1,0:T(8,128)(2,1)S(1)}, bf16[400,128]{1,0:T(8,128)(2,1)S(1)}, u32[]{:S(2)}, u32[]{:S(2)}) %collective-permute-start.38) | collective-permute-done | bytes 102432 | tf_op jit(solution)/shard_map/ppermute | solution.py:874
  239.1 4.0 %collective-permute-done.37 = bf16[400,128]{1,0:T(8,128)(2,1)S(1)} collective-permute-done((bf16[400,128]{1,0:T(8,128)(2,1)S(1)}, bf16[400,128]{1,0:T(8,128)(2,1)S(1)}, u32[]{:S(2)}, u32[]{:S(2)}) %collective-permute-start.37) | collective-permute-done | bytes 102432 | tf_op jit(solution)/shard_map/ppermute | solution.py:874
  (233 shorter events, 59.2 us)
Async XLA Ops:
  7.2 82.2 %all-gather.6.cloned.1.call-start = ((), (), s32[]{:S(2)}) async-start(), calls=%async_computation.2 | async-start | bytes 3944448 | tf_op jit(solution)/shard_map/all_gather | solution.py:947
  7.2 27.1 %collective-permute-start.11 = (bf16[256,128]{1,0:T(8,128)(2,1)}, bf16[256,128]{1,0:T(8,128)(2,1)S(1)}, u32[]{:S(2)}, u32[]{:S(2)}) collective-permute-start(bf16[256,128]{1,0:T(8,128)(2,1)} %param.17), channel_id=1, source_target_pairs={{0,16},{8,24},{16,0},{24,8},{1,17},{9,25},{17,1},{25,9},{2,18},{10... | collective-permute-start | bytes 196616 | tf_op jit(solution)/shard_map/ppermute | solution.py:834
  10.3 24.1 %collective-permute-start.10 = (bf16[256,128]{1,0:T(8,128)(2,1)}, bf16[256,128]{1,0:T(8,128)(2,1)S(1)}, u32[]{:S(2)}, u32[]{:S(2)}) collective-permute-start(bf16[256,128]{1,0:T(8,128)(2,1)} %param.17), channel_id=1, source_target_pairs={{0,8},{8,0},{16,24},{24,16},{1,9},{9,1},{17,25},{25,17},{2,10},{10... | collective-permute-start | bytes 196616 | tf_op jit(solution)/shard_map/ppermute | solution.py:834
  11.8 22.6 %collective-permute-start.12 = (bf16[256,128]{1,0:T(8,128)(2,1)}, bf16[256,128]{1,0:T(8,128)(2,1)S(1)}, u32[]{:S(2)}, u32[]{:S(2)}) collective-permute-start(bf16[256,128]{1,0:T(8,128)(2,1)} %param.17), channel_id=1, source_target_pairs={{0,24},{8,16},{16,8},{24,0},{1,25},{9,17},{17,9},{25,1},{2,26},{10... | collective-permute-start | bytes 196616 | tf_op jit(solution)/shard_map/ppermute | solution.py:834
  11.8 22.6 %collective-permute-start.1 = (bf16[256,1024]{1,0:T(8,128)(2,1)}, bf16[256,1024]{1,0:T(8,128)(2,1)S(1)}, u32[]{:S(2)}, u32[]{:S(2)}) collective-permute-start(bf16[256,1024]{1,0:T(8,128)(2,1)} %bitcast.96), channel_id=1, source_target_pairs={{0,16},{8,24},{16,0},{24,8},{1,17},{9,25},{17,1},{25,9},{2,18},{10... | collective-permute-start | bytes 1572872 | tf_op jit(solution)/shard_map/ppermute | solution.py:930
  13.7 20.7 %collective-permute-start = (bf16[256,1024]{1,0:T(8,128)(2,1)}, bf16[256,1024]{1,0:T(8,128)(2,1)S(1)}, u32[]{:S(2)}, u32[]{:S(2)}) collective-permute-start(bf16[256,1024]{1,0:T(8,128)(2,1)} %bitcast.97), channel_id=1, source_target_pairs={{0,8},{8,0},{16,24},{24,16},{1,9},{9,1},{17,25},{25,17},{2,10},{10... | collective-permute-start | bytes 1572872 | tf_op jit(solution)/shard_map/ppermute | solution.py:930
  34.4 34.1 %copy-start.14 = (bf16[256,1024]{1,0:T(8,128)(2,1)}, bf16[256,1024]{1,0:T(8,128)(2,1)S(1)}, u32[]{:S(2)}) copy-start(bf16[256,1024]{1,0:T(8,128)(2,1)S(1)} %collective-permute-done.1.refs_2_.refs_6_) | copy-start | bytes 1572868
  34.5 34.1 %copy-start.17 = (bf16[256,1024]{1,0:T(8,128)(2,1)}, bf16[256,1024]{1,0:T(8,128)(2,1)S(1)}, u32[]{:S(2)}) copy-start(bf16[256,1024]{1,0:T(8,128)(2,1)S(1)} %collective-permute-done.refs_1_.refs_5_) | copy-start | bytes 1572868
  35.4 25.2 %copy-start.47 = (bf16[4,400,128]{2,1,0:T(8,128)(2,1)}, bf16[4,400,128]{2,1,0:T(8,128)(2,1)S(1)}, u32[]{:S(2)}) copy-start(bf16[4,400,128]{2,1,0:T(8,128)(2,1)S(1)} %get-tuple-element.122.refs_0_) | copy-start | bytes 1228804
  36.3 77.8 %all-gather.8.cloned.1.call-start = ((), (), s32[]{:S(2)}) async-start(), calls=%async_computation.3 | async-start | bytes 3170304 | tf_op jit(solution)/shard_map/all_gather | solution.py:1005
  36.3 20.6 %collective-permute-start.6 = (bf16[4,400,128]{2,1,0:T(8,128)(2,1)S(1)}, bf16[4,400,128]{2,1,0:T(8,128)(2,1)S(1)}, u32[]{:S(2)}, u32[]{:S(2)}) collective-permute-start(bf16[4,400,128]{2,1,0:T(8,128)(2,1)S(1)} %get-tuple-element.122.refs_0_), channel_id=1, source_target_pairs={{0,24},{8,16},{16,8},{24,0},{1,25},{9,17},{17,9},{25,1},{2,26},{10... | collective-permute-start | bytes 1228808 | tf_op jit(solution)/shard_map/ppermute | solution.py:834
  36.9 20.2 %collective-permute-start.4 = (bf16[4,400,128]{2,1,0:T(8,128)(2,1)S(1)}, bf16[4,400,128]{2,1,0:T(8,128)(2,1)S(1)}, u32[]{:S(2)}, u32[]{:S(2)}) collective-permute-start(bf16[4,400,128]{2,1,0:T(8,128)(2,1)S(1)} %get-tuple-element.122.refs_0_), channel_id=1, source_target_pairs={{0,16},{8,24},{16,0},{24,8},{1,17},{9,25},{17,1},{25,9},{2,18},{10... | collective-permute-start | bytes 1228808 | tf_op jit(solution)/shard_map/ppermute | solution.py:834
  38.4 18.5 %collective-permute-start.2 = (bf16[4,400,128]{2,1,0:T(8,128)(2,1)S(1)}, bf16[4,400,128]{2,1,0:T(8,128)(2,1)S(1)}, u32[]{:S(2)}, u32[]{:S(2)}) collective-permute-start(bf16[4,400,128]{2,1,0:T(8,128)(2,1)S(1)} %get-tuple-element.122.refs_0_), channel_id=1, source_target_pairs={{0,8},{8,0},{16,24},{24,16},{1,9},{9,1},{17,25},{25,17},{2,10},{10... | collective-permute-start | bytes 1228808 | tf_op jit(solution)/shard_map/ppermute | solution.py:834
  56.9 1.8 collective-permute-start.7
  57.1 2.3 collective-permute-start.5
  57.5 2.5 collective-permute-start.3
  68.6 9.5 %collective-permute-start.8 = (bf16[9,176,128]{2,1,0:T(8,128)(2,1)}, bf16[9,176,128]{2,1,0:T(8,128)(2,1)S(1)}, u32[]{:S(2)}, u32[]{:S(2)}) collective-permute-start(bf16[9,176,128]{2,1,0:T(8,128)(2,1)} %get-tuple-element.134), channel_id=1, source_target_pairs={{0,1},{1,2},{2,3},{3,4},{4,5},{5,6},{6,7},{8,9},{9,10},{10,11},{11... | collective-permute-start | bytes 1216520 | tf_op jit(solution)/shard_map/ppermute | solution.py:868
  78.1 167.1 %reduce-scatter.2.cloned.1.call-start = ((), (), s32[]{:S(2)}) async-start(), calls=%async_computation.1 | async-start | bytes 4755456 | tf_op jit(solution)/shard_map/reduce_scatter | solution.py:1042
  78.1 4.8 %collective-permute-start.9 = (bf16[9,176,128]{2,1,0:T(8,128)(2,1)S(1)}, bf16[9,176,128]{2,1,0:T(8,128)(2,1)S(1)}, u32[]{:S(2)}, u32[]{:S(2)}) collective-permute-start(bf16[9,176,128]{2,1,0:T(8,128)(2,1)S(1)} %collective-permute-done.8.one_ref), channel_id=1, source_target_pairs={{0,1},{1,2},{2,3},{3,4},{4,5},{5,6},{6,7},{8,9},{9,10},{10,11},{11... | collective-permute-start | bytes 1216520 | tf_op jit(solution)/shard_map/ppermute | solution.py:868
  81.3 25.3 %collective-permute-start.19 = (bf16[256,1024]{1,0:T(8,128)(2,1)S(1)}, bf16[256,1024]{1,0:T(8,128)(2,1)S(1)}, u32[]{:S(2)}, u32[]{:S(2)}) collective-permute-start(bf16[256,1024]{1,0:T(8,128)(2,1)S(1)} %bitcast.98), channel_id=1, source_target_pairs={{0,24},{8,16},{16,8},{24,0},{1,25},{9,17},{17,9},{25,1},{2,26},{10... | collective-permute-start | bytes 1572872 | tf_op jit(solution)/shard_map/ppermute | solution.py:1000
  95.2 7.1 %collective-permute-start.13 = (bf16[128,1024]{1,0:T(8,128)(2,1)}, bf16[128,1024]{1,0:T(8,128)(2,1)}, u32[]{:S(2)}, u32[]{:S(2)}) collective-permute-start(bf16[128,1024]{1,0:T(8,128)(2,1)} %get-tuple-element.164.first_ref.refs_0_), channel_id=1, source_target_pairs={{0,8},{8,0},{16,24},{24,16},{1,9},{9,1},{17,25},{25,17},{2,10},{10... | collective-permute-start | bytes 786440 | tf_op jit(solution)/shard_map/ppermute | solution.py:857
  96.6 7.8 %collective-permute-start.16 = (bf16[128,1024]{1,0:T(8,128)(2,1)}, bf16[128,1024]{1,0:T(8,128)(2,1)}, u32[]{:S(2)}, u32[]{:S(2)}) collective-permute-start(bf16[128,1024]{1,0:T(8,128)(2,1)} %get-tuple-element.165.second_ref.refs_1_), channel_id=1, source_target_pairs={{0,16},{8,24},{16,0},{24,8},{1,17},{9,25},{17,1},{25,9},{2,18},{10... | collective-permute-start | bytes 786440 | tf_op jit(solution)/shard_map/ppermute | solution.py:857
  102.3 14.4 %collective-permute-start.17 = (bf16[128,1024]{1,0:T(8,128)(2,1)}, bf16[128,1024]{1,0:T(8,128)(2,1)}, u32[]{:S(2)}, u32[]{:S(2)}) collective-permute-start(bf16[128,1024]{1,0:T(8,128)(2,1)} %collective-permute-done.13.first_ref.refs_2_), channel_id=1, source_target_pairs={{0,16},{8,24},{16,0},{24,8},{1,17},{9,25},{17,1},{25,9},{2,18},{10... | collective-permute-start | bytes 786440 | tf_op jit(solution)/shard_map/ppermute | solution.py:857
  104.5 12.2 %collective-permute-start.18 = (bf16[128,1024]{1,0:T(8,128)(2,1)}, bf16[128,1024]{1,0:T(8,128)(2,1)}, u32[]{:S(2)}, u32[]{:S(2)}) collective-permute-start(bf16[128,1024]{1,0:T(8,128)(2,1)} %collective-permute-done.16.second_ref.refs_5_), channel_id=1, source_target_pairs={{0,8},{8,0},{16,24},{24,16},{1,9},{9,1},{17,25},{25,17},{2,10},{10... | collective-permute-start | bytes 786440 | tf_op jit(solution)/shard_map/ppermute | solution.py:857
  104.7 15.2 %collective-permute-start.15 = (bf16[128,1024]{1,0:T(8,128)(2,1)}, bf16[128,1024]{1,0:T(8,128)(2,1)}, u32[]{:S(2)}, u32[]{:S(2)}) collective-permute-start(bf16[128,1024]{1,0:T(8,128)(2,1)} %get-tuple-element.164.first_ref.refs_0_), channel_id=1, source_target_pairs={{0,16},{8,24},{16,0},{24,8},{1,17},{9,25},{17,1},{25,9},{2,18},{10... | collective-permute-start | bytes 786440 | tf_op jit(solution)/shard_map/ppermute | solution.py:857
  106.2 19.2 %collective-permute-start.14 = (bf16[128,1024]{1,0:T(8,128)(2,1)}, bf16[128,1024]{1,0:T(8,128)(2,1)}, u32[]{:S(2)}, u32[]{:S(2)}) collective-permute-start(bf16[128,1024]{1,0:T(8,128)(2,1)} %get-tuple-element.165.second_ref.refs_1_), channel_id=1, source_target_pairs={{0,8},{8,0},{16,24},{24,16},{1,9},{9,1},{17,25},{25,17},{2,10},{10... | collective-permute-start | bytes 786440 | tf_op jit(solution)/shard_map/ppermute | solution.py:857
  119.9 16.9 %collective-permute-start.22 = (bf16[256,1024]{1,0:T(8,128)(2,1)S(1)}, bf16[256,1024]{1,0:T(8,128)(2,1)S(1)}, u32[]{:S(2)}, u32[]{:S(2)}) collective-permute-start(bf16[256,1024]{1,0:T(8,128)(2,1)S(1)} %get-tuple-element.169), channel_id=1, source_target_pairs={{0,24},{8,16},{16,8},{24,0},{1,25},{9,17},{17,9},{25,1},{2,26},{10... | collective-permute-start | bytes 1572872 | tf_op jit(solution)/shard_map/ppermute | solution.py:834
  125.4 20.7 %collective-permute-start.21 = (bf16[256,1024]{1,0:T(8,128)(2,1)S(1)}, bf16[256,1024]{1,0:T(8,128)(2,1)S(1)}, u32[]{:S(2)}, u32[]{:S(2)}) collective-permute-start(bf16[256,1024]{1,0:T(8,128)(2,1)S(1)} %get-tuple-element.168), channel_id=1, source_target_pairs={{0,16},{8,24},{16,0},{24,8},{1,17},{9,25},{17,1},{25,9},{2,18},{10... | collective-permute-start | bytes 1572872 | tf_op jit(solution)/shard_map/ppermute | solution.py:834
  129.2 17.0 %collective-permute-start.20 = (bf16[256,1024]{1,0:T(8,128)(2,1)S(1)}, bf16[256,1024]{1,0:T(8,128)(2,1)S(1)}, u32[]{:S(2)}, u32[]{:S(2)}) collective-permute-start(bf16[256,1024]{1,0:T(8,128)(2,1)S(1)} %get-tuple-element.167), channel_id=1, source_target_pairs={{0,8},{8,0},{16,24},{24,16},{1,9},{9,1},{17,25},{25,17},{2,10},{10... | collective-permute-start | bytes 1572872 | tf_op jit(solution)/shard_map/ppermute | solution.py:834
  150.4 5.2 %collective-permute-start.27 = (bf16[4,4,256,128]{3,2,1,0:T(8,128)(2,1)S(1)}, bf16[4,4,256,128]{3,2,1,0:T(8,128)(2,1)S(1)}, u32[]{:S(2)}, u32[]{:S(2)}) collective-permute-start(bf16[4,4,256,128]{3,2,1,0:T(8,128)(2,1)S(1)} %get-tuple-element.215), channel_id=1, source_target_pairs={{0,1},{1,0},{2,3},{3,2},{4,5},{5,4},{6,7},{7,6},{8,9},{9,8},{10,11... | collective-permute-start | bytes 3145736 | tf_op jit(solution)/shard_map/ppermute | solution.py:1037
  154.2 13.8 %collective-permute-start.25 = (bf16[9,176,128]{2,1,0:T(8,128)(2,1)S(1)}, bf16[9,176,128]{2,1,0:T(8,128)(2,1)S(1)}, u32[]{:S(2)}, u32[]{:S(2)}) collective-permute-start(bf16[9,176,128]{2,1,0:T(8,128)(2,1)S(1)} %get-tuple-element.202), channel_id=1, source_target_pairs={{1,0},{2,1},{3,2},{4,3},{5,4},{6,5},{7,6},{9,8},{10,9},{11,10},{12... | collective-permute-start | bytes 1216520 | tf_op jit(solution)/shard_map/ppermute | solution.py:868
  156.9 19.2 %collective-permute-start.28 = (bf16[4,256,128]{2,1,0:T(8,128)(2,1)}, bf16[4,256,128]{2,1,0:T(8,128)(2,1)}, u32[]{:S(2)}, u32[]{:S(2)}) collective-permute-start(bf16[4,256,128]{2,1,0:T(8,128)(2,1)} %get-tuple-element.335), channel_id=1, source_target_pairs={{0,8},{8,0},{16,24},{24,16},{1,9},{9,1},{17,25},{25,17},{2,10},{10... | collective-permute-start | bytes 786440 | tf_op jit(solution)/shard_map/ppermute | solution.py:834
  158.3 17.8 %collective-permute-start.30 = (bf16[4,256,128]{2,1,0:T(8,128)(2,1)}, bf16[4,256,128]{2,1,0:T(8,128)(2,1)}, u32[]{:S(2)}, u32[]{:S(2)}) collective-permute-start(bf16[4,256,128]{2,1,0:T(8,128)(2,1)} %get-tuple-element.336), channel_id=1, source_target_pairs={{0,24},{8,16},{16,8},{24,0},{1,25},{9,17},{17,9},{25,1},{2,26},{10... | collective-permute-start | bytes 786440 | tf_op jit(solution)/shard_map/ppermute | solution.py:834
  159.8 16.3 %collective-permute-start.29 = (bf16[4,256,128]{2,1,0:T(8,128)(2,1)}, bf16[4,256,128]{2,1,0:T(8,128)(2,1)}, u32[]{:S(2)}, u32[]{:S(2)}) collective-permute-start(bf16[4,256,128]{2,1,0:T(8,128)(2,1)} %get-tuple-element.337), channel_id=1, source_target_pairs={{0,16},{8,24},{16,0},{24,8},{1,17},{9,25},{17,1},{25,9},{2,18},{10... | collective-permute-start | bytes 786440 | tf_op jit(solution)/shard_map/ppermute | solution.py:834
  168.0 9.5 %collective-permute-start.26 = (bf16[9,176,128]{2,1,0:T(8,128)(2,1)S(1)}, bf16[9,176,128]{2,1,0:T(8,128)(2,1)S(1)}, u32[]{:S(2)}, u32[]{:S(2)}) collective-permute-start(bf16[9,176,128]{2,1,0:T(8,128)(2,1)S(1)} %collective-permute-done.25.one_ref), channel_id=1, source_target_pairs={{1,0},{2,1},{3,2},{4,3},{5,4},{6,5},{7,6},{9,8},{10,9},{11,10},{12... | collective-permute-start | bytes 1216520 | tf_op jit(solution)/shard_map/ppermute | solution.py:868
  178.7 14.6 %collective-permute-start.23 = (bf16[256,1024]{1,0:T(8,128)(2,1)S(1)}, bf16[256,1024]{1,0:T(8,128)(2,1)S(1)}, u32[]{:S(2)}, u32[]{:S(2)}) collective-permute-start(bf16[256,1024]{1,0:T(8,128)(2,1)S(1)} %copy-done.46), channel_id=1, source_target_pairs={{0,8},{8,0},{16,24},{24,16},{1,9},{9,1},{17,25},{25,17},{2,10},{10... | collective-permute-start | bytes 1572872 | tf_op jit(solution)/shard_map/ppermute | solution.py:1046
  180.1 14.7 %collective-permute-start.24 = (bf16[256,1024]{1,0:T(8,128)(2,1)S(1)}, bf16[256,1024]{1,0:T(8,128)(2,1)S(1)}, u32[]{:S(2)}, u32[]{:S(2)}) collective-permute-start(bf16[256,1024]{1,0:T(8,128)(2,1)S(1)} %copy-done.44), channel_id=1, source_target_pairs={{0,16},{8,24},{16,0},{24,8},{1,17},{9,25},{17,1},{25,9},{2,18},{10... | collective-permute-start | bytes 1572872 | tf_op jit(solution)/shard_map/ppermute | solution.py:1046
  194.8 3.8 %collective-permute-start.32 = (bf16[4,4,400,128]{3,2,1,0:T(8,128)(2,1)}, bf16[4,4,400,128]{3,2,1,0:T(8,128)(2,1)S(1)}, u32[]{:S(2)}, u32[]{:S(2)}) collective-permute-start(bf16[4,4,400,128]{3,2,1,0:T(8,128)(2,1)} %get-tuple-element.228), channel_id=1, source_target_pairs={{0,1},{1,0},{2,3},{3,2},{4,5},{5,4},{6,7},{7,6},{8,9},{9,8},{10,11... | collective-permute-start | bytes 4915208 | tf_op jit(solution)/shard_map/ppermute | solution.py:1037
  195.6 15.8 %collective-permute-start.31 = (bf16[256,1024]{1,0:T(8,128)(2,1)S(1)}, bf16[256,1024]{1,0:T(8,128)(2,1)}, u32[]{:S(2)}, u32[]{:S(2)}) collective-permute-start(bf16[256,1024]{1,0:T(8,128)(2,1)S(1)} %copy-done.42), channel_id=1, source_target_pairs={{0,24},{8,16},{16,8},{24,0},{1,25},{9,17},{17,9},{25,1},{2,26},{10... | collective-permute-start | bytes 1572872 | tf_op jit(solution)/shard_map/ppermute | solution.py:1049
  200.2 19.9 %collective-permute-start.33 = (bf16[4,400,128]{2,1,0:T(8,128)(2,1)S(1)}, bf16[4,400,128]{2,1,0:T(8,128)(2,1)S(1)}, u32[]{:S(2)}, u32[]{:S(2)}) collective-permute-start(bf16[4,400,128]{2,1,0:T(8,128)(2,1)S(1)} %get-tuple-element.332), channel_id=1, source_target_pairs={{0,8},{8,0},{16,24},{24,16},{1,9},{9,1},{17,25},{25,17},{2,10},{10... | collective-permute-start | bytes 1228808 | tf_op jit(solution)/shard_map/ppermute | solution.py:834
  201.0 27.1 %collective-permute-start.35 = (bf16[4,400,128]{2,1,0:T(8,128)(2,1)S(1)}, bf16[4,400,128]{2,1,0:T(8,128)(2,1)S(1)}, u32[]{:S(2)}, u32[]{:S(2)}) collective-permute-start(bf16[4,400,128]{2,1,0:T(8,128)(2,1)S(1)} %get-tuple-element.333), channel_id=1, source_target_pairs={{0,24},{8,16},{16,8},{24,0},{1,25},{9,17},{17,9},{25,1},{2,26},{10... | collective-permute-start | bytes 1228808 | tf_op jit(solution)/shard_map/ppermute | solution.py:834
  203.1 24.9 %collective-permute-start.34 = (bf16[4,400,128]{2,1,0:T(8,128)(2,1)S(1)}, bf16[4,400,128]{2,1,0:T(8,128)(2,1)S(1)}, u32[]{:S(2)}, u32[]{:S(2)}) collective-permute-start(bf16[4,400,128]{2,1,0:T(8,128)(2,1)S(1)} %get-tuple-element.334), channel_id=1, source_target_pairs={{0,16},{8,24},{16,0},{24,8},{1,17},{9,25},{17,1},{25,9},{2,18},{10... | collective-permute-start | bytes 1228808 | tf_op jit(solution)/shard_map/ppermute | solution.py:834
  203.8 29.6 %collective-permute-start.39 = (bf16[256,128]{1,0:T(8,128)(2,1)S(1)}, bf16[256,128]{1,0:T(8,128)(2,1)S(1)}, u32[]{:S(2)}, u32[]{:S(2)}) collective-permute-start(bf16[256,128]{1,0:T(8,128)(2,1)S(1)} %get-tuple-element.346), channel_id=1, source_target_pairs={{0,2},{1,3},{2,0},{3,1},{4,6},{5,7},{6,4},{7,5},{8,10},{9,11},{10,... | collective-permute-start | bytes 196616 | tf_op jit(solution)/shard_map/ppermute | solution.py:874
  211.4 21.9 %collective-permute-start.41 = (bf16[256,128]{1,0:T(8,128)(2,1)S(1)}, bf16[256,128]{1,0:T(8,128)(2,1)S(1)}, u32[]{:S(2)}, u32[]{:S(2)}) collective-permute-start(bf16[256,128]{1,0:T(8,128)(2,1)S(1)} %get-tuple-element.347), channel_id=1, source_target_pairs={{0,6},{1,7},{2,4},{3,5},{4,2},{5,3},{6,0},{7,1},{8,14},{9,15},{10,... | collective-permute-start | bytes 196616 | tf_op jit(solution)/shard_map/ppermute | solution.py:874
  220.1 13.3 %collective-permute-start.40 = (bf16[256,128]{1,0:T(8,128)(2,1)S(1)}, bf16[256,128]{1,0:T(8,128)(2,1)S(1)}, u32[]{:S(2)}, u32[]{:S(2)}) collective-permute-start(bf16[256,128]{1,0:T(8,128)(2,1)S(1)} %get-tuple-element.348), channel_id=1, source_target_pairs={{0,4},{1,5},{2,6},{3,7},{4,0},{5,1},{6,2},{7,3},{8,12},{9,13},{10,... | collective-permute-start | bytes 196616 | tf_op jit(solution)/shard_map/ppermute | solution.py:874
  229.3 5.7 %collective-permute-start.36 = (bf16[400,128]{1,0:T(8,128)(2,1)S(1)}, bf16[400,128]{1,0:T(8,128)(2,1)S(1)}, u32[]{:S(2)}, u32[]{:S(2)}) collective-permute-start(bf16[400,128]{1,0:T(8,128)(2,1)S(1)} %get-tuple-element.343), channel_id=1, source_target_pairs={{0,2},{1,3},{2,0},{3,1},{4,6},{5,7},{6,4},{7,5},{8,10},{9,11},{10,... | collective-permute-start | bytes 307208 | tf_op jit(solution)/shard_map/ppermute | solution.py:874
  231.8 7.3 %collective-permute-start.38 = (bf16[400,128]{1,0:T(8,128)(2,1)S(1)}, bf16[400,128]{1,0:T(8,128)(2,1)S(1)}, u32[]{:S(2)}, u32[]{:S(2)}) collective-permute-start(bf16[400,128]{1,0:T(8,128)(2,1)S(1)} %get-tuple-element.344), channel_id=1, source_target_pairs={{0,6},{1,7},{2,4},{3,5},{4,2},{5,3},{6,0},{7,1},{8,14},{9,15},{10,... | collective-permute-start | bytes 307208 | tf_op jit(solution)/shard_map/ppermute | solution.py:874
  233.3 9.8 %collective-permute-start.37 = (bf16[400,128]{1,0:T(8,128)(2,1)S(1)}, bf16[400,128]{1,0:T(8,128)(2,1)S(1)}, u32[]{:S(2)}, u32[]{:S(2)}) collective-permute-start(bf16[400,128]{1,0:T(8,128)(2,1)S(1)} %get-tuple-element.345), channel_id=1, source_target_pairs={{0,4},{1,5},{2,6},{3,7},{4,0},{5,1},{6,2},{7,3},{8,12},{9,13},{10,... | collective-permute-start | bytes 307208 | tf_op jit(solution)/shard_map/ppermute | solution.py:874
  (60 other events, 310.2 us)
Sparse Core Ops, SparseCore 0:
  36.4 40.0 all-gather.5
  78.7 35.3 all-gather.7
  177.7 56.7 reduce-scatter.1
